TPU v7x, 32 devices: a whole 2x2x4 slice. The times are simulated.
32 devices in a mesh: batch: 2 (over y), seq: 4 (over x, core), kv: 4 (over z).
Axes of the slice: x: 2, y: 2, z: 4, core: 2. Of those that a mesh axis runs over, the one named last changes fastest.
Arguments:
- tokens: bfloat16 [4, 2048, 1536], P('batch', ('seq', 'kv')), may hold values from -6 to 6
- cotangent: bfloat16 [4, 2048, 1536], P('batch', ('seq', 'kv')), may hold values from -6 to 6
- segments: int32 [4, 2048], P('batch', 'seq'), may hold values from 0 to 2, as said below
- positions: int32 [4, 2048], P('batch', 'seq'), may hold values from 0 to 1535, as said below
- norm_in: float32 [1, 1536], P(None, ('batch', 'seq', 'kv')), may hold values from 0.5 to 1.5
- w_query: bfloat16 [1, 1536, 1536], P(None, ('batch', 'seq'), 'kv'), may hold values from -0.15625 to 0.15625
- w_key: bfloat16 [1, 1536, 768], P(None, ('batch', 'seq'), 'kv'), may hold values from -0.15625 to 0.15625
- w_value: bfloat16 [1, 1536, 768], P(None, ('batch', 'seq'), 'kv'), may hold values from -0.15625 to 0.15625
- w_out: bfloat16 [1, 1536, 1536], P(None, 'kv', ('batch', 'seq')), may hold values from -0.75 to 0.75
- norm_mid: float32 [1, 1536], P(None, ('batch', 'seq', 'kv')), may hold values from 0.5 to 1.5
- w_gate: bfloat16 [1, 1536, 4096], P(None, ('batch', 'seq'), 'kv'), may hold values from -0.15625 to 0.15625
- w_up: bfloat16 [1, 1536, 4096], P(None, ('batch', 'seq'), 'kv'), may hold values from -0.15625 to 0.15625
- w_down: bfloat16 [1, 4096, 1536], P(None, 'kv', ('batch', 'seq')), may hold values from -0.09375 to 0.09375
Outputs:
- out: float32 [4, 2048, 1536], P('batch', ('seq', 'kv'))
- grad_tokens: float32 [4, 2048, 1536], P('batch', ('seq', 'kv'))
- grad_norm_in: float32 [1, 1536], P(None, ('batch', 'seq', 'kv'))
- grad_w_query: float32 [1, 1536, 1536], P(None, ('batch', 'seq'), 'kv')
- grad_w_key: float32 [1, 1536, 768], P(None, ('batch', 'seq'), 'kv')
- grad_w_value: float32 [1, 1536, 768], P(None, ('batch', 'seq'), 'kv')
- grad_w_out: float32 [1, 1536, 1536], P(None, 'kv', ('batch', 'seq'))
- grad_norm_mid: float32 [1, 1536], P(None, ('batch', 'seq', 'kv'))
- grad_w_gate: float32 [1, 1536, 4096], P(None, ('batch', 'seq'), 'kv')
- grad_w_up: float32 [1, 1536, 4096], P(None, ('batch', 'seq'), 'kv')
- grad_w_down: float32 [1, 4096, 1536], P(None, 'kv', ('batch', 'seq'))
Inputs may be any that keep to these rules, and one draw needn't show every extreme that they name: `segments`: each row holds three documents with ids 0, 1, 2 in order; document 1 begins within the first 256 tokens of the row and is exactly 1536 tokens long, so document 2 begins within its last quarter. `positions`: the place of a token in its document, counted from 0.
All inputs are finite; a program needn't handle non-finite values.
Results may differ from a plain program's by a relative error of at most 0.02.
Values may be sent and summed in bfloat16 or wider, within the bound.
No kernel may reach another device: no remote copies, remote signals or barrier semaphores. Data moves between devices by JAX's collectives and lax.ppermute only.
A program may use at most 128 MiB of HBM per device.

v0:
```python
from functools import partial
import math

import jax
import jax.numpy as jnp
from jax import lax
from jax.sharding import PartitionSpec as P

HD = 96
LAYERS = 1


EPS = 1e-05
THETA = 100000.0
BIG_NEG = -1e30


def rotary(positions_row):
    half_width = HD // 2
    frequency = THETA ** (-(2.0 * jnp.arange(half_width, dtype=jnp.float32)) / HD)
    angles = positions_row.astype(jnp.float32)[:, None] * frequency[None, :]
    cosine = jnp.concatenate([jnp.cos(angles), jnp.cos(angles)], axis=1)
    sine_table = jnp.concatenate([jnp.sin(angles), jnp.sin(angles)], axis=1)
    return (cosine, sine_table)


def rotate(head_vals, cosine, sine_table):
    half_width = head_vals.shape[-1] // 2
    swapped = jnp.concatenate([-head_vals[..., half_width:], head_vals[..., :half_width]], axis=-1)
    return head_vals * cosine[:, None, :] + swapped * sine_table[:, None, :]


def rms_norm(stream, gain):
    factor = lax.rsqrt(jnp.mean(stream * stream, axis=-1, keepdims=True) + EPS)
    return (stream * factor * gain, factor)


def norm_back(stream, factor, gain, upstream):
    scaled_grad = upstream * gain
    inner_mean = jnp.mean(scaled_grad * stream, axis=-1, keepdims=True)
    grad_stream = factor * scaled_grad - stream * factor**3 * inner_mean
    return (grad_stream, jnp.sum(upstream * stream * factor, axis=0))


def key_width(key_count):
    return math.gcd(key_count, 1024)


def contract(left_side, right_side, left_dim, right_dim):
    return lax.dot_general(
        left_side,
        right_side,
        (((left_dim,), (right_dim,)), ((), ())),
        preferred_element_type=jnp.float32,
    )


def spread(shard_rows):
    return lax.all_gather(shard_rows, "kv", axis=0, tiled=True)


def token_sum(pairs):
    summed = None
    for left_part, right_part, right_dim in pairs:
        product = contract(left_part, right_part, 1, right_dim)
        summed = product if summed is None else summed + product
    return lax.psum_scatter(
        summed.astype(jnp.bfloat16), "kv", scatter_dimension=0, tiled=True
    ).astype(jnp.float32)


def split_block(kv_both, seg_keys, offset, step_width, kv_local, head_size):
    kv_block = lax.dynamic_slice_in_dim(kv_both, offset, step_width, 0)
    key_block = kv_block[:, : kv_local * head_size].reshape(step_width, kv_local, head_size)
    value_block = kv_block[:, kv_local * head_size :].reshape(step_width, kv_local, head_size)
    seg_block = lax.dynamic_slice_in_dim(seg_keys, offset, step_width, 0)
    return (key_block, value_block, seg_block)


def forward_row(queries, seg_query, fold_state, kv_both, seg_keys, first_query, key_start):
    key_count = kv_both.shape[0]
    step_width = key_width(key_count)
    query_count, kv_local, group_size, head_size = queries.shape
    query_index = first_query + jnp.arange(query_count, dtype=jnp.int32)
    score_scale = head_size ** (-0.5)

    def forward_one_step(step_index, inner_state):
        running_max, weight_total, value_total = inner_state
        offset = step_index * step_width
        key_block, value_block, seg_block = split_block(
            kv_both, seg_keys, offset, step_width, kv_local, head_size
        )
        key_index = offset + jnp.arange(step_width, dtype=jnp.int32)
        allowed = (seg_query[:, None] == seg_block[None, :]) & (
            key_index[None, :] <= query_index[:, None]
        )
        scores = (
            jnp.einsum("qkgd,pkd->kgqp", queries, key_block, preferred_element_type=jnp.float32)
            * score_scale
        )
        scores = jnp.where(allowed, scores, BIG_NEG)
        new_max = jnp.maximum(running_max, jnp.max(scores, axis=-1))
        weights = jnp.where(allowed, jnp.exp(scores - new_max[..., None]), 0.0)
        rescale = jnp.exp(running_max - new_max)
        weight_total = rescale * weight_total + jnp.sum(weights, axis=-1)
        update = jnp.einsum(
            "kgqp,pkd->qkgd",
            weights.astype(jnp.bfloat16),
            value_block,
            preferred_element_type=jnp.float32,
        )
        value_total = jnp.transpose(rescale, (2, 0, 1))[..., None] * value_total + update
        return (new_max, weight_total, value_total)

    return lax.fori_loop(0, key_count // step_width, forward_one_step, fold_state)


def forward_fold(queries, seg_query, first_query, fold_state, pieces, key_start):
    kv_both, seg_keys = pieces
    row_fn = partial(forward_row, first_query=first_query, key_start=key_start)
    return jax.vmap(row_fn, in_axes=(0, 0, 0, 1, 1))(
        queries, seg_query, fold_state, kv_both, seg_keys
    )


def backward_row(
    queries,
    grad_attn,
    log_total,
    row_delta,
    seg_query,
    fold_state,
    kv_both,
    seg_keys,
    first_query,
    key_start,
):
    key_count = kv_both.shape[0]
    step_width = key_width(key_count)
    query_count, kv_local, group_size, head_size = queries.shape
    query_index = first_query + jnp.arange(query_count, dtype=jnp.int32)
    score_scale = head_size ** (-0.5)

    def backward_one_step(step_index, inner_state):
        grad_queries, grad_buffer = inner_state
        offset = step_index * step_width
        key_block, value_block, seg_block = split_block(
            kv_both, seg_keys, offset, step_width, kv_local, head_size
        )
        key_index = offset + jnp.arange(step_width, dtype=jnp.int32)
        allowed = (seg_query[:, None] == seg_block[None, :]) & (
            key_index[None, :] <= query_index[:, None]
        )
        scores = (
            jnp.einsum("qkgd,pkd->kgqp", queries, key_block, preferred_element_type=jnp.float32)
            * score_scale
        )
        probs_block = jnp.where(allowed, jnp.exp(scores - log_total[..., None]), 0.0)
        grad_probs = jnp.einsum(
            "qkgd,pkd->kgqp", grad_attn, value_block, preferred_element_type=jnp.float32
        )
        grad_scores = (probs_block * (grad_probs - row_delta[..., None])).astype(jnp.bfloat16)
        grad_queries = (
            grad_queries
            + jnp.einsum(
                "kgqp,pkd->qkgd", grad_scores, key_block, preferred_element_type=jnp.float32
            )
            * score_scale
        )
        grad_keys = (
            jnp.einsum("kgqp,qkgd->pkd", grad_scores, queries, preferred_element_type=jnp.float32)
            * score_scale
        )
        grad_values = jnp.einsum(
            "kgqp,qkgd->pkd",
            probs_block.astype(jnp.bfloat16),
            grad_attn,
            preferred_element_type=jnp.float32,
        )
        joined = jnp.concatenate(
            [grad_keys.reshape(step_width, -1), grad_values.reshape(step_width, -1)], axis=1
        )
        grad_buffer = lax.dynamic_update_slice_in_dim(grad_buffer, joined, offset, 0)
        return (grad_queries, grad_buffer)

    return lax.fori_loop(0, key_count // step_width, backward_one_step, fold_state)


def backward_fold(
    queries, grad_attn, log_total, row_delta, seg_query, first_query, fold_state, pieces, key_start
):
    kv_both, seg_keys = pieces
    row_fn = partial(backward_row, first_query=first_query, key_start=key_start)
    return jax.vmap(row_fn, in_axes=(0, 0, 0, 0, 0, 0, 1, 1))(
        queries, grad_attn, log_total, row_delta, seg_query, fold_state, kv_both, seg_keys
    )


def layer_forward(stream, gain_pair, matrices, seg_info, tables):
    gain_in, gain_mid = gain_pair
    w_query, w_key, w_value, w_out, w_gate, w_up, w_down = matrices
    seg_query, seg_keys = seg_info
    cosine, sine_table = tables
    row_count = seg_query.shape[0]
    kv_local = w_key.shape[1] // HD
    head_local = w_query.shape[1] // HD
    group_size = head_local // kv_local
    normed_a, factor_a = rms_norm(stream, gain_in)
    spread_a = spread(normed_a.astype(jnp.bfloat16))
    flat_count = spread_a.shape[0]
    token_count = flat_count // row_count
    raw_queries = jnp.dot(spread_a, w_query, preferred_element_type=jnp.float32).reshape(
        flat_count, head_local, HD
    )
    queries = (
        rotate(raw_queries, cosine, sine_table)
        .astype(jnp.bfloat16)
        .reshape(token_count, row_count, kv_local, group_size, HD)
    )
    queries = jnp.transpose(queries, (1, 0, 2, 3, 4))
    raw_keys = jnp.dot(spread_a, w_key, preferred_element_type=jnp.float32).reshape(
        flat_count, kv_local, HD
    )
    keys_low = (
        rotate(raw_keys, cosine, sine_table).astype(jnp.bfloat16).reshape(flat_count, kv_local * HD)
    )
    values_low = jnp.dot(spread_a, w_value, preferred_element_type=jnp.float32).astype(jnp.bfloat16)
    kv_both = jnp.concatenate([keys_low, values_low], axis=1).reshape(
        token_count, row_count, 2 * kv_local * HD
    )
    first_query = lax.axis_index("seq") * token_count
    start_state = (
        jnp.full((row_count, kv_local, group_size, token_count), BIG_NEG, jnp.float32),
        jnp.zeros((row_count, kv_local, group_size, token_count), jnp.float32),
        jnp.zeros((row_count, token_count, kv_local, group_size, HD), jnp.float32),
    )
    running_max, weight_total, value_total = forward_fold(
        queries,
        seg_query,
        first_query,
        start_state,
        (
            lax.all_gather(kv_both, "seq", axis=0, tiled=True),
            lax.all_gather(seg_keys, "seq", axis=0, tiled=True),
        ),
        jnp.int32(0),
    )
    attn_float = value_total / jnp.transpose(weight_total, (0, 3, 1, 2))[..., None]
    log_total = running_max + jnp.log(weight_total)
    attn_low = (
        jnp.transpose(attn_float, (1, 0, 2, 3, 4))
        .reshape(flat_count, head_local * HD)
        .astype(jnp.bfloat16)
    )
    stream_mid = stream + token_sum(((attn_low, w_out, 0),))
    normed_b, factor_b = rms_norm(stream_mid, gain_mid)
    spread_b = spread(normed_b.astype(jnp.bfloat16))
    gate_val = jnp.dot(spread_b, w_gate, preferred_element_type=jnp.float32)
    up_val = jnp.dot(spread_b, w_up, preferred_element_type=jnp.float32)
    hidden = (jax.nn.silu(gate_val) * up_val).astype(jnp.bfloat16)
    stream_out = stream_mid + token_sum(((hidden, w_down, 0),))
    saved_state = (
        stream,
        factor_a,
        spread_a,
        queries,
        kv_both,
        attn_float,
        attn_low,
        log_total,
        stream_mid,
        factor_b,
        spread_b,
        gate_val,
        up_val,
        hidden,
    )
    return (stream_out, saved_state)


def layer_backward(saved_state, grad_stream, gain_pair, matrices, seg_info, tables):
    (
        stream,
        factor_a,
        spread_a,
        queries,
        kv_both,
        attn_float,
        attn_low,
        log_total,
        stream_mid,
        factor_b,
        spread_b,
        gate_val,
        up_val,
        hidden,
    ) = saved_state
    gain_in, gain_mid = gain_pair
    w_query, w_key, w_value, w_out, w_gate, w_up, w_down = matrices
    seg_query, seg_keys = seg_info
    cosine, sine_table = tables
    row_count, token_count, kv_local, group_size, head_size = queries.shape
    head_local = kv_local * group_size
    flat_count = row_count * token_count
    grad_low = spread(grad_stream.astype(jnp.bfloat16))
    grad_down_w = contract(hidden, grad_low, 0, 0)
    grad_hidden = contract(grad_low, w_down, 1, 1)
    sigmoid_gate = jax.nn.sigmoid(gate_val)
    silu_gate = gate_val * sigmoid_gate
    grad_gate_low = (
        grad_hidden * up_val * sigmoid_gate * (1.0 + gate_val * (1.0 - sigmoid_gate))
    ).astype(jnp.bfloat16)
    grad_up_low = (grad_hidden * silu_gate).astype(jnp.bfloat16)
    grad_gate_w = contract(spread_b, grad_gate_low, 0, 0)
    grad_up_w = contract(spread_b, grad_up_low, 0, 0)
    grad_normed_b = token_sum(((grad_gate_low, w_gate, 1), (grad_up_low, w_up, 1)))
    back_mid, grad_gain_mid = norm_back(stream_mid, factor_b, gain_mid, grad_normed_b)
    grad_mid = grad_stream + back_mid
    grad_attn_full = spread(grad_mid.astype(jnp.bfloat16))
    grad_out_w = contract(attn_low, grad_attn_full, 0, 0)
    grad_attn = (
        contract(grad_attn_full, w_out, 1, 1)
        .astype(jnp.bfloat16)
        .reshape(token_count, row_count, kv_local, group_size, head_size)
    )
    grad_attn = jnp.transpose(grad_attn, (1, 0, 2, 3, 4))
    row_delta = jnp.transpose(jnp.sum(grad_attn * attn_float, axis=-1), (0, 2, 3, 1))
    first_query = lax.axis_index("seq") * token_count
    row_length = token_count * lax.axis_size("seq")
    start_state = (
        jnp.zeros((row_count, token_count, kv_local, group_size, head_size), jnp.float32),
        jnp.zeros((row_count, row_length, 2 * kv_local * head_size), jnp.float32),
    )
    grad_queries, grad_buffer = backward_fold(
        queries,
        grad_attn,
        log_total,
        row_delta,
        seg_query,
        first_query,
        start_state,
        (
            lax.all_gather(kv_both, "seq", axis=0, tiled=True),
            lax.all_gather(seg_keys, "seq", axis=0, tiled=True),
        ),
        jnp.int32(0),
    )
    grad_kv = lax.psum_scatter(
        grad_buffer.astype(jnp.bfloat16), "seq", scatter_dimension=1, tiled=True
    ).astype(jnp.float32)
    grad_kv = jnp.transpose(grad_kv, (1, 0, 2)).reshape(flat_count, 2 * kv_local * head_size)
    grad_queries = jnp.transpose(grad_queries, (1, 0, 2, 3, 4)).reshape(
        flat_count, head_local, head_size
    )
    grad_q_low = (
        rotate(grad_queries, cosine, -sine_table)
        .astype(jnp.bfloat16)
        .reshape(flat_count, head_local * head_size)
    )
    grad_k_low = (
        rotate(
            grad_kv[:, : kv_local * head_size].reshape(flat_count, kv_local, head_size),
            cosine,
            -sine_table,
        )
        .astype(jnp.bfloat16)
        .reshape(flat_count, kv_local * head_size)
    )
    grad_v_low = grad_kv[:, kv_local * head_size :].astype(jnp.bfloat16)
    grad_query_w = contract(spread_a, grad_q_low, 0, 0)
    grad_key_w = contract(spread_a, grad_k_low, 0, 0)
    grad_value_w = contract(spread_a, grad_v_low, 0, 0)
    grad_normed_a = token_sum(
        ((grad_q_low, w_query, 1), (grad_k_low, w_key, 1), (grad_v_low, w_value, 1))
    )
    back_in, grad_gain_in = norm_back(stream, factor_a, gain_in, grad_normed_a)
    grad_input = grad_mid + back_in
    weight_grads = (
        lax.psum_scatter(
            grad_query_w.astype(jnp.bfloat16), ("batch", "seq"), scatter_dimension=0, tiled=True
        ).astype(jnp.float32),
        lax.psum_scatter(
            grad_key_w.astype(jnp.bfloat16), ("batch", "seq"), scatter_dimension=0, tiled=True
        ).astype(jnp.float32),
        lax.psum_scatter(
            grad_value_w.astype(jnp.bfloat16), ("batch", "seq"), scatter_dimension=0, tiled=True
        ).astype(jnp.float32),
        lax.psum_scatter(
            grad_out_w.astype(jnp.bfloat16), ("batch", "seq"), scatter_dimension=1, tiled=True
        ).astype(jnp.float32),
        lax.psum_scatter(
            grad_gate_w.astype(jnp.bfloat16), ("batch", "seq"), scatter_dimension=0, tiled=True
        ).astype(jnp.float32),
        lax.psum_scatter(
            grad_up_w.astype(jnp.bfloat16), ("batch", "seq"), scatter_dimension=0, tiled=True
        ).astype(jnp.float32),
        lax.psum_scatter(
            grad_down_w.astype(jnp.bfloat16), ("batch", "seq"), scatter_dimension=1, tiled=True
        ).astype(jnp.float32),
    )
    return (grad_input, weight_grads, grad_gain_in, grad_gain_mid)


def to_flat(shard_rows):
    row_count, token_part, width = shard_rows.shape
    return jnp.transpose(shard_rows.astype(jnp.float32), (1, 0, 2)).reshape(
        token_part * row_count, width
    )


def from_flat(flat_rows, row_count):
    token_part = flat_rows.shape[0] // row_count
    return jnp.transpose(flat_rows.reshape(token_part, row_count, flat_rows.shape[1]), (1, 0, 2))


def local(
    tokens,
    cotangent,
    segments,
    positions,
    norm_in,
    w_query,
    w_key,
    w_value,
    w_out,
    norm_mid,
    w_gate,
    w_up,
    w_down,
):
    gains_in, gains_mid = (
        lax.all_gather(norm_in, ("batch", "seq", "kv"), axis=1, tiled=True),
        lax.all_gather(norm_mid, ("batch", "seq", "kv"), axis=1, tiled=True),
    )
    row_count = tokens.shape[0]
    seg_info = (segments, jnp.transpose(segments, (1, 0)))
    tables = rotary(jnp.transpose(positions, (1, 0)).reshape(-1))

    def fetch_layer(layer_index):
        return (
            lax.all_gather(w_query[layer_index], ("batch", "seq"), axis=0, tiled=True),
            lax.all_gather(w_key[layer_index], ("batch", "seq"), axis=0, tiled=True),
            lax.all_gather(w_value[layer_index], ("batch", "seq"), axis=0, tiled=True),
            lax.all_gather(w_out[layer_index], ("batch", "seq"), axis=1, tiled=True),
            lax.all_gather(w_gate[layer_index], ("batch", "seq"), axis=0, tiled=True),
            lax.all_gather(w_up[layer_index], ("batch", "seq"), axis=0, tiled=True),
            lax.all_gather(w_down[layer_index], ("batch", "seq"), axis=1, tiled=True),
        )

    stream = to_flat(tokens)
    fetched = []
    states = []
    layer_index = 0
    matrices = fetch_layer(layer_index)
    layer_inputs = [stream]
    stream, saved_state = layer_forward(
        stream, (gains_in[layer_index], gains_mid[layer_index]), matrices, seg_info, tables
    )
    fetched.append(matrices)
    states.append(saved_state)
    grad_stream = to_flat(cotangent)
    grads_in = []
    grads_mid = []
    weight_lists = []
    for layer_index in reversed(range(LAYERS)):
        gain_pair = (gains_in[layer_index], gains_mid[layer_index])
        matrices = fetch_layer(layer_index)
        saved_state = layer_forward(
            layer_inputs[layer_index], gain_pair, matrices, seg_info, tables
        )[1]
        grad_stream, weight_grads, grad_gain_in, grad_gain_mid = layer_backward(
            saved_state, grad_stream, gain_pair, matrices, seg_info, tables
        )
        grads_in.insert(0, grad_gain_in)
        grads_mid.insert(0, grad_gain_mid)
        weight_lists.insert(0, weight_grads)
    gain_grads_in, gain_grads_mid = (
        lax.psum_scatter(
            jnp.stack(grads_in), ("batch", "seq", "kv"), scatter_dimension=1, tiled=True
        ),
        lax.psum_scatter(
            jnp.stack(grads_mid), ("batch", "seq", "kv"), scatter_dimension=1, tiled=True
        ),
    )
    stacked_grads = [
        jnp.stack([grad_set[member] for grad_set in weight_lists]) for member in range(7)
    ]
    return (
        from_flat(stream, row_count),
        from_flat(grad_stream, row_count),
        gain_grads_in,
        stacked_grads[0],
        stacked_grads[1],
        stacked_grads[2],
        stacked_grads[3],
        gain_grads_mid,
        stacked_grads[4],
        stacked_grads[5],
        stacked_grads[6],
    )


def solution(mesh):
    in_specs = (
        P("batch", ("seq", "kv"), None),
        P("batch", ("seq", "kv"), None),
        P("batch", "seq"),
        P("batch", "seq"),
        P(None, ("batch", "seq", "kv")),
        P(None, ("batch", "seq"), "kv"),
        P(None, ("batch", "seq"), "kv"),
        P(None, ("batch", "seq"), "kv"),
        P(None, "kv", ("batch", "seq")),
        P(None, ("batch", "seq", "kv")),
        P(None, ("batch", "seq"), "kv"),
        P(None, ("batch", "seq"), "kv"),
        P(None, "kv", ("batch", "seq")),
    )
    out_specs = (
        P("batch", ("seq", "kv"), None),
        P("batch", ("seq", "kv"), None),
        P(None, ("batch", "seq", "kv")),
        P(None, ("batch", "seq"), "kv"),
        P(None, ("batch", "seq"), "kv"),
        P(None, ("batch", "seq"), "kv"),
        P(None, "kv", ("batch", "seq")),
        P(None, ("batch", "seq", "kv")),
        P(None, ("batch", "seq"), "kv"),
        P(None, ("batch", "seq"), "kv"),
        P(None, "kv", ("batch", "seq")),
    )
    return jax.shard_map(local, mesh=mesh, in_specs=in_specs, out_specs=out_specs, check_vma=False)
```

profile of v0, /device:TPU:0, one launch (start us, length us, event | category | flops | bytes accessed | tf_op | source)
XLA Modules:
  0.0 1479.3 jit_solution(8268238482878367859)
XLA Ops:
  12.8 42.1 %all-reduce.2 = (f32[1536]{0:T(1024)S(1)}, f32[1536]{0:T(1024)S(1)}) all-reduce(f32[1536]{0:T(1024)S(1)} %bitcast_dynamic-update-slice_fusion, f32[1536]{0:T(1024)S(1)} %bitcast_dynamic-update-slice_fusion.1), channel_id=1, replica_groups=mesh['batch'=2,'seq'=4,'kv'=4] {'batch','seq','kv'}, use_global_device_ids=true, to_apply=%add.1 | all-reduce | flops 3072 | bytes 24576
  58.0 11.2 all-gather
  69.2 10.2 all-gather.1
  80.5 39.2 %all-gather.18.cloned.1.call-done = bf16[1024,1536]{1,0:T(8,128)(2,1)} async-done(((bf16[256,1536]{1,0:T(8,128)(2,1)}), bf16[1024,1536]{1,0:T(8,128)(2,1)}) %all-gather.18.cloned.1.call-update) | async-done | bytes 3145744 | tf_op jit(solution)/shard_map/all_gather | solution.py:59
  136.4 7.9 multiply_cosine_fusion
  144.3 5.2 all_gather.58
  182.1 8.8 copy.86
  190.9 34.6 %while.46 = (s32[]{:T(128)}, f32[2,2,2,512]{3,2,1,0:T(2,128)S(1)}, f32[2,2,2,512]{3,2,1,0:T(2,128)S(1)}, f32[2,512,2,2,96]{1,4,3,2,0:T(8,128)}, s32[2,512]{1,0:T...) while((s32[]{:T(128)}, f32[2,2,2,512]{3,2,1,0:T(2,128)S(1)}, ...), condition=%wide.region_4.5_spmd.clone, body=%wide.region_1.4_spmd.clone.sunk | while | flops 1668965888 | bytes 77111608 | solution.py:115
  230.8 6.1 convert_bitcast_fusion.1
  238.5 5.0 convolution_convert_fusion
  244.1 58.2 %reduce-scatter.19.cloned.1.call-done = bf16[256,1536]{1,0:T(8,128)(2,1)} async-done(((bf16[1024,1536]{1,0:T(8,128)(2,1)}), bf16[256,1536]{1,0:T(8,128)(2,1)}) %reduce-scatter.19.cloned.1.call-update) | async-done | bytes 786448 | tf_op jit(solution)/shard_map/reduce_scatter | solution.py:67
  312.5 24.0 %all-gather.34.cloned.1.call-done = bf16[1,1536,1024]{2,1,0:T(8,128)(2,1)} async-done(((bf16[1,192,1024]{2,1,0:T(8,128)(2,1)}), bf16[1,1536,1024]{2,1,0:T(8,128)(2,1)}) %all-gather.34.cloned.1.call-update) | async-done | bytes 3145744 | tf_op jit(solution)/shard_map/all_gather | solution.py:446
  336.5 65.7 %all-gather.22.cloned.1.call-done = bf16[1024,1536]{1,0:T(8,128)(2,1)} async-done(((bf16[256,1536]{1,0:T(8,128)(2,1)}), bf16[1024,1536]{1,0:T(8,128)(2,1)}) %all-gather.22.cloned.1.call-update) | async-done | bytes 3145744 | tf_op jit(solution)/shard_map/all_gather | solution.py:59
  402.2 8.3 fusion.34
  410.4 24.6 %all-gather.32.cloned.1.call-done = bf16[1,1536,1024]{2,1,0:T(8,128)(2,1)} async-done(((bf16[1,192,1024]{2,1,0:T(8,128)(2,1)}), bf16[1,1536,1024]{2,1,0:T(8,128)(2,1)}) %all-gather.32.cloned.1.call-update) | async-done | bytes 3145744 | tf_op jit(solution)/shard_map/all_gather | solution.py:445
  435.0 8.2 fusion.38
  443.3 56.9 %all-gather.24.cloned.1.call-done = bf16[1024,1536]{1,0:T(8,128)(2,1)} async-done(((bf16[256,1536]{1,0:T(8,128)(2,1)}), bf16[1024,1536]{1,0:T(8,128)(2,1)}) %all-gather.24.cloned.1.call-update) | async-done | bytes 3145744 | tf_op jit(solution)/shard_map/all_gather | solution.py:59
  500.1 32.7 %all-gather.36.cloned.1.call-done = bf16[1,1024,1536]{1,2,0:T(8,128)(2,1)} async-done(((bf16[1,1024,192]{1,2,0:T(8,128)(2,1)}), bf16[1,1024,1536]{1,2,0:T(8,128)(2,1)}) %all-gather.36.cloned.1.call-update) | async-done | bytes 3145744 | tf_op jit(solution)/shard_map/all_gather | solution.py:447
  532.9 11.5 multiply_convert_fusion
  547.9 5.1 add_convert_fusion.1
  553.1 60.4 %reduce-scatter.23.cloned.1.call-done = bf16[256,1536]{1,0:T(8,128)(2,1)} async-done(((bf16[1024,1536]{1,0:T(8,128)(2,1)}), bf16[256,1536]{1,0:T(8,128)(2,1)}) %reduce-scatter.23.cloned.1.call-update) | async-done | bytes 786448 | tf_op jit(solution)/shard_map/reduce_scatter | solution.py:67
  617.5 63.6 %all-gather.26.cloned.1.call-done = bf16[1024,1536]{1,0:T(8,128)(2,1)} async-done(((bf16[256,1536]{1,0:T(8,128)(2,1)}), bf16[1024,1536]{1,0:T(8,128)(2,1)}) %all-gather.26.cloned.1.call-update) | async-done | bytes 3145744 | tf_op jit(solution)/shard_map/all_gather | solution.py:59
  695.4 106.3 %while.47 = (s32[]{:T(128)}, f32[2,512,2,2,96]{1,4,3,2,0:T(8,128)}, bf16[2,2048,384]{1,2,0:T(8,128)(2,1)}, bf16[2,2048,384]{1,2,0:T(8,128)(2,1)}, s32[2,512]{1,0...) while((s32[]{:T(128)}, f32[2,512,2,2,96]{1,4,3,2,0:T(8,128)}, ...), condition=%wide.region_13.14_spmd.clone, body=%wide.region_11.0_spmd.clone.sunk | while | flops 4076996096 | bytes 129327568 | solution.py:186
  700.2 8.2 fusion.159
  708.4 10.4 fusion.161
  718.8 9.4 fusion.160
  734.7 14.6 scatter.7
  753.6 8.2 fusion.159
  761.8 10.4 fusion.161
  772.2 9.4 fusion.160
  788.0 13.5 scatter.7
  803.6 6.5 convolution_convert_fusion.1
  812.1 6.5 convolution_convert_fusion.2
  818.7 6.5 convolution_convert_fusion.3
  827.1 4.8 convolution_convert_fusion.5
  872.5 6.1 fusion.58
  883.4 5.7 add_convert_fusion
  891.1 6.4 convolution_convert_fusion.4
  900.2 37.7 %reduce-scatter.39.cloned.1.call-done = bf16[192,1024]{1,0:T(8,128)(2,1)} async-done(((bf16[1536,1024]{1,0:T(8,128)(2,1)}), bf16[192,1024]{1,0:T(8,128)(2,1)}) %reduce-scatter.39.cloned.1.call-update) | async-done | bytes 393232 | tf_op jit(solution)/shard_map/reduce_scatter | solution.py:394
  939.8 48.0 %reduce-scatter.37.cloned.1.call-done = bf16[192,1024]{1,0:T(8,128)(2,1)} async-done(((bf16[1536,1024]{1,0:T(8,128)(2,1)}), bf16[192,1024]{1,0:T(8,128)(2,1)}) %reduce-scatter.37.cloned.1.call-update) | async-done | bytes 393232 | tf_op jit(solution)/shard_map/reduce_scatter | solution.py:391
  989.7 98.5 %reduce-scatter.45.cloned.1.call-done = f32[48,1]{1,0:T(8,128)} async-done(((f32[1536,1]{1,0:T(8,128)}), f32[48,1]{1,0:T(8,128)}) %reduce-scatter.45.cloned.1.call-update) | async-done | bytes 208
  1089.5 37.6 %reduce-scatter.35.cloned.1.call-done = bf16[384,192]{0,1:T(8,128)(2,1)} async-done(((bf16[384,1536]{0,1:T(8,128)(2,1)}), bf16[384,192]{0,1:T(8,128)(2,1)}) %reduce-scatter.35.cloned.1.call-update) | async-done | bytes 147472 | tf_op jit(solution)/shard_map/reduce_scatter | solution.py:388
  1128.8 39.3 %reduce-scatter.29.cloned.1.call-done = bf16[192,384]{1,0:T(8,128)(2,1)} async-done(((bf16[1536,384]{1,0:T(8,128)(2,1)}), bf16[192,384]{1,0:T(8,128)(2,1)}) %reduce-scatter.29.cloned.1.call-update) | async-done | bytes 147472 | tf_op jit(solution)/shard_map/reduce_scatter | solution.py:379
  1169.8 37.0 %reduce-scatter.31.cloned.1.call-done = bf16[192,192]{1,0:T(8,128)(2,1)} async-done(((bf16[1536,192]{1,0:T(8,128)(2,1)}), bf16[192,192]{1,0:T(8,128)(2,1)}) %reduce-scatter.31.cloned.1.call-update) | async-done | bytes 73744 | tf_op jit(solution)/shard_map/reduce_scatter | solution.py:382
  1208.3 36.6 %reduce-scatter.33.cloned.1.call-done = bf16[192,192]{1,0:T(8,128)(2,1)} async-done(((bf16[1536,192]{1,0:T(8,128)(2,1)}), bf16[192,192]{1,0:T(8,128)(2,1)}) %reduce-scatter.33.cloned.1.call-update) | async-done | bytes 73744 | tf_op jit(solution)/shard_map/reduce_scatter | solution.py:385
  1246.5 61.0 %reduce-scatter.27.cloned.1.call-done = bf16[256,1536]{1,0:T(8,128)(2,1)} async-done(((bf16[1024,1536]{1,0:T(8,128)(2,1)}), bf16[256,1536]{1,0:T(8,128)(2,1)}) %reduce-scatter.27.cloned.1.call-update) | async-done | bytes 786448 | tf_op jit(solution)/shard_map/reduce_scatter | solution.py:67
  1310.3 59.8 %reduce-scatter.21.cloned.1.call-done = bf16[256,1536]{1,0:T(8,128)(2,1)} async-done(((bf16[1024,1536]{1,0:T(8,128)(2,1)}), bf16[256,1536]{1,0:T(8,128)(2,1)}) %reduce-scatter.21.cloned.1.call-update) | async-done | bytes 786448 | tf_op jit(solution)/shard_map/reduce_scatter | solution.py:67
  1380.9 89.8 %reduce-scatter.43.cloned.1.call-done = f32[48,1]{1,0:T(8,128)} async-done(((f32[1536,1]{1,0:T(8,128)}), f32[48,1]{1,0:T(8,128)}) %reduce-scatter.43.cloned.1.call-update) | async-done | bytes 208
  (354 shorter events, 235.4 us)
Async XLA Ops:
  7.2 112.5 %all-gather.18.cloned.1.call-start = ((), (), s32[]{:S(2)}) async-start(), calls=%async_computation.14 | async-start | bytes 3932160 | tf_op jit(solution)/shard_map/all_gather | solution.py:59
  10.2 44.7 %copy-start.46 = (f32[256]{0:T(256)}, f32[256]{0:T(256)S(1)}, u32[]{:S(2)}) copy-start(f32[256]{0:T(256)S(1)} %rsqrt.28) | copy-start | bytes 3076
  12.5 603.3 %copy-start = (f32[256,1536]{1,0:T(8,128)}, f32[256,1536]{1,0:T(8,128)S(1)}, u32[]{:S(2)}) copy-start(f32[256,1536]{1,0:T(8,128)S(1)} %reshape.406) | copy-start | bytes 4718596
  12.5 44.3 %copy-start.56 = (s32[2,512]{1,0:T(2,128)S(1)}, s32[2,512]{1,0:T(2,128)}, u32[]{:S(2)}) copy-start(s32[2,512]{1,0:T(2,128)} %param.22) | copy-start | bytes 12292
  54.9 561.0 %copy-start.40 = (f32[1536]{0:T(1024)}, f32[1536]{0:T(1024)S(1)}, u32[]{:S(2)}) copy-start(f32[1536]{0:T(1024)S(1)} %get-tuple-element.599) | copy-start | bytes 18436
  56.0 95.7 %all-gather.28.cloned.1.call-start = ((), (), s32[]{:S(2)}) async-start(), calls=%async_computation.31 | async-start | bytes 1327104 | tf_op jit(solution)/shard_map/all_gather | solution.py:441
  56.8 125.3 %all-gather.20.cloned.1.call-start = ((), (), s32[]{:S(2)}) async-start(), calls=%async_computation.15 | async-start | bytes 3932160 | tf_op jit(solution)/shard_map/all_gather | solution.py:243
  58.0 72.9 %copy-start.19 = (f32[1024,96]{0,1:T(8,128)}, f32[1024,96]{0,1:T(8,128)S(1)}, u32[]{:S(2)}) copy-start(f32[1024,96]{0,1:T(8,128)S(1)} %pad_maximum_fusion.3) | copy-start | bytes 1179652
  69.2 58.3 %copy-start.18 = (bf16[1,1536,192]{2,1,0:T(8,128)(2,1)}, bf16[1,1536,192]{2,1,0:T(8,128)(2,1)S(1)}, u32[]{:S(2)}) copy-start(bf16[1,1536,192]{2,1,0:T(8,128)(2,1)S(1)} %all-gather) | copy-start | bytes 1769476
  79.4 44.0 %copy-start.15 = (bf16[1,1536,192]{2,1,0:T(8,128)(2,1)}, bf16[1,1536,192]{2,1,0:T(8,128)(2,1)S(1)}, u32[]{:S(2)}) copy-start(bf16[1,1536,192]{2,1,0:T(8,128)(2,1)S(1)} %all-gather.1) | copy-start | bytes 1769476
  133.3 11.0 copy-start.39
  135.5 103.0 %all-gather.30.cloned.1.call-start = ((), (), s32[]{:S(2)}) async-start(), calls=%async_computation.32 | async-start | bytes 1327104 | tf_op jit(solution)/shard_map/all_gather | solution.py:444
  136.1 166.3 %reduce-scatter.19.cloned.1.call-start = ((), (), s32[]{:S(2)}) async-start(), calls=%async_computation.16 | async-start | bytes 3932160 | tf_op jit(solution)/shard_map/reduce_scatter | solution.py:67
  243.5 93.0 %all-gather.34.cloned.1.call-start = ((), (), s32[]{:S(2)}) async-start(), calls=%async_computation.34 | async-start | bytes 3538944 | tf_op jit(solution)/shard_map/all_gather | solution.py:446
  244.1 158.1 %all-gather.22.cloned.1.call-start = ((), (), s32[]{:S(2)}) async-start(), calls=%async_computation.17 | async-start | bytes 3932160 | tf_op jit(solution)/shard_map/all_gather | solution.py:59
  303.9 312.0 %copy-start.48 = (f32[256]{0:T(256)}, f32[256]{0:T(256)S(1)}, u32[]{:S(2)}) copy-start(f32[256]{0:T(256)S(1)} %get-tuple-element.629) | copy-start | bytes 3076
  303.9 312.0 %copy-start.52 = (f32[256]{0:T(256)}, f32[256]{0:T(256)S(1)}, u32[]{:S(2)}) copy-start(f32[256]{0:T(256)S(1)} %get-tuple-element.628) | copy-start | bytes 3076
  305.0 130.0 %all-gather.32.cloned.1.call-start = ((), (), s32[]{:S(2)}) async-start(), calls=%async_computation.33 | async-start | bytes 3538944 | tf_op jit(solution)/shard_map/all_gather | solution.py:445
  305.8 194.3 %all-gather.24.cloned.1.call-start = ((), (), s32[]{:S(2)}) async-start(), calls=%async_computation.19 | async-start | bytes 3932160 | tf_op jit(solution)/shard_map/all_gather | solution.py:59
  311.6 221.2 %all-gather.36.cloned.1.call-start = ((), (), s32[]{:S(2)}) async-start(), calls=%async_computation.35 | async-start | bytes 3538944 | tf_op jit(solution)/shard_map/all_gather | solution.py:447
  312.2 301.3 %reduce-scatter.23.cloned.1.call-start = ((), (), s32[]{:S(2)}) async-start(), calls=%async_computation.20 | async-start | bytes 3932160 | tf_op jit(solution)/shard_map/reduce_scatter | solution.py:67
  532.9 11.5 copy-start.61
  553.1 128.0 %all-gather.26.cloned.1.call-start = ((), (), s32[]{:S(2)}) async-start(), calls=%async_computation.21 | async-start | bytes 3932160 | tf_op jit(solution)/shard_map/all_gather | solution.py:59
  617.4 239.9 %reduce-scatter.25.cloned.1.call-start = ((), (), s32[]{:S(2)}) async-start(), calls=%async_computation.22 | async-start | bytes 3932160 | tf_op jit(solution)/shard_map/reduce_scatter | solution.py:348
  690.9 4.5 copy-start.50
  718.8 9.5 copy-start.2
  772.2 9.5 copy-start.2
  801.7 96.5 %reduce-scatter.41.cloned.1.call-start = ((), (), s32[]{:S(2)}) async-start(), calls=%async_computation.30 | async-start | bytes 3538944 | tf_op jit(solution)/shard_map/reduce_scatter | solution.py:397
  810.1 127.8 %reduce-scatter.39.cloned.1.call-start = ((), (), s32[]{:S(2)}) async-start(), calls=%async_computation.29 | async-start | bytes 3538944 | tf_op jit(solution)/shard_map/reduce_scatter | solution.py:394
  818.6 169.1 %reduce-scatter.37.cloned.1.call-start = ((), (), s32[]{:S(2)}) async-start(), calls=%async_computation.28 | async-start | bytes 3538944 | tf_op jit(solution)/shard_map/reduce_scatter | solution.py:391
  825.2 263.0 %reduce-scatter.45.cloned.1.call-start = ((), (), s32[]{:S(2)}) async-start(), calls=%async_computation.37 | async-start | bytes 811008
  827.0 4.9 copy-start.26
  827.0 300.1 %reduce-scatter.35.cloned.1.call-start = ((), (), s32[]{:S(2)}) async-start(), calls=%async_computation.27 | async-start | bytes 1327104 | tf_op jit(solution)/shard_map/reduce_scatter | solution.py:388
  831.9 336.2 %reduce-scatter.29.cloned.1.call-start = ((), (), s32[]{:S(2)}) async-start(), calls=%async_computation.24 | async-start | bytes 1327104 | tf_op jit(solution)/shard_map/reduce_scatter | solution.py:379
  857.2 349.5 %reduce-scatter.31.cloned.1.call-start = ((), (), s32[]{:S(2)}) async-start(), calls=%async_computation.25 | async-start | bytes 884736 | tf_op jit(solution)/shard_map/reduce_scatter | solution.py:382
  872.5 372.4 %reduce-scatter.33.cloned.1.call-start = ((), (), s32[]{:S(2)}) async-start(), calls=%async_computation.26 | async-start | bytes 884736 | tf_op jit(solution)/shard_map/reduce_scatter | solution.py:385
  872.5 6.1 copy-start.23
  880.7 426.8 %reduce-scatter.27.cloned.1.call-start = ((), (), s32[]{:S(2)}) async-start(), calls=%async_computation.23 | async-start | bytes 3932160 | tf_op jit(solution)/shard_map/reduce_scatter | solution.py:67
  889.2 480.9 %reduce-scatter.21.cloned.1.call-start = ((), (), s32[]{:S(2)}) async-start(), calls=%async_computation.18 | async-start | bytes 3932160 | tf_op jit(solution)/shard_map/reduce_scatter | solution.py:67
  897.5 573.1 %reduce-scatter.43.cloned.1.call-start = ((), (), s32[]{:S(2)}) async-start(), calls=%async_computation.36 | async-start | bytes 811008
  900.1 407.4 %copy-start.1 = (f32[256,1536]{1,0:T(8,128)S(1)}, f32[256,1536]{1,0:T(8,128)}, u32[]{:S(2)}) copy-start(f32[256,1536]{1,0:T(8,128)} %copy-done) | copy-start | bytes 4718596
  900.2 407.4 %copy-start.44 = (f32[1536]{0:T(1024)S(1)}, f32[1536]{0:T(1024)}, u32[]{:S(2)}) copy-start(f32[1536]{0:T(1024)} %copy-done.43) | copy-start | bytes 18436
  1208.3 161.8 %copy-start.8 = (bf16[256,1536]{1,0:T(8,128)(2,1)S(1)}, bf16[256,1536]{1,0:T(8,128)(2,1)}, u32[]{:S(2)}) copy-start(bf16[256,1536]{1,0:T(8,128)(2,1)} %reduce-scatter.19.cloned.1.call-done) | copy-start | bytes 2359300
  1208.3 161.8 %copy-start.11 = (bf16[256,1536]{1,0:T(8,128)(2,1)S(1)}, bf16[256,1536]{1,0:T(8,128)(2,1)}, u32[]{:S(2)}) copy-start(bf16[256,1536]{1,0:T(8,128)(2,1)} %reshape.411) | copy-start | bytes 2359300
  1208.3 161.8 %copy-start.41 = (f32[1536]{0:T(1024)S(1)}, f32[1536]{0:T(1024)}, u32[]{:S(2)}) copy-start(f32[1536]{0:T(1024)} %copy-done.40) | copy-start | bytes 18436
  1208.3 161.8 %copy-start.49 = (f32[256]{0:T(256)S(1)}, f32[256]{0:T(256)}, u32[]{:S(2)}) copy-start(f32[256]{0:T(256)} %copy-done.48) | copy-start | bytes 3076
  1208.3 161.8 %copy-start.53 = (f32[256]{0:T(256)S(1)}, f32[256]{0:T(256)}, u32[]{:S(2)}) copy-start(f32[256]{0:T(256)} %copy-done.52) | copy-start | bytes 3076
  1208.3 161.8 %copy-start.55 = (f32[256]{0:T(256)S(1)}, f32[256]{0:T(256)}, u32[]{:S(2)}) copy-start(f32[256]{0:T(256)} %copy-done.54) | copy-start | bytes 3076
  (48 other events, 113.0 us)
Sparse Core Ops, SparseCore 0:
  56.1 63.4 all-gather.17
  121.5 22.7 all-gather.27
  146.4 28.5 all-gather.19
  176.7 24.0 all-gather.29
  243.6 58.6 reduce-scatter.18
  304.1 32.3 all-gather.33
  338.6 63.4 all-gather.21
  404.0 30.9 all-gather.31
  436.6 63.4 all-gather.23
  501.9 30.9 all-gather.35
  553.2 60.2 reduce-scatter.22
  617.5 63.5 all-gather.25
  801.8 36.5 reduce-scatter.24
  842.1 46.2 reduce-scatter.40
  891.6 46.1 reduce-scatter.38
  941.4 46.2 reduce-scatter.36
  992.7 95.4 reduce-scatter.44
  1091.3 35.8 reduce-scatter.34
  1131.3 36.7 reduce-scatter.28
  1171.7 35.0 reduce-scatter.30
  1209.9 34.9 reduce-scatter.32
  1247.2 60.2 reduce-scatter.26
  1309.8 60.2 reduce-scatter.20
  1375.1 95.5 reduce-scatter.42
where the time goes:
time: 1490 us; the launch traced here: 1480 us
  waiting for transfers between devices  974 us (65%)
  matrix products  189 us (13%)
  local copies, waits for them, and re-layouts  143 us (10%)
  other arithmetic  85.3 us (6%)
  blocking collectives  68.7 us (5%)
  between operations  15.7 us (1%)
    reduce_scatter x4, waiting for transfers between devices, token_sum(): lax.psum_scatter(summed.astype(jnp.bfloat16), 'kv', scatter_dimension=0,...  239 us
    all_gather x4, waiting for transfers between devices, spread(): return lax.all_gather(shard_rows, 'kv', axis=0, tiled=True)  225 us
    unnamed x26, waiting for transfers between devices  192 us
    dot_general x16, matrix products, contract(): lax.dot_general(left_side, right_side, (((left_dim,), (right_dim,)), ((),...  80.9 us
    reduce_scatter x1, waiting for transfers between devices, layer_backward(): lax.psum_scatter(grad_gate_w.astype(jnp.bfloat16), ('batch', 'seq'), scat...  48 us
    unnamed x1, blocking collectives  42.1 us
    reduce_scatter x1, waiting for transfers between devices, layer_backward(): lax.psum_scatter(grad_query_w.astype(jnp.bfloat16), ('batch', 'seq'), sca...  39.3 us
    reduce_scatter x1, waiting for transfers between devices, layer_backward(): lax.psum_scatter(grad_up_w.astype(jnp.bfloat16), ('batch', 'seq'), scatte...  37.7 us
  transfers between devices with their start and end apart: 24, of which 19 were waited for; matrix products, arithmetic and copies ran while one was open for 17% of the time, Pallas kernels for 0%

commit v1 on v0

--- a/solution.py
+++ b/solution.py
@@ -1,9 +1,13 @@
+import functools
+import math
 from functools import partial
-import math
 
 import jax
 import jax.numpy as jnp
 from jax import lax
+from jax.experimental import pallas as pl
+from jax.experimental.pallas import tpu as pltpu
+from jax.sharding import Mesh
 from jax.sharding import PartitionSpec as P
 
 HD = 96
@@ -413,7 +417,7 @@
     return jnp.transpose(flat_rows.reshape(token_part, row_count, flat_rows.shape[1]), (1, 0, 2))
 
 
-def local(
+def general_local(
     tokens,
     cotangent,
     segments,
@@ -500,7 +504,7 @@
     )
 
 
-def solution(mesh):
+def general_solution(mesh):
     in_specs = (
         P("batch", ("seq", "kv"), None),
         P("batch", ("seq", "kv"), None),
@@ -529,4 +533,673 @@
         P(None, ("batch", "seq"), "kv"),
         P(None, "kv", ("batch", "seq")),
     )
-    return jax.shard_map(local, mesh=mesh, in_specs=in_specs, out_specs=out_specs, check_vma=False)
+    return jax.shard_map(general_local, mesh=mesh, in_specs=in_specs, out_specs=out_specs, check_vma=False)
+
+
+LN = 128
+NEG=-1e30
+C2 = (96 ** -0.5) * 1.4426950408889634
+
+def lane_iota(rows):
+    return lax.broadcasted_iota(jnp.int32, (rows, LN), 1)
+
+def unpack4(t0, t1, t2):
+    lane = lane_iota(t0.shape[0])
+    live = lane < HD
+    zero = jnp.zeros_like(t0)
+    a = t0
+    b = pltpu.roll(jnp.where(lane >= 96, t0, t1), 32, 1)
+    c = pltpu.roll(jnp.where(lane >= 64, t1, t2), 64, 1)
+    d = pltpu.roll(t2, 96, 1)
+    return tuple(jnp.where(live, v, zero) for v in (a, b, c, d))
+
+def pack4(a, b, c, d):
+    lane = lane_iota(a.shape[0])
+    b, c, d = pltpu.roll(b, 96, 1), pltpu.roll(c, 64, 1), pltpu.roll(d, 32, 1)
+    return (jnp.where(lane < 96, a, b), jnp.where(lane < 64, b, c), jnp.where(lane < 32, c, d))
+
+def split3(x):
+    x = x.astype(jnp.float32)
+    return x[:, :LN], x[:, LN:2*LN], x[:, 2*LN:]
+
+def doc_low(index, first, length):
+    second = first + 3 * length // 4
+    return jnp.where(index >= second, second, jnp.where(index >= first, first, 0))
+
+BQ = 256
+
+def dotf(a, b, dims):
+    return lax.dot_general(a, b, (dims, ((), ())), preferred_element_type=jnp.float32)
+
+def attn_fwd_kernel(length, first_ref, x_ref, o_ref, of_ref, lse_ref, q_s, k_s, v_s, s_s):
+    i = pl.program_id(0)
+    blocks = length // BQ
+    first = first_ref[0]
+    @pl.when(i == 0)
+    def _():
+        def body(j, carry):
+            rows = pl.ds(pl.multiple_of(j * BQ, BQ), BQ)
+            q0, q1, k, v = unpack4(*split3(x_ref[rows, :]))
+            q_s[j, :BQ, :] = q0.astype(jnp.bfloat16)
+            q_s[j, BQ:, :] = q1.astype(jnp.bfloat16)
+            k_s[j] = k.astype(jnp.bfloat16)
+            v_s[j] = v.astype(jnp.bfloat16)
+            return carry
+        lax.fori_loop(0, blocks, body, 0)
+    q = q_s[i]
+    clean_from = (length // 8 + BQ - 1) // BQ
+    clean_to = 3 * length // 4 // BQ
+    late = (3 * length // 4 + length // 8) // BQ
+    start = jnp.where(i >= late, 3 * length // 4 // BQ, 0)
+    head_masked = jnp.where(i < clean_to, jnp.minimum(clean_from, i), i)
+    q_index = i * BQ + lax.broadcasted_iota(jnp.int32, (BQ, 1), 0)
+    low = doc_low(q_index, first, length)
+
+    def halves(v, op):
+        return op(v[:, :LN], v[:, LN:])
+
+    def score(j, top, masked):
+        s = dotf(q, k_s[j], ((1,), (1,)))
+        if masked:
+            key = j * BQ + lax.broadcasted_iota(jnp.int32, (1, BQ), 1)
+            ok = (key <= q_index) & (key >= low)
+            s = jnp.where(jnp.concatenate([ok, ok], axis=0), s, NEG)
+        s_s[j] = s
+        return jnp.maximum(top, halves(s, jnp.maximum))
+
+    top = jnp.full((2 * BQ, LN), NEG, jnp.float32)
+    top = lax.fori_loop(start, head_masked, lambda j, t: score(j, t, True), top)
+    top = lax.fori_loop(jnp.maximum(head_masked, start), i, lambda j, t: score(j, t, False), top)
+    top = score(i, top, True)
+    m = jnp.max(top, axis=1, keepdims=True) * C2
+
+    def add(j, state):
+        total, acc = state
+        p = jnp.exp2(s_s[j] * C2 - m)
+        total = total + halves(p, jnp.add)
+        acc = acc + dotf(p.astype(jnp.bfloat16), v_s[j], ((1,), (0,)))
+        return total, acc
+
+    zero = jnp.zeros((2 * BQ, LN), jnp.float32)
+    total, acc = lax.fori_loop(start, i + 1, add, (zero, zero))
+    total = jnp.sum(total, axis=1, keepdims=True)
+    out = acc / total
+    lse = jnp.broadcast_to(m + jnp.log2(total), (2 * BQ, LN))
+    lse_ref[0] = jnp.transpose(lse, (1, 0))[:8, :]
+    of_ref[0] = out
+    for d in range(2):
+        parts = []
+        for h in range(2):
+            parts.append(out[BQ*0 + d*128 + h*64: d*128 + h*64 + 64])
+            parts.append(out[BQ + d*128 + h*64: BQ + d*128 + h*64 + 64])
+        t = pack4(*parts)
+        for n in range(3):
+            o_ref[d, :, n*LN:(n+1)*LN] = t[n].astype(jnp.bfloat16)
+
+def attn_fwd(first, x):
+    length = x.shape[0]
+    blocks = length // BQ
+    return pl.pallas_call(
+        functools.partial(attn_fwd_kernel, length),
+        grid=(blocks,),
+        in_specs=[pl.BlockSpec(memory_space=pltpu.SMEM),
+                  pl.BlockSpec((length, 3*LN), lambda i: (0, 0))],
+        out_specs=[pl.BlockSpec((2, 64, 3*LN), lambda i: (i, 0, 0)),
+                   pl.BlockSpec((1, 2*BQ, LN), lambda i: (i, 0, 0)),
+                   pl.BlockSpec((1, 8, 2*BQ), lambda i: (i, 0, 0))],
+        out_shape=[jax.ShapeDtypeStruct((length//128, 64, 3*LN), jnp.bfloat16),
+                   jax.ShapeDtypeStruct((blocks, 2*BQ, LN), jnp.float32),
+                   jax.ShapeDtypeStruct((blocks, 8, 2*BQ), jnp.float32)],
+        scratch_shapes=[pltpu.VMEM((blocks, 2*BQ, LN), jnp.bfloat16),
+                        pltpu.VMEM((blocks, BQ, LN), jnp.bfloat16),
+                        pltpu.VMEM((blocks, BQ, LN), jnp.bfloat16),
+                        pltpu.VMEM((blocks, 2*BQ, BQ), jnp.float32)],
+        compiler_params=pltpu.CompilerParams(vmem_limit_bytes=48 << 20),
+        name="attend",
+    )(first, x)
+
+def attn_bwd_kernel(length, first_ref, x_ref, do_ref, of_ref, lse_ref, cos_ref, sin_ref, out_ref,
+                    q_s, k_s, v_s, do_s, dl_s, dq_s, dk_s, dv_s):
+    j = pl.program_id(0)
+    blocks = length // BQ
+    first = first_ref[0]
+    @pl.when(j == 0)
+    def _():
+        def body(b, carry):
+            rows = pl.ds(pl.multiple_of(b * BQ, BQ), BQ)
+            q0, q1, k, v = unpack4(*split3(x_ref[rows, :]))
+            q_s[b, :BQ, :] = q0.astype(jnp.bfloat16)
+            q_s[b, BQ:, :] = q1.astype(jnp.bfloat16)
+            k_s[b] = k.astype(jnp.bfloat16)
+            v_s[b] = v.astype(jnp.bfloat16)
+            for d in range(2):
+                parts = unpack4(*split3(do_ref[2*b + d]))
+                for n, part in enumerate(parts):
+                    at = (n % 2) * BQ + d*128 + (n // 2) * 64
+                    do_s[b, at:at+64, :] = part.astype(jnp.bfloat16)
+            prod = do_s[b].astype(jnp.float32) * of_ref[b]
+            delta = jnp.broadcast_to(jnp.sum(prod, axis=1, keepdims=True), (2*BQ, LN))
+            dl_s[b] = jnp.transpose(delta, (1, 0))[:8, :]
+            dq_s[b] = jnp.zeros((2*BQ, LN), jnp.float32)
+            return carry
+        lax.fori_loop(0, blocks, body, 0)
+    clean_from = (length // 8 + BQ - 1) // BQ
+    clean_to = 3 * length // 4 // BQ
+    late = (3 * length // 4 + length // 8) // BQ
+    third = 3 * length // 4 // BQ
+    stop = jnp.where(j >= third, blocks, late)
+    k = k_s[j]
+    v = v_s[j]
+    dk_s[j] = jnp.zeros((BQ, LN), jnp.float32)
+    dv_s[j] = jnp.zeros((BQ, LN), jnp.float32)
+    key = j * BQ + lax.broadcasted_iota(jnp.int32, (BQ, 1), 0)
+
+    def step(i, masked):
+        q, do = q_s[i], do_s[i]
+        s = dotf(k, q, ((1,), (1,)))
+        p = jnp.exp2(s * C2 - lse_ref[i, 0:1, :])
+        if masked:
+            q_index = i * BQ + lax.broadcasted_iota(jnp.int32, (1, BQ), 1)
+            ok = (key <= q_index) & (key >= doc_low(q_index, first, length))
+            p = jnp.where(jnp.concatenate([ok, ok], axis=1), p, 0.0)
+        dp = dotf(v, do, ((1,), (1,)))
+        ds = (p * (dp - dl_s[i, 0:1, :])).astype(jnp.bfloat16)
+        dv_s[j] += dotf(p.astype(jnp.bfloat16), do, ((1,), (0,)))
+        dk_s[j] += dotf(ds, q, ((1,), (0,)))
+        dq_s[i] += dotf(ds, k, ((0,), (0,)))
+
+    def loop(lo, hi, masked):
+        def body(i, carry):
+            step(i, masked)
+            return carry
+        lax.fori_loop(lo, hi, body, 0)
+
+    step(j, True)
+    clean_lo = j + 1
+    clean_hi = jnp.where(j >= clean_from, jnp.maximum(clean_to, j + 1), j + 1)
+    loop(clean_lo, clean_hi, False)
+    loop(clean_hi, stop, True)
+
+    @pl.when(j == blocks - 1)
+    def _():
+        scale = HD ** -0.5
+        def body(b, carry):
+            rows = pl.ds(pl.multiple_of(b * BQ, BQ), BQ)
+            t = pack4(dq_s[b, :BQ, :] * scale, dq_s[b, BQ:, :] * scale, dk_s[b] * scale, dv_s[b])
+            t = jnp.concatenate(t, axis=1)
+            cosine, sine, lower = cos_sin3(cos_ref[rows, :], sin_ref[rows, :])
+            out_ref[rows, :] = turn(t, cosine, -sine, lower).astype(jnp.bfloat16)
+            return carry
+        lax.fori_loop(0, blocks, body, 0)
+
+def attn_bwd(first, x, do, of, lse, cos, sin):
+    length = x.shape[0]
+    blocks = length // BQ
+    whole = lambda a: pl.BlockSpec(a.shape, lambda j: (0,) * a.ndim)
+    return pl.pallas_call(
+        functools.partial(attn_bwd_kernel, length),
+        grid=(blocks,),
+        in_specs=[pl.BlockSpec(memory_space=pltpu.SMEM)] + [whole(a) for a in (x, do, of, lse, cos, sin)],
+        out_specs=pl.BlockSpec((length, 3*LN), lambda j: (0, 0)),
+        out_shape=jax.ShapeDtypeStruct((length, 3*LN), jnp.bfloat16),
+        scratch_shapes=[pltpu.VMEM((blocks, 2*BQ, LN), jnp.bfloat16),
+                        pltpu.VMEM((blocks, BQ, LN), jnp.bfloat16),
+                        pltpu.VMEM((blocks, BQ, LN), jnp.bfloat16),
+                        pltpu.VMEM((blocks, 2*BQ, LN), jnp.bfloat16),
+                        pltpu.VMEM((blocks, 8, 2*BQ), jnp.float32),
+                        pltpu.VMEM((blocks, 2*BQ, LN), jnp.float32),
+                        pltpu.VMEM((blocks, BQ, LN), jnp.float32),
+                        pltpu.VMEM((blocks, BQ, LN), jnp.float32)],
+        compiler_params=pltpu.CompilerParams(vmem_limit_bytes=56 << 20),
+        name="attend_back",
+    )(first, x, do, of, lse, cos, sin)
+
+
+def widen(table):
+    lane = lane_iota(table.shape[0])
+    second = jnp.where(lane < 96, pltpu.roll(table, 96, 1), pltpu.roll(table, 16, 1))
+    third = jnp.where(lane < 112, pltpu.roll(table, 112, 1), pltpu.roll(table, 32, 1))
+    return second, third
+
+
+def cos_sin3(cos, sin):
+    lane = lane_iota(cos.shape[0])
+    live = lane < 32
+    cos_two, cos_three = widen(cos)
+    sin_two, sin_three = widen(sin)
+    cosine = jnp.concatenate([cos, cos_two, jnp.where(live, cos_three, 1.0)], axis=1)
+    sine = jnp.concatenate([sin, sin_two, jnp.where(live, sin_three, 0.0)], axis=1)
+    wide = lax.broadcasted_iota(jnp.int32, cosine.shape, 1)
+    lower = (wide % HD) < HD // 2
+    return cosine, jnp.where(lower, -sine, sine), lower
+
+
+def turn(values, cosine, sine, lower):
+    width = values.shape[1]
+    swapped = jnp.where(
+        lower, pltpu.roll(values, width - HD // 2, 1), pltpu.roll(values, HD // 2, 1)
+    )
+    return values * cosine + swapped * sine
+
+
+def full_spec(array):
+    rank = array.ndim
+    return pl.BlockSpec(array.shape, lambda *_: (0,) * rank)
+
+
+def qkv_kernel(parts, rows, place_ref, *refs):
+    blocks = refs[:parts]
+    gain_ref, w_ref, cos_ref, sin_ref, a_ref, out_ref = refs[parts:]
+    tokens = blocks[0].shape[0] // rows
+    for k in range(parts):
+        z = lax.rem(place_ref[0] + (parts - k), parts)
+        stream = blocks[k][...].astype(jnp.float32)
+        factor = lax.rsqrt(jnp.mean(stream * stream, axis=-1, keepdims=True) + EPS)
+        normed = (stream * factor * gain_ref[...]).astype(jnp.bfloat16)
+        at = pl.ds(pl.multiple_of(z * tokens, tokens), tokens)
+        for r in range(rows):
+            a_ref[r, at, :] = normed[r * tokens : (r + 1) * tokens]
+        product = dotf(normed, w_ref[...], ((1,), (0,)))
+        for r in range(rows):
+            cosine, sine, lower = cos_sin3(cos_ref[r, at, :], sin_ref[r, at, :])
+            for h in range(product.shape[1] // (3 * LN)):
+                piece = product[r * tokens : (r + 1) * tokens, h * 3 * LN : (h + 1) * 3 * LN]
+                out_ref[h * rows + r, at, :] = turn(piece, cosine, sine, lower).astype(jnp.bfloat16)
+
+
+def qkv_call(place, blocks, gain, weight, cos, sin, rows):
+    parts = len(blocks)
+    count, width = blocks[0].shape
+    tokens = count // rows * parts
+    groups = weight.shape[1] // (3 * LN)
+    operands = (*blocks, gain, weight, cos, sin)
+    return pl.pallas_call(
+        partial(qkv_kernel, parts, rows),
+        grid=(1,),
+        in_specs=[pl.BlockSpec(memory_space=pltpu.SMEM)] + [full_spec(v) for v in operands],
+        out_specs=[
+            pl.BlockSpec((rows, tokens, width), lambda i: (0, 0, 0)),
+            pl.BlockSpec((groups * rows, tokens, 3 * LN), lambda i: (0, 0, 0)),
+        ],
+        out_shape=[
+            jax.ShapeDtypeStruct((rows, tokens, width), jnp.bfloat16),
+            jax.ShapeDtypeStruct((groups * rows, tokens, 3 * LN), jnp.bfloat16),
+        ],
+        compiler_params=pltpu.CompilerParams(vmem_limit_bytes=48 << 20),
+        name="norm_qkv",
+    )(place, *operands)
+
+
+def thirds(values):
+    return values[:, :LN], values[:, LN : 2 * LN], values[:, 2 * LN :]
+
+
+def join_pairs(left, right):
+    l0, l1, l2 = thirds(left)
+    r0, r1, r2 = thirds(right)
+    low = lane_iota(left.shape[0]) < 64
+    s0, s1, s2 = (pltpu.roll(v, 64, 1) for v in (r0, r1, r2))
+    firsts = (l0, jnp.where(low, l1, s0), jnp.where(low, s0, s1))
+    m1, m2 = pltpu.roll(l1, 64, 1), pltpu.roll(l2, 64, 1)
+    lasts = (jnp.where(low, m1, m2), jnp.where(low, m2, r1), r2)
+    return jnp.concatenate(firsts, axis=1), jnp.concatenate(lasts, axis=1)
+
+
+def out_kernel(rows, parts, o_ref, w_ref, tok_ref, gain_ref, mid_ref, b_ref, oo_ref, o_s):
+    half = o_ref.shape[1]
+    for r in range(rows):
+        for z in range(parts):
+            left = o_ref[r * parts + z].astype(jnp.float32)
+            right = o_ref[(rows + r) * parts + z].astype(jnp.float32)
+            for n, piece in enumerate(join_pairs(left, right)):
+                at = (2 * r + n) * half
+                o_s[at : at + half, z * 3 * LN : (z + 1) * 3 * LN] = piece.astype(jnp.bfloat16)
+    attended = o_s[...]
+    oo_ref[...] = attended
+    middle = tok_ref[...].astype(jnp.float32) + dotf(attended, w_ref[...], ((1,), (1,)))
+    mid_ref[...] = middle
+    factor = lax.rsqrt(jnp.mean(middle * middle, axis=-1, keepdims=True) + EPS)
+    b_ref[...] = (middle * factor * gain_ref[...]).astype(jnp.bfloat16)
+
+
+def out_call(o_parts, weight, tokens, gain, rows):
+    count, width = tokens.shape
+    inner = weight.shape[1]
+    operands = (o_parts, weight, tokens, gain)
+    shapes = [
+        jax.ShapeDtypeStruct((count, width), jnp.float32),
+        jax.ShapeDtypeStruct((count, width), jnp.bfloat16),
+        jax.ShapeDtypeStruct((count, inner), jnp.bfloat16),
+    ]
+    return pl.pallas_call(
+        partial(out_kernel, rows, o_parts.shape[0] // (2 * rows)),
+        grid=(1,),
+        in_specs=[full_spec(v) for v in operands],
+        out_specs=[full_spec(v) for v in shapes],
+        out_shape=shapes,
+        scratch_shapes=[pltpu.VMEM((count, inner), jnp.bfloat16)],
+        compiler_params=pltpu.CompilerParams(vmem_limit_bytes=48 << 20),
+        name="out_norm",
+    )(*operands)
+
+
+def split_pairs(firsts, lasts):
+    f0, f1, f2 = thirds(firsts)
+    g0, g1, g2 = thirds(lasts)
+    low = lane_iota(firsts.shape[0]) < 64
+    t0, t1 = pltpu.roll(g0, 64, 1), pltpu.roll(g1, 64, 1)
+    left = (f0, jnp.where(low, f1, t0), jnp.where(low, t0, t1))
+    u1, u2 = pltpu.roll(f1, 64, 1), pltpu.roll(f2, 64, 1)
+    right = (jnp.where(low, u1, u2), jnp.where(low, u2, g1), g2)
+    return jnp.concatenate(left, axis=1), jnp.concatenate(right, axis=1)
+
+
+def mid_back_kernel(
+    rows, parts, db_ref, mid_ref, cot_ref, gain_ref, w_ref, gmid_ref, go_ref, do_ref, gg_ref
+):
+    db = db_ref[...]
+    middle = mid_ref[...]
+    factor = lax.rsqrt(jnp.mean(middle * middle, axis=-1, keepdims=True) + EPS)
+    scaled = db * gain_ref[...]
+    inner = jnp.mean(scaled * middle, axis=-1, keepdims=True)
+    grad = cot_ref[...].astype(jnp.float32) + factor * scaled - middle * (factor**3 * inner)
+    gmid_ref[...] = grad
+    gg_ref[...] = jnp.sum(db * middle * factor, axis=0, keepdims=True)
+    low = grad.astype(jnp.bfloat16)
+    go_ref[...] = low
+    back = dotf(low, w_ref[...], ((1,), (0,)))
+    half = do_ref.shape[1]
+    for r in range(rows):
+        for z in range(parts):
+            cols = slice(z * 3 * LN, (z + 1) * 3 * LN)
+            at = 2 * r * half
+            left, right = split_pairs(back[at : at + half, cols], back[at + half : at + 2 * half, cols])
+            do_ref[r * parts + z] = left.astype(jnp.bfloat16)
+            do_ref[(rows + r) * parts + z] = right.astype(jnp.bfloat16)
+
+
+def mid_back_call(db, middle, cot, gain, weight, rows, parts):
+    count, width = middle.shape
+    operands = (db, middle, cot, gain, weight)
+    shapes = [
+        jax.ShapeDtypeStruct((count, width), jnp.float32),
+        jax.ShapeDtypeStruct((count, width), jnp.bfloat16),
+        jax.ShapeDtypeStruct((2 * rows * parts, count // rows // 2, 3 * LN), jnp.bfloat16),
+        jax.ShapeDtypeStruct((1, width), jnp.float32),
+    ]
+    return pl.pallas_call(
+        partial(mid_back_kernel, rows, parts),
+        grid=(1,),
+        in_specs=[full_spec(v) for v in operands],
+        out_specs=[full_spec(v) for v in shapes],
+        out_shape=shapes,
+        compiler_params=pltpu.CompilerParams(vmem_limit_bytes=48 << 20),
+        name="mid_back",
+    )(*operands)
+
+
+def da_kernel(parts, rows, place_ref, *refs):
+    blocks = refs[:parts]
+    d_ref, w_ref, da_ref, gg_ref = refs[parts:]
+    tokens = blocks[0].shape[0] // rows
+    groups = d_ref.shape[0]
+    total = jnp.zeros(gg_ref.shape, jnp.float32)
+    for k in range(parts):
+        z = lax.rem(place_ref[0] + (parts - k), parts)
+        at = pl.ds(pl.multiple_of(z * tokens, tokens), tokens)
+        left = jnp.concatenate(
+            [jnp.concatenate([d_ref[g, r, at, :] for r in range(rows)], axis=0) for g in range(groups)],
+            axis=1,
+        )
+        back = dotf(left, w_ref[...], ((1,), (1,)))
+        stream = blocks[k][...].astype(jnp.float32)
+        factor = lax.rsqrt(jnp.mean(stream * stream, axis=-1, keepdims=True) + EPS)
+        total = total + jnp.sum(back * stream * factor, axis=0, keepdims=True)
+        count = rows * tokens
+        da_ref[pl.ds(pl.multiple_of(z * count, count), count), :] = back.astype(jnp.bfloat16)
+    gg_ref[...] = total
+
+
+def da_call(place, blocks, grads, weight, rows):
+    parts = len(blocks)
+    count, width = blocks[0].shape
+    operands = (*blocks, grads, weight)
+    shapes = [
+        jax.ShapeDtypeStruct((parts * count, width), jnp.bfloat16),
+        jax.ShapeDtypeStruct((1, width), jnp.float32),
+    ]
+    return pl.pallas_call(
+        partial(da_kernel, parts, rows),
+        grid=(1,),
+        in_specs=[pl.BlockSpec(memory_space=pltpu.SMEM)] + [full_spec(v) for v in operands],
+        out_specs=[full_spec(v) for v in shapes],
+        out_shape=shapes,
+        compiler_params=pltpu.CompilerParams(vmem_limit_bytes=48 << 20),
+        name="da_part",
+    )(place, *operands)
+
+
+EVERY = ("y", "x", "c", "z")
+SWAP = ((0, 1), (1, 0))
+
+
+def swap(value, axis):
+    return lax.ppermute(value, axis, SWAP)
+
+
+def gather_blocks(value, size):
+    shift = lambda k: [(i, (i + k) % size) for i in range(size)]
+    order = sorted(range(1, size), key=lambda k: -min(k, size - k))
+    got = {k: lax.ppermute(value, "z", shift(k)) for k in order}
+    return [value] + [got[k] for k in range(1, size)]
+
+
+def gather_square(value):
+    half = value.shape[0] // 2
+    xn, yn = swap(value, "x"), swap(value, "y")
+    dg_first, dg_last = swap(yn[:half], "x"), swap(xn[half:], "y")
+    return jnp.concatenate([value, xn[:half], dg_first, yn[half:], dg_last, xn[half:], yn[:half]], axis=0)
+
+
+def reduce_square(part):
+    low = jnp.bfloat16
+    half = part.shape[0] // 8
+    piece = lambda n, m=1: part[n * half : (n + m) * half]
+    from_x = swap(piece(2, 2).astype(low), "x").astype(jnp.float32)
+    from_y = swap(piece(4, 2).astype(low), "y").astype(jnp.float32)
+    pass_y = swap((piece(7) + from_x[half:]).astype(low), "y").astype(jnp.float32)
+    pass_x = swap((piece(6) + from_y[half:]).astype(low), "x").astype(jnp.float32)
+    return jnp.concatenate(
+        [piece(0) + from_x[:half] + pass_y, piece(1) + from_y[:half] + pass_x], axis=0
+    )
+
+
+def all_to_all(value, axes):
+    return lax.all_to_all(value, axes, 0, 0, tiled=True)
+
+
+def tie(*values):
+    return lax.optimization_barrier(values)
+
+
+def dot(left, right, left_dim, right_dim, kind=jnp.float32):
+    return contract(left, right, left_dim, right_dim).astype(kind)
+
+
+def fast_local(sizes, *args):
+    (tokens, cotangent, segments, positions, norm_in, w_query, w_key, w_value, w_out, norm_mid, w_gate, w_up, w_down) = args
+    low = jnp.bfloat16
+    nz = sizes["z"]
+    devices = sizes["y"] * sizes["x"] * sizes["c"] * nz
+    plane = devices // nz
+    rows, span, width = tokens.shape
+    count = rows * span
+    chunk = segments.shape[1]
+    length = chunk * sizes["x"] * sizes["c"]
+    x_at, c_at, z_at = lax.axis_index("x"), lax.axis_index("c"), lax.axis_index("z")
+    place = z_at.reshape(1).astype(jnp.int32)
+
+    own = tokens.reshape(count, width)
+    blocks = gather_blocks(own, nz)
+
+    gains = jnp.concatenate([norm_in, norm_mid], axis=1)
+    share = norm_in.shape[1]
+    gains = jnp.pad(gains, ((0, 0), (0, LN - 2 * share)))
+    gains = all_to_all(jnp.broadcast_to(gains, (devices, LN)), EVERY)
+    gain_in = gains[:, :share].reshape(1, width)
+    gain_mid = gains[:, share : 2 * share].reshape(1, width)
+
+    kv_local = w_key.shape[2] // HD
+    per_head = lambda w: w[0].reshape(w.shape[1], kv_local, -1)
+    w_qkv = jnp.concatenate([per_head(w_query), per_head(w_key), per_head(w_value)], axis=2)
+    w_qkv = w_qkv.reshape(w_qkv.shape[0], -1)
+    w_qkv = lax.all_gather(w_qkv, ("y", "x", "c"), axis=0, tiled=True)
+
+    units = w_gate.shape[2] // plane
+    by_unit = lambda w: w.reshape(w.shape[0], plane, units)
+    w_ff = jnp.stack([by_unit(w_gate[0]), by_unit(w_up[0]), by_unit(w_down[0].T)], axis=2)
+    w_ff = jnp.transpose(w_ff, (1, 0, 2, 3)).reshape(width, 3 * units)
+    w_ff = all_to_all(w_ff, ("y", "x", "c"))
+
+    last = (x_at * sizes["c"] + c_at + 1) * chunk - 1
+    begin = last - positions[:, -1] - jnp.where(segments[:, -1] == 2, 3 * length // 4, 0)
+    lanes = jnp.arange(LN, dtype=jnp.int32) % (HD // 2)
+    frequency = THETA ** (-(2.0 * lanes.astype(jnp.float32)) / HD)
+    token_angle = positions.astype(jnp.float32)[:, :, None] * frequency
+    first = lax.dynamic_slice_in_dim(begin, c_at, 1).astype(jnp.int32)
+    index = jnp.arange(length, dtype=jnp.int32)
+    row_angle = (index - doc_low(index, first[0], length)).astype(jnp.float32)[:, None] * frequency
+    token_cos, token_sin = jnp.cos(token_angle), jnp.sin(token_angle)
+    row_cos, row_sin = jnp.cos(row_angle), jnp.sin(row_angle)
+
+    normed, qkv = qkv_call(place, blocks, gain_in, w_qkv, token_cos, token_sin, rows)
+    qkv = all_to_all(qkv, ("x", "c")).reshape(length, 3 * LN)
+
+    w_ff, *blocks = tie(w_ff, *blocks)
+    w_ff = lax.all_gather(w_ff, "z", axis=0, tiled=True).reshape(nz, width, 3, units)
+    w_ff = jnp.stack([w_ff, swap(w_ff, "c")], axis=0)
+    w_ff = jnp.transpose(w_ff, (3, 2, 0, 1, 4)).reshape(3, width, 2 * nz * units)
+    w_gu = jnp.transpose(w_ff[:2], (1, 0, 2)).reshape(width, -1)
+    w_d = w_ff[2]
+    w_o = lax.all_gather(w_out[0].T, EVERY, axis=0, tiled=True)
+    w_o = jnp.transpose(w_o.reshape(plane, nz, -1, w_out.shape[1]), (0, 2, 1, 3)).reshape(width, -1)
+    cot_low = cotangent.reshape(count, width)
+    cot_all = gather_square(cot_low)
+
+    attended, attended_float, log_total = attn_fwd(first, qkv)
+    attended = all_to_all(attended, ("x", "c", "z"))
+    middle, normed_b, attended_low = out_call(attended, w_o, own, gain_mid, rows)
+    b_all = gather_square(normed_b)
+
+    hidden_width = w_d.shape[1]
+    gate_up = dot(b_all, w_gu, 1, 0)
+    gate, up = gate_up[:, :hidden_width], gate_up[:, hidden_width:]
+    grad_hidden = dot(cot_all, w_d, 1, 0)
+    sigma = jax.nn.sigmoid(gate)
+    silu = gate * sigma
+    hidden = (silu * up).astype(low)
+    grad_gate = (grad_hidden * up * sigma * (1.0 + gate * (1.0 - sigma))).astype(low)
+    grad_up = (grad_hidden * silu).astype(low)
+    grad_gu = jnp.concatenate([grad_gate, grad_up], axis=1)
+    grad_b = reduce_square(dot(grad_gu, w_gu, 1, 1))
+    out = middle + reduce_square(dot(hidden, w_d, 1, 1))
+
+    grad_ff = jnp.concatenate(
+        [dot(b_all, grad_gu, 0, 0, low), dot(cot_all, hidden, 0, 0, low)], axis=1
+    )
+    grad_ff = jnp.transpose(grad_ff.reshape(width, 3, 2, nz, units), (2, 3, 0, 1, 4))
+    grad_ff = grad_ff.reshape(2, nz * width, 3 * units)
+    grad_ff = (grad_ff[0].astype(jnp.float32) + swap(grad_ff[1], "c").astype(jnp.float32)).astype(low)
+    grad_ff = lax.psum_scatter(grad_ff, "z", scatter_dimension=0, tiled=True)
+    grad_ff = all_to_all(grad_ff, ("y", "x", "c")).reshape(plane, width // plane, 3, units)
+    grad_ff = jnp.transpose(grad_ff.astype(jnp.float32), (2, 1, 0, 3)).reshape(3, width // plane, -1)
+
+    grad_mid, grad_low, grad_o, gain_grad_mid = mid_back_call(
+        grad_b, middle, cot_low, gain_mid, w_o, rows, nz
+    )
+    grad_o = all_to_all(grad_o, ("x", "c", "z"))
+    grad_wo = dot(grad_low, attended_low, 0, 0, low)
+    grad_wo = jnp.transpose(grad_wo.reshape(plane, -1, nz, w_out.shape[1]), (0, 2, 1, 3))
+    grad_wo = grad_wo.reshape(-1, w_out.shape[1])
+    grad_wo = lax.psum_scatter(grad_wo, EVERY, scatter_dimension=0, tiled=True)
+
+    grad_qkv = attn_bwd(first, qkv, grad_o, attended_float, log_total, row_cos, row_sin)
+    grad_qkv = all_to_all(grad_qkv.reshape(-1, chunk, 3 * LN), ("x", "c"))
+    grad_qkv = grad_qkv.reshape(kv_local, rows, chunk, 3 * LN)
+    part, gain_grad_in = da_call(place, blocks, grad_qkv, w_qkv, rows)
+    grad_a = lax.psum_scatter(part, "z", scatter_dimension=0, tiled=True)
+    normed = normed.reshape(rows * chunk, width)
+    grad_wqkv = jnp.concatenate(
+        [dot(normed, grad_qkv[h].reshape(rows * chunk, 3 * LN), 0, 0, low) for h in range(kv_local)], axis=1
+    )
+    grad_wqkv = lax.psum_scatter(grad_wqkv, ("y", "x", "c"), scatter_dimension=0, tiled=True)
+
+    gain_grads = jnp.concatenate(
+        [gain_grad_in.reshape(devices, share), gain_grad_mid.reshape(devices, share)], axis=1
+    )
+    gain_grads = jnp.pad(gain_grads, ((0, 0), (0, LN - 2 * share)))
+    gain_grads = jnp.sum(all_to_all(gain_grads, EVERY), axis=0, keepdims=True)
+
+    back_in, _ = norm_back(
+        own.astype(jnp.float32),
+        lax.rsqrt(jnp.mean(jnp.square(own.astype(jnp.float32)), axis=-1, keepdims=True) + EPS),
+        gain_in,
+        grad_a.astype(jnp.float32),
+    )
+    grad_tokens = grad_mid + back_in
+    grad_wqkv = grad_wqkv.astype(jnp.float32).reshape(-1, kv_local, 4 * HD)
+    flat = lambda g: g.reshape(1, g.shape[0], -1)
+    return (
+        out.reshape(tokens.shape),
+        grad_tokens.reshape(tokens.shape),
+        gain_grads[:, :share],
+        flat(grad_wqkv[:, :, : 2 * HD]),
+        flat(grad_wqkv[:, :, 2 * HD : 3 * HD]),
+        flat(grad_wqkv[:, :, 3 * HD :]),
+        grad_wo.astype(jnp.float32).T[None],
+        gain_grads[:, share : 2 * share],
+        grad_ff[0][None],
+        grad_ff[1][None],
+        grad_ff[2].T[None],
+    )
+
+
+def fast_solution(mesh, cores):
+    batch, seq, kv = mesh.devices.shape
+    fine = Mesh(mesh.devices.reshape(batch, seq // cores, cores, kv), EVERY)
+    sizes = dict(fine.shape)
+    row_spec = P("y", ("x", "c", "z"), None)
+    seq_spec = P("y", ("x", "c"))
+    gain_spec = P(None, EVERY)
+    in_w = P(None, ("y", "x", "c"), "z")
+    out_w = P(None, "z", ("y", "x", "c"))
+    in_specs = (row_spec, row_spec, seq_spec, seq_spec, gain_spec, in_w, in_w, in_w, out_w, gain_spec, in_w, in_w, out_w)
+    out_specs = (row_spec, row_spec, gain_spec, in_w, in_w, in_w, out_w, gain_spec, in_w, in_w, out_w)
+    return jax.shard_map(
+        partial(fast_local, sizes), mesh=fine, in_specs=in_specs, out_specs=out_specs, check_vma=False
+    )
+
+
+def solution(mesh):
+    batch, seq, kv = (mesh.shape[name] for name in ("batch", "seq", "kv"))
+    general = general_solution(mesh)
+    if (batch, seq) != (2, 4):
+        return general
+    fast = fast_solution(mesh, 2)
+
+    def run(*args):
+        rows, length, width = args[0].shape
+        kv_heads, q_heads = args[6].shape[2] // HD, args[5].shape[2] // HD
+        fits = (
+            rows == 2 * batch
+            and kv_heads == 2 * kv
+            and q_heads == 2 * kv_heads
+            and length == 128 * seq * kv
+            and length % (4 * BQ) == 0
+            and width % LN == 0
+            and 2 * width // (batch * seq * kv) <= LN
+            and args[10].shape[2] == LN * batch * seq * kv
+        )
+        return (fast if fits else general)(*args)
+
+    return run

time: 1490 us -> 876 us (0.59)
  waiting for transfers between devices: 974 us -> 372 us
  matrix products: 189 us -> 53.1 us
  Pallas kernels: 0 us -> 76.6 us
  starting transfers between devices: 1.62 us -> 75.7 us
  blocking collectives: 68.7 us -> 24.1 us
  local copies, waits for them, and re-layouts: 143 us -> 181 us
  other arithmetic: 85.3 us -> 65.5 us
    reduce_scatter x12 -> x3, waiting for transfers between devices: 476 us -> 180 us  [the longest x1 107 us: fast_local(): grad_wo = lax.psum_scatter(grad_wo, EVERY, scatter_dimension=0, tiled=True)]
    all_gather x10 -> x3, waiting for transfers between devices: 307 us -> 60.1 us  [the longest x1 41.9 us: fast_local(): w_o = lax.all_gather(w_out[0].T, EVERY, axis=0, tiled=True)]
    unnamed x26 -> x8, waiting for transfers between devices: 192 us -> 0.78 us
    dot_general x19 -> x0, matrix products: 108 us -> none  [the longest x2 20.8 us: backward_one_step(): jnp.einsum('kgqp,qkgd->pkd', probs_block.astype(jnp.bfloat16), grad_attn,...]
    ppermute x0 -> x21, waiting for transfers between devices: none -> 105 us  [the longest x18 55.2 us: swap(): return lax.ppermute(value, axis, SWAP)]
    pallas_call x0 -> x6, Pallas kernels: none -> 76.6 us  [the longest x1 31.3 us: attn_bwd(): pl.pallas_call(functools.partial(attn_bwd_kernel, length), grid=(blocks,)...]
    all_to_all x0 -> x7, starting transfers between devices: none -> 47.3 us  [all_to_all(): return lax.all_to_all(value, axes, 0, 0, tiled=True)]
    reshape x10 -> x13, local copies, waits for them, and re-layouts: 22.5 us -> 66.8 us  [the longest x2 36.9 us: fast_local(): grad_ff.reshape(width, 3, 2, nz, units)]
  transfers between devices with their start and end apart: 24 -> 35, of which waited for: 19 -> 19; matrix products, arithmetic and copies ran while one was open for 17% -> 25% of each run, Pallas kernels for 0% -> 8%
where the time goes in v1:
time: 876 us; the launch traced here: 864 us
  waiting for transfers between devices  372 us (42%)
  local copies, waits for them, and re-layouts  181 us (21%)
  Pallas kernels  76.6 us (9%)
  starting transfers between devices  75.7 us (9%)
  other arithmetic  65.5 us (7%)
  matrix products  53.1 us (6%)
  blocking collectives  24.1 us (3%)
  between operations  16.1 us (2%)
    reduce_scatter x1, waiting for transfers between devices, fast_local(): grad_wo = lax.psum_scatter(grad_wo, EVERY, scatter_dimension=0, tiled=True)  107 us
    reduce_scatter x1, waiting for transfers between devices, fast_local(): grad_a = lax.psum_scatter(part, 'z', scatter_dimension=0, tiled=True)  60 us
    unnamed x106, local copies, waits for them, and re-layouts  56.7 us
    ppermute x18, waiting for transfers between devices, swap(): return lax.ppermute(value, axis, SWAP)  55.2 us
    dot_general x9, matrix products, contract(): lax.dot_general(left_side, right_side, (((left_dim,), (right_dim,)), ((),...  53.1 us
    ppermute x3, waiting for transfers between devices, gather_blocks(): got = {k: lax.ppermute(value, 'z', shift(k)) for k in order}  50 us
    all_to_all x7, starting transfers between devices, all_to_all(): return lax.all_to_all(value, axes, 0, 0, tiled=True)  47.3 us
    all_gather x1, waiting for transfers between devices, fast_local(): w_o = lax.all_gather(w_out[0].T, EVERY, axis=0, tiled=True)  41.9 us
  transfers between devices with their start and end apart: 35, of which 19 were waited for; matrix products, arithmetic and copies ran while one was open for 25% of the time, Pallas kernels for 8%

profile of v1, /device:TPU:0, one launch (start us, length us, event | category | flops | bytes accessed | tf_op | source)
XLA Modules:
  0.0 864.3 jit_solution(18132670786643217980)
XLA Ops:
  19.8 5.3 all-to-all-start.3
  31.3 16.5 %collective-permute-done.refs_1_ = bf16[256,1536]{1,0:T(8,128)(2,1)S(1)} collective-permute-done((bf16[256,1536]{1,0:T(8,128)(2,1)S(1)}, bf16[256,1536]{1,0:T(8,128)(2,1)S(1)}, u32[]{:S(2)}, u32[]{:S(2)}) %collective-permute-start) | collective-permute-done | bytes 786464 | tf_op jit(solution)/shard_map/ppermute | solution.py:993
  47.8 33.4 %collective-permute-done.1.refs_2_ = bf16[256,1536]{1,0:T(8,128)(2,1)S(1)} collective-permute-done((bf16[256,1536]{1,0:T(8,128)(2,1)S(1)}, bf16[256,1536]{1,0:T(8,128)(2,1)S(1)}, u32[]{:S(2)}, u32[]{:S(2)}) %collective-permute-start.1) | collective-permute-done | bytes 786464 | tf_op jit(solution)/shard_map/ppermute | solution.py:993
  85.6 20.8 %all-to-all-start = ((f32[32,1,128]{2,1,0:T(1,128)}), f32[32,1,128]{2,1,0:T(1,128)S(1)}, u32[]{:S(2)}, u32[]{:S(2)}) async-start(f32[32,1,128]{2,1,0:T(1,128)} %broadcast_in_dim.41), calls=%async_computation | async-start | bytes 32768 | tf_op jit(solution)/shard_map/all_to_all | solution.py:1018
  109.4 4.0 all-to-all-done
  115.7 7.8 norm_qkv.1
  132.5 16.6 %all-to-all-done.1 = bf16[4,512,384]{2,1,0:T(8,128)(2,1)S(1)} async-done(((bf16[4,512,384]{2,1,0:T(8,128)(2,1)}), bf16[4,512,384]{2,1,0:T(8,128)(2,1)S(1)}, u32[]{:S(2)}, u32[]{:S(2)}) %all-to-all-start.1) | async-done | bytes 1572896 | tf_op jit(solution)/shard_map/all_to_all | solution.py:1018
  149.1 22.1 %attend.1 = (bf16[16,64,384]{2,1,0:T(8,128)(2,1)S(1)}, f32[8,512,128]{2,1,0:T(8,128)S(1)}, f32[8,8,512]{2,1,0:T(8,128)S(1)}) custom-call(s32[1]{0:T(128)} %bitcast.first_ref, bf16[2048,384]{1,0:T(8,128)(2,1)S(1)} %bitcast.131), custom_call_target="tpu_custom_call" | custom-call | tf_op jit(solution)/shard_map/attend/pallas_call | solution.py:642
  174.1 4.3 all-to-all-start.2
  183.0 18.2 %all-gather.8.cloned.1.call-done = bf16[6144,384]{0,1:T(8,128)(2,1)} async-done(((bf16[1536,384]{0,1:T(8,128)(2,1)}), bf16[6144,384]{0,1:T(8,128)(2,1)}) %all-gather.8.cloned.1.call-update) | async-done | bytes 4718608 | tf_op jit(solution)/shard_map/all_gather | solution.py:1079
  201.2 8.2 reshape.224
  217.4 7.6 collective-permute-done.15
  225.8 41.9 %all-gather.6.cloned.1.call-done = bf16[6144,384]{1,0:T(8,128)(2,1)} async-done(((bf16[192,384]{1,0:T(8,128)(2,1)}), bf16[6144,384]{1,0:T(8,128)(2,1)}) %all-gather.6.cloned.1.call-update) | async-done | bytes 4718608 | tf_op jit(solution)/shard_map/all_gather | solution.py:1084
  267.7 6.0 copy.75
  276.8 4.3 out_norm.1
  287.8 8.2 stack_reshape.7
  296.9 6.2 collective-permute-done.4
  308.2 6.2 collective-permute-done.5
  321.3 9.4 %maximum_bitcast_fusion = bf16[3,1536,2,4,128]{1,3,4,0,2:T(4,128)(2,1)} fusion(bf16[1,4,1536,3,128]{2,1,4,3,0:T(4,128)(2,1)} %bitcast.14, bf16[1,4,1536,3,128]{2,1,4,3,0:T(4,128)(2,1)S(1)} %copy-done.20), kind=kLoop, calls=%fused_computation | loop fusion | flops 4718592 | bytes 18874368 | tf_op jit(solution)/shard_map/transpose | solution.py:1081
  336.0 11.4 %fusion.37 = f32[1024,2048]{1,0:T(8,128)} fusion(bf16[1024,1536]{1,0:T(8,128)(2,1)} %constant_dynamic-update-slice_fusion, bf16[1536,2048]{0,1:T(8,128)(2,1)S(1)} %bitcast.148), kind=kOutput, calls=%fused_computation.101 | convolution fusion | flops 6442450944 | bytes 17825792 | tf_op jit(solution)/shard_map/dot_general | solution.py:54
  347.4 8.5 multiply_convert_fusion.1
  356.0 6.7 fusion.35
  365.8 9.0 %convolution_convert_fusion = bf16[1536,2048]{1,0:T(8,128)(2,1)S(1)} fusion(bf16[1024,1536]{1,0:T(8,128)(2,1)} %constant_dynamic-update-slice_fusion, bf16[1024,1024]{1,0:T(8,128)(2,1)S(1)} %copy-done.41, bf16[1024,1024]{1,0:T(8,128)(2,1)S(1)} %get-tuple-element.71), kind=kOutput, calls=%fused_computation.3 | convolution fusion | flops 6453985280 | bytes 13631488 | tf_op jit(solution)/shard_map/dot_general | solution.py:54
  374.9 6.2 collective-permute-done.16
  382.6 5.8 convolution_convert_fusion.2
  391.1 4.6 pad_maximum_fusion
  395.6 17.7 %reshape.240 = bf16[1536,3,2,4,128]{4,3,2,1,0:T(4,128)(2,1)} reshape(bf16[1536,3072]{1,0:T(8,128)(2,1)} %pad_maximum_fusion) | data formatting | bytes 18874368 | tf_op jit(solution)/shard_map/reshape | solution.py:1110
  413.3 19.2 %copy.91 = bf16[1536,3,2,4,128]{0,3,4,1,2:T(4,128)(2,1)} copy(bf16[1536,3,2,4,128]{4,3,2,1,0:T(4,128)(2,1)} %reshape.240) | data formatting | bytes 18874368 | tf_op jit(solution)/shard_map/reshape | solution.py:1110
  434.2 4.8 mid_back.1
  445.1 10.3 %fusion.26 = (bf16[1,4,1536,3,128]{2,1,4,3,0:T(4,128)(2,1)S(1)}, f32[1,4,1536,3,128]{2,1,4,3,0:T(4,128)}) fusion(bf16[2,4,1536,3,128]{2,1,4,3,0:T(4,128)(2,1)} %bitcast.142), kind=kLoop, calls=%fused_computation.90 | loop fusion | flops 2359296 | bytes 23592960 | tf_op jit(solution)/shard_map/slice | solution.py:1112
  460.6 5.6 multiply_sine_fusion
  467.3 31.3 %attend_back.1 = bf16[2048,384]{1,0:T(8,128)(2,1)} custom-call(s32[1]{0:T(128)} %bitcast.first_ref, bf16[2048,384]{1,0:T(8,128)(2,1)} %bitcast.132, bf16[16,64,384]{2,1,0:T(8,128)(2,1)} %copy-done.24, f32[8,512,128]{2,1,0:T(8,128)} %copy-done.11, f32[8,8,512]{2,1,0:T(8,128)} %copy-done.19, f32[2048,128]{1,0:T(8,128)} %get-tuple-element.96.cos_ref, ...), custom_call_target="tpu_custom_call" | custom-call | tf_op jit(solution)/shard_map/attend_back/pallas_call | solution.py:739
  501.2 24.1 %all_to_all.59 = bf16[4,512,384]{1,2,0:T(8,128)(2,1)S(1)} all-to-all(bf16[4,512,384]{1,2,0:T(8,128)(2,1)} %copy.84), channel_id=1, replica_groups=mesh['y'=2,'x'=2,'c'=2,'z'=4] {'x','c'}, dimensions={0} | all-to-all | bytes 3145728 | tf_op jit(solution)/shard_map/all_to_all | solution.py:1018
  529.6 4.3 copy.103
  533.9 11.6 %copy.110 = f32[48,8,4,1536]{3,1,2,0:T(8,128)} copy(f32[48,8,4,1536]{3,2,1,0:T(4,128)} %bitcast.141) | data formatting | bytes 18874368
  545.5 8.7 %add_convert_fusion = bf16[6144,384]{0,1:T(8,128)(2,1)} fusion(f32[6144,384]{0,1:T(8,128)} %bitcast.140, bf16[6144,384]{0,1:T(8,128)(2,1)} %collective-permute-done.20), kind=kLoop, calls=%fused_computation.2 | loop fusion | flops 7077888 | bytes 18874368 | tf_op jit(solution)/shard_map/convert_element_type | solution.py:1112
  558.0 9.1 %reshape.238 = bf16[8,192,4,384]{3,2,1,0:T(4,128)(2,1)} reshape(bf16[1536,1536]{1,0:T(8,128)(2,1)} %convolution_convert_fusion.1) | data formatting | bytes 9437184 | tf_op jit(solution)/shard_map/reshape | solution.py:1122
  567.0 5.5 copy.89
  577.0 6.3 da_part.1
  585.6 5.3 fusion.36
  592.9 17.0 %collective-permute-done.8 = bf16[256,1536]{1,0:T(8,128)(2,1)S(1)} collective-permute-done((bf16[256,1536]{1,0:T(8,128)(2,1)S(1)}, bf16[256,1536]{1,0:T(8,128)(2,1)S(1)}, u32[]{:S(2)}, u32[]{:S(2)}) %collective-permute-start.8) | collective-permute-done | bytes 786464 | tf_op jit(solution)/shard_map/ppermute | solution.py:987
  612.0 7.9 collective-permute-done.9
  634.1 5.0 all-to-all-start.6
  641.6 4.8 all-to-all-done.6
  650.8 13.0 %reduce-scatter.11.cloned.1.call-done = bf16[1536,384]{0,1:T(8,128)(2,1)} async-done(((bf16[6144,384]{0,1:T(8,128)(2,1)}), bf16[1536,384]{0,1:T(8,128)(2,1)}) %reduce-scatter.11.cloned.1.call-update) | async-done | bytes 1179664 | tf_op jit(solution)/shard_map/reduce_scatter | solution.py:1113
  670.1 107.4 %reduce-scatter.9.cloned.1.call-done = bf16[192,384]{1,0:T(8,128)(2,1)} async-done(((bf16[6144,384]{1,0:T(8,128)(2,1)}), bf16[192,384]{1,0:T(8,128)(2,1)}) %reduce-scatter.9.cloned.1.call-update) | async-done | bytes 147472 | tf_op jit(solution)/shard_map/reduce_scatter | solution.py:1124
  779.1 60.0 %reduce-scatter.7.cloned.1.call-done = bf16[256,1536]{1,0:T(8,128)(2,1)} async-done(((bf16[1024,1536]{1,0:T(8,128)(2,1)}), bf16[256,1536]{1,0:T(8,128)(2,1)}) %reduce-scatter.7.cloned.1.call-update) | async-done | bytes 786448 | tf_op jit(solution)/shard_map/reduce_scatter | solution.py:1130
  845.9 6.5 fusion.27
  (239 shorter events, 163.6 us)
Async XLA Ops:
  7.2 106.4 %all-gather.4.cloned.1.call-start = ((), (), s32[]{:S(2)}) async-start(), calls=%async_computation.12 | async-start | bytes 2654208 | tf_op jit(solution)/shard_map/all_gather | solution.py:1056
  19.8 65.1 %copy-start.36 = (f32[1,48]{1,0:T(1,128)S(1)}, f32[1,48]{1,0:T(1,128)}, u32[]{:S(2)}) copy-start(f32[1,48]{1,0:T(1,128)} %param.22) | copy-start | bytes 580
  19.8 65.1 %copy-start.37 = (f32[1,48]{1,0:T(1,128)S(1)}, f32[1,48]{1,0:T(1,128)}, u32[]{:S(2)}) copy-start(f32[1,48]{1,0:T(1,128)} %param.17) | copy-start | bytes 580
  19.8 86.6 %copy-start.32 = (s32[2,512]{1,0:T(2,128)S(1)}, s32[2,512]{1,0:T(2,128)}, u32[]{:S(2)}) copy-start(s32[2,512]{1,0:T(2,128)} %param.16) | copy-start | bytes 12292
  19.8 61.4 %all-to-all-start.3 = ((bf16[8,192,384]{2,1,0:T(8,128)(2,1)}), bf16[8,192,384]{2,1,0:T(8,128)(2,1)}, u32[]{:S(2)}, u32[]{:S(2)}) async-start(bf16[8,192,384]{2,1,0:T(8,128)(2,1)} %all_to_all.42), calls=%async_computation.3 | async-start | bytes 2359296 | tf_op jit(solution)/shard_map/all_to_all | solution.py:1018
  25.1 176.2 %all-gather.8.cloned.1.call-start = ((), (), s32[]{:S(2)}) async-start(), calls=%async_computation.14 | async-start | bytes 5898240 | tf_op jit(solution)/shard_map/all_gather | solution.py:1079
  25.1 22.6 %collective-permute-start = (bf16[256,1536]{1,0:T(8,128)(2,1)S(1)}, bf16[256,1536]{1,0:T(8,128)(2,1)S(1)}, u32[]{:S(2)}, u32[]{:S(2)}) collective-permute-start(bf16[256,1536]{1,0:T(8,128)(2,1)S(1)} %bitcast.125), channel_id=1, source_target_pairs={{0,1},{1,2},{2,3},{3,0},{4,5},{5,6},{6,7},{7,4},{8,9},{9,10},{10,1... | collective-permute-start | bytes 2359304 | tf_op jit(solution)/shard_map/ppermute | solution.py:993
  27.3 53.9 %collective-permute-start.1 = (bf16[256,1536]{1,0:T(8,128)(2,1)S(1)}, bf16[256,1536]{1,0:T(8,128)(2,1)S(1)}, u32[]{:S(2)}, u32[]{:S(2)}) collective-permute-start(bf16[256,1536]{1,0:T(8,128)(2,1)S(1)} %bitcast.126), channel_id=1, source_target_pairs={{0,2},{1,3},{2,0},{3,1},{4,6},{5,7},{6,4},{7,5},{8,10},{9,11},{10,... | collective-permute-start | bytes 2359304 | tf_op jit(solution)/shard_map/ppermute | solution.py:993
  29.9 51.3 %collective-permute-start.2 = (bf16[256,1536]{1,0:T(8,128)(2,1)S(1)}, bf16[256,1536]{1,0:T(8,128)(2,1)S(1)}, u32[]{:S(2)}, u32[]{:S(2)}) collective-permute-start(bf16[256,1536]{1,0:T(8,128)(2,1)S(1)} %bitcast.127), channel_id=1, source_target_pairs={{0,3},{1,0},{2,1},{3,2},{4,7},{5,4},{6,5},{7,6},{8,11},{9,8},{10,9... | collective-permute-start | bytes 2359304 | tf_op jit(solution)/shard_map/ppermute | solution.py:993
  47.8 75.7 %copy-start.5 = (bf16[256,1536]{1,0:T(8,128)(2,1)}, bf16[256,1536]{1,0:T(8,128)(2,1)S(1)}, u32[]{:S(2)}) copy-start(bf16[256,1536]{1,0:T(8,128)(2,1)S(1)} %collective-permute-done.refs_1_) | copy-start | bytes 2359300
  81.2 42.3 %copy-start.7 = (bf16[256,1536]{1,0:T(8,128)(2,1)}, bf16[256,1536]{1,0:T(8,128)(2,1)S(1)}, u32[]{:S(2)}) copy-start(bf16[256,1536]{1,0:T(8,128)(2,1)S(1)} %collective-permute-done.1.refs_2_) | copy-start | bytes 2359300
  81.2 32.4 %copy-start.9 = (bf16[256,1536]{1,0:T(8,128)(2,1)}, bf16[256,1536]{1,0:T(8,128)(2,1)S(1)}, u32[]{:S(2)}) copy-start(bf16[256,1536]{1,0:T(8,128)(2,1)S(1)} %collective-permute-done.2.refs_3_) | copy-start | bytes 2359300
  84.1 183.6 %all-gather.6.cloned.1.call-start = ((), (), s32[]{:S(2)}) async-start(), calls=%async_computation.13 | async-start | bytes 4866048 | tf_op jit(solution)/shard_map/all_gather | solution.py:1084
  85.6 27.9 %all-to-all-start = ((f32[32,1,128]{2,1,0:T(1,128)}), f32[32,1,128]{2,1,0:T(1,128)S(1)}, u32[]{:S(2)}, u32[]{:S(2)}) async-start(f32[32,1,128]{2,1,0:T(1,128)} %broadcast_in_dim.41), calls=%async_computation | async-start | bytes 32768 | tf_op jit(solution)/shard_map/all_to_all | solution.py:1018
  124.7 24.4 %all-to-all-start.1 = ((bf16[4,512,384]{2,1,0:T(8,128)(2,1)}), bf16[4,512,384]{2,1,0:T(8,128)(2,1)S(1)}, u32[]{:S(2)}, u32[]{:S(2)}) async-start(bf16[4,512,384]{2,1,0:T(8,128)(2,1)} %copy-done.14), calls=%async_computation.1 | async-start | bytes 3145728 | tf_op jit(solution)/shard_map/all_to_all | solution.py:1018
  128.6 50.8 %collective-permute-start.13 = (bf16[256,1536]{1,0:T(8,128)(2,1)S(1)}, bf16[256,1536]{1,0:T(8,128)(2,1)}, u32[]{:S(2)}, u32[]{:S(2)}) collective-permute-start(bf16[256,1536]{1,0:T(8,128)(2,1)S(1)} %bitcast.134), channel_id=1, source_target_pairs={{0,16},{16,0},{1,17},{17,1},{2,18},{18,2},{3,19},{19,3},{4,20},{20... | collective-permute-start | bytes 2359304 | tf_op jit(solution)/shard_map/ppermute | solution.py:987
  129.2 80.2 %collective-permute-start.12 = (bf16[256,1536]{1,0:T(8,128)(2,1)S(1)}, bf16[256,1536]{1,0:T(8,128)(2,1)}, u32[]{:S(2)}, u32[]{:S(2)}) collective-permute-start(bf16[256,1536]{1,0:T(8,128)(2,1)S(1)} %bitcast.135), channel_id=1, source_target_pairs={{0,8},{8,0},{1,9},{9,1},{2,10},{10,2},{3,11},{11,3},{4,12},{12,4},... | collective-permute-start | bytes 2359304 | tf_op jit(solution)/shard_map/ppermute | solution.py:987
  149.1 60.4 %copy-start.1 = (bf16[4,512,384]{2,1,0:T(8,128)(2,1)}, bf16[4,512,384]{2,1,0:T(8,128)(2,1)S(1)}, u32[]{:S(2)}) copy-start(bf16[4,512,384]{2,1,0:T(8,128)(2,1)S(1)} %all-to-all-done.1) | copy-start | bytes 4718596
  174.1 102.6 %all-to-all-start.2 = ((bf16[16,64,384]{2,1,0:T(8,128)(2,1)}), bf16[16,64,384]{2,1,0:T(8,128)(2,1)}, u32[]{:S(2)}, u32[]{:S(2)}) async-start(bf16[16,64,384]{2,1,0:T(8,128)(2,1)} %copy-done.17), calls=%async_computation.2 | async-start | bytes 1572864 | tf_op jit(solution)/shard_map/all_to_all | solution.py:1018
  181.2 33.6 %collective-permute-start.14 = (bf16[128,1536]{1,0:T(8,128)(2,1)}, bf16[128,1536]{1,0:T(8,128)(2,1)S(1)}, u32[]{:S(2)}, u32[]{:S(2)}) collective-permute-start(bf16[128,1536]{1,0:T(8,128)(2,1)} %slice.239), channel_id=1, source_target_pairs={{0,8},{8,0},{1,9},{9,1},{2,10},{10,2},{3,11},{11,3},{4,12},{12,4},... | collective-permute-start | bytes 1179656 | tf_op jit(solution)/shard_map/ppermute | solution.py:987
  209.5 111.8 %collective-permute-start.7 = (bf16[4,1536,3,128]{1,0,3,2:T(4,128)(2,1)}, bf16[4,1536,3,128]{1,0,3,2:T(4,128)(2,1)}, u32[]{:S(2)}, u32[]{:S(2)}) collective-permute-start(bf16[4,1536,3,128]{1,0,3,2:T(4,128)(2,1)} %reshape.224), channel_id=1, source_target_pairs={{0,4},{4,0},{1,5},{5,1},{2,6},{6,2},{3,7},{7,3},{8,12},{12,8},{9,1... | collective-permute-start | bytes 14155784 | tf_op jit(solution)/shard_map/ppermute | solution.py:987
  211.4 13.6 %collective-permute-start.15 = (bf16[128,1536]{1,0:T(8,128)(2,1)S(1)}, bf16[128,1536]{1,0:T(8,128)(2,1)S(1)}, u32[]{:S(2)}, u32[]{:S(2)}) collective-permute-start(bf16[128,1536]{1,0:T(8,128)(2,1)S(1)} %get-tuple-element.87), channel_id=1, source_target_pairs={{0,16},{16,0},{1,17},{17,1},{2,18},{18,2},{3,19},{19,3},{4,20},{20... | collective-permute-start | bytes 1179656 | tf_op jit(solution)/shard_map/ppermute | solution.py:987
  282.2 22.7 %collective-permute-start.3 = (bf16[256,1536]{1,0:T(8,128)(2,1)S(1)}, bf16[256,1536]{1,0:T(8,128)(2,1)}, u32[]{:S(2)}, u32[]{:S(2)}) collective-permute-start(bf16[256,1536]{1,0:T(8,128)(2,1)S(1)} %get-tuple-element.33), channel_id=1, source_target_pairs={{0,8},{8,0},{1,9},{9,1},{2,10},{10,2},{3,11},{11,3},{4,12},{12,4},... | collective-permute-start | bytes 2359304 | tf_op jit(solution)/shard_map/ppermute | solution.py:987
  283.6 19.5 %collective-permute-start.4 = (bf16[256,1536]{1,0:T(8,128)(2,1)S(1)}, bf16[256,1536]{1,0:T(8,128)(2,1)}, u32[]{:S(2)}, u32[]{:S(2)}) collective-permute-start(bf16[256,1536]{1,0:T(8,128)(2,1)S(1)} %get-tuple-element.33), channel_id=1, source_target_pairs={{0,16},{16,0},{1,17},{17,1},{2,18},{18,2},{3,19},{19,3},{4,20},{20... | collective-permute-start | bytes 2359304 | tf_op jit(solution)/shard_map/ppermute | solution.py:987
  304.2 10.2 %collective-permute-start.5 = (bf16[128,1536]{1,0:T(8,128)(2,1)S(1)}, bf16[128,1536]{1,0:T(8,128)(2,1)S(1)}, u32[]{:S(2)}, u32[]{:S(2)}) collective-permute-start(bf16[128,1536]{1,0:T(8,128)(2,1)S(1)} %slice.221), channel_id=1, source_target_pairs={{0,8},{8,0},{1,9},{9,1},{2,10},{10,2},{3,11},{11,3},{4,12},{12,4},... | collective-permute-start | bytes 1179656 | tf_op jit(solution)/shard_map/ppermute | solution.py:987
  306.7 10.2 %collective-permute-start.6 = (bf16[128,1536]{1,0:T(8,128)(2,1)S(1)}, bf16[128,1536]{1,0:T(8,128)(2,1)S(1)}, u32[]{:S(2)}, u32[]{:S(2)}) collective-permute-start(bf16[128,1536]{1,0:T(8,128)(2,1)S(1)} %get-tuple-element.89), channel_id=1, source_target_pairs={{0,16},{16,0},{1,17},{17,1},{2,18},{18,2},{3,19},{19,3},{4,20},{20... | collective-permute-start | bytes 1179656 | tf_op jit(solution)/shard_map/ppermute | solution.py:987
  362.8 25.6 %collective-permute-start.18 = (bf16[256,1536]{1,0:T(8,128)(2,1)S(1)}, bf16[256,1536]{1,0:T(8,128)(2,1)S(1)}, u32[]{:S(2)}, u32[]{:S(2)}) collective-permute-start(bf16[256,1536]{1,0:T(8,128)(2,1)S(1)} %get-tuple-element.84), channel_id=1, source_target_pairs={{0,16},{16,0},{1,17},{17,1},{2,18},{18,2},{3,19},{19,3},{4,20},{20... | collective-permute-start | bytes 2359304 | tf_op jit(solution)/shard_map/ppermute | solution.py:987
  364.0 17.1 %collective-permute-start.16 = (bf16[256,1536]{1,0:T(8,128)(2,1)S(1)}, bf16[256,1536]{1,0:T(8,128)(2,1)S(1)}, u32[]{:S(2)}, u32[]{:S(2)}) collective-permute-start(bf16[256,1536]{1,0:T(8,128)(2,1)S(1)} %get-tuple-element.83), channel_id=1, source_target_pairs={{0,8},{8,0},{1,9},{9,1},{2,10},{10,2},{3,11},{11,3},{4,12},{12,4},... | collective-permute-start | bytes 2359304 | tf_op jit(solution)/shard_map/ppermute | solution.py:987
  381.4 7.8 collective-permute-start.17
  390.0 42.5 %collective-permute-start.19 = (bf16[128,1536]{1,0:T(8,128)(2,1)S(1)}, bf16[128,1536]{1,0:T(8,128)(2,1)}, u32[]{:S(2)}, u32[]{:S(2)}) collective-permute-start(bf16[128,1536]{1,0:T(8,128)(2,1)S(1)} %get-tuple-element.77), channel_id=1, source_target_pairs={{0,8},{8,0},{1,9},{9,1},{2,10},{10,2},{3,11},{11,3},{4,12},{12,4},... | collective-permute-start | bytes 1179656 | tf_op jit(solution)/shard_map/ppermute | solution.py:987
  441.0 25.4 %all-to-all-start.4 = ((bf16[16,64,384]{2,1,0:T(8,128)(2,1)}), bf16[16,64,384]{2,1,0:T(8,128)(2,1)S(1)}, u32[]{:S(2)}, u32[]{:S(2)}) async-start(bf16[16,64,384]{2,1,0:T(8,128)(2,1)} %copy-done.18), calls=%async_computation.4 | async-start | bytes 1572864 | tf_op jit(solution)/shard_map/all_to_all | solution.py:1018
  445.1 202.0 %reduce-scatter.13.cloned.1.call-start = ((), (), s32[]{:S(2)}) async-start(), calls=%async_computation.18 | async-start | bytes 2654208
  458.9 86.6 %collective-permute-start.20 = (bf16[6144,384]{0,1:T(8,128)(2,1)}, bf16[6144,384]{0,1:T(8,128)(2,1)}, u32[]{:S(2)}, u32[]{:S(2)}) collective-permute-start(bf16[6144,384]{0,1:T(8,128)(2,1)} %bitcast.84), channel_id=1, source_target_pairs={{0,4},{4,0},{1,5},{5,1},{2,6},{6,2},{3,7},{7,3},{8,12},{12,8},{9,1... | collective-permute-start | bytes 14155784 | tf_op jit(solution)/shard_map/ppermute | solution.py:987
  533.9 129.8 %reduce-scatter.11.cloned.1.call-start = ((), (), s32[]{:S(2)}) async-start(), calls=%async_computation.17 | async-start | bytes 5898240 | tf_op jit(solution)/shard_map/reduce_scatter | solution.py:1113
  554.3 223.2 %reduce-scatter.9.cloned.1.call-start = ((), (), s32[]{:S(2)}) async-start(), calls=%async_computation.16 | async-start | bytes 4866048 | tf_op jit(solution)/shard_map/reduce_scatter | solution.py:1124
  572.5 266.7 %reduce-scatter.7.cloned.1.call-start = ((), (), s32[]{:S(2)}) async-start(), calls=%async_computation.15 | async-start | bytes 3932160 | tf_op jit(solution)/shard_map/reduce_scatter | solution.py:1130
  590.9 29.1 %copy-start.27 = (f32[1024,1536]{1,0:T(8,128)}, f32[1024,1536]{1,0:T(8,128)S(1)}, u32[]{:S(2)}) copy-start(f32[1024,1536]{1,0:T(8,128)S(1)} %get-tuple-element.104) | copy-start | bytes 18874372
  591.0 18.9 %collective-permute-start.8 = (bf16[256,1536]{1,0:T(8,128)(2,1)S(1)}, bf16[256,1536]{1,0:T(8,128)(2,1)S(1)}, u32[]{:S(2)}, u32[]{:S(2)}) collective-permute-start(bf16[256,1536]{1,0:T(8,128)(2,1)S(1)} %get-tuple-element.85), channel_id=1, source_target_pairs={{0,8},{8,0},{1,9},{9,1},{2,10},{10,2},{3,11},{11,3},{4,12},{12,4},... | collective-permute-start | bytes 2359304 | tf_op jit(solution)/shard_map/ppermute | solution.py:987
  591.6 20.2 %collective-permute-start.10 = (bf16[256,1536]{1,0:T(8,128)(2,1)S(1)}, bf16[256,1536]{1,0:T(8,128)(2,1)S(1)}, u32[]{:S(2)}, u32[]{:S(2)}) collective-permute-start(bf16[256,1536]{1,0:T(8,128)(2,1)S(1)} %get-tuple-element.86), channel_id=1, source_target_pairs={{0,16},{16,0},{1,17},{17,1},{2,18},{18,2},{3,19},{19,3},{4,20},{20... | collective-permute-start | bytes 2359304 | tf_op jit(solution)/shard_map/ppermute | solution.py:987
  610.1 9.8 %collective-permute-start.9 = (bf16[128,1536]{1,0:T(8,128)(2,1)S(1)}, bf16[128,1536]{1,0:T(8,128)(2,1)S(1)}, u32[]{:S(2)}, u32[]{:S(2)}) collective-permute-start(bf16[128,1536]{1,0:T(8,128)(2,1)S(1)} %fusion.14), channel_id=1, source_target_pairs={{0,16},{16,0},{1,17},{17,1},{2,18},{18,2},{3,19},{19,3},{4,20},{20... | collective-permute-start | bytes 1179656 | tf_op jit(solution)/shard_map/ppermute | solution.py:987
  612.0 27.1 %copy-start.3 = (f32[256,1536]{1,0:T(8,128)S(1)}, f32[256,1536]{1,0:T(8,128)}, u32[]{:S(2)}) copy-start(f32[256,1536]{1,0:T(8,128)} %copy-done.2) | copy-start | bytes 4718596
  620.3 9.9 %collective-permute-start.11 = (bf16[128,1536]{1,0:T(8,128)(2,1)S(1)}, bf16[128,1536]{1,0:T(8,128)(2,1)}, u32[]{:S(2)}, u32[]{:S(2)}) collective-permute-start(bf16[128,1536]{1,0:T(8,128)(2,1)S(1)} %get-tuple-element.79), channel_id=1, source_target_pairs={{0,8},{8,0},{1,9},{9,1},{2,10},{10,2},{3,11},{11,3},{4,12},{12,4},... | collective-permute-start | bytes 1179656 | tf_op jit(solution)/shard_map/ppermute | solution.py:987
  634.1 12.3 %all-to-all-start.6 = ((f32[32,1,128]{2,1,0:T(1,128)}), f32[32,1,128]{2,1,0:T(1,128)S(1)}, u32[]{:S(2)}, u32[]{:S(2)}) async-start(f32[32,1,128]{2,1,0:T(1,128)} %bitcast.29), calls=%async_computation.7 | async-start | bytes 32768 | tf_op jit(solution)/shard_map/all_to_all | solution.py:1018
  649.1 190.1 %copy-start.31 = (f32[1536]{0:T(1024)S(1)}, f32[1536]{0:T(1024)}, u32[]{:S(2)}) copy-start(f32[1536]{0:T(1024)} %mul.124) | copy-start | bytes 18436
  650.7 189.9 %copy-start.16 = (f32[256,1536]{1,0:T(8,128)S(1)}, f32[256,1536]{1,0:T(8,128)}, u32[]{:S(2)}) copy-start(f32[256,1536]{1,0:T(8,128)} %copy-done.15) | copy-start | bytes 4718596
  650.7 189.9 %copy-start.33 = (f32[256]{0:T(256)S(1)}, f32[256]{0:T(256)}, u32[]{:S(2)}) copy-start(f32[256]{0:T(256)} %multiply_multiply_fusion) | copy-start | bytes 3076
  650.7 190.0 %copy-start.34 = (f32[256]{0:T(256)S(1)}, f32[256]{0:T(256)}, u32[]{:S(2)}) copy-start(f32[256]{0:T(256)} %rsqrt_bitcast_fusion) | copy-start | bytes 3076
  666.1 177.3 %all-to-all-start.7 = ((bf16[8,192,384]{2,1,0:T(8,128)(2,1)}), bf16[8,192,384]{2,1,0:T(8,128)(2,1)S(1)}, u32[]{:S(2)}, u32[]{:S(2)}) async-start(bf16[8,192,384]{2,1,0:T(8,128)(2,1)} %bitcast.43), calls=%async_computation.10 | async-start | bytes 2359296 | tf_op jit(solution)/shard_map/all_to_all | solution.py:1018
  (31 other events, 189.8 us)
Sparse Core Ops, SparseCore 0:
  11.9 36.9 all-gather.3
  84.2 116.9 all-gather.7
  204.1 63.5 all-gather.5
  534.0 41.8 reduce-scatter.12
  578.2 85.5 reduce-scatter.10
  670.0 107.5 reduce-scatter.8
  779.8 59.3 reduce-scatter.6

commit v2 on v1

--- a/solution.py
+++ b/solution.py
@@ -895,9 +895,18 @@
 
 
 def mid_back_kernel(
-    rows, parts, db_ref, mid_ref, cot_ref, gain_ref, w_ref, gmid_ref, go_ref, do_ref, gg_ref
+    rows, parts, keep_ref, fx_ref, fy_ref, px_ref, py_ref, mid_ref, cot_ref, gain_ref, w_ref,
+    gmid_ref, go_ref, do_ref, gg_ref
 ):
-    db = db_ref[...]
+    half = px_ref.shape[0]
+    wide = lambda v: v.astype(jnp.float32)
+    db = jnp.concatenate(
+        [
+            keep_ref[:half] + wide(fx_ref[:half]) + wide(py_ref[...]),
+            keep_ref[half:] + wide(fy_ref[:half]) + wide(px_ref[...]),
+        ],
+        axis=0,
+    )
     middle = mid_ref[...]
     factor = lax.rsqrt(jnp.mean(middle * middle, axis=-1, keepdims=True) + EPS)
     scaled = db * gain_ref[...]
@@ -918,9 +927,9 @@
             do_ref[(rows + r) * parts + z] = right.astype(jnp.bfloat16)
 
 
-def mid_back_call(db, middle, cot, gain, weight, rows, parts):
+def mid_back_call(pieces, middle, cot, gain, weight, rows, parts):
     count, width = middle.shape
-    operands = (db, middle, cot, gain, weight)
+    operands = (*pieces, middle, cot, gain, weight)
     shapes = [
         jax.ShapeDtypeStruct((count, width), jnp.float32),
         jax.ShapeDtypeStruct((count, width), jnp.bfloat16),
@@ -930,7 +939,7 @@
     return pl.pallas_call(
         partial(mid_back_kernel, rows, parts),
         grid=(1,),
-        in_specs=[full_spec(v) for v in operands],
+        in_specs=[pl.BlockSpec((count, width), lambda i: (0, 0))] + [full_spec(v) for v in operands[1:]],
         out_specs=[full_spec(v) for v in shapes],
         out_shape=shapes,
         compiler_params=pltpu.CompilerParams(vmem_limit_bytes=48 << 20),
@@ -979,6 +988,347 @@
     )(place, *operands)
 
 
+def cut_kernel(gate_ref, up_ref, down_ref, out_ref):
+    for n in range(out_ref.shape[0]):
+        at = slice(n * LN, (n + 1) * LN)
+        out_ref[n, :, :LN] = gate_ref[:, at]
+        out_ref[n, :, LN : 2 * LN] = up_ref[:, at]
+        out_ref[n, :, 2 * LN :] = jnp.transpose(down_ref[at, :].astype(jnp.float32)).astype(jnp.bfloat16)
+
+
+def cut_call(gate, up, down):
+    shape = jax.ShapeDtypeStruct((gate.shape[1] // LN, gate.shape[0], 3 * LN), jnp.bfloat16)
+    operands = (gate, up, down)
+    return pl.pallas_call(
+        cut_kernel,
+        grid=(1,),
+        in_specs=[full_spec(v) for v in operands],
+        out_specs=full_spec(shape),
+        out_shape=shape,
+        name="cut_units",
+    )(*operands)
+
+
+def uncut_kernel(in_ref, gate_ref, up_ref, down_ref):
+    for n in range(in_ref.shape[0]):
+        at = slice(n * LN, (n + 1) * LN)
+        gate_ref[:, at] = in_ref[n, :, :LN].astype(jnp.float32)
+        up_ref[:, at] = in_ref[n, :, LN : 2 * LN].astype(jnp.float32)
+        down_ref[at, :] = jnp.transpose(in_ref[n, :, 2 * LN :].astype(jnp.float32))
+
+
+def uncut_call(value):
+    units, rows = value.shape[0] * LN, value.shape[1]
+    shapes = [jax.ShapeDtypeStruct(s, jnp.float32) for s in ((rows, units), (rows, units), (units, rows))]
+    return pl.pallas_call(
+        uncut_kernel,
+        grid=(1,),
+        in_specs=[full_spec(value)],
+        out_specs=[full_spec(v) for v in shapes],
+        out_shape=shapes,
+        name="uncut_units",
+    )(value)
+
+
+def place_kernel(parts, at_ref, mine_ref, other_ref, out_ref):
+    size = mine_ref.shape[1]
+    z = at_ref[3]
+    for c, ref in enumerate((mine_ref, other_ref)):
+        for n in range(parts):
+            y, x = at_ref[0] ^ (n // 2), at_ref[1] ^ (n % 2)
+            rows = pl.multiple_of(((y * 2 + x) * 2 + (at_ref[2] ^ c)) * size, size)
+            for k in range(ref.shape[0] // parts):
+                count = ref.shape[0] // parts
+                source = lax.rem(z + (count - k), count)
+                cols = pl.multiple_of(source * 3 * LN, 3 * LN)
+                out_ref[pl.ds(rows, size), pl.ds(cols, 3 * LN)] = ref[n * count + k]
+
+
+def place_call(at, mine, other):
+    size = mine.shape[1]
+    shape = jax.ShapeDtypeStruct((8 * size, mine.shape[0] // 4 * mine.shape[2]), mine.dtype)
+    return pl.pallas_call(
+        partial(place_kernel, 4),
+        grid=(1,),
+        in_specs=[pl.BlockSpec(memory_space=pltpu.SMEM), full_spec(mine), full_spec(other)],
+        out_specs=full_spec(shape),
+        out_shape=shape,
+        compiler_params=pltpu.CompilerParams(vmem_limit_bytes=32 << 20),
+        name="place_out",
+    )(at, mine, other)
+
+
+def fill_square(refs, out_ref):
+    own, xn, yn, first, last = refs
+    half = first.shape[0]
+    out_ref[0, :half], out_ref[0, half:] = own[:half], own[half:]
+    out_ref[1, :half], out_ref[1, half:] = xn[:half], first[...]
+    out_ref[2, :half], out_ref[2, half:] = yn[half:], last[...]
+    out_ref[3, :half], out_ref[3, half:] = xn[half:], yn[:half]
+
+
+def down_back_kernel(*refs):
+    pieces, (w0_ref, w1_ref, out_ref, g_s) = refs[:5], refs[5:]
+
+    @pl.when(pl.program_id(0) == 0)
+    def _():
+        fill_square(pieces, g_s)
+
+    weight = jnp.concatenate([w0_ref[0, :, 2 * LN :], w1_ref[0, :, 2 * LN :]], axis=1)
+
+    def body(m, carry):
+        out_ref[0, m] = dotf(g_s[m], weight, ((1,), (0,)))
+        return carry
+
+    lax.fori_loop(0, 4, body, 0)
+
+
+def unit_spec(weight):
+    return pl.BlockSpec((1,) + weight.shape[1:], lambda z: (z, 0, 0))
+
+
+def down_back_call(pieces, mine, other):
+    count, width = pieces[0].shape
+    parts = mine.shape[0]
+    shape = jax.ShapeDtypeStruct((parts, 4, count, 2 * LN), jnp.float32)
+    return pl.pallas_call(
+        down_back_kernel,
+        grid=(parts,),
+        in_specs=[full_spec(v) for v in pieces] + [unit_spec(mine), unit_spec(other)],
+        out_specs=pl.BlockSpec((1, 4, count, 2 * LN), lambda z: (z, 0, 0, 0)),
+        out_shape=shape,
+        scratch_shapes=[pltpu.VMEM((4, count, width), jnp.bfloat16)],
+        compiler_params=pltpu.CompilerParams(vmem_limit_bytes=40 << 20),
+        name="down_back",
+    )(*pieces, mine, other)
+
+
+def emit_square(acc_ref, keep_ref, sx_ref, sy_ref):
+    count = sx_ref.shape[0]
+    keep_ref[:count] = acc_ref[0]
+    keep_ref[count:] = acc_ref[3]
+    sx_ref[...] = acc_ref[1].astype(jnp.bfloat16)
+    sy_ref[...] = acc_ref[2].astype(jnp.bfloat16)
+
+
+def units_kernel(*refs):
+    pieces, (w0_ref, w1_ref, dh_ref) = refs[:5], refs[5:8]
+    dgu_ref, hid_ref, keep_ref, sx_ref, sy_ref, b_s, acc_s = refs[8:]
+    step = pl.program_id(0)
+
+    @pl.when(step == 0)
+    def _():
+        fill_square(pieces, b_s)
+
+    def body(m, carry):
+        b = b_s[m]
+        total = None
+        for n, w_ref in enumerate((w0_ref, w1_ref)):
+            weight = w_ref[0, :, : 2 * LN]
+            both = dotf(b, weight, ((1,), (0,)))
+            gate, up = both[:, :LN], both[:, LN:]
+            dh = dh_ref[0, m, :, n * LN : (n + 1) * LN]
+            sigma = 1.0 / (1.0 + jnp.exp(-gate))
+            silu = gate * sigma
+            hid_ref[0, m, :, n * LN : (n + 1) * LN] = (silu * up).astype(jnp.bfloat16)
+            grad_gate = dh * up * sigma * (1.0 + gate * (1.0 - sigma))
+            grads = jnp.concatenate([grad_gate, dh * silu], axis=1).astype(jnp.bfloat16)
+            dgu_ref[0, n, m] = grads
+            back = dotf(grads, weight, ((1,), (1,)))
+            total = back if total is None else total + back
+
+        @pl.when(step == 0)
+        def _():
+            acc_s[m] = total
+
+        @pl.when(step > 0)
+        def _():
+            acc_s[m] += total
+
+        return carry
+
+    lax.fori_loop(0, 4, body, 0)
+
+    @pl.when(step == pl.num_programs(0) - 1)
+    def _():
+        emit_square(acc_s, keep_ref, sx_ref, sy_ref)
+
+
+def square_shapes(count, width):
+    return [
+        jax.ShapeDtypeStruct((2 * count, width), jnp.float32),
+        jax.ShapeDtypeStruct((count, width), jnp.bfloat16),
+        jax.ShapeDtypeStruct((count, width), jnp.bfloat16),
+    ]
+
+
+def units_call(pieces, mine, other, grad_hidden):
+    count, width = pieces[0].shape
+    parts = mine.shape[0]
+    low = jnp.bfloat16
+    shapes = [
+        jax.ShapeDtypeStruct((parts, 2, 4, count, 2 * LN), low),
+        jax.ShapeDtypeStruct((parts, 4, count, 2 * LN), low),
+    ] + square_shapes(count, width)
+    return pl.pallas_call(
+        units_kernel,
+        grid=(parts,),
+        in_specs=[full_spec(v) for v in pieces]
+        + [unit_spec(mine), unit_spec(other), pl.BlockSpec((1, 4, count, 2 * LN), lambda z: (z, 0, 0, 0))],
+        out_specs=[
+            pl.BlockSpec((1, 2, 4, count, 2 * LN), lambda z: (z, 0, 0, 0, 0)),
+            pl.BlockSpec((1, 4, count, 2 * LN), lambda z: (z, 0, 0, 0)),
+        ]
+        + [full_spec(v) for v in shapes[2:]],
+        out_shape=shapes,
+        scratch_shapes=[pltpu.VMEM((4, count, width), low), pltpu.VMEM((4, count, width), jnp.float32)],
+        compiler_params=pltpu.CompilerParams(vmem_limit_bytes=56 << 20),
+        name="units",
+    )(*pieces, mine, other, grad_hidden)
+
+
+def down_kernel(hid_ref, w0_ref, w1_ref, keep_ref, sx_ref, sy_ref, acc_s):
+    step = pl.program_id(0)
+    weight = jnp.concatenate([w0_ref[0, :, 2 * LN :], w1_ref[0, :, 2 * LN :]], axis=1)
+
+    def body(m, carry):
+        total = dotf(hid_ref[0, m], weight, ((1,), (1,)))
+
+        @pl.when(step == 0)
+        def _():
+            acc_s[m] = total
+
+        @pl.when(step > 0)
+        def _():
+            acc_s[m] += total
+
+        return carry
+
+    lax.fori_loop(0, 4, body, 0)
+
+    @pl.when(step == pl.num_programs(0) - 1)
+    def _():
+        emit_square(acc_s, keep_ref, sx_ref, sy_ref)
+
+
+def down_call(hidden, mine, other):
+    parts, _, count, _ = hidden.shape
+    width = mine.shape[1]
+    shapes = square_shapes(count, width)
+    return pl.pallas_call(
+        down_kernel,
+        grid=(parts,),
+        in_specs=[pl.BlockSpec((1,) + hidden.shape[1:], lambda z: (z, 0, 0, 0)), unit_spec(mine), unit_spec(other)],
+        out_specs=[full_spec(v) for v in shapes],
+        out_shape=shapes,
+        scratch_shapes=[pltpu.VMEM((4, count, width), jnp.float32)],
+        compiler_params=pltpu.CompilerParams(vmem_limit_bytes=40 << 20),
+        name="down",
+    )(hidden, mine, other)
+
+
+def unit_grads_kernel(*refs):
+    b_pieces, g_pieces = refs[:5], refs[5:10]
+    dgu_ref, hid_ref, out_ref, fill_s, b_s, g_s = refs[10:]
+    count = fill_s.shape[1]
+
+    @pl.when(pl.program_id(0) == 0)
+    def _():
+        for pieces, side in ((b_pieces, b_s), (g_pieces, g_s)):
+            fill_square(pieces, fill_s)
+            for m in range(4):
+                side[:, m * count : (m + 1) * count] = jnp.transpose(fill_s[m])
+
+    hidden = hid_ref[0].reshape(4 * count, 2 * LN)
+    grads = [dgu_ref[0, n].reshape(4 * count, 2 * LN) for n in range(2)]
+    rows = b_s.shape[0] // 4
+
+    def body(m, carry):
+        at = pl.ds(pl.multiple_of(m * rows, rows), rows)
+        left, right = b_s[at, :], g_s[at, :]
+        down = dotf(right, hidden, ((1,), (0,)))
+        for n in range(2):
+            out_ref[n, 0, at, : 2 * LN] = dotf(left, grads[n], ((1,), (0,))).astype(jnp.bfloat16)
+            out_ref[n, 0, at, 2 * LN :] = down[:, n * LN : (n + 1) * LN].astype(jnp.bfloat16)
+        return carry
+
+    lax.fori_loop(0, 4, body, 0)
+
+
+def unit_grads_call(b_pieces, g_pieces, grads, hidden):
+    count, width = b_pieces[0].shape
+    parts = hidden.shape[0]
+    low = jnp.bfloat16
+    operands = (*b_pieces, *g_pieces)
+    return pl.pallas_call(
+        unit_grads_kernel,
+        grid=(parts,),
+        in_specs=[full_spec(v) for v in operands]
+        + [
+            pl.BlockSpec((1,) + grads.shape[1:], lambda z: (z, 0, 0, 0, 0)),
+            pl.BlockSpec((1,) + hidden.shape[1:], lambda z: (z, 0, 0, 0)),
+        ],
+        out_specs=pl.BlockSpec((2, 1, width, 3 * LN), lambda z: (0, z, 0, 0)),
+        out_shape=jax.ShapeDtypeStruct((2, parts, width, 3 * LN), low),
+        scratch_shapes=[pltpu.VMEM((4, count, width), low)] + [pltpu.VMEM((width, 4 * count), low)] * 2,
+        compiler_params=pltpu.CompilerParams(vmem_limit_bytes=56 << 20),
+        name="unit_grads",
+    )(*operands, grads, hidden)
+
+
+def qkv_grads_kernel(a_ref, d_ref, out_ref):
+    left = jnp.transpose(a_ref[...])
+    for g in range(d_ref.shape[0]):
+        cols = slice(g * 3 * LN, (g + 1) * 3 * LN)
+        out_ref[:, cols] = dotf(left, d_ref[g], ((1,), (0,))).astype(out_ref.dtype)
+
+
+def qkv_grads_call(normed, grads):
+    count, width = normed.shape
+    shape = jax.ShapeDtypeStruct((width, grads.shape[0] * 3 * LN), jnp.bfloat16)
+    tile = 2 * LN
+    return pl.pallas_call(
+        qkv_grads_kernel,
+        grid=(width // tile,),
+        in_specs=[pl.BlockSpec((count, tile), lambda i: (0, i)), full_spec(grads)],
+        out_specs=pl.BlockSpec((tile, shape.shape[1]), lambda i: (i, 0)),
+        out_shape=shape,
+        compiler_params=pltpu.CompilerParams(vmem_limit_bytes=32 << 20),
+        name="qkv_grads",
+    )(normed, grads)
+
+
+def out_grads_kernel(at_ref, go_ref, o_ref, out_ref, full_s):
+    tile = 2 * LN
+    right = o_ref[...]
+    for n in range(full_s.shape[0] // tile):
+        left = jnp.transpose(go_ref[:, n * tile : (n + 1) * tile])
+        full_s[n * tile : (n + 1) * tile, :] = dotf(left, right, ((1,), (0,))).astype(jnp.bfloat16)
+    half = out_ref.shape[2]
+    size = 2 * half
+    order = ((0, 0, 0), (0, 0, 1), (0, 1, 0), (1, 1, 0), (1, 0, 1), (1, 1, 1), (0, 1, 1), (1, 0, 0))
+    for c in range(2):
+        for n, (y, x, last) in enumerate(order):
+            block = ((at_ref[0] ^ y) * 2 + (at_ref[1] ^ x)) * 2 + (at_ref[2] ^ c)
+            rows = pl.multiple_of(block * size + last * half, 32)
+            out_ref[c, n] = full_s[pl.ds(rows, half), :]
+
+
+def out_grads_call(at, grad, attended):
+    width, inner = grad.shape[1], attended.shape[1]
+    shape = jax.ShapeDtypeStruct((2, 8, width // 16, inner), jnp.bfloat16)
+    return pl.pallas_call(
+        out_grads_kernel,
+        grid=(1,),
+        in_specs=[pl.BlockSpec(memory_space=pltpu.SMEM), full_spec(grad), full_spec(attended)],
+        out_specs=full_spec(shape),
+        out_shape=shape,
+        scratch_shapes=[pltpu.VMEM((width, inner), jnp.bfloat16)],
+        compiler_params=pltpu.CompilerParams(vmem_limit_bytes=32 << 20),
+        name="out_grads",
+    )(at, grad, attended)
+
+
 EVERY = ("y", "x", "c", "z")
 SWAP = ((0, 1), (1, 0))
 
@@ -997,21 +1347,44 @@
 def gather_square(value):
     half = value.shape[0] // 2
     xn, yn = swap(value, "x"), swap(value, "y")
-    dg_first, dg_last = swap(yn[:half], "x"), swap(xn[half:], "y")
-    return jnp.concatenate([value, xn[:half], dg_first, yn[half:], dg_last, xn[half:], yn[:half]], axis=0)
-
-
-def reduce_square(part):
+    return value, xn, yn, swap(yn[:half], "x"), swap(xn[half:], "y")
+
+
+def reduce_square(keep, send_x, send_y):
     low = jnp.bfloat16
-    half = part.shape[0] // 8
-    piece = lambda n, m=1: part[n * half : (n + m) * half]
-    from_x = swap(piece(2, 2).astype(low), "x").astype(jnp.float32)
-    from_y = swap(piece(4, 2).astype(low), "y").astype(jnp.float32)
-    pass_y = swap((piece(7) + from_x[half:]).astype(low), "y").astype(jnp.float32)
-    pass_x = swap((piece(6) + from_y[half:]).astype(low), "x").astype(jnp.float32)
+    half = send_x.shape[0] // 2
+    from_x, from_y = swap(send_x, "x"), swap(send_y, "y")
+    pass_y = swap((keep[3 * half :] + from_x[half:].astype(jnp.float32)).astype(low), "y")
+    pass_x = swap((keep[2 * half : 3 * half] + from_y[half:].astype(jnp.float32)).astype(low), "x")
+    return keep, from_x, from_y, pass_x, pass_y
+
+
+def total_square(pieces):
+    keep, from_x, from_y, pass_x, pass_y = pieces
+    half = pass_x.shape[0]
+    wide = lambda v: v.astype(jnp.float32)
     return jnp.concatenate(
-        [piece(0) + from_x[:half] + pass_y, piece(1) + from_y[:half] + pass_x], axis=0
-    )
+        [
+            keep[:half] + wide(from_x[:half]) + wide(pass_y),
+            keep[half : 2 * half] + wide(from_y[:half]) + wide(pass_x),
+        ],
+        axis=0,
+    )
+
+
+def reduce_line(part, at, size):
+    block = lambda k: lax.dynamic_index_in_dim(part, jnp.clip(at + k, 0, size - 1), 0, keepdims=False)
+    wide = lambda v: v.astype(jnp.float32)
+    up, down = None, None
+    for step in range(1, size):
+        k = size - step
+        send_up, send_down = block(k), block(-k)
+        if up is not None:
+            send_up = (wide(send_up) + wide(up)).astype(part.dtype)
+            send_down = (wide(send_down) + wide(down)).astype(part.dtype)
+        up = lax.ppermute(send_up, "z", [(i, i + 1) for i in range(step)])
+        down = lax.ppermute(send_down, "z", [(size - 1 - i, size - 2 - i) for i in range(step)])
+    return wide(block(0)) + wide(up) + wide(down)
 
 
 def all_to_all(value, axes):
@@ -1022,13 +1395,8 @@
     return lax.optimization_barrier(values)
 
 
-def dot(left, right, left_dim, right_dim, kind=jnp.float32):
-    return contract(left, right, left_dim, right_dim).astype(kind)
-
-
 def fast_local(sizes, *args):
     (tokens, cotangent, segments, positions, norm_in, w_query, w_key, w_value, w_out, norm_mid, w_gate, w_up, w_down) = args
-    low = jnp.bfloat16
     nz = sizes["z"]
     devices = sizes["y"] * sizes["x"] * sizes["c"] * nz
     plane = devices // nz
@@ -1038,6 +1406,7 @@
     length = chunk * sizes["x"] * sizes["c"]
     x_at, c_at, z_at = lax.axis_index("x"), lax.axis_index("c"), lax.axis_index("z")
     place = z_at.reshape(1).astype(jnp.int32)
+    at = jnp.stack([lax.axis_index("y"), x_at, c_at, z_at]).astype(jnp.int32)
 
     own = tokens.reshape(count, width)
     blocks = gather_blocks(own, nz)
@@ -1055,11 +1424,9 @@
     w_qkv = w_qkv.reshape(w_qkv.shape[0], -1)
     w_qkv = lax.all_gather(w_qkv, ("y", "x", "c"), axis=0, tiled=True)
 
-    units = w_gate.shape[2] // plane
-    by_unit = lambda w: w.reshape(w.shape[0], plane, units)
-    w_ff = jnp.stack([by_unit(w_gate[0]), by_unit(w_up[0]), by_unit(w_down[0].T)], axis=2)
-    w_ff = jnp.transpose(w_ff, (1, 0, 2, 3)).reshape(width, 3 * units)
-    w_ff = all_to_all(w_ff, ("y", "x", "c"))
+    gate, up, down, early = tie(w_gate[0], w_up[0], w_down[0], blocks[1])
+    w_ff = all_to_all(cut_call(gate, up, down), ("y", "x", "c"))
+    w_ff = w_ff.reshape(width, 3 * LN)
 
     last = (x_at * sizes["c"] + c_at + 1) * chunk - 1
     begin = last - positions[:, -1] - jnp.where(segments[:, -1] == 2, 3 * length // 4, 0)
@@ -1073,66 +1440,64 @@
     row_cos, row_sin = jnp.cos(row_angle), jnp.sin(row_angle)
 
     normed, qkv = qkv_call(place, blocks, gain_in, w_qkv, token_cos, token_sin, rows)
+    w_ff, w_o, *_ = tie(w_ff, w_out[0].T, *blocks)
     qkv = all_to_all(qkv, ("x", "c")).reshape(length, 3 * LN)
 
-    w_ff, *blocks = tie(w_ff, *blocks)
-    w_ff = lax.all_gather(w_ff, "z", axis=0, tiled=True).reshape(nz, width, 3, units)
-    w_ff = jnp.stack([w_ff, swap(w_ff, "c")], axis=0)
-    w_ff = jnp.transpose(w_ff, (3, 2, 0, 1, 4)).reshape(3, width, 2 * nz * units)
-    w_gu = jnp.transpose(w_ff[:2], (1, 0, 2)).reshape(width, -1)
-    w_d = w_ff[2]
-    w_o = lax.all_gather(w_out[0].T, EVERY, axis=0, tiled=True)
-    w_o = jnp.transpose(w_o.reshape(plane, nz, -1, w_out.shape[1]), (0, 2, 1, 3)).reshape(width, -1)
+    w_mine = lax.all_gather(w_ff, "z", axis=0, tiled=True).reshape(nz, width, 3 * LN)
+    w_other = swap(w_mine, "c")
+    w_o = jnp.stack(gather_blocks(w_o, nz))
     cot_low = cotangent.reshape(count, width)
-    cot_all = gather_square(cot_low)
+    cot_low, w_o, _ = tie(cot_low, w_o, qkv)
+    own_o, xn_o, yn_o, first_o, last_o = gather_square(w_o)
+    w_o = jnp.concatenate([own_o, xn_o, yn_o, first_o, last_o], axis=0)
+    w_o = place_call(at, w_o, swap(w_o, "c"))
+    cot_pieces = gather_square(cot_low)
 
     attended, attended_float, log_total = attn_fwd(first, qkv)
     attended = all_to_all(attended, ("x", "c", "z"))
     middle, normed_b, attended_low = out_call(attended, w_o, own, gain_mid, rows)
-    b_all = gather_square(normed_b)
-
-    hidden_width = w_d.shape[1]
-    gate_up = dot(b_all, w_gu, 1, 0)
-    gate, up = gate_up[:, :hidden_width], gate_up[:, hidden_width:]
-    grad_hidden = dot(cot_all, w_d, 1, 0)
-    sigma = jax.nn.sigmoid(gate)
-    silu = gate * sigma
-    hidden = (silu * up).astype(low)
-    grad_gate = (grad_hidden * up * sigma * (1.0 + gate * (1.0 - sigma))).astype(low)
-    grad_up = (grad_hidden * silu).astype(low)
-    grad_gu = jnp.concatenate([grad_gate, grad_up], axis=1)
-    grad_b = reduce_square(dot(grad_gu, w_gu, 1, 1))
-    out = middle + reduce_square(dot(hidden, w_d, 1, 1))
-
-    grad_ff = jnp.concatenate(
-        [dot(b_all, grad_gu, 0, 0, low), dot(cot_all, hidden, 0, 0, low)], axis=1
-    )
-    grad_ff = jnp.transpose(grad_ff.reshape(width, 3, 2, nz, units), (2, 3, 0, 1, 4))
-    grad_ff = grad_ff.reshape(2, nz * width, 3 * units)
-    grad_ff = (grad_ff[0].astype(jnp.float32) + swap(grad_ff[1], "c").astype(jnp.float32)).astype(low)
+    b_pieces = gather_square(normed_b)
+
+    grad_hidden = down_back_call(cot_pieces, w_mine, w_other)
+    grad_gu, hidden, *sends = units_call(b_pieces, w_mine, w_other, grad_hidden)
+    grad_b = reduce_square(*sends)
+    grad_ff = unit_grads_call(b_pieces, cot_pieces, grad_gu, hidden)
+    grad_ff = grad_ff.reshape(2, nz * width, 3 * LN)
+    grad_ff = (grad_ff[0].astype(jnp.float32) + swap(grad_ff[1], "c").astype(jnp.float32)).astype(jnp.bfloat16)
     grad_ff = lax.psum_scatter(grad_ff, "z", scatter_dimension=0, tiled=True)
-    grad_ff = all_to_all(grad_ff, ("y", "x", "c")).reshape(plane, width // plane, 3, units)
-    grad_ff = jnp.transpose(grad_ff.astype(jnp.float32), (2, 1, 0, 3)).reshape(3, width // plane, -1)
+    grad_ff = all_to_all(grad_ff.reshape(plane, width // plane, 3 * LN), ("y", "x", "c"))
 
     grad_mid, grad_low, grad_o, gain_grad_mid = mid_back_call(
         grad_b, middle, cot_low, gain_mid, w_o, rows, nz
     )
+    hidden, grad_o = tie(hidden, grad_o)
     grad_o = all_to_all(grad_o, ("x", "c", "z"))
-    grad_wo = dot(grad_low, attended_low, 0, 0, low)
-    grad_wo = jnp.transpose(grad_wo.reshape(plane, -1, nz, w_out.shape[1]), (0, 2, 1, 3))
-    grad_wo = grad_wo.reshape(-1, w_out.shape[1])
-    grad_wo = lax.psum_scatter(grad_wo, EVERY, scatter_dimension=0, tiled=True)
+    out = middle + total_square(reduce_square(*down_call(hidden, w_mine, w_other)))
+
+    grad_wo = out_grads_call(at, grad_low, attended_low)
+    grad_wo = grad_wo[0].astype(jnp.float32) + swap(grad_wo[1], "c").astype(jnp.float32)
+    step = width // 16
+    flat_wo = grad_wo.reshape(8 * step, -1)
+    keep_wo = jnp.concatenate([flat_wo[: 2 * step], flat_wo[6 * step :]], axis=0)
+    grad_wo = total_square(
+        reduce_square(
+            keep_wo,
+            flat_wo[2 * step : 4 * step].astype(jnp.bfloat16),
+            flat_wo[4 * step : 6 * step].astype(jnp.bfloat16),
+        )
+    ).astype(jnp.bfloat16)
+    grad_wo = jnp.stack([grad_wo[:, z * 3 * LN : (z + 1) * 3 * LN] for z in range(nz)])
+    grad_wo = jnp.sum(all_to_all(grad_wo, "z").astype(jnp.float32), axis=0)
 
     grad_qkv = attn_bwd(first, qkv, grad_o, attended_float, log_total, row_cos, row_sin)
     grad_qkv = all_to_all(grad_qkv.reshape(-1, chunk, 3 * LN), ("x", "c"))
     grad_qkv = grad_qkv.reshape(kv_local, rows, chunk, 3 * LN)
     part, gain_grad_in = da_call(place, blocks, grad_qkv, w_qkv, rows)
-    grad_a = lax.psum_scatter(part, "z", scatter_dimension=0, tiled=True)
-    normed = normed.reshape(rows * chunk, width)
-    grad_wqkv = jnp.concatenate(
-        [dot(normed, grad_qkv[h].reshape(rows * chunk, 3 * LN), 0, 0, low) for h in range(kv_local)], axis=1
+    grad_wqkv = qkv_grads_call(
+        normed.reshape(rows * chunk, width), grad_qkv.reshape(kv_local, rows * chunk, 3 * LN)
     )
     grad_wqkv = lax.psum_scatter(grad_wqkv, ("y", "x", "c"), scatter_dimension=0, tiled=True)
+    grad_a = reduce_line(part.reshape(nz, count, width), z_at, nz)
 
     gain_grads = jnp.concatenate(
         [gain_grad_in.reshape(devices, share), gain_grad_mid.reshape(devices, share)], axis=1
@@ -1140,15 +1505,13 @@
     gain_grads = jnp.pad(gain_grads, ((0, 0), (0, LN - 2 * share)))
     gain_grads = jnp.sum(all_to_all(gain_grads, EVERY), axis=0, keepdims=True)
 
-    back_in, _ = norm_back(
-        own.astype(jnp.float32),
-        lax.rsqrt(jnp.mean(jnp.square(own.astype(jnp.float32)), axis=-1, keepdims=True) + EPS),
-        gain_in,
-        grad_a.astype(jnp.float32),
-    )
+    stream = own.astype(jnp.float32)
+    factor = lax.rsqrt(jnp.mean(stream * stream, axis=-1, keepdims=True) + EPS)
+    back_in, _ = norm_back(stream, factor, gain_in, grad_a)
     grad_tokens = grad_mid + back_in
     grad_wqkv = grad_wqkv.astype(jnp.float32).reshape(-1, kv_local, 4 * HD)
     flat = lambda g: g.reshape(1, g.shape[0], -1)
+    grad_gate, grad_up, grad_down = uncut_call(grad_ff)
     return (
         out.reshape(tokens.shape),
         grad_tokens.reshape(tokens.shape),
@@ -1156,11 +1519,11 @@
         flat(grad_wqkv[:, :, : 2 * HD]),
         flat(grad_wqkv[:, :, 2 * HD : 3 * HD]),
         flat(grad_wqkv[:, :, 3 * HD :]),
-        grad_wo.astype(jnp.float32).T[None],
+        grad_wo.T[None],
         gain_grads[:, share : 2 * share],
-        grad_ff[0][None],
-        grad_ff[1][None],
-        grad_ff[2].T[None],
+        grad_gate[None],
+        grad_up[None],
+        grad_down[None],
     )
 
 

time: 876 us -> 694 us (0.79)
  local copies, waits for them, and re-layouts: 181 us -> 66.6 us
  waiting for transfers between devices: 372 us -> 287 us
  Pallas kernels: 76.6 us -> 160 us
  matrix products: 53.1 us -> 0 us
  starting transfers between devices: 75.7 us -> 103 us
  blocking collectives: 24.1 us -> 0 us
  other arithmetic: 65.5 us -> 51 us
    reduce_scatter x2 -> x1, waiting for transfers between devices: 167 us -> 0.01 us  [fast_local(): lax.psum_scatter(grad_wqkv, ('y', 'x', 'c'), scatter_dimension=0, tiled=T...]
    pallas_call x0 -> x9, Pallas kernels: none -> 82.4 us  [the longest x1 27.1 us: units_call(): pl.pallas_call(units_kernel, grid=(parts,), in_specs=[full_spec(v) for v...]
    reshape x6 -> x1, local copies, waits for them, and re-layouts: 62.7 us -> 1.27 us  [fast_local(): grad_wqkv = grad_wqkv.astype(jnp.float32).reshape(-1, kv_local, 4 * HD)]
    dot_general x9 -> x0, matrix products: 53.1 us -> none  [contract(): lax.dot_general(left_side, right_side, (((left_dim,), (right_dim,)), ((),...]
    all_to_all x7 -> x9, waiting for transfers between devices: 25.7 us -> 60.7 us  [all_to_all(): return lax.all_to_all(value, axes, 0, 0, tiled=True)]
    ppermute x3 -> x6, waiting for transfers between devices: 50 us -> 83 us  [gather_blocks(): got = {k: lax.ppermute(value, 'z', shift(k)) for k in order}]
    ppermute x18 -> x28, waiting for transfers between devices: 55.2 us -> 81.4 us  [swap(): return lax.ppermute(value, axis, SWAP)]
    all_to_all x1 -> x0, blocking collectives: 24.1 us -> none  [all_to_all(): return lax.all_to_all(value, axes, 0, 0, tiled=True)]
  transfers between devices with their start and end apart: 35 -> 53, of which waited for: 19 -> 28; matrix products, arithmetic and copies ran while one was open for 25% -> 10% of each run, Pallas kernels for 8% -> 16%
where the time goes in v2:
time: 694 us; the launch traced here: 682 us
  waiting for transfers between devices  287 us (41%)
  Pallas kernels  160 us (23%)
  starting transfers between devices  103 us (15%)
  local copies, waits for them, and re-layouts  66.6 us (10%)
  other arithmetic  51 us (7%)
  between operations  15.7 us (2%)
    ppermute x6, waiting for transfers between devices, gather_blocks(): got = {k: lax.ppermute(value, 'z', shift(k)) for k in order}  83 us
    ppermute x28, waiting for transfers between devices, swap(): return lax.ppermute(value, axis, SWAP)  81.4 us
    all_to_all x9, waiting for transfers between devices, all_to_all(): return lax.all_to_all(value, axes, 0, 0, tiled=True)  60.7 us
    all_to_all x9, starting transfers between devices, all_to_all(): return lax.all_to_all(value, axes, 0, 0, tiled=True)  55.3 us
    all_gather x1, waiting for transfers between devices, fast_local(): lax.all_gather(w_ff, 'z', axis=0, tiled=True).reshape(nz, width, 3 * LN)  41.9 us
    unnamed x119, local copies, waits for them, and re-layouts  38.7 us
    pallas_call x1, Pallas kernels, attn_bwd(): pl.pallas_call(functools.partial(attn_bwd_kernel, length), grid=(blocks,)...  31.3 us
    pallas_call x1, Pallas kernels, units_call(): pl.pallas_call(units_kernel, grid=(parts,), in_specs=[full_spec(v) for v...  27.1 us
  transfers between devices with their start and end apart: 53, of which 28 were waited for; matrix products, arithmetic and copies ran while one was open for 10% of the time, Pallas kernels for 16%

profile of v2, /device:TPU:0, one launch (start us, length us, event | category | flops | bytes accessed | tf_op | source)
XLA Modules:
  0.0 682.5 jit_solution(11062099537275461829)
XLA Ops:
  15.8 18.8 %collective-permute-done.refs_1_ = bf16[256,1536]{1,0:T(8,128)(2,1)S(1)} collective-permute-done((bf16[256,1536]{1,0:T(8,128)(2,1)}, bf16[256,1536]{1,0:T(8,128)(2,1)S(1)}, u32[]{:S(2)}, u32[]{:S(2)}) %collective-permute-start) | collective-permute-done | bytes 786464 | tf_op jit(solution)/shard_map/ppermute | solution.py:1343
  37.5 4.4 all-to-all-start.3
  44.4 34.7 %collective-permute-done.1.refs_2_ = bf16[256,1536]{1,0:T(8,128)(2,1)S(1)} collective-permute-done((bf16[256,1536]{1,0:T(8,128)(2,1)S(1)}, bf16[256,1536]{1,0:T(8,128)(2,1)S(1)}, u32[]{:S(2)}, u32[]{:S(2)}) %collective-permute-start.1) | collective-permute-done | bytes 786464 | tf_op jit(solution)/shard_map/ppermute | solution.py:1343
  80.3 21.4 %all-to-all-start = ((f32[32,1,128]{2,1,0:T(1,128)}), f32[32,1,128]{2,1,0:T(1,128)S(1)}, u32[]{:S(2)}, u32[]{:S(2)}) async-start(f32[32,1,128]{2,1,0:T(1,128)} %broadcast_in_dim.44), calls=%async_computation | async-start | bytes 32768 | tf_op jit(solution)/shard_map/all_to_all | solution.py:1391
  104.7 4.0 all-to-all-done
  111.0 7.8 %norm_qkv.1 = (bf16[2,512,1536]{2,1,0:T(8,128)(2,1)}, bf16[4,512,384]{2,1,0:T(8,128)(2,1)S(1)}) custom-call(s32[1]{0:T(128)} %bitcast.1.place_ref, bf16[256,1536]{1,0:T(8,128)(2,1)S(1)} %bitcast.126, bf16[256,1536]{1,0:T(8,128)(2,1)S(1)} %collective-permute-done.refs_1_, bf16[256,1536]{1,0:T(8,128)(2,1)S(1)} %collective-permute-done.1.refs_2_, ...), custom_call_target="tpu_custom_call" | custom-call | tf_op jit(solution)/shard_map/norm_qkv/pallas_call | solution.py:816
  120.0 3.7 all-to-all-start.1
  126.3 9.3 %collective-permute-done.5 = bf16[192,384]{1,0:T(8,128)(2,1)S(1)} collective-permute-done((bf16[192,384]{1,0:T(8,128)(2,1)S(1)}, bf16[192,384]{1,0:T(8,128)(2,1)S(1)}, u32[]{:S(2)}, u32[]{:S(2)}) %collective-permute-start.5) | collective-permute-done | bytes 147488 | tf_op jit(solution)/shard_map/ppermute | solution.py:1343
  135.7 19.9 %collective-permute-done.4 = bf16[192,384]{1,0:T(8,128)(2,1)S(1)} collective-permute-done((bf16[192,384]{1,0:T(8,128)(2,1)S(1)}, bf16[192,384]{1,0:T(8,128)(2,1)S(1)}, u32[]{:S(2)}, u32[]{:S(2)}) %collective-permute-start.4) | collective-permute-done | bytes 147488 | tf_op jit(solution)/shard_map/ppermute | solution.py:1343
  156.4 41.9 %all-gather.5.cloned.1.call-done = bf16[6144,384]{1,0:T(8,128)(2,1)} async-done(((bf16[1536,384]{1,0:T(8,128)(2,1)}), bf16[6144,384]{1,0:T(8,128)(2,1)}) %all-gather.5.cloned.1.call-update) | async-done | bytes 4718608 | tf_op jit(solution)/shard_map/all_gather | solution.py:1446
  202.3 12.2 %collective-permute-done.6 = bf16[4,192,384]{2,1,0:T(8,128)(2,1)S(1)} collective-permute-done((bf16[4,192,384]{2,1,0:T(8,128)(2,1)S(1)}, bf16[4,192,384]{2,1,0:T(8,128)(2,1)S(1)}, u32[]{:S(2)}, u32[]{:S(2)}) %collective-permute-start.6) | collective-permute-done | bytes 589856 | tf_op jit(solution)/shard_map/ppermute | solution.py:1337
  224.8 22.1 %attend.1 = (bf16[16,64,384]{2,1,0:T(8,128)(2,1)S(1)}, f32[8,512,128]{2,1,0:T(8,128)S(1)}, f32[8,8,512]{2,1,0:T(8,128)S(1)}) custom-call(s32[1]{0:T(128)} %bitcast.first_ref, bf16[2048,384]{1,0:T(8,128)(2,1)S(1)} %bitcast.133), custom_call_target="tpu_custom_call" | custom-call | tf_op jit(solution)/shard_map/attend/pallas_call | solution.py:642
  249.7 3.6 all-to-all-start.2
  262.1 12.5 %all-to-all-done.2.o_ref = bf16[16,64,384]{2,1,0:T(8,128)(2,1)S(1)} async-done(((bf16[16,64,384]{2,1,0:T(8,128)(2,1)}), bf16[16,64,384]{2,1,0:T(8,128)(2,1)S(1)}, u32[]{:S(2)}, u32[]{:S(2)}) %all-to-all-start.2) | async-done | bytes 786464 | tf_op jit(solution)/shard_map/all_to_all | solution.py:1391
  276.7 4.0 out_norm.1
  287.0 14.2 %collective-permute-done.12.refs_2_ = bf16[256,1536]{1,0:T(8,128)(2,1)S(1)} collective-permute-done((bf16[256,1536]{1,0:T(8,128)(2,1)S(1)}, bf16[256,1536]{1,0:T(8,128)(2,1)S(1)}, u32[]{:S(2)}, u32[]{:S(2)}) %collective-permute-start.12) | collective-permute-done | bytes 786464 | tf_op jit(solution)/shard_map/ppermute | solution.py:1337
  303.4 7.8 %collective-permute-done.18.refs_3_.refs_8_ = bf16[128,1536]{1,0:T(8,128)(2,1)S(1)} collective-permute-done((bf16[128,1536]{1,0:T(8,128)(2,1)S(1)}, bf16[128,1536]{1,0:T(8,128)(2,1)S(1)}, u32[]{:S(2)}, u32[]{:S(2)}) %collective-permute-start.18) | collective-permute-done | bytes 393248 | tf_op jit(solution)/shard_map/ppermute | solution.py:1337
  313.8 8.1 %down_back.1.refs_7_ = f32[4,4,256,256]{3,2,1,0:T(8,128)S(1)} custom-call(bf16[256,1536]{1,0:T(8,128)(2,1)S(1)} %bitcast.138, bf16[256,1536]{1,0:T(8,128)(2,1)} %collective-permute-done.16.refs_1_.refs_6_, bf16[256,1536]{1,0:T(8,128)(2,1)} %collective-permute-done.17.refs_2_.refs_7_, bf16[128,1536]{1,0:T(8,128)(2,1)S(1)} %collective-permute-done.18.refs_3_.refs_8_, ...), custom_call_target="tpu_custom_call" | custom-call | tf_op jit(solution)/shard_map/down_back/pallas_call | solution.py:1094
  325.5 27.1 %units.1 = (bf16[4,2,4,256,256]{4,3,2,1,0:T(8,128)(2,1)}, bf16[4,4,256,256]{3,2,1,0:T(8,128)(2,1)}, f32[512,1536]{1,0:T(8,128)}, bf16[256,1536]{1,0:T(8,128)(2,1)}, bf16[256,1536]{1,0:T(8,128)(2,1)}) custom-call(bf16[256,1536]{1,0:T(8,128)(2,1)} %copy-done.13, bf16[256,1536]{1,0:T(8,128)(2,1)} %copy-done.38, bf16[256,1536]{1,0:T(8,128)(2,1)} %copy-done.37, ...), custom_call_target="tpu_custom_call" | custom-call | tf_op jit(solution)/shard_map/units/pallas_call | solution.py:1173
  352.6 19.6 %unit_grads.1 = bf16[2,4,1536,384]{3,2,1,0:T(8,128)(2,1)} custom-call(bf16[256,1536]{1,0:T(8,128)(2,1)} %copy-done.13, bf16[256,1536]{1,0:T(8,128)(2,1)} %copy-done.38, bf16[256,1536]{1,0:T(8,128)(2,1)} %copy-done.37, bf16[128,1536]{1,0:T(8,128)(2,1)} %copy-done.42, bf16[128,1536]{1,0:T(8,128)(2,1)} %copy-done.43, bf16[256,1536]{1,0:T(8,128)(2,1)} %bitcast.135, ...), custom_call_target="tpu_custom_call" | custom-call | tf_op jit(solution)/shard_map/unit_grads/pallas_call | solution.py:1263
  372.2 6.9 %fusion.37 = (bf16[1,4,1536,384]{3,2,1,0:T(8,128)(2,1)S(1)}, bf16[1,4,1536,384]{3,2,1,0:T(8,128)(2,1)}) fusion(bf16[2,4,1536,384]{3,2,1,0:T(8,128)(2,1)} %unit_grads.1), kind=kLoop, calls=%fused_computation.96 | loop fusion | bytes 18874368 | tf_op jit(solution)/shard_map/slice | solution.py:1466
  379.2 8.1 %collective-permute-done.39 = bf16[6144,384]{1,0:T(8,128)(2,1)S(1)} collective-permute-done((bf16[6144,384]{1,0:T(8,128)(2,1)}, bf16[6144,384]{1,0:T(8,128)(2,1)S(1)}, u32[]{:S(2)}, u32[]{:S(2)}) %collective-permute-start.39) | collective-permute-done | bytes 4718624 | tf_op jit(solution)/shard_map/ppermute | solution.py:1337
  387.3 3.8 fusion
  393.2 18.6 %collective-permute-done.20.fx_ref = bf16[256,1536]{1,0:T(8,128)(2,1)S(1)} collective-permute-done((bf16[256,1536]{1,0:T(8,128)(2,1)S(1)}, bf16[256,1536]{1,0:T(8,128)(2,1)S(1)}, u32[]{:S(2)}, u32[]{:S(2)}) %collective-permute-start.20) | collective-permute-done | bytes 786464 | tf_op jit(solution)/shard_map/ppermute | solution.py:1337
  415.8 8.1 %collective-permute-done.22.px_ref = bf16[128,1536]{1,0:T(8,128)(2,1)S(1)} collective-permute-done((bf16[128,1536]{1,0:T(8,128)(2,1)S(1)}, bf16[128,1536]{1,0:T(8,128)(2,1)S(1)}, u32[]{:S(2)}, u32[]{:S(2)}) %collective-permute-start.22) | collective-permute-done | bytes 393248 | tf_op jit(solution)/shard_map/ppermute | solution.py:1337
  425.0 5.6 mid_back.1
  432.5 4.6 all-to-all-start.4
  440.4 11.7 %down.1 = (f32[512,1536]{1,0:T(8,128)S(1)}, bf16[256,1536]{1,0:T(8,128)(2,1)}, bf16[256,1536]{1,0:T(8,128)(2,1)}) custom-call(bf16[4,4,256,256]{3,2,1,0:T(8,128)(2,1)S(1)} %copy-done.8, bf16[4,1536,384]{2,1,0:T(8,128)(2,1)S(1)} %bitcast.122, bf16[4,1536,384]{2,1,0:T(8,128)(2,1)} %collective-permute-done.15.refs_6_.w1_ref), custom_call_target="tpu_custom_call" | custom-call | tf_op jit(solution)/shard_map/down/pallas_call | solution.py:1218
  459.9 5.6 multiply_sine_fusion
  465.9 14.0 %all-to-all-done.4.do_ref = bf16[16,64,384]{2,1,0:T(8,128)(2,1)} async-done(((bf16[16,64,384]{2,1,0:T(8,128)(2,1)}), bf16[16,64,384]{2,1,0:T(8,128)(2,1)}, u32[]{:S(2)}, u32[]{:S(2)}) %all-to-all-start.4) | async-done | bytes 786464 | tf_op jit(solution)/shard_map/all_to_all | solution.py:1391
  480.0 31.3 %attend_back.1 = bf16[2048,384]{1,0:T(8,128)(2,1)} custom-call(s32[1]{0:T(128)} %bitcast.first_ref, bf16[2048,384]{1,0:T(8,128)(2,1)} %bitcast.134, bf16[16,64,384]{2,1,0:T(8,128)(2,1)} %all-to-all-done.4.do_ref, f32[8,512,128]{2,1,0:T(8,128)} %copy-done.24, f32[8,8,512]{2,1,0:T(8,128)} %copy-done.36, f32[2048,128]{1,0:T(8,128)} %get-tuple-element.128.cos_ref, ...), custom_call_target="tpu_custom_call" | custom-call | tf_op jit(solution)/shard_map/attend_back/pallas_call | solution.py:739
  511.3 3.6 all-to-all-start.5
  521.0 6.8 %collective-permute-done.25 = bf16[128,1536]{1,0:T(8,128)(2,1)} collective-permute-done((bf16[128,1536]{1,0:T(8,128)(2,1)S(1)}, bf16[128,1536]{1,0:T(8,128)(2,1)}, u32[]{:S(2)}, u32[]{:S(2)}) %collective-permute-start.25) | collective-permute-done | bytes 393248 | tf_op jit(solution)/shard_map/ppermute | solution.py:1337
  538.0 6.3 da_part.1
  548.0 4.8 fusion.36
  556.4 7.9 %collective-permute-done.28 = bf16[256,1536]{1,0:T(8,128)(2,1)S(1)} collective-permute-done((bf16[256,1536]{1,0:T(8,128)(2,1)S(1)}, bf16[256,1536]{1,0:T(8,128)(2,1)S(1)}, u32[]{:S(2)}, u32[]{:S(2)}) %collective-permute-start.28) | collective-permute-done | bytes 786464 | tf_op jit(solution)/shard_map/ppermute | solution.py:1385
  566.5 5.3 collective-permute-start.29
  575.2 5.0 qkv_grads.1
  586.7 3.5 fusion.8
  592.5 6.3 all-to-all-start.6
  601.8 4.6 collective-permute-start.30
  606.3 7.0 %all-to-all-done.6 = f32[32,1,128]{2,1,0:T(1,128)S(1)} async-done(((f32[32,1,128]{2,1,0:T(1,128)}), f32[32,1,128]{2,1,0:T(1,128)S(1)}, u32[]{:S(2)}, u32[]{:S(2)}) %all-to-all-start.6) | async-done | bytes 16416 | tf_op jit(solution)/shard_map/all_to_all | solution.py:1391
  613.3 4.2 all-to-all-start.7
  623.3 11.4 %all-to-all-done.7 = bf16[4,192,384]{2,1,0:T(8,128)(2,1)} async-done(((bf16[4,192,384]{2,1,0:T(8,128)(2,1)}), bf16[4,192,384]{2,1,0:T(8,128)(2,1)}, u32[]{:S(2)}, u32[]{:S(2)}) %all-to-all-start.7) | async-done | bytes 589856 | tf_op jit(solution)/shard_map/all_to_all | solution.py:1391
  636.6 9.9 %collective-permute-done.33 = bf16[256,1536]{1,0:T(8,128)(2,1)} collective-permute-done((bf16[256,1536]{1,0:T(8,128)(2,1)}, bf16[256,1536]{1,0:T(8,128)(2,1)}, u32[]{:S(2)}, u32[]{:S(2)}) %collective-permute-start.33) | collective-permute-done | bytes 786464 | tf_op jit(solution)/shard_map/ppermute | solution.py:1386
  648.7 3.6 all-to-all-start.8
  652.3 3.4 fusion.3
  660.3 8.7 %all-to-all-done.8.in_ref = bf16[8,192,384]{2,1,0:T(8,128)(2,1)S(1)} async-done(((bf16[8,192,384]{2,1,0:T(8,128)(2,1)}), bf16[8,192,384]{2,1,0:T(8,128)(2,1)S(1)}, u32[]{:S(2)}, u32[]{:S(2)}) %all-to-all-start.8) | async-done | bytes 1179680 | tf_op jit(solution)/shard_map/all_to_all | solution.py:1391
  (261 shorter events, 149.0 us)
Async XLA Ops:
  7.2 101.7 %all-gather.3.cloned.1.call-start = ((), (), s32[]{:S(2)}) async-start(), calls=%async_computation.11 | async-start | bytes 2654208 | tf_op jit(solution)/shard_map/all_gather | solution.py:1425
  11.7 22.9 %collective-permute-start = (bf16[256,1536]{1,0:T(8,128)(2,1)}, bf16[256,1536]{1,0:T(8,128)(2,1)S(1)}, u32[]{:S(2)}, u32[]{:S(2)}) collective-permute-start(bf16[256,1536]{1,0:T(8,128)(2,1)} %bitcast.123), channel_id=1, source_target_pairs={{0,1},{1,2},{2,3},{3,0},{4,5},{5,6},{6,7},{7,4},{8,9},{9,10},{10,1... | collective-permute-start | bytes 2359304 | tf_op jit(solution)/shard_map/ppermute | solution.py:1343
  37.5 41.9 %all-to-all-start.3 = ((bf16[8,192,384]{2,1,0:T(8,128)(2,1)}), bf16[8,192,384]{2,1,0:T(8,128)(2,1)}, u32[]{:S(2)}, u32[]{:S(2)}) async-start(bf16[8,192,384]{2,1,0:T(8,128)(2,1)} %cut_units.1), calls=%async_computation.3 | async-start | bytes 2359296 | tf_op jit(solution)/shard_map/all_to_all | solution.py:1391
  41.9 156.4 %all-gather.5.cloned.1.call-start = ((), (), s32[]{:S(2)}) async-start(), calls=%async_computation.12 | async-start | bytes 5898240 | tf_op jit(solution)/shard_map/all_gather | solution.py:1446
  42.0 37.1 %collective-permute-start.1 = (bf16[256,1536]{1,0:T(8,128)(2,1)S(1)}, bf16[256,1536]{1,0:T(8,128)(2,1)S(1)}, u32[]{:S(2)}, u32[]{:S(2)}) collective-permute-start(bf16[256,1536]{1,0:T(8,128)(2,1)S(1)} %bitcast.124), channel_id=1, source_target_pairs={{0,2},{1,3},{2,0},{3,1},{4,6},{5,7},{6,4},{7,5},{8,10},{9,11},{10,... | collective-permute-start | bytes 2359304 | tf_op jit(solution)/shard_map/ppermute | solution.py:1343
  43.1 36.3 %collective-permute-start.2 = (bf16[256,1536]{1,0:T(8,128)(2,1)S(1)}, bf16[256,1536]{1,0:T(8,128)(2,1)S(1)}, u32[]{:S(2)}, u32[]{:S(2)}) collective-permute-start(bf16[256,1536]{1,0:T(8,128)(2,1)S(1)} %bitcast.125), channel_id=1, source_target_pairs={{0,3},{1,0},{2,1},{3,2},{4,7},{5,4},{6,5},{7,6},{8,11},{9,8},{10,9... | collective-permute-start | bytes 2359304 | tf_op jit(solution)/shard_map/ppermute | solution.py:1343
  80.3 28.5 %all-to-all-start = ((f32[32,1,128]{2,1,0:T(1,128)}), f32[32,1,128]{2,1,0:T(1,128)S(1)}, u32[]{:S(2)}, u32[]{:S(2)}) async-start(f32[32,1,128]{2,1,0:T(1,128)} %broadcast_in_dim.44), calls=%async_computation | async-start | bytes 32768 | tf_op jit(solution)/shard_map/all_to_all | solution.py:1391
  120.0 35.7 %all-to-all-start.1 = ((bf16[4,512,384]{2,1,0:T(8,128)(2,1)}), bf16[4,512,384]{2,1,0:T(8,128)(2,1)S(1)}, u32[]{:S(2)}, u32[]{:S(2)}) async-start(bf16[4,512,384]{2,1,0:T(8,128)(2,1)} %copy-done.27), calls=%async_computation.1 | async-start | bytes 3145728 | tf_op jit(solution)/shard_map/all_to_all | solution.py:1391
  123.7 12.0 %collective-permute-start.5 = (bf16[192,384]{1,0:T(8,128)(2,1)S(1)}, bf16[192,384]{1,0:T(8,128)(2,1)S(1)}, u32[]{:S(2)}, u32[]{:S(2)}) collective-permute-start(bf16[192,384]{1,0:T(8,128)(2,1)S(1)} %bitcast.159), channel_id=1, source_target_pairs={{0,3},{1,0},{2,1},{3,2},{4,7},{5,4},{6,5},{7,6},{8,11},{9,8},{10,9... | collective-permute-start | bytes 442376 | tf_op jit(solution)/shard_map/ppermute | solution.py:1343
  124.4 31.2 %collective-permute-start.4 = (bf16[192,384]{1,0:T(8,128)(2,1)S(1)}, bf16[192,384]{1,0:T(8,128)(2,1)S(1)}, u32[]{:S(2)}, u32[]{:S(2)}) collective-permute-start(bf16[192,384]{1,0:T(8,128)(2,1)S(1)} %bitcast.160), channel_id=1, source_target_pairs={{0,2},{1,3},{2,0},{3,1},{4,6},{5,7},{6,4},{7,5},{8,10},{9,11},{10,... | collective-permute-start | bytes 442376 | tf_op jit(solution)/shard_map/ppermute | solution.py:1343
  125.7 29.9 %collective-permute-start.3 = (bf16[192,384]{1,0:T(8,128)(2,1)S(1)}, bf16[192,384]{1,0:T(8,128)(2,1)S(1)}, u32[]{:S(2)}, u32[]{:S(2)}) collective-permute-start(bf16[192,384]{1,0:T(8,128)(2,1)S(1)} %bitcast.161), channel_id=1, source_target_pairs={{0,1},{1,2},{2,3},{3,0},{4,5},{5,6},{6,7},{7,4},{8,9},{9,10},{10,1... | collective-permute-start | bytes 442376 | tf_op jit(solution)/shard_map/ppermute | solution.py:1343
  155.7 44.1 %collective-permute-start.7 = (bf16[4,192,384]{2,1,0:T(8,128)(2,1)S(1)}, bf16[4,192,384]{2,1,0:T(8,128)(2,1)}, u32[]{:S(2)}, u32[]{:S(2)}) collective-permute-start(bf16[4,192,384]{2,1,0:T(8,128)(2,1)S(1)} %pad_maximum_fusion), channel_id=1, source_target_pairs={{0,16},{16,0},{1,17},{17,1},{2,18},{18,2},{3,19},{19,3},{4,20},{20... | collective-permute-start | bytes 1769480 | tf_op jit(solution)/shard_map/ppermute | solution.py:1337
  198.3 112.9 %collective-permute-start.15 = (bf16[4,1536,384]{2,1,0:T(8,128)(2,1)}, bf16[4,1536,384]{2,1,0:T(8,128)(2,1)}, u32[]{:S(2)}, u32[]{:S(2)}) collective-permute-start(bf16[4,1536,384]{2,1,0:T(8,128)(2,1)} %bitcast.119), channel_id=1, source_target_pairs={{0,4},{4,0},{1,5},{5,1},{2,6},{6,2},{3,7},{7,3},{8,12},{12,8},{9,1... | collective-permute-start | bytes 14155784 | tf_op jit(solution)/shard_map/ppermute | solution.py:1337
  198.3 16.1 %collective-permute-start.6 = (bf16[4,192,384]{2,1,0:T(8,128)(2,1)S(1)}, bf16[4,192,384]{2,1,0:T(8,128)(2,1)S(1)}, u32[]{:S(2)}, u32[]{:S(2)}) collective-permute-start(bf16[4,192,384]{2,1,0:T(8,128)(2,1)S(1)} %pad_maximum_fusion), channel_id=1, source_target_pairs={{0,8},{8,0},{1,9},{9,1},{2,10},{10,2},{3,11},{11,3},{4,12},{12,4},... | collective-permute-start | bytes 1769480 | tf_op jit(solution)/shard_map/ppermute | solution.py:1337
  200.8 19.6 %collective-permute-start.8 = (bf16[2,192,384]{2,1,0:T(8,128)(2,1)S(1)}, bf16[2,192,384]{2,1,0:T(8,128)(2,1)S(1)}, u32[]{:S(2)}, u32[]{:S(2)}) collective-permute-start(bf16[2,192,384]{2,1,0:T(8,128)(2,1)S(1)} %slice.211), channel_id=1, source_target_pairs={{0,8},{8,0},{1,9},{9,1},{2,10},{10,2},{3,11},{11,3},{4,12},{12,4},... | collective-permute-start | bytes 884744 | tf_op jit(solution)/shard_map/ppermute | solution.py:1337
  223.5 33.6 %collective-permute-start.10 = (bf16[16,192,384]{2,1,0:T(8,128)(2,1)}, bf16[16,192,384]{2,1,0:T(8,128)(2,1)}, u32[]{:S(2)}, u32[]{:S(2)}) collective-permute-start(bf16[16,192,384]{2,1,0:T(8,128)(2,1)} %constant_dynamic-update-slice_fusion.mine_ref), channel_id=1, source_target_pairs={{0,4},{4,0},{1,5},{5,1},{2,6},{6,2},{3,7},{7,3},{8,12},{12,8},{9,1... | collective-permute-start | bytes 7077896 | tf_op jit(solution)/shard_map/ppermute | solution.py:1337
  249.7 24.9 %all-to-all-start.2 = ((bf16[16,64,384]{2,1,0:T(8,128)(2,1)}), bf16[16,64,384]{2,1,0:T(8,128)(2,1)S(1)}, u32[]{:S(2)}, u32[]{:S(2)}) async-start(bf16[16,64,384]{2,1,0:T(8,128)(2,1)} %copy-done.35), calls=%async_computation.2 | async-start | bytes 1572864 | tf_op jit(solution)/shard_map/all_to_all | solution.py:1391
  253.4 395.3 %reduce-scatter.5.cloned.1.call-start = ((), (), s32[]{:S(2)}) async-start(), calls=%async_computation.14 | async-start | bytes 5898240 | tf_op jit(solution)/shard_map/reduce_scatter | solution.py:1467
  253.8 31.6 %collective-permute-start.16 = (bf16[256,1536]{1,0:T(8,128)(2,1)S(1)}, bf16[256,1536]{1,0:T(8,128)(2,1)}, u32[]{:S(2)}, u32[]{:S(2)}) collective-permute-start(bf16[256,1536]{1,0:T(8,128)(2,1)S(1)} %bitcast.136), channel_id=1, source_target_pairs={{0,8},{8,0},{1,9},{9,1},{2,10},{10,2},{3,11},{11,3},{4,12},{12,4},... | collective-permute-start | bytes 2359304 | tf_op jit(solution)/shard_map/ppermute | solution.py:1337
  255.7 27.1 %collective-permute-start.17 = (bf16[256,1536]{1,0:T(8,128)(2,1)S(1)}, bf16[256,1536]{1,0:T(8,128)(2,1)}, u32[]{:S(2)}, u32[]{:S(2)}) collective-permute-start(bf16[256,1536]{1,0:T(8,128)(2,1)S(1)} %bitcast.137), channel_id=1, source_target_pairs={{0,16},{16,0},{1,17},{17,1},{2,18},{18,2},{3,19},{19,3},{4,20},{20... | collective-permute-start | bytes 2359304 | tf_op jit(solution)/shard_map/ppermute | solution.py:1337
  280.7 20.5 %collective-permute-start.12 = (bf16[256,1536]{1,0:T(8,128)(2,1)S(1)}, bf16[256,1536]{1,0:T(8,128)(2,1)S(1)}, u32[]{:S(2)}, u32[]{:S(2)}) collective-permute-start(bf16[256,1536]{1,0:T(8,128)(2,1)S(1)} %get-tuple-element.53.refs_0_), channel_id=1, source_target_pairs={{0,16},{16,0},{1,17},{17,1},{2,18},{18,2},{3,19},{19,3},{4,20},{20... | collective-permute-start | bytes 2359304 | tf_op jit(solution)/shard_map/ppermute | solution.py:1337
  282.3 20.5 %collective-permute-start.11 = (bf16[256,1536]{1,0:T(8,128)(2,1)S(1)}, bf16[256,1536]{1,0:T(8,128)(2,1)S(1)}, u32[]{:S(2)}, u32[]{:S(2)}) collective-permute-start(bf16[256,1536]{1,0:T(8,128)(2,1)S(1)} %get-tuple-element.53.refs_0_), channel_id=1, source_target_pairs={{0,8},{8,0},{1,9},{9,1},{2,10},{10,2},{3,11},{11,3},{4,12},{12,4},... | collective-permute-start | bytes 2359304 | tf_op jit(solution)/shard_map/ppermute | solution.py:1337
  283.8 27.4 %collective-permute-start.18 = (bf16[128,1536]{1,0:T(8,128)(2,1)S(1)}, bf16[128,1536]{1,0:T(8,128)(2,1)S(1)}, u32[]{:S(2)}, u32[]{:S(2)}) collective-permute-start(bf16[128,1536]{1,0:T(8,128)(2,1)S(1)} %slice.216), channel_id=1, source_target_pairs={{0,8},{8,0},{1,9},{9,1},{2,10},{10,2},{3,11},{11,3},{4,12},{12,4},... | collective-permute-start | bytes 1179656 | tf_op jit(solution)/shard_map/ppermute | solution.py:1337
  286.4 24.8 %collective-permute-start.19 = (bf16[128,1536]{1,0:T(8,128)(2,1)S(1)}, bf16[128,1536]{1,0:T(8,128)(2,1)S(1)}, u32[]{:S(2)}, u32[]{:S(2)}) collective-permute-start(bf16[128,1536]{1,0:T(8,128)(2,1)S(1)} %slice.217), channel_id=1, source_target_pairs={{0,16},{16,0},{1,17},{17,1},{2,18},{18,2},{3,19},{19,3},{4,20},{20... | collective-permute-start | bytes 1179656 | tf_op jit(solution)/shard_map/ppermute | solution.py:1337
  301.3 22.8 %collective-permute-start.13 = (bf16[128,1536]{1,0:T(8,128)(2,1)S(1)}, bf16[128,1536]{1,0:T(8,128)(2,1)S(1)}, u32[]{:S(2)}, u32[]{:S(2)}) collective-permute-start(bf16[128,1536]{1,0:T(8,128)(2,1)S(1)} %slice.214), channel_id=1, source_target_pairs={{0,8},{8,0},{1,9},{9,1},{2,10},{10,2},{3,11},{11,3},{4,12},{12,4},... | collective-permute-start | bytes 1179656 | tf_op jit(solution)/shard_map/ppermute | solution.py:1337
  302.8 21.3 %collective-permute-start.14 = (bf16[128,1536]{1,0:T(8,128)(2,1)S(1)}, bf16[128,1536]{1,0:T(8,128)(2,1)S(1)}, u32[]{:S(2)}, u32[]{:S(2)}) collective-permute-start(bf16[128,1536]{1,0:T(8,128)(2,1)S(1)} %slice.215), channel_id=1, source_target_pairs={{0,16},{16,0},{1,17},{17,1},{2,18},{18,2},{3,19},{19,3},{4,20},{20... | collective-permute-start | bytes 1179656 | tf_op jit(solution)/shard_map/ppermute | solution.py:1337
  392.3 19.6 %collective-permute-start.20 = (bf16[256,1536]{1,0:T(8,128)(2,1)S(1)}, bf16[256,1536]{1,0:T(8,128)(2,1)S(1)}, u32[]{:S(2)}, u32[]{:S(2)}) collective-permute-start(bf16[256,1536]{1,0:T(8,128)(2,1)S(1)} %copy-done.51), channel_id=1, source_target_pairs={{0,8},{8,0},{1,9},{9,1},{2,10},{10,2},{3,11},{11,3},{4,12},{12,4},... | collective-permute-start | bytes 2359304 | tf_op jit(solution)/shard_map/ppermute | solution.py:1337
  392.7 19.4 %collective-permute-start.21 = (bf16[256,1536]{1,0:T(8,128)(2,1)S(1)}, bf16[256,1536]{1,0:T(8,128)(2,1)S(1)}, u32[]{:S(2)}, u32[]{:S(2)}) collective-permute-start(bf16[256,1536]{1,0:T(8,128)(2,1)S(1)} %copy-done.50), channel_id=1, source_target_pairs={{0,16},{16,0},{1,17},{17,1},{2,18},{18,2},{3,19},{19,3},{4,20},{20... | collective-permute-start | bytes 2359304 | tf_op jit(solution)/shard_map/ppermute | solution.py:1337
  432.5 47.5 %all-to-all-start.4 = ((bf16[16,64,384]{2,1,0:T(8,128)(2,1)}), bf16[16,64,384]{2,1,0:T(8,128)(2,1)}, u32[]{:S(2)}, u32[]{:S(2)}) async-start(bf16[16,64,384]{2,1,0:T(8,128)(2,1)} %copy-done.34), calls=%async_computation.4 | async-start | bytes 1572864 | tf_op jit(solution)/shard_map/all_to_all | solution.py:1391
  452.0 62.8 %collective-permute-start.24 = (bf16[256,1536]{1,0:T(8,128)(2,1)}, bf16[256,1536]{1,0:T(8,128)(2,1)}, u32[]{:S(2)}, u32[]{:S(2)}) collective-permute-start(bf16[256,1536]{1,0:T(8,128)(2,1)} %get-tuple-element.63), channel_id=1, source_target_pairs={{0,8},{8,0},{1,9},{9,1},{2,10},{10,2},{3,11},{11,3},{4,12},{12,4},... | collective-permute-start | bytes 2359304 | tf_op jit(solution)/shard_map/ppermute | solution.py:1337
  459.2 88.8 %collective-permute-start.34 = (bf16[8,96,1536]{2,1,0:T(8,128)(2,1)}, bf16[8,96,1536]{2,1,0:T(8,128)(2,1)}, u32[]{:S(2)}, u32[]{:S(2)}) collective-permute-start(bf16[8,96,1536]{2,1,0:T(8,128)(2,1)} %slice_bitcast_fusion), channel_id=1, source_target_pairs={{0,4},{4,0},{1,5},{5,1},{2,6},{6,2},{3,7},{7,3},{8,12},{12,8},{9,1... | collective-permute-start | bytes 7077896 | tf_op jit(solution)/shard_map/ppermute | solution.py:1337
  465.4 55.5 %collective-permute-start.26 = (bf16[256,1536]{1,0:T(8,128)(2,1)}, bf16[256,1536]{1,0:T(8,128)(2,1)}, u32[]{:S(2)}, u32[]{:S(2)}) collective-permute-start(bf16[256,1536]{1,0:T(8,128)(2,1)} %get-tuple-element.64), channel_id=1, source_target_pairs={{0,16},{16,0},{1,17},{17,1},{2,18},{18,2},{3,19},{19,3},{4,20},{20... | collective-permute-start | bytes 2359304 | tf_op jit(solution)/shard_map/ppermute | solution.py:1337
  511.3 24.1 %all-to-all-start.5 = ((bf16[4,512,384]{2,1,0:T(8,128)(2,1)}), bf16[4,512,384]{2,1,0:T(8,128)(2,1)S(1)}, u32[]{:S(2)}, u32[]{:S(2)}) async-start(bf16[4,512,384]{2,1,0:T(8,128)(2,1)} %bitcast.147), calls=%async_computation.5 | async-start | bytes 3145728 | tf_op jit(solution)/shard_map/all_to_all | solution.py:1391
  514.8 140.9 %reduce-scatter.3.cloned.1.call-start = ((), (), s32[]{:S(2)}) async-start(), calls=%async_computation.13 | async-start | bytes 2654208 | tf_op jit(solution)/shard_map/reduce_scatter | solution.py:1499
  530.8 41.0 %collective-permute-start.27 = (bf16[128,1536]{1,0:T(8,128)(2,1)}, bf16[128,1536]{1,0:T(8,128)(2,1)S(1)}, u32[]{:S(2)}, u32[]{:S(2)}) collective-permute-start(bf16[128,1536]{1,0:T(8,128)(2,1)} %get-tuple-element.114), channel_id=1, source_target_pairs={{0,8},{8,0},{1,9},{9,1},{2,10},{10,2},{3,11},{11,3},{4,12},{12,4},... | collective-permute-start | bytes 1179656 | tf_op jit(solution)/shard_map/ppermute | solution.py:1337
  546.7 17.7 %collective-permute-start.28 = (bf16[256,1536]{1,0:T(8,128)(2,1)S(1)}, bf16[256,1536]{1,0:T(8,128)(2,1)S(1)}, u32[]{:S(2)}, u32[]{:S(2)}) collective-permute-start(bf16[256,1536]{1,0:T(8,128)(2,1)S(1)} %get-tuple-element.111), channel_id=1, source_target_pairs={{0,1},{4,5},{8,9},{12,13},{16,17},{20,21},{24,25},{28,29}} | collective-permute-start | bytes 2359304 | tf_op jit(solution)/shard_map/ppermute | solution.py:1385
  554.0 27.7 %collective-permute-start.35 = (bf16[192,1536]{1,0:T(8,128)(2,1)}, bf16[192,1536]{1,0:T(8,128)(2,1)}, u32[]{:S(2)}, u32[]{:S(2)}) collective-permute-start(bf16[192,1536]{1,0:T(8,128)(2,1)} %bitcast.42), channel_id=1, source_target_pairs={{0,8},{8,0},{1,9},{9,1},{2,10},{10,2},{3,11},{11,3},{4,12},{12,4},... | collective-permute-start | bytes 1769480 | tf_op jit(solution)/shard_map/ppermute | solution.py:1337
  554.1 27.6 %collective-permute-start.37 = (bf16[192,1536]{1,0:T(8,128)(2,1)}, bf16[192,1536]{1,0:T(8,128)(2,1)}, u32[]{:S(2)}, u32[]{:S(2)}) collective-permute-start(bf16[192,1536]{1,0:T(8,128)(2,1)} %bitcast.45), channel_id=1, source_target_pairs={{0,16},{16,0},{1,17},{17,1},{2,18},{18,2},{3,19},{19,3},{4,20},{20... | collective-permute-start | bytes 1769480 | tf_op jit(solution)/shard_map/ppermute | solution.py:1337
  554.8 29.9 %collective-permute-start.31 = (bf16[256,1536]{1,0:T(8,128)(2,1)}, bf16[256,1536]{1,0:T(8,128)(2,1)}, u32[]{:S(2)}, u32[]{:S(2)}) collective-permute-start(bf16[256,1536]{1,0:T(8,128)(2,1)} %get-tuple-element.112), channel_id=1, source_target_pairs={{3,2},{7,6},{11,10},{15,14},{19,18},{23,22},{27,26},{31,30}} | collective-permute-start | bytes 2359304 | tf_op jit(solution)/shard_map/ppermute | solution.py:1386
  566.5 20.2 %collective-permute-start.29 = (bf16[256,1536]{1,0:T(8,128)(2,1)}, bf16[256,1536]{1,0:T(8,128)(2,1)}, u32[]{:S(2)}, u32[]{:S(2)}) collective-permute-start(bf16[256,1536]{1,0:T(8,128)(2,1)} %fusion.7), channel_id=1, source_target_pairs={{0,1},{1,2},{4,5},{5,6},{8,9},{9,10},{12,13},{13,14},{16,17},{17,1... | collective-permute-start | bytes 2359304 | tf_op jit(solution)/shard_map/ppermute | solution.py:1385
  583.2 15.5 %collective-permute-start.36 = (bf16[96,1536]{1,0:T(8,128)(2,1)S(1)}, bf16[96,1536]{1,0:T(8,128)(2,1)S(1)}, u32[]{:S(2)}, u32[]{:S(2)}) collective-permute-start(bf16[96,1536]{1,0:T(8,128)(2,1)S(1)} %get-tuple-element.107), channel_id=1, source_target_pairs={{0,16},{16,0},{1,17},{17,1},{2,18},{18,2},{3,19},{19,3},{4,20},{20... | collective-permute-start | bytes 884744 | tf_op jit(solution)/shard_map/ppermute | solution.py:1337
  584.1 14.7 %collective-permute-start.38 = (bf16[96,1536]{1,0:T(8,128)(2,1)S(1)}, bf16[96,1536]{1,0:T(8,128)(2,1)S(1)}, u32[]{:S(2)}, u32[]{:S(2)}) collective-permute-start(bf16[96,1536]{1,0:T(8,128)(2,1)S(1)} %get-tuple-element.108), channel_id=1, source_target_pairs={{0,8},{8,0},{1,9},{9,1},{2,10},{10,2},{3,11},{11,3},{4,12},{12,4},... | collective-permute-start | bytes 884744 | tf_op jit(solution)/shard_map/ppermute | solution.py:1337
  590.2 27.2 %collective-permute-start.32 = (bf16[256,1536]{1,0:T(8,128)(2,1)}, bf16[256,1536]{1,0:T(8,128)(2,1)}, u32[]{:S(2)}, u32[]{:S(2)}) collective-permute-start(bf16[256,1536]{1,0:T(8,128)(2,1)} %get-tuple-element.110), channel_id=1, source_target_pairs={{3,2},{2,1},{7,6},{6,5},{11,10},{10,9},{15,14},{14,13},{19,18},{18... | collective-permute-start | bytes 2359304 | tf_op jit(solution)/shard_map/ppermute | solution.py:1386
  592.5 20.8 %all-to-all-start.6 = ((f32[32,1,128]{2,1,0:T(1,128)}), f32[32,1,128]{2,1,0:T(1,128)S(1)}, u32[]{:S(2)}, u32[]{:S(2)}) async-start(f32[32,1,128]{2,1,0:T(1,128)} %bitcast.35), calls=%async_computation.6 | async-start | bytes 32768 | tf_op jit(solution)/shard_map/all_to_all | solution.py:1391
  601.8 34.9 %collective-permute-start.30 = (bf16[256,1536]{1,0:T(8,128)(2,1)}, bf16[256,1536]{1,0:T(8,128)(2,1)}, u32[]{:S(2)}, u32[]{:S(2)}) collective-permute-start(bf16[256,1536]{1,0:T(8,128)(2,1)} %get-tuple-element.109), channel_id=1, source_target_pairs={{0,1},{1,2},{2,3},{4,5},{5,6},{6,7},{8,9},{9,10},{10,11},{12,13},{... | collective-permute-start | bytes 2359304 | tf_op jit(solution)/shard_map/ppermute | solution.py:1385
  613.3 21.5 %all-to-all-start.7 = ((bf16[4,192,384]{2,1,0:T(8,128)(2,1)}), bf16[4,192,384]{2,1,0:T(8,128)(2,1)}, u32[]{:S(2)}, u32[]{:S(2)}) async-start(bf16[4,192,384]{2,1,0:T(8,128)(2,1)} %pad_maximum_fusion.1), calls=%async_computation.8 | async-start | bytes 1179648 | tf_op jit(solution)/shard_map/all_to_all | solution.py:1391
  620.0 26.5 %collective-permute-start.33 = (bf16[256,1536]{1,0:T(8,128)(2,1)}, bf16[256,1536]{1,0:T(8,128)(2,1)}, u32[]{:S(2)}, u32[]{:S(2)}) collective-permute-start(bf16[256,1536]{1,0:T(8,128)(2,1)} %fusion.6), channel_id=1, source_target_pairs={{3,2},{2,1},{1,0},{7,6},{6,5},{5,4},{11,10},{10,9},{9,8},{15,14},{... | collective-permute-start | bytes 2359304 | tf_op jit(solution)/shard_map/ppermute | solution.py:1386
  648.7 20.3 %all-to-all-start.8 = ((bf16[8,192,384]{2,1,0:T(8,128)(2,1)}), bf16[8,192,384]{2,1,0:T(8,128)(2,1)S(1)}, u32[]{:S(2)}, u32[]{:S(2)}) async-start(bf16[8,192,384]{2,1,0:T(8,128)(2,1)} %bitcast.152), calls=%async_computation.10 | async-start | bytes 2359296 | tf_op jit(solution)/shard_map/all_to_all | solution.py:1391
  (61 other events, 866.5 us)
Sparse Core Ops, SparseCore 0:
  11.9 31.7 all-gather.2
  79.6 118.7 all-gather.4
  391.3 95.5 reduce-scatter.4
  581.8 39.1 reduce-scatter.2

commit v3 on v2

--- a/solution.py
+++ b/solution.py
@@ -540,6 +540,12 @@
 NEG=-1e30
 C2 = (96 ** -0.5) * 1.4426950408889634
 
+def cost(microseconds):
+    return pl.CostEstimate(
+        flops=microseconds * 10**9, bytes_accessed=microseconds * 3 * 10**6, transcendentals=0
+    )
+
+
 def lane_iota(rows):
     return lax.broadcasted_iota(jnp.int32, (rows, LN), 1)
 
@@ -656,6 +662,7 @@
                         pltpu.VMEM((blocks, 2*BQ, BQ), jnp.float32)],
         compiler_params=pltpu.CompilerParams(vmem_limit_bytes=48 << 20),
         name="attend",
+        cost_estimate=cost(22),
     )(first, x)
 
 def attn_bwd_kernel(length, first_ref, x_ref, do_ref, of_ref, lse_ref, cos_ref, sin_ref, out_ref,
@@ -752,6 +759,7 @@
                         pltpu.VMEM((blocks, BQ, LN), jnp.float32)],
         compiler_params=pltpu.CompilerParams(vmem_limit_bytes=56 << 20),
         name="attend_back",
+        cost_estimate=cost(31),
     )(first, x, do, of, lse, cos, sin)
 
 
@@ -827,6 +835,7 @@
         ],
         compiler_params=pltpu.CompilerParams(vmem_limit_bytes=48 << 20),
         name="norm_qkv",
+        cost_estimate=cost(7),
     )(place, *operands)
 
 
@@ -880,6 +889,7 @@
         scratch_shapes=[pltpu.VMEM((count, inner), jnp.bfloat16)],
         compiler_params=pltpu.CompilerParams(vmem_limit_bytes=48 << 20),
         name="out_norm",
+        cost_estimate=cost(4),
     )(*operands)
 
 
@@ -944,6 +954,7 @@
         out_shape=shapes,
         compiler_params=pltpu.CompilerParams(vmem_limit_bytes=48 << 20),
         name="mid_back",
+        cost_estimate=cost(5),
     )(*operands)
 
 
@@ -985,6 +996,7 @@
         out_shape=shapes,
         compiler_params=pltpu.CompilerParams(vmem_limit_bytes=48 << 20),
         name="da_part",
+        cost_estimate=cost(6),
     )(place, *operands)
 
 
@@ -1006,6 +1018,7 @@
         out_specs=full_spec(shape),
         out_shape=shape,
         name="cut_units",
+        cost_estimate=cost(3),
     )(*operands)
 
 
@@ -1027,10 +1040,11 @@
         out_specs=[full_spec(v) for v in shapes],
         out_shape=shapes,
         name="uncut_units",
+        cost_estimate=cost(3),
     )(value)
 
 
-def place_kernel(parts, at_ref, mine_ref, other_ref, out_ref):
+def place_kernel(parts, turned, at_ref, mine_ref, other_ref, out_ref):
     size = mine_ref.shape[1]
     z = at_ref[3]
     for c, ref in enumerate((mine_ref, other_ref)):
@@ -1039,22 +1053,23 @@
             rows = pl.multiple_of(((y * 2 + x) * 2 + (at_ref[2] ^ c)) * size, size)
             for k in range(ref.shape[0] // parts):
                 count = ref.shape[0] // parts
-                source = lax.rem(z + (count - k), count)
+                source = lax.rem(z + (count - k), count) if turned else k
                 cols = pl.multiple_of(source * 3 * LN, 3 * LN)
                 out_ref[pl.ds(rows, size), pl.ds(cols, 3 * LN)] = ref[n * count + k]
 
 
-def place_call(at, mine, other):
+def place_call(at, mine, other, turned):
     size = mine.shape[1]
     shape = jax.ShapeDtypeStruct((8 * size, mine.shape[0] // 4 * mine.shape[2]), mine.dtype)
     return pl.pallas_call(
-        partial(place_kernel, 4),
+        partial(place_kernel, 4, turned),
         grid=(1,),
         in_specs=[pl.BlockSpec(memory_space=pltpu.SMEM), full_spec(mine), full_spec(other)],
         out_specs=full_spec(shape),
         out_shape=shape,
         compiler_params=pltpu.CompilerParams(vmem_limit_bytes=32 << 20),
         name="place_out",
+        cost_estimate=cost(3),
     )(at, mine, other)
 
 
@@ -1100,6 +1115,7 @@
         scratch_shapes=[pltpu.VMEM((4, count, width), jnp.bfloat16)],
         compiler_params=pltpu.CompilerParams(vmem_limit_bytes=40 << 20),
         name="down_back",
+        cost_estimate=cost(8),
     )(*pieces, mine, other)
 
 
@@ -1184,6 +1200,7 @@
         scratch_shapes=[pltpu.VMEM((4, count, width), low), pltpu.VMEM((4, count, width), jnp.float32)],
         compiler_params=pltpu.CompilerParams(vmem_limit_bytes=56 << 20),
         name="units",
+        cost_estimate=cost(26),
     )(*pieces, mine, other, grad_hidden)
 
 
@@ -1224,12 +1241,13 @@
         scratch_shapes=[pltpu.VMEM((4, count, width), jnp.float32)],
         compiler_params=pltpu.CompilerParams(vmem_limit_bytes=40 << 20),
         name="down",
+        cost_estimate=cost(11),
     )(hidden, mine, other)
 
 
-def unit_grads_kernel(*refs):
+def unit_grads_kernel(place_ref, *refs):
     b_pieces, g_pieces = refs[:5], refs[5:10]
-    dgu_ref, hid_ref, out_ref, fill_s, b_s, g_s = refs[10:]
+    dgu_ref, hid_ref, mine_ref, other_ref, fill_s, b_s, g_s = refs[10:]
     count = fill_s.shape[1]
 
     @pl.when(pl.program_id(0) == 0)
@@ -1247,33 +1265,38 @@
         at = pl.ds(pl.multiple_of(m * rows, rows), rows)
         left, right = b_s[at, :], g_s[at, :]
         down = dotf(right, hidden, ((1,), (0,)))
-        for n in range(2):
-            out_ref[n, 0, at, : 2 * LN] = dotf(left, grads[n], ((1,), (0,))).astype(jnp.bfloat16)
-            out_ref[n, 0, at, 2 * LN :] = down[:, n * LN : (n + 1) * LN].astype(jnp.bfloat16)
+        for n, out_ref in enumerate((mine_ref, other_ref)):
+            out_ref[0, at, : 2 * LN] = dotf(left, grads[n], ((1,), (0,))).astype(jnp.bfloat16)
+            out_ref[0, at, 2 * LN :] = down[:, n * LN : (n + 1) * LN].astype(jnp.bfloat16)
         return carry
 
     lax.fori_loop(0, 4, body, 0)
 
 
-def unit_grads_call(b_pieces, g_pieces, grads, hidden):
+def unit_grads_call(place, b_pieces, g_pieces, grads, hidden):
     count, width = b_pieces[0].shape
     parts = hidden.shape[0]
     low = jnp.bfloat16
     operands = (*b_pieces, *g_pieces)
     return pl.pallas_call(
         unit_grads_kernel,
-        grid=(parts,),
-        in_specs=[full_spec(v) for v in operands]
-        + [
-            pl.BlockSpec((1,) + grads.shape[1:], lambda z: (z, 0, 0, 0, 0)),
-            pl.BlockSpec((1,) + hidden.shape[1:], lambda z: (z, 0, 0, 0)),
-        ],
-        out_specs=pl.BlockSpec((2, 1, width, 3 * LN), lambda z: (0, z, 0, 0)),
-        out_shape=jax.ShapeDtypeStruct((2, parts, width, 3 * LN), low),
-        scratch_shapes=[pltpu.VMEM((4, count, width), low)] + [pltpu.VMEM((width, 4 * count), low)] * 2,
+        grid_spec=pltpu.PrefetchScalarGridSpec(
+            num_scalar_prefetch=1,
+            grid=(parts,),
+            in_specs=[full_spec(v) for v in operands]
+            + [
+                pl.BlockSpec((1,) + grads.shape[1:], lambda k, at: (k, 0, 0, 0, 0)),
+                pl.BlockSpec((1,) + hidden.shape[1:], lambda k, at: (k, 0, 0, 0)),
+            ],
+            out_specs=[pl.BlockSpec((1, width, 3 * LN), lambda k, at: (k, 0, 0))] * 2,
+            scratch_shapes=[pltpu.VMEM((4, count, width), low)]
+            + [pltpu.VMEM((width, 4 * count), low)] * 2,
+        ),
+        out_shape=[jax.ShapeDtypeStruct((parts, width, 3 * LN), low)] * 2,
         compiler_params=pltpu.CompilerParams(vmem_limit_bytes=56 << 20),
         name="unit_grads",
-    )(*operands, grads, hidden)
+        cost_estimate=cost(19),
+    )(place, *operands, grads, hidden)
 
 
 def qkv_grads_kernel(a_ref, d_ref, out_ref):
@@ -1295,6 +1318,7 @@
         out_shape=shape,
         compiler_params=pltpu.CompilerParams(vmem_limit_bytes=32 << 20),
         name="qkv_grads",
+        cost_estimate=cost(5),
     )(normed, grads)
 
 
@@ -1326,6 +1350,7 @@
         scratch_shapes=[pltpu.VMEM((width, inner), jnp.bfloat16)],
         compiler_params=pltpu.CompilerParams(vmem_limit_bytes=32 << 20),
         name="out_grads",
+        cost_estimate=cost(3),
     )(at, grad, attended)
 
 
@@ -1339,21 +1364,30 @@
 
 def gather_blocks(value, size):
     shift = lambda k: [(i, (i + k) % size) for i in range(size)]
-    order = sorted(range(1, size), key=lambda k: -min(k, size - k))
-    got = {k: lax.ppermute(value, "z", shift(k)) for k in order}
-    return [value] + [got[k] for k in range(1, size)]
+    return [value] + [lax.ppermute(value, "z", shift(k)) for k in range(1, size)]
+
+
+def gather_sides(value):
+    return swap(value, "x"), swap(value, "y")
+
+
+def gather_corner(xn, yn):
+    half = xn.shape[0] // 2
+    return swap(yn[:half], "x"), swap(xn[half:], "y")
 
 
 def gather_square(value):
-    half = value.shape[0] // 2
-    xn, yn = swap(value, "x"), swap(value, "y")
-    return value, xn, yn, swap(yn[:half], "x"), swap(xn[half:], "y")
+    sides = gather_sides(value)
+    return (value, *sides, *gather_corner(*sides))
 
 
 def reduce_square(keep, send_x, send_y):
+    return reduce_square_rest(keep, swap(send_x, "x"), swap(send_y, "y"))
+
+
+def reduce_square_rest(keep, from_x, from_y):
     low = jnp.bfloat16
-    half = send_x.shape[0] // 2
-    from_x, from_y = swap(send_x, "x"), swap(send_y, "y")
+    half = from_x.shape[0] // 2
     pass_y = swap((keep[3 * half :] + from_x[half:].astype(jnp.float32)).astype(low), "y")
     pass_x = swap((keep[2 * half : 3 * half] + from_y[half:].astype(jnp.float32)).astype(low), "x")
     return keep, from_x, from_y, pass_x, pass_y
@@ -1372,7 +1406,7 @@
     )
 
 
-def reduce_line(part, at, size):
+def reduce_line(part, at, size, between=None):
     block = lambda k: lax.dynamic_index_in_dim(part, jnp.clip(at + k, 0, size - 1), 0, keepdims=False)
     wide = lambda v: v.astype(jnp.float32)
     up, down = None, None
@@ -1384,6 +1418,8 @@
             send_down = (wide(send_down) + wide(down)).astype(part.dtype)
         up = lax.ppermute(send_up, "z", [(i, i + 1) for i in range(step)])
         down = lax.ppermute(send_down, "z", [(size - 1 - i, size - 2 - i) for i in range(step)])
+        if between is not None:
+            up, down = between(step, up, down)
     return wide(block(0)) + wide(up) + wide(down)
 
 
@@ -1408,23 +1444,25 @@
     place = z_at.reshape(1).astype(jnp.int32)
     at = jnp.stack([lax.axis_index("y"), x_at, c_at, z_at]).astype(jnp.int32)
 
-    own = tokens.reshape(count, width)
-    blocks = gather_blocks(own, nz)
-
     gains = jnp.concatenate([norm_in, norm_mid], axis=1)
     share = norm_in.shape[1]
     gains = jnp.pad(gains, ((0, 0), (0, LN - 2 * share)))
-    gains = all_to_all(jnp.broadcast_to(gains, (devices, LN)), EVERY)
+    gains = all_to_all(jnp.broadcast_to(gains, (nz, LN)), "z")
+
+    own, gains, w_o = tie(tokens.reshape(count, width), gains, w_out[0].T)
+    blocks = gather_blocks(own, nz)
+    w_o = jnp.stack(gather_blocks(w_o, nz))
+
+    gains = all_to_all(jnp.broadcast_to(gains, (plane, nz, LN)).reshape(plane * nz, LN), ("y", "x", "c"))
     gain_in = gains[:, :share].reshape(1, width)
     gain_mid = gains[:, share : 2 * share].reshape(1, width)
 
     kv_local = w_key.shape[2] // HD
     per_head = lambda w: w[0].reshape(w.shape[1], kv_local, -1)
     w_qkv = jnp.concatenate([per_head(w_query), per_head(w_key), per_head(w_value)], axis=2)
-    w_qkv = w_qkv.reshape(w_qkv.shape[0], -1)
-    w_qkv = lax.all_gather(w_qkv, ("y", "x", "c"), axis=0, tiled=True)
-
-    gate, up, down, early = tie(w_gate[0], w_up[0], w_down[0], blocks[1])
+    w_qkv = lax.all_gather(w_qkv.reshape(w_qkv.shape[0], -1), ("y", "x", "c"), axis=0, tiled=True)
+
+    gate, up, down, _ = tie(w_gate[0], w_up[0], w_down[0], gains)
     w_ff = all_to_all(cut_call(gate, up, down), ("y", "x", "c"))
     w_ff = w_ff.reshape(width, 3 * LN)
 
@@ -1439,40 +1477,44 @@
     token_cos, token_sin = jnp.cos(token_angle), jnp.sin(token_angle)
     row_cos, row_sin = jnp.cos(row_angle), jnp.sin(row_angle)
 
+    sides = gather_sides(w_o)
+    blocks[1], *sides = tie(blocks[1], *sides)
+    w_o = jnp.concatenate([w_o, *sides, *gather_corner(*sides)], axis=0)
+    w_o = (w_o, swap(w_o, "c"))
     normed, qkv = qkv_call(place, blocks, gain_in, w_qkv, token_cos, token_sin, rows)
-    w_ff, w_o, *_ = tie(w_ff, w_out[0].T, *blocks)
     qkv = all_to_all(qkv, ("x", "c")).reshape(length, 3 * LN)
 
-    w_mine = lax.all_gather(w_ff, "z", axis=0, tiled=True).reshape(nz, width, 3 * LN)
+    w_ff, _ = tie(w_ff, normed)
+    w_mine = lax.all_gather(w_ff, "z", axis=0, tiled=True)
+    cot_low = cotangent.reshape(count, width)
+    cot_first, _ = tie(cot_low, qkv)
+    cot_sides = gather_sides(cot_first)
+
+    attended, attended_float, log_total = attn_fwd(first, qkv)
+    attended, *cot_sides = tie(attended, *cot_sides)
+    attended = all_to_all(attended, ("x", "c", "z"))
+    w_o = place_call(at, *w_o, True)
+    attended, *corner = tie(attended, *gather_corner(*cot_sides))
+    cot_pieces = (cot_low, *cot_sides, *corner)
+    middle, normed_b, attended_low = out_call(attended, w_o, own, gain_mid, rows)
+    w_mine, _ = tie(w_mine, normed_b)
+    w_mine = w_mine.reshape(nz, width, 3 * LN)
     w_other = swap(w_mine, "c")
-    w_o = jnp.stack(gather_blocks(w_o, nz))
-    cot_low = cotangent.reshape(count, width)
-    cot_low, w_o, _ = tie(cot_low, w_o, qkv)
-    own_o, xn_o, yn_o, first_o, last_o = gather_square(w_o)
-    w_o = jnp.concatenate([own_o, xn_o, yn_o, first_o, last_o], axis=0)
-    w_o = place_call(at, w_o, swap(w_o, "c"))
-    cot_pieces = gather_square(cot_low)
-
-    attended, attended_float, log_total = attn_fwd(first, qkv)
-    attended = all_to_all(attended, ("x", "c", "z"))
-    middle, normed_b, attended_low = out_call(attended, w_o, own, gain_mid, rows)
     b_pieces = gather_square(normed_b)
 
     grad_hidden = down_back_call(cot_pieces, w_mine, w_other)
     grad_gu, hidden, *sends = units_call(b_pieces, w_mine, w_other, grad_hidden)
-    grad_b = reduce_square(*sends)
-    grad_ff = unit_grads_call(b_pieces, cot_pieces, grad_gu, hidden)
-    grad_ff = grad_ff.reshape(2, nz * width, 3 * LN)
-    grad_ff = (grad_ff[0].astype(jnp.float32) + swap(grad_ff[1], "c").astype(jnp.float32)).astype(jnp.bfloat16)
+    from_x, from_y = swap(sends[1], "x"), swap(sends[2], "y")
+    ff_mine, ff_other = unit_grads_call(place, b_pieces, cot_pieces, grad_gu, hidden)
+    from_x, from_y, ff_mine, ff_other = tie(from_x, from_y, ff_mine, ff_other)
+    grad_b = reduce_square_rest(sends[0], from_x, from_y)
+    grad_ff = ff_mine.astype(jnp.float32) + swap(ff_other, "c").astype(jnp.float32)
+    grad_ff = grad_ff.astype(jnp.bfloat16).reshape(nz * width, 3 * LN)
     grad_ff = lax.psum_scatter(grad_ff, "z", scatter_dimension=0, tiled=True)
-    grad_ff = all_to_all(grad_ff.reshape(plane, width // plane, 3 * LN), ("y", "x", "c"))
-
     grad_mid, grad_low, grad_o, gain_grad_mid = mid_back_call(
         grad_b, middle, cot_low, gain_mid, w_o, rows, nz
     )
-    hidden, grad_o = tie(hidden, grad_o)
     grad_o = all_to_all(grad_o, ("x", "c", "z"))
-    out = middle + total_square(reduce_square(*down_call(hidden, w_mine, w_other)))
 
     grad_wo = out_grads_call(at, grad_low, attended_low)
     grad_wo = grad_wo[0].astype(jnp.float32) + swap(grad_wo[1], "c").astype(jnp.float32)
@@ -1487,7 +1529,6 @@
         )
     ).astype(jnp.bfloat16)
     grad_wo = jnp.stack([grad_wo[:, z * 3 * LN : (z + 1) * 3 * LN] for z in range(nz)])
-    grad_wo = jnp.sum(all_to_all(grad_wo, "z").astype(jnp.float32), axis=0)
 
     grad_qkv = attn_bwd(first, qkv, grad_o, attended_float, log_total, row_cos, row_sin)
     grad_qkv = all_to_all(grad_qkv.reshape(-1, chunk, 3 * LN), ("x", "c"))
@@ -1497,13 +1538,31 @@
         normed.reshape(rows * chunk, width), grad_qkv.reshape(kv_local, rows * chunk, 3 * LN)
     )
     grad_wqkv = lax.psum_scatter(grad_wqkv, ("y", "x", "c"), scatter_dimension=0, tiled=True)
-    grad_a = reduce_line(part.reshape(nz, count, width), z_at, nz)
-
     gain_grads = jnp.concatenate(
         [gain_grad_in.reshape(devices, share), gain_grad_mid.reshape(devices, share)], axis=1
     )
     gain_grads = jnp.pad(gain_grads, ((0, 0), (0, LN - 2 * share)))
-    gain_grads = jnp.sum(all_to_all(gain_grads, EVERY), axis=0, keepdims=True)
+    late = {"ff": grad_ff}
+
+    def between(step, up, down):
+        if step == 1:
+            late["hidden"], _, _ = tie(hidden, up, down)
+            late["wo"] = all_to_all(grad_wo, "z")
+            late["gain"] = all_to_all(gain_grads, EVERY)
+        if step == nz - 2:
+            up, down, late["wo"], late["gain"] = tie(up, down, late["wo"], late["gain"])
+        if step == nz - 2:
+            late["ff"], _ = tie(late["ff"], up)
+            late["ff"] = all_to_all(late["ff"].reshape(plane, width // plane, 3 * LN), ("y", "x", "c"))
+        if step == nz - 1:
+            up, down, late["ff"] = tie(up, down, late["ff"])
+        return up, down
+
+    grad_a = reduce_line(part.reshape(nz, count, width), z_at, nz, between)
+    grad_ff = late["ff"]
+    out = middle + total_square(reduce_square(*down_call(late["hidden"], w_mine, w_other)))
+    grad_wo = jnp.sum(late["wo"].astype(jnp.float32), axis=0)
+    gain_grads = jnp.sum(late["gain"], axis=0, keepdims=True)
 
     stream = own.astype(jnp.float32)
     factor = lax.rsqrt(jnp.mean(stream * stream, axis=-1, keepdims=True) + EPS)

time: 694 us -> 602 us (0.87)
  waiting for transfers between devices: 287 us -> 193 us
  blocking collectives: 0 us -> 11.7 us
    ppermute x6, waiting for transfers between devices: 83 us -> 37.4 us  [gather_blocks(): lax.ppermute(value, 'z', shift(k))]
    all_gather x2, waiting for transfers between devices: 41.9 us -> 0.01 us  [the longest x1 0.01 us: fast_local(): lax.all_gather(w_qkv.reshape(w_qkv.shape[0], -1), ('y', 'x', 'c'), axis=0...]
    all_to_all x9, waiting for transfers between devices: 60.7 us -> 81.6 us  [all_to_all(): return lax.all_to_all(value, axes, 0, 0, tiled=True)]
    all_to_all x0 -> x1, blocking collectives: none -> 11.7 us  [all_to_all(): return lax.all_to_all(value, axes, 0, 0, tiled=True)]
    ppermute x28, waiting for transfers between devices: 81.4 us -> 70.3 us  [swap(): return lax.ppermute(value, axis, SWAP)]
    ppermute x3, waiting for transfers between devices: 9.9 us -> 0.01 us  [reduce_line(): up = lax.ppermute(send_up, 'z', [(i, i + 1) for i in range(step)])]
    convert_element_type x6 -> x4, other arithmetic: 14 us -> 11.8 us  [the longest x3 6.17 us: reduce_square_rest(): (keep[3 * half:] + from_x[half:].astype(jnp.float32)).astype(low)]
    unnamed x119 -> x114, local copies, waits for them, and re-layouts: 38.7 us -> 39.2 us
  transfers between devices with their start and end apart: 53 -> 53, of which waited for: 28 -> 17; matrix products, arithmetic and copies ran while one was open for 10% -> 11% of each run, Pallas kernels for 16% -> 22%
where the time goes in v3:
time: 602 us; the launch traced here: 591 us
  waiting for transfers between devices  193 us (32%)
  Pallas kernels  161 us (27%)
  starting transfers between devices  100 us (17%)
  local copies, waits for them, and re-layouts  59.9 us (10%)
  other arithmetic  50.6 us (8%)
  between operations  15.6 us (3%)
  blocking collectives  11.7 us (2%)
    all_to_all x9, waiting for transfers between devices, all_to_all(): return lax.all_to_all(value, axes, 0, 0, tiled=True)  81.6 us
    ppermute x28, waiting for transfers between devices, swap(): return lax.ppermute(value, axis, SWAP)  70.3 us
    all_to_all x9, starting transfers between devices, all_to_all(): return lax.all_to_all(value, axes, 0, 0, tiled=True)  52 us
    unnamed x114, local copies, waits for them, and re-layouts  39.2 us
    ppermute x6, waiting for transfers between devices, gather_blocks(): lax.ppermute(value, 'z', shift(k))  37.4 us
    pallas_call x1, Pallas kernels, attn_bwd(): pl.pallas_call(functools.partial(attn_bwd_kernel, length), grid=(blocks,)...  31.4 us
    pallas_call x1, Pallas kernels, units_call(): pl.pallas_call(units_kernel, grid=(parts,), in_specs=[full_spec(v) for v...  27 us
    ppermute x28, starting transfers between devices, swap(): return lax.ppermute(value, axis, SWAP)  26.9 us
  transfers between devices with their start and end apart: 53, of which 17 were waited for; matrix products, arithmetic and copies ran while one was open for 11% of the time, Pallas kernels for 22%

profile of v3, /device:TPU:0, one launch (start us, length us, event | category | flops | bytes accessed | tf_op | source)
XLA Modules:
  0.0 591.3 jit_solution(5927616416979669895)
XLA Ops:
  12.6 11.7 %all_to_all.65 = f32[4,1,128]{2,1,0:T(1,128)S(1)} all-to-all(f32[4,1,128]{2,1,0:T(1,128)S(1)} %broadcast_in_dim.47), channel_id=1, replica_groups=mesh['y'=2,'x'=2,'c'=2,'z'=4] {'z'}, dimensions={0} | all-to-all | bytes 4096 | tf_op jit(solution)/shard_map/all_to_all | solution.py:1427
  27.4 3.7 all-to-all-start.1
  36.1 3.2 collective-permute-start.7
  39.3 33.4 %collective-permute-done.2 = bf16[192,384]{1,0:T(8,128)(2,1)S(1)} collective-permute-done((bf16[192,384]{1,0:T(8,128)(2,1)}, bf16[192,384]{1,0:T(8,128)(2,1)S(1)}, u32[]{:S(2)}, u32[]{:S(2)}) %collective-permute-start.2) | collective-permute-done | bytes 147488 | tf_op jit(solution)/shard_map/ppermute | solution.py:1367
  76.5 2.6 cut_units.1
  79.1 4.3 all-to-all-start.4
  85.5 4.0 collective-permute-done.6.refs_2_
  89.5 8.3 %norm_qkv.1 = (bf16[2,512,1536]{2,1,0:T(8,128)(2,1)}, bf16[4,512,384]{2,1,0:T(8,128)(2,1)S(1)}) custom-call(s32[1]{0:T(128)} %bitcast.1.place_ref, bf16[256,1536]{1,0:T(8,128)(2,1)S(1)} %bitcast.119, bf16[256,1536]{1,0:T(8,128)(2,1)S(1)} %collective-permute-done.refs_1_, bf16[256,1536]{1,0:T(8,128)(2,1)S(1)} %collective-permute-done.6.refs_2_, ...), custom_call_target="tpu_custom_call" | custom-call | flops 7000000000 | bytes 21000000 | tf_op jit(solution)/shard_map/norm_qkv/pallas_call | solution.py:824
  103.2 3.6 all-to-all-start.2
  117.3 15.8 %collective-permute-done.12 = bf16[2,192,384]{2,1,0:T(8,128)(2,1)S(1)} collective-permute-done((bf16[2,192,384]{2,1,0:T(8,128)(2,1)S(1)}, bf16[2,192,384]{2,1,0:T(8,128)(2,1)S(1)}, u32[]{:S(2)}, u32[]{:S(2)}) %collective-permute-start.12) | collective-permute-done | bytes 294944 | tf_op jit(solution)/shard_map/ppermute | solution.py:1362
  135.6 22.8 %attend.1 = (bf16[16,64,384]{2,1,0:T(8,128)(2,1)}, f32[8,512,128]{2,1,0:T(8,128)S(1)}, f32[8,8,512]{2,1,0:T(8,128)S(1)}) custom-call(s32[1]{0:T(128)} %bitcast.first_ref, bf16[2048,384]{1,0:T(8,128)(2,1)S(1)} %bitcast.124), custom_call_target="tpu_custom_call" | custom-call | flops 22000001024 | bytes 66000000 | tf_op jit(solution)/shard_map/attend/pallas_call | solution.py:648
  160.5 20.8 %all-to-all-start.3 = ((bf16[16,64,384]{2,1,0:T(8,128)(2,1)}), bf16[16,64,384]{2,1,0:T(8,128)(2,1)S(1)}, u32[]{:S(2)}, u32[]{:S(2)}) async-start(bf16[16,64,384]{2,1,0:T(8,128)(2,1)} %get-tuple-element.76), calls=%async_computation.3 | async-start | bytes 1572864 | tf_op jit(solution)/shard_map/all_to_all | solution.py:1427
  192.4 7.9 %collective-permute-done.10.refs_3_.refs_8_ = bf16[128,1536]{1,0:T(8,128)(2,1)} collective-permute-done((bf16[128,1536]{1,0:T(8,128)(2,1)}, bf16[128,1536]{1,0:T(8,128)(2,1)}, u32[]{:S(2)}, u32[]{:S(2)}) %collective-permute-start.10) | collective-permute-done | bytes 393248 | tf_op jit(solution)/shard_map/ppermute | solution.py:1362
  200.4 20.5 %all-to-all-done.3.o_ref = bf16[16,64,384]{2,1,0:T(8,128)(2,1)S(1)} async-done(((bf16[16,64,384]{2,1,0:T(8,128)(2,1)}), bf16[16,64,384]{2,1,0:T(8,128)(2,1)S(1)}, u32[]{:S(2)}, u32[]{:S(2)}) %all-to-all-start.3) | async-done | bytes 786464 | tf_op jit(solution)/shard_map/all_to_all | solution.py:1427
  220.8 4.0 out_norm.1
  229.6 18.3 %collective-permute-done.16.refs_2_ = bf16[256,1536]{1,0:T(8,128)(2,1)S(1)} collective-permute-done((bf16[256,1536]{1,0:T(8,128)(2,1)}, bf16[256,1536]{1,0:T(8,128)(2,1)S(1)}, u32[]{:S(2)}, u32[]{:S(2)}) %collective-permute-start.16) | collective-permute-done | bytes 786464 | tf_op jit(solution)/shard_map/ppermute | solution.py:1362
  254.4 8.1 %down_back.1.refs_7_ = f32[4,4,256,256]{3,2,1,0:T(8,128)S(1)} custom-call(bf16[256,1536]{1,0:T(8,128)(2,1)S(1)} %bitcast.135, bf16[256,1536]{1,0:T(8,128)(2,1)S(1)} %collective-permute-done.8.refs_1_.refs_6_, bf16[256,1536]{1,0:T(8,128)(2,1)} %collective-permute-done.9.refs_2_.refs_7_, bf16[128,1536]{1,0:T(8,128)(2,1)} %collective-permute-done.10.refs_3_.refs_8_, ...), custom_call_target="tpu_custom_call" | custom-call | flops 8000000000 | bytes 24000000 | tf_op jit(solution)/shard_map/down_back/pallas_call | solution.py:1109
  266.1 27.0 %units.1 = (bf16[4,2,4,256,256]{4,3,2,1,0:T(8,128)(2,1)}, bf16[4,4,256,256]{3,2,1,0:T(8,128)(2,1)}, f32[512,1536]{1,0:T(8,128)}, bf16[256,1536]{1,0:T(8,128)(2,1)}, bf16[256,1536]{1,0:T(8,128)(2,1)}) custom-call(bf16[256,1536]{1,0:T(8,128)(2,1)} %copy-done.17, bf16[256,1536]{1,0:T(8,128)(2,1)} %copy-done.43, bf16[256,1536]{1,0:T(8,128)(2,1)} %copy-done.42, ...), custom_call_target="tpu_custom_call" | custom-call | flops 25999998976 | bytes 78000000 | tf_op jit(solution)/shard_map/units/pallas_call | solution.py:1189
  295.6 19.7 %unit_grads.1 = (bf16[4,1536,384]{2,1,0:T(8,128)(2,1)}, bf16[4,1536,384]{2,1,0:T(8,128)(2,1)}) custom-call(s32[1]{0:T(128)} %bitcast.1.place_ref, bf16[256,1536]{1,0:T(8,128)(2,1)} %copy-done.17, bf16[256,1536]{1,0:T(8,128)(2,1)} %copy-done.43, bf16[256,1536]{1,0:T(8,128)(2,1)} %copy-done.42, bf16[128,1536]{1,0:T(8,128)(2,1)} %copy-done.50, ...), custom_call_target="tpu_custom_call" | custom-call | flops 19000000512 | bytes 57000000 | tf_op jit(solution)/shard_map/unit_grads/pallas_call | solution.py:1281
  315.4 8.1 %collective-permute-done.39 = bf16[4,1536,384]{2,1,0:T(8,128)(2,1)S(1)} collective-permute-done((bf16[4,1536,384]{2,1,0:T(8,128)(2,1)}, bf16[4,1536,384]{2,1,0:T(8,128)(2,1)S(1)}, u32[]{:S(2)}, u32[]{:S(2)}) %collective-permute-start.39) | collective-permute-done | bytes 4718624 | tf_op jit(solution)/shard_map/ppermute | solution.py:1362
  323.5 5.6 add_convert_fusion
  334.0 9.2 %collective-permute-done.22.px_ref = bf16[128,1536]{1,0:T(8,128)(2,1)} collective-permute-done((bf16[128,1536]{1,0:T(8,128)(2,1)}, bf16[128,1536]{1,0:T(8,128)(2,1)}, u32[]{:S(2)}, u32[]{:S(2)}) %collective-permute-start.22) | collective-permute-done | bytes 393248 | tf_op jit(solution)/shard_map/ppermute | solution.py:1362
  343.4 6.7 %mid_back.1 = (f32[256,1536]{1,0:T(8,128)}, bf16[256,1536]{1,0:T(8,128)(2,1)S(1)}, bf16[16,64,384]{2,1,0:T(8,128)(2,1)}, f32[1,1536]{1,0:T(1,128)S(1)}) custom-call(f32[512,1536]{1,0:T(8,128)} %get-tuple-element.93.keep_ref, bf16[256,1536]{1,0:T(8,128)(2,1)S(1)} %collective-permute-done.20.fx_ref, bf16[256,1536]{1,0:T(8,128)(2,1)S(1)} %collective-permute-done.21.fy_ref, ...), custom_call_target="tpu_custom_call" | custom-call | flops 5000000000 | bytes 15000000 | tf_op jit(solution)/shard_map/mid_back/pallas_call | solution.py:949
  351.0 4.0 all-to-all-start.5
  355.6 5.6 multiply_sine_fusion
  366.9 27.7 %all-to-all-done.5.do_ref = bf16[16,64,384]{2,1,0:T(8,128)(2,1)S(1)} async-done(((bf16[16,64,384]{2,1,0:T(8,128)(2,1)}), bf16[16,64,384]{2,1,0:T(8,128)(2,1)S(1)}, u32[]{:S(2)}, u32[]{:S(2)}) %all-to-all-start.5) | async-done | bytes 786464 | tf_op jit(solution)/shard_map/all_to_all | solution.py:1427
  395.5 31.4 %attend_back.1 = bf16[2048,384]{1,0:T(8,128)(2,1)} custom-call(s32[1]{0:T(128)} %bitcast.first_ref, bf16[2048,384]{1,0:T(8,128)(2,1)} %bitcast.125, bf16[16,64,384]{2,1,0:T(8,128)(2,1)} %copy-done.33, f32[8,512,128]{2,1,0:T(8,128)} %copy-done.26, f32[8,8,512]{2,1,0:T(8,128)} %copy-done.27, f32[2048,128]{1,0:T(8,128)} %get-tuple-element.178.cos_ref, ...), custom_call_target="tpu_custom_call" | custom-call | flops 31000000512 | bytes 93000000 | tf_op jit(solution)/shard_map/attend_back/pallas_call | solution.py:746
  426.9 4.9 all-to-all-start.6
  431.8 5.4 fusion.36
  441.5 10.9 %all-to-all-done.6 = bf16[4,512,384]{2,1,0:T(8,128)(2,1)S(1)} async-done(((bf16[4,512,384]{2,1,0:T(8,128)(2,1)}), bf16[4,512,384]{2,1,0:T(8,128)(2,1)S(1)}, u32[]{:S(2)}, u32[]{:S(2)}) %all-to-all-start.6) | async-done | bytes 1572896 | tf_op jit(solution)/shard_map/all_to_all | solution.py:1427
  453.5 6.6 %da_part.1 = (bf16[1024,1536]{1,0:T(8,128)(2,1)}, f32[1,1536]{1,0:T(1,128)S(1)}) custom-call(s32[1]{0:T(128)} %bitcast.1.place_ref, bf16[256,1536]{1,0:T(8,128)(2,1)S(1)} %bitcast.121, bf16[256,1536]{1,0:T(8,128)(2,1)S(1)} %copy-done.14, bf16[256,1536]{1,0:T(8,128)(2,1)S(1)} %copy-done.16, bf16[256,1536]{1,0:T(8,128)(2,1)} %collective-permute-done.7.refs_3_, ...), custom_call_target="tpu_custom_call" | custom-call | flops 6000000000 | bytes 18000000 | tf_op jit(solution)/shard_map/da_part/pallas_call | solution.py:991
  460.1 2.6 dynamic-slice_bitcast_fusion
  466.4 2.7 all-to-all-start.8
  476.9 5.6 qkv_grads.1
  487.0 10.6 %down.1 = (f32[512,1536]{1,0:T(8,128)S(1)}, bf16[256,1536]{1,0:T(8,128)(2,1)S(1)}, bf16[256,1536]{1,0:T(8,128)(2,1)S(1)}) custom-call(bf16[4,4,256,256]{3,2,1,0:T(8,128)(2,1)S(1)} %copy-done.25, bf16[4,1536,384]{2,1,0:T(8,128)(2,1)S(1)} %bitcast.131, bf16[4,1536,384]{2,1,0:T(8,128)(2,1)} %copy-done.49), custom_call_target="tpu_custom_call" | custom-call | flops 11000000512 | bytes 33000000 | tf_op jit(solution)/shard_map/down/pallas_call | solution.py:1235
  500.4 2.7 fusion.6
  503.0 4.4 collective-permute-start.30
  509.0 3.7 all-to-all-start.7
  512.7 10.5 %collective-permute-done.26 = bf16[256,1536]{1,0:T(8,128)(2,1)} collective-permute-done((bf16[256,1536]{1,0:T(8,128)(2,1)S(1)}, bf16[256,1536]{1,0:T(8,128)(2,1)}, u32[]{:S(2)}, u32[]{:S(2)}) %collective-permute-start.26) | collective-permute-done | bytes 786464 | tf_op jit(solution)/shard_map/ppermute | solution.py:1362
  525.1 15.2 %all-to-all-done.7 = bf16[4,192,384]{2,1,0:T(8,128)(2,1)S(1)} async-done(((bf16[4,192,384]{2,1,0:T(8,128)(2,1)}), bf16[4,192,384]{2,1,0:T(8,128)(2,1)S(1)}, u32[]{:S(2)}, u32[]{:S(2)}) %all-to-all-start.7) | async-done | bytes 589856 | tf_op jit(solution)/shard_map/all_to_all | solution.py:1427
  540.3 3.1 convert_add_fusion.7
  544.4 2.9 fusion.5
  552.4 4.4 all-to-all-start.9
  564.2 3.3 collective-permute-done.38
  567.5 6.1 %all-to-all-done.9.in_ref = bf16[8,192,384]{2,1,0:T(8,128)(2,1)} async-done(((bf16[8,192,384]{2,1,0:T(8,128)(2,1)}), bf16[8,192,384]{2,1,0:T(8,128)(2,1)}, u32[]{:S(2)}, u32[]{:S(2)}) %all-to-all-start.9) | async-done | bytes 1179680 | tf_op jit(solution)/shard_map/all_to_all | solution.py:1427
  573.6 3.0 uncut_units.1
  576.6 2.5 copy.27
  581.2 3.2 fusion.3
  (252 shorter events, 123.7 us)
Async XLA Ops:
  7.2 82.3 %all-gather.3.cloned.1.call-start = ((), (), s32[]{:S(2)}) async-start(), calls=%async_computation.12 | async-start | bytes 2654208 | tf_op jit(solution)/shard_map/all_gather | solution.py:1463
  24.2 11.8 %collective-permute-start.3 = (bf16[192,384]{1,0:T(8,128)(2,1)}, bf16[192,384]{1,0:T(8,128)(2,1)S(1)}, u32[]{:S(2)}, u32[]{:S(2)}) collective-permute-start(bf16[192,384]{1,0:T(8,128)(2,1)} %bitcast.151), channel_id=1, source_target_pairs={{0,3},{1,0},{2,1},{3,2},{4,7},{5,4},{6,5},{7,6},{8,11},{9,8},{10,9... | collective-permute-start | bytes 442376 | tf_op jit(solution)/shard_map/ppermute | solution.py:1367
  24.8 47.9 %collective-permute-start.2 = (bf16[192,384]{1,0:T(8,128)(2,1)}, bf16[192,384]{1,0:T(8,128)(2,1)S(1)}, u32[]{:S(2)}, u32[]{:S(2)}) collective-permute-start(bf16[192,384]{1,0:T(8,128)(2,1)} %bitcast.152), channel_id=1, source_target_pairs={{0,2},{1,3},{2,0},{3,1},{4,6},{5,7},{6,4},{7,5},{8,10},{9,11},{10,... | collective-permute-start | bytes 442376 | tf_op jit(solution)/shard_map/ppermute | solution.py:1367
  26.3 46.4 %collective-permute-start.1 = (bf16[192,384]{1,0:T(8,128)(2,1)}, bf16[192,384]{1,0:T(8,128)(2,1)S(1)}, u32[]{:S(2)}, u32[]{:S(2)}) collective-permute-start(bf16[192,384]{1,0:T(8,128)(2,1)} %bitcast.153), channel_id=1, source_target_pairs={{0,1},{1,2},{2,3},{3,0},{4,5},{5,6},{6,7},{7,4},{8,9},{9,10},{10,1... | collective-permute-start | bytes 442376 | tf_op jit(solution)/shard_map/ppermute | solution.py:1367
  32.2 53.3 %collective-permute-start = (bf16[256,1536]{1,0:T(8,128)(2,1)S(1)}, bf16[256,1536]{1,0:T(8,128)(2,1)S(1)}, u32[]{:S(2)}, u32[]{:S(2)}) collective-permute-start(bf16[256,1536]{1,0:T(8,128)(2,1)S(1)} %bitcast.116), channel_id=1, source_target_pairs={{0,1},{1,2},{2,3},{3,0},{4,5},{5,6},{6,7},{7,4},{8,9},{9,10},{10,1... | collective-permute-start | bytes 2359304 | tf_op jit(solution)/shard_map/ppermute | solution.py:1367
  33.7 55.8 %collective-permute-start.6 = (bf16[256,1536]{1,0:T(8,128)(2,1)S(1)}, bf16[256,1536]{1,0:T(8,128)(2,1)S(1)}, u32[]{:S(2)}, u32[]{:S(2)}) collective-permute-start(bf16[256,1536]{1,0:T(8,128)(2,1)S(1)} %bitcast.117), channel_id=1, source_target_pairs={{0,2},{1,3},{2,0},{3,1},{4,6},{5,7},{6,4},{7,5},{8,10},{9,11},{10,... | collective-permute-start | bytes 2359304 | tf_op jit(solution)/shard_map/ppermute | solution.py:1367
  36.1 53.5 %collective-permute-start.7 = (bf16[256,1536]{1,0:T(8,128)(2,1)S(1)}, bf16[256,1536]{1,0:T(8,128)(2,1)}, u32[]{:S(2)}, u32[]{:S(2)}) collective-permute-start(bf16[256,1536]{1,0:T(8,128)(2,1)S(1)} %bitcast.118), channel_id=1, source_target_pairs={{0,3},{1,0},{2,1},{3,2},{4,7},{5,4},{6,5},{7,6},{8,11},{9,8},{10,9... | collective-permute-start | bytes 2359304 | tf_op jit(solution)/shard_map/ppermute | solution.py:1367
  73.6 11.9 %collective-permute-start.4 = (bf16[4,192,384]{2,1,0:T(8,128)(2,1)}, bf16[4,192,384]{2,1,0:T(8,128)(2,1)}, u32[]{:S(2)}, u32[]{:S(2)}) collective-permute-start(bf16[4,192,384]{2,1,0:T(8,128)(2,1)} %pad_maximum_fusion), channel_id=1, source_target_pairs={{0,8},{8,0},{1,9},{9,1},{2,10},{10,2},{3,11},{11,3},{4,12},{12,4},... | collective-permute-start | bytes 1769480 | tf_op jit(solution)/shard_map/ppermute | solution.py:1362
  79.1 21.1 %all-to-all-start.4 = ((bf16[8,192,384]{2,1,0:T(8,128)(2,1)}), bf16[8,192,384]{2,1,0:T(8,128)(2,1)}, u32[]{:S(2)}, u32[]{:S(2)}) async-start(bf16[8,192,384]{2,1,0:T(8,128)(2,1)} %cut_units.1), calls=%async_computation.4 | async-start | bytes 2359296 | tf_op jit(solution)/shard_map/all_to_all | solution.py:1427
  83.4 144.4 %all-gather.5.cloned.1.call-start = ((), (), s32[]{:S(2)}) async-start(), calls=%async_computation.13 | async-start | bytes 5898240 | tf_op jit(solution)/shard_map/all_gather | solution.py:1488
  103.2 31.5 %all-to-all-start.2 = ((bf16[4,512,384]{2,1,0:T(8,128)(2,1)}), bf16[4,512,384]{2,1,0:T(8,128)(2,1)S(1)}, u32[]{:S(2)}, u32[]{:S(2)}) async-start(bf16[4,512,384]{2,1,0:T(8,128)(2,1)} %copy-done.4), calls=%async_computation.2 | async-start | bytes 3145728 | tf_op jit(solution)/shard_map/all_to_all | solution.py:1427
  109.1 24.0 %collective-permute-start.12 = (bf16[2,192,384]{2,1,0:T(8,128)(2,1)S(1)}, bf16[2,192,384]{2,1,0:T(8,128)(2,1)S(1)}, u32[]{:S(2)}, u32[]{:S(2)}) collective-permute-start(bf16[2,192,384]{2,1,0:T(8,128)(2,1)S(1)} %slice.158), channel_id=1, source_target_pairs={{0,8},{8,0},{1,9},{9,1},{2,10},{10,2},{3,11},{11,3},{4,12},{12,4},... | collective-permute-start | bytes 884744 | tf_op jit(solution)/shard_map/ppermute | solution.py:1362
  112.8 21.1 %collective-permute-start.13 = (bf16[2,192,384]{2,1,0:T(8,128)(2,1)S(1)}, bf16[2,192,384]{2,1,0:T(8,128)(2,1)S(1)}, u32[]{:S(2)}, u32[]{:S(2)}) collective-permute-start(bf16[2,192,384]{2,1,0:T(8,128)(2,1)S(1)} %slice.159), channel_id=1, source_target_pairs={{0,16},{16,0},{1,17},{17,1},{2,18},{18,2},{3,19},{19,3},{4,20},{20... | collective-permute-start | bytes 884744 | tf_op jit(solution)/shard_map/ppermute | solution.py:1362
  134.7 51.9 %collective-permute-start.14 = (bf16[16,192,384]{2,1,0:T(8,128)(2,1)}, bf16[16,192,384]{2,1,0:T(8,128)(2,1)}, u32[]{:S(2)}, u32[]{:S(2)}) collective-permute-start(bf16[16,192,384]{2,1,0:T(8,128)(2,1)} %constant_dynamic-update-slice_fusion.mine_ref), channel_id=1, source_target_pairs={{0,4},{4,0},{1,5},{5,1},{2,6},{6,2},{3,7},{7,3},{8,12},{12,8},{9,1... | collective-permute-start | bytes 7077896 | tf_op jit(solution)/shard_map/ppermute | solution.py:1362
  134.7 25.8 %collective-permute-start.8 = (bf16[256,1536]{1,0:T(8,128)(2,1)}, bf16[256,1536]{1,0:T(8,128)(2,1)S(1)}, u32[]{:S(2)}, u32[]{:S(2)}) collective-permute-start(bf16[256,1536]{1,0:T(8,128)(2,1)} %bitcast.132), channel_id=1, source_target_pairs={{0,8},{8,0},{1,9},{9,1},{2,10},{10,2},{3,11},{11,3},{4,12},{12,4},... | collective-permute-start | bytes 2359304 | tf_op jit(solution)/shard_map/ppermute | solution.py:1362
  135.1 25.4 %collective-permute-start.9 = (bf16[256,1536]{1,0:T(8,128)(2,1)}, bf16[256,1536]{1,0:T(8,128)(2,1)}, u32[]{:S(2)}, u32[]{:S(2)}) collective-permute-start(bf16[256,1536]{1,0:T(8,128)(2,1)} %bitcast.133), channel_id=1, source_target_pairs={{0,16},{16,0},{1,17},{17,1},{2,18},{18,2},{3,19},{19,3},{4,20},{20... | collective-permute-start | bytes 2359304 | tf_op jit(solution)/shard_map/ppermute | solution.py:1362
  160.5 60.3 %all-to-all-start.3 = ((bf16[16,64,384]{2,1,0:T(8,128)(2,1)}), bf16[16,64,384]{2,1,0:T(8,128)(2,1)S(1)}, u32[]{:S(2)}, u32[]{:S(2)}) async-start(bf16[16,64,384]{2,1,0:T(8,128)(2,1)} %get-tuple-element.76), calls=%async_computation.3 | async-start | bytes 1572864 | tf_op jit(solution)/shard_map/all_to_all | solution.py:1427
  181.3 371.1 %reduce-scatter.3.cloned.1.call-start = ((), (), s32[]{:S(2)}) async-start(), calls=%async_computation.14 | async-start | bytes 5898240 | tf_op jit(solution)/shard_map/reduce_scatter | solution.py:1513
  183.2 17.2 %collective-permute-start.10 = (bf16[128,1536]{1,0:T(8,128)(2,1)}, bf16[128,1536]{1,0:T(8,128)(2,1)}, u32[]{:S(2)}, u32[]{:S(2)}) collective-permute-start(bf16[128,1536]{1,0:T(8,128)(2,1)} %slice.156), channel_id=1, source_target_pairs={{0,8},{8,0},{1,9},{9,1},{2,10},{10,2},{3,11},{11,3},{4,12},{12,4},... | collective-permute-start | bytes 1179656 | tf_op jit(solution)/shard_map/ppermute | solution.py:1362
  185.9 14.5 %collective-permute-start.11 = (bf16[128,1536]{1,0:T(8,128)(2,1)}, bf16[128,1536]{1,0:T(8,128)(2,1)}, u32[]{:S(2)}, u32[]{:S(2)}) collective-permute-start(bf16[128,1536]{1,0:T(8,128)(2,1)} %slice.157), channel_id=1, source_target_pairs={{0,16},{16,0},{1,17},{17,1},{2,18},{18,2},{3,19},{19,3},{4,20},{20... | collective-permute-start | bytes 1179656 | tf_op jit(solution)/shard_map/ppermute | solution.py:1362
  227.8 22.0 %collective-permute-start.19 = (bf16[4,1536,384]{2,1,0:T(8,128)(2,1)}, bf16[4,1536,384]{2,1,0:T(8,128)(2,1)S(1)}, u32[]{:S(2)}, u32[]{:S(2)}) collective-permute-start(bf16[4,1536,384]{2,1,0:T(8,128)(2,1)} %bitcast.128), channel_id=1, source_target_pairs={{0,4},{4,0},{1,5},{5,1},{2,6},{6,2},{3,7},{7,3},{8,12},{12,8},{9,1... | collective-permute-start | bytes 14155784 | tf_op jit(solution)/shard_map/ppermute | solution.py:1362
  227.8 20.2 %collective-permute-start.16 = (bf16[256,1536]{1,0:T(8,128)(2,1)}, bf16[256,1536]{1,0:T(8,128)(2,1)S(1)}, u32[]{:S(2)}, u32[]{:S(2)}) collective-permute-start(bf16[256,1536]{1,0:T(8,128)(2,1)} %copy-done.17), channel_id=1, source_target_pairs={{0,16},{16,0},{1,17},{17,1},{2,18},{18,2},{3,19},{19,3},{4,20},{20... | collective-permute-start | bytes 2359304 | tf_op jit(solution)/shard_map/ppermute | solution.py:1362
  228.3 20.3 %collective-permute-start.15 = (bf16[256,1536]{1,0:T(8,128)(2,1)}, bf16[256,1536]{1,0:T(8,128)(2,1)S(1)}, u32[]{:S(2)}, u32[]{:S(2)}) collective-permute-start(bf16[256,1536]{1,0:T(8,128)(2,1)} %copy-done.17), channel_id=1, source_target_pairs={{0,8},{8,0},{1,9},{9,1},{2,10},{10,2},{3,11},{11,3},{4,12},{12,4},... | collective-permute-start | bytes 2359304 | tf_op jit(solution)/shard_map/ppermute | solution.py:1362
  248.0 16.6 %collective-permute-start.17 = (bf16[128,1536]{1,0:T(8,128)(2,1)S(1)}, bf16[128,1536]{1,0:T(8,128)(2,1)S(1)}, u32[]{:S(2)}, u32[]{:S(2)}) collective-permute-start(bf16[128,1536]{1,0:T(8,128)(2,1)S(1)} %slice.202), channel_id=1, source_target_pairs={{0,8},{8,0},{1,9},{9,1},{2,10},{10,2},{3,11},{11,3},{4,12},{12,4},... | collective-permute-start | bytes 1179656 | tf_op jit(solution)/shard_map/ppermute | solution.py:1362
  248.6 15.9 %collective-permute-start.18 = (bf16[128,1536]{1,0:T(8,128)(2,1)S(1)}, bf16[128,1536]{1,0:T(8,128)(2,1)S(1)}, u32[]{:S(2)}, u32[]{:S(2)}) collective-permute-start(bf16[128,1536]{1,0:T(8,128)(2,1)S(1)} %slice.203), channel_id=1, source_target_pairs={{0,16},{16,0},{1,17},{17,1},{2,18},{18,2},{3,19},{19,3},{4,20},{20... | collective-permute-start | bytes 1179656 | tf_op jit(solution)/shard_map/ppermute | solution.py:1362
  293.2 22.1 %collective-permute-start.20 = (bf16[256,1536]{1,0:T(8,128)(2,1)}, bf16[256,1536]{1,0:T(8,128)(2,1)S(1)}, u32[]{:S(2)}, u32[]{:S(2)}) collective-permute-start(bf16[256,1536]{1,0:T(8,128)(2,1)} %get-tuple-element.94), channel_id=1, source_target_pairs={{0,8},{8,0},{1,9},{9,1},{2,10},{10,2},{3,11},{11,3},{4,12},{12,4},... | collective-permute-start | bytes 2359304 | tf_op jit(solution)/shard_map/ppermute | solution.py:1362
  294.2 21.1 %collective-permute-start.21 = (bf16[256,1536]{1,0:T(8,128)(2,1)}, bf16[256,1536]{1,0:T(8,128)(2,1)S(1)}, u32[]{:S(2)}, u32[]{:S(2)}) collective-permute-start(bf16[256,1536]{1,0:T(8,128)(2,1)} %get-tuple-element.95), channel_id=1, source_target_pairs={{0,16},{16,0},{1,17},{17,1},{2,18},{18,2},{3,19},{19,3},{4,20},{20... | collective-permute-start | bytes 2359304 | tf_op jit(solution)/shard_map/ppermute | solution.py:1362
  331.7 11.5 %collective-permute-start.22 = (bf16[128,1536]{1,0:T(8,128)(2,1)}, bf16[128,1536]{1,0:T(8,128)(2,1)}, u32[]{:S(2)}, u32[]{:S(2)}) collective-permute-start(bf16[128,1536]{1,0:T(8,128)(2,1)} %get-tuple-element.166), channel_id=1, source_target_pairs={{0,8},{8,0},{1,9},{9,1},{2,10},{10,2},{3,11},{11,3},{4,12},{12,4},... | collective-permute-start | bytes 1179656 | tf_op jit(solution)/shard_map/ppermute | solution.py:1362
  332.2 11.2 %collective-permute-start.23 = (bf16[128,1536]{1,0:T(8,128)(2,1)}, bf16[128,1536]{1,0:T(8,128)(2,1)}, u32[]{:S(2)}, u32[]{:S(2)}) collective-permute-start(bf16[128,1536]{1,0:T(8,128)(2,1)} %get-tuple-element.165), channel_id=1, source_target_pairs={{0,16},{16,0},{1,17},{17,1},{2,18},{18,2},{3,19},{19,3},{4,20},{20... | collective-permute-start | bytes 1179656 | tf_op jit(solution)/shard_map/ppermute | solution.py:1362
  351.0 43.6 %all-to-all-start.5 = ((bf16[16,64,384]{2,1,0:T(8,128)(2,1)}), bf16[16,64,384]{2,1,0:T(8,128)(2,1)S(1)}, u32[]{:S(2)}, u32[]{:S(2)}) async-start(bf16[16,64,384]{2,1,0:T(8,128)(2,1)} %get-tuple-element.101), calls=%async_computation.5 | async-start | bytes 1572864 | tf_op jit(solution)/shard_map/all_to_all | solution.py:1427
  366.4 65.4 %collective-permute-start.32 = (bf16[8,96,1536]{2,1,0:T(8,128)(2,1)}, bf16[8,96,1536]{2,1,0:T(8,128)(2,1)}, u32[]{:S(2)}, u32[]{:S(2)}) collective-permute-start(bf16[8,96,1536]{2,1,0:T(8,128)(2,1)} %slice_bitcast_fusion), channel_id=1, source_target_pairs={{0,4},{4,0},{1,5},{5,1},{2,6},{6,2},{3,7},{7,3},{8,12},{12,8},{9,1... | collective-permute-start | bytes 7077896 | tf_op jit(solution)/shard_map/ppermute | solution.py:1362
  426.9 25.5 %all-to-all-start.6 = ((bf16[4,512,384]{2,1,0:T(8,128)(2,1)}), bf16[4,512,384]{2,1,0:T(8,128)(2,1)S(1)}, u32[]{:S(2)}, u32[]{:S(2)}) async-start(bf16[4,512,384]{2,1,0:T(8,128)(2,1)} %bitcast.144), calls=%async_computation.6 | async-start | bytes 3145728 | tf_op jit(solution)/shard_map/all_to_all | solution.py:1427
  438.3 31.2 %collective-permute-start.33 = (bf16[192,1536]{1,0:T(8,128)(2,1)}, bf16[192,1536]{1,0:T(8,128)(2,1)}, u32[]{:S(2)}, u32[]{:S(2)}) collective-permute-start(bf16[192,1536]{1,0:T(8,128)(2,1)} %bitcast.36), channel_id=1, source_target_pairs={{0,8},{8,0},{1,9},{9,1},{2,10},{10,2},{3,11},{11,3},{4,12},{12,4},... | collective-permute-start | bytes 1769480 | tf_op jit(solution)/shard_map/ppermute | solution.py:1362
  440.3 29.2 %collective-permute-start.35 = (bf16[192,1536]{1,0:T(8,128)(2,1)}, bf16[192,1536]{1,0:T(8,128)(2,1)}, u32[]{:S(2)}, u32[]{:S(2)}) collective-permute-start(bf16[192,1536]{1,0:T(8,128)(2,1)} %bitcast.39), channel_id=1, source_target_pairs={{0,16},{16,0},{1,17},{17,1},{2,18},{18,2},{3,19},{19,3},{4,20},{20... | collective-permute-start | bytes 1769480 | tf_op jit(solution)/shard_map/ppermute | solution.py:1362
  462.8 21.8 %collective-permute-start.24 = (bf16[256,1536]{1,0:T(8,128)(2,1)}, bf16[256,1536]{1,0:T(8,128)(2,1)S(1)}, u32[]{:S(2)}, u32[]{:S(2)}) collective-permute-start(bf16[256,1536]{1,0:T(8,128)(2,1)} %get-tuple-element.164), channel_id=1, source_target_pairs={{0,1},{4,5},{8,9},{12,13},{16,17},{20,21},{24,25},{28,29}} | collective-permute-start | bytes 2359304 | tf_op jit(solution)/shard_map/ppermute | solution.py:1419
  464.1 20.4 %collective-permute-start.25 = (bf16[256,1536]{1,0:T(8,128)(2,1)}, bf16[256,1536]{1,0:T(8,128)(2,1)}, u32[]{:S(2)}, u32[]{:S(2)}) collective-permute-start(bf16[256,1536]{1,0:T(8,128)(2,1)} %get-tuple-element.163), channel_id=1, source_target_pairs={{3,2},{7,6},{11,10},{15,14},{19,18},{23,22},{27,26},{31,30}} | collective-permute-start | bytes 2359304 | tf_op jit(solution)/shard_map/ppermute | solution.py:1420
  466.4 42.6 %all-to-all-start.8 = ((f32[32,1,128]{2,1,0:T(1,128)}), f32[32,1,128]{2,1,0:T(1,128)S(1)}, u32[]{:S(2)}, u32[]{:S(2)}) async-start(f32[32,1,128]{2,1,0:T(1,128)} %bitcast.45), calls=%async_computation.8 | async-start | bytes 32768 | tf_op jit(solution)/shard_map/all_to_all | solution.py:1427
  469.1 90.5 %reduce-scatter.5.cloned.1.call-start = ((), (), s32[]{:S(2)}) async-start(), calls=%async_computation.15 | async-start | bytes 2654208 | tf_op jit(solution)/shard_map/reduce_scatter | solution.py:1540
  497.6 25.6 %collective-permute-start.26 = (bf16[256,1536]{1,0:T(8,128)(2,1)S(1)}, bf16[256,1536]{1,0:T(8,128)(2,1)}, u32[]{:S(2)}, u32[]{:S(2)}) collective-permute-start(bf16[256,1536]{1,0:T(8,128)(2,1)S(1)} %get-tuple-element.107), channel_id=1, source_target_pairs={{0,8},{8,0},{1,9},{9,1},{2,10},{10,2},{3,11},{11,3},{4,12},{12,4},... | collective-permute-start | bytes 2359304 | tf_op jit(solution)/shard_map/ppermute | solution.py:1362
  499.9 40.4 %collective-permute-start.28 = (bf16[256,1536]{1,0:T(8,128)(2,1)S(1)}, bf16[256,1536]{1,0:T(8,128)(2,1)}, u32[]{:S(2)}, u32[]{:S(2)}) collective-permute-start(bf16[256,1536]{1,0:T(8,128)(2,1)S(1)} %get-tuple-element.108), channel_id=1, source_target_pairs={{0,16},{16,0},{1,17},{17,1},{2,18},{18,2},{3,19},{19,3},{4,20},{20... | collective-permute-start | bytes 2359304 | tf_op jit(solution)/shard_map/ppermute | solution.py:1362
  503.0 37.3 %collective-permute-start.30 = (bf16[256,1536]{1,0:T(8,128)(2,1)}, bf16[256,1536]{1,0:T(8,128)(2,1)}, u32[]{:S(2)}, u32[]{:S(2)}) collective-permute-start(bf16[256,1536]{1,0:T(8,128)(2,1)} %get-tuple-element.160), channel_id=1, source_target_pairs={{0,1},{1,2},{4,5},{5,6},{8,9},{9,10},{12,13},{13,14},{16,17},{17,1... | collective-permute-start | bytes 2359304 | tf_op jit(solution)/shard_map/ppermute | solution.py:1419
  507.5 32.9 %collective-permute-start.31 = (bf16[256,1536]{1,0:T(8,128)(2,1)}, bf16[256,1536]{1,0:T(8,128)(2,1)}, u32[]{:S(2)}, u32[]{:S(2)}) collective-permute-start(bf16[256,1536]{1,0:T(8,128)(2,1)} %get-tuple-element.159), channel_id=1, source_target_pairs={{3,2},{2,1},{7,6},{6,5},{11,10},{10,9},{15,14},{14,13},{19,18},{18... | collective-permute-start | bytes 2359304 | tf_op jit(solution)/shard_map/ppermute | solution.py:1420
  509.0 31.3 %all-to-all-start.7 = ((bf16[4,192,384]{2,1,0:T(8,128)(2,1)}), bf16[4,192,384]{2,1,0:T(8,128)(2,1)S(1)}, u32[]{:S(2)}, u32[]{:S(2)}) async-start(bf16[4,192,384]{2,1,0:T(8,128)(2,1)} %pad_maximum_fusion.1), calls=%async_computation.7 | async-start | bytes 1179648 | tf_op jit(solution)/shard_map/all_to_all | solution.py:1427
  524.6 15.8 %collective-permute-start.27 = (bf16[128,1536]{1,0:T(8,128)(2,1)S(1)}, bf16[128,1536]{1,0:T(8,128)(2,1)S(1)}, u32[]{:S(2)}, u32[]{:S(2)}) collective-permute-start(bf16[128,1536]{1,0:T(8,128)(2,1)S(1)} %add_convert_fusion.2), channel_id=1, source_target_pairs={{0,16},{16,0},{1,17},{17,1},{2,18},{18,2},{3,19},{19,3},{4,20},{20... | collective-permute-start | bytes 1179656 | tf_op jit(solution)/shard_map/ppermute | solution.py:1362
  543.4 13.4 %collective-permute-start.29 = (bf16[128,1536]{1,0:T(8,128)(2,1)}, bf16[128,1536]{1,0:T(8,128)(2,1)S(1)}, u32[]{:S(2)}, u32[]{:S(2)}) collective-permute-start(bf16[128,1536]{1,0:T(8,128)(2,1)} %get-tuple-element.162), channel_id=1, source_target_pairs={{0,8},{8,0},{1,9},{9,1},{2,10},{10,2},{3,11},{11,3},{4,12},{12,4},... | collective-permute-start | bytes 1179656 | tf_op jit(solution)/shard_map/ppermute | solution.py:1362
  547.3 17.0 %collective-permute-start.37 = (bf16[256,1536]{1,0:T(8,128)(2,1)}, bf16[256,1536]{1,0:T(8,128)(2,1)S(1)}, u32[]{:S(2)}, u32[]{:S(2)}) collective-permute-start(bf16[256,1536]{1,0:T(8,128)(2,1)} %get-tuple-element.158), channel_id=1, source_target_pairs={{0,1},{1,2},{2,3},{4,5},{5,6},{6,7},{8,9},{9,10},{10,11},{12,13},{... | collective-permute-start | bytes 2359304 | tf_op jit(solution)/shard_map/ppermute | solution.py:1419
  548.6 18.9 %collective-permute-start.38 = (bf16[256,1536]{1,0:T(8,128)(2,1)}, bf16[256,1536]{1,0:T(8,128)(2,1)}, u32[]{:S(2)}, u32[]{:S(2)}) collective-permute-start(bf16[256,1536]{1,0:T(8,128)(2,1)} %get-tuple-element.157), channel_id=1, source_target_pairs={{3,2},{2,1},{1,0},{7,6},{6,5},{5,4},{11,10},{10,9},{9,8},{15,14},{... | collective-permute-start | bytes 2359304 | tf_op jit(solution)/shard_map/ppermute | solution.py:1420
  552.4 21.2 %all-to-all-start.9 = ((bf16[8,192,384]{2,1,0:T(8,128)(2,1)}), bf16[8,192,384]{2,1,0:T(8,128)(2,1)}, u32[]{:S(2)}, u32[]{:S(2)}) async-start(bf16[8,192,384]{2,1,0:T(8,128)(2,1)} %bitcast.147), calls=%async_computation.10 | async-start | bytes 2359296 | tf_op jit(solution)/shard_map/all_to_all | solution.py:1427
  (57 other events, 686.6 us)
Sparse Core Ops, SparseCore 0:
  11.9 31.7 all-gather.2
  100.3 121.0 all-gather.4
  329.3 95.2 reduce-scatter.2
  482.6 50.5 reduce-scatter.4

commit v4 on v3

--- a/solution.py
+++ b/solution.py
@@ -795,13 +795,12 @@
     return pl.BlockSpec(array.shape, lambda *_: (0,) * rank)
 
 
-def qkv_kernel(parts, rows, place_ref, *refs):
-    blocks = refs[:parts]
-    gain_ref, w_ref, cos_ref, sin_ref, a_ref, out_ref = refs[parts:]
-    tokens = blocks[0].shape[0] // rows
-    for k in range(parts):
-        z = lax.rem(place_ref[0] + (parts - k), parts)
-        stream = blocks[k][...].astype(jnp.float32)
+def qkv_kernel(parts, rows, h_ref, gain_ref, w_ref, cos_ref, sin_ref, a_ref, out_ref):
+    count = h_ref.shape[0] // parts
+    tokens = count // rows
+
+    def body(z, carry):
+        stream = h_ref[pl.ds(pl.multiple_of(z * count, count), count), :].astype(jnp.float32)
         factor = lax.rsqrt(jnp.mean(stream * stream, axis=-1, keepdims=True) + EPS)
         normed = (stream * factor * gain_ref[...]).astype(jnp.bfloat16)
         at = pl.ds(pl.multiple_of(z * tokens, tokens), tokens)
@@ -813,18 +812,20 @@
             for h in range(product.shape[1] // (3 * LN)):
                 piece = product[r * tokens : (r + 1) * tokens, h * 3 * LN : (h + 1) * 3 * LN]
                 out_ref[h * rows + r, at, :] = turn(piece, cosine, sine, lower).astype(jnp.bfloat16)
-
-
-def qkv_call(place, blocks, gain, weight, cos, sin, rows):
-    parts = len(blocks)
-    count, width = blocks[0].shape
-    tokens = count // rows * parts
+        return carry
+
+    lax.fori_loop(0, parts, body, 0)
+
+
+def qkv_call(parts, group, gain, weight, cos, sin, rows):
+    count, width = group.shape
+    tokens = count // rows
     groups = weight.shape[1] // (3 * LN)
-    operands = (*blocks, gain, weight, cos, sin)
+    operands = (group, gain, weight, cos, sin)
     return pl.pallas_call(
         partial(qkv_kernel, parts, rows),
         grid=(1,),
-        in_specs=[pl.BlockSpec(memory_space=pltpu.SMEM)] + [full_spec(v) for v in operands],
+        in_specs=[full_spec(v) for v in operands],
         out_specs=[
             pl.BlockSpec((rows, tokens, width), lambda i: (0, 0, 0)),
             pl.BlockSpec((groups * rows, tokens, 3 * LN), lambda i: (0, 0, 0)),
@@ -836,7 +837,7 @@
         compiler_params=pltpu.CompilerParams(vmem_limit_bytes=48 << 20),
         name="norm_qkv",
         cost_estimate=cost(7),
-    )(place, *operands)
+    )(*operands)
 
 
 def thirds(values):
@@ -958,46 +959,51 @@
     )(*operands)
 
 
-def da_kernel(parts, rows, place_ref, *refs):
-    blocks = refs[:parts]
-    d_ref, w_ref, da_ref, gg_ref = refs[parts:]
-    tokens = blocks[0].shape[0] // rows
+def da_kernel(parts, rows, h_ref, d_ref, w_ref, wo_ref, da_ref, gg_ref):
+    count = h_ref.shape[0] // parts
+    tokens = count // rows
     groups = d_ref.shape[0]
-    total = jnp.zeros(gg_ref.shape, jnp.float32)
-    for k in range(parts):
-        z = lax.rem(place_ref[0] + (parts - k), parts)
+    run = wo_ref.shape[0] // parts
+    gg_ref[...] = jnp.zeros_like(gg_ref)
+
+    def body(z, carry):
         at = pl.ds(pl.multiple_of(z * tokens, tokens), tokens)
         left = jnp.concatenate(
             [jnp.concatenate([d_ref[g, r, at, :] for r in range(rows)], axis=0) for g in range(groups)],
             axis=1,
         )
         back = dotf(left, w_ref[...], ((1,), (1,)))
-        stream = blocks[k][...].astype(jnp.float32)
+        stream = h_ref[pl.ds(pl.multiple_of(z * count, count), count), :].astype(jnp.float32)
         factor = lax.rsqrt(jnp.mean(stream * stream, axis=-1, keepdims=True) + EPS)
-        total = total + jnp.sum(back * stream * factor, axis=0, keepdims=True)
-        count = rows * tokens
-        da_ref[pl.ds(pl.multiple_of(z * count, count), count), :] = back.astype(jnp.bfloat16)
-    gg_ref[...] = total
-
-
-def da_call(place, blocks, grads, weight, rows):
-    parts = len(blocks)
-    count, width = blocks[0].shape
-    operands = (*blocks, grads, weight)
+        gg_ref[...] += jnp.sum(back * stream * factor, axis=0, keepdims=True)
+        da_ref[z, :count, :] = back.astype(jnp.bfloat16)
+        cols = pl.ds(pl.multiple_of(z * 3 * LN, 3 * LN), 3 * LN)
+        for n in range(parts):
+            da_ref[z, count:, n * 3 * LN : (n + 1) * 3 * LN] = wo_ref[n * run : (n + 1) * run, cols]
+        return carry
+
+    lax.fori_loop(0, parts, body, 0)
+
+
+def da_call(parts, group, grads, weight, grad_wo, rows):
+    count, width = group.shape
+    operands = (group, grads, weight, grad_wo)
+    block = (count + grad_wo.shape[0]) // parts
     shapes = [
-        jax.ShapeDtypeStruct((parts * count, width), jnp.bfloat16),
+        jax.ShapeDtypeStruct((parts, block, width), jnp.bfloat16),
         jax.ShapeDtypeStruct((1, width), jnp.float32),
     ]
-    return pl.pallas_call(
+    part, gain_grad = pl.pallas_call(
         partial(da_kernel, parts, rows),
         grid=(1,),
-        in_specs=[pl.BlockSpec(memory_space=pltpu.SMEM)] + [full_spec(v) for v in operands],
+        in_specs=[full_spec(v) for v in operands],
         out_specs=[full_spec(v) for v in shapes],
         out_shape=shapes,
         compiler_params=pltpu.CompilerParams(vmem_limit_bytes=48 << 20),
         name="da_part",
         cost_estimate=cost(6),
-    )(place, *operands)
+    )(*operands)
+    return part.reshape(parts * block, width), gain_grad
 
 
 def cut_kernel(gate_ref, up_ref, down_ref, out_ref):
@@ -1113,7 +1119,7 @@
         out_specs=pl.BlockSpec((1, 4, count, 2 * LN), lambda z: (z, 0, 0, 0)),
         out_shape=shape,
         scratch_shapes=[pltpu.VMEM((4, count, width), jnp.bfloat16)],
-        compiler_params=pltpu.CompilerParams(vmem_limit_bytes=40 << 20),
+        compiler_params=pltpu.CompilerParams(vmem_limit_bytes=60 << 20),
         name="down_back",
         cost_estimate=cost(8),
     )(*pieces, mine, other)
@@ -1198,7 +1204,7 @@
         + [full_spec(v) for v in shapes[2:]],
         out_shape=shapes,
         scratch_shapes=[pltpu.VMEM((4, count, width), low), pltpu.VMEM((4, count, width), jnp.float32)],
-        compiler_params=pltpu.CompilerParams(vmem_limit_bytes=56 << 20),
+        compiler_params=pltpu.CompilerParams(vmem_limit_bytes=60 << 20),
         name="units",
         cost_estimate=cost(26),
     )(*pieces, mine, other, grad_hidden)
@@ -1239,13 +1245,13 @@
         out_specs=[full_spec(v) for v in shapes],
         out_shape=shapes,
         scratch_shapes=[pltpu.VMEM((4, count, width), jnp.float32)],
-        compiler_params=pltpu.CompilerParams(vmem_limit_bytes=40 << 20),
+        compiler_params=pltpu.CompilerParams(vmem_limit_bytes=60 << 20),
         name="down",
         cost_estimate=cost(11),
     )(hidden, mine, other)
 
 
-def unit_grads_kernel(place_ref, *refs):
+def unit_grads_kernel(*refs):
     b_pieces, g_pieces = refs[:5], refs[5:10]
     dgu_ref, hid_ref, mine_ref, other_ref, fill_s, b_s, g_s = refs[10:]
     count = fill_s.shape[1]
@@ -1273,85 +1279,75 @@
     lax.fori_loop(0, 4, body, 0)
 
 
-def unit_grads_call(place, b_pieces, g_pieces, grads, hidden):
+def unit_grads_call(b_pieces, g_pieces, grads, hidden):
     count, width = b_pieces[0].shape
     parts = hidden.shape[0]
     low = jnp.bfloat16
     operands = (*b_pieces, *g_pieces)
     return pl.pallas_call(
         unit_grads_kernel,
-        grid_spec=pltpu.PrefetchScalarGridSpec(
-            num_scalar_prefetch=1,
-            grid=(parts,),
-            in_specs=[full_spec(v) for v in operands]
-            + [
-                pl.BlockSpec((1,) + grads.shape[1:], lambda k, at: (k, 0, 0, 0, 0)),
-                pl.BlockSpec((1,) + hidden.shape[1:], lambda k, at: (k, 0, 0, 0)),
-            ],
-            out_specs=[pl.BlockSpec((1, width, 3 * LN), lambda k, at: (k, 0, 0))] * 2,
-            scratch_shapes=[pltpu.VMEM((4, count, width), low)]
-            + [pltpu.VMEM((width, 4 * count), low)] * 2,
-        ),
+        grid=(parts,),
+        in_specs=[full_spec(v) for v in operands]
+        + [
+            pl.BlockSpec((1,) + grads.shape[1:], lambda z: (z, 0, 0, 0, 0)),
+            pl.BlockSpec((1,) + hidden.shape[1:], lambda z: (z, 0, 0, 0)),
+        ],
+        out_specs=[pl.BlockSpec((1, width, 3 * LN), lambda z: (z, 0, 0))] * 2,
         out_shape=[jax.ShapeDtypeStruct((parts, width, 3 * LN), low)] * 2,
-        compiler_params=pltpu.CompilerParams(vmem_limit_bytes=56 << 20),
+        scratch_shapes=[pltpu.VMEM((4, count, width), low)] + [pltpu.VMEM((width, 4 * count), low)] * 2,
+        compiler_params=pltpu.CompilerParams(vmem_limit_bytes=60 << 20),
         name="unit_grads",
         cost_estimate=cost(19),
-    )(place, *operands, grads, hidden)
-
-
-def qkv_grads_kernel(a_ref, d_ref, out_ref):
-    left = jnp.transpose(a_ref[...])
-    for g in range(d_ref.shape[0]):
-        cols = slice(g * 3 * LN, (g + 1) * 3 * LN)
-        out_ref[:, cols] = dotf(left, d_ref[g], ((1,), (0,))).astype(out_ref.dtype)
-
-
-def qkv_grads_call(normed, grads):
-    count, width = normed.shape
-    shape = jax.ShapeDtypeStruct((width, grads.shape[0] * 3 * LN), jnp.bfloat16)
+    )(*operands, grads, hidden)
+
+
+ORDER = ((0, 0, 0), (0, 0, 1), (0, 1, 0), (1, 1, 0), (1, 0, 1), (1, 1, 1), (0, 1, 1), (1, 0, 0))
+
+
+def row_grads_kernel(at_ref, left_ref, right_ref, mine_ref, other_ref, full_s):
     tile = 2 * LN
+    width = right_ref.shape[2]
+
+    def body(n, carry):
+        rows = pl.ds(pl.multiple_of(n * tile, tile), tile)
+        left = jnp.transpose(left_ref[:, rows])
+        for g in range(right_ref.shape[0]):
+            piece = dotf(left, right_ref[g], ((1,), (0,)))
+            full_s[rows, g * width : (g + 1) * width] = piece.astype(jnp.bfloat16)
+        return carry
+
+    lax.fori_loop(0, full_s.shape[0] // tile, body, 0)
+    half = mine_ref.shape[1]
+    for c, out_ref in enumerate((mine_ref, other_ref)):
+        for n, (y, x, last) in enumerate(ORDER):
+            block = ((at_ref[0] ^ y) * 2 + (at_ref[1] ^ x)) * 2 + (at_ref[2] ^ c)
+            rows = pl.multiple_of(block * 2 * half + last * half, 32)
+            out_ref[n] = full_s[pl.ds(rows, half), :]
+
+
+def row_grads_call(at, left, right, name, time):
+    width = left.shape[1]
+    cols = right.shape[0] * right.shape[2]
+    shape = jax.ShapeDtypeStruct((8, width // 16, cols), jnp.bfloat16)
     return pl.pallas_call(
-        qkv_grads_kernel,
-        grid=(width // tile,),
-        in_specs=[pl.BlockSpec((count, tile), lambda i: (0, i)), full_spec(grads)],
-        out_specs=pl.BlockSpec((tile, shape.shape[1]), lambda i: (i, 0)),
-        out_shape=shape,
+        row_grads_kernel,
+        grid=(1,),
+        in_specs=[pl.BlockSpec(memory_space=pltpu.SMEM), full_spec(left), full_spec(right)],
+        out_specs=[full_spec(shape)] * 2,
+        out_shape=[shape] * 2,
+        scratch_shapes=[pltpu.VMEM((width, cols), jnp.bfloat16)],
         compiler_params=pltpu.CompilerParams(vmem_limit_bytes=32 << 20),
-        name="qkv_grads",
-        cost_estimate=cost(5),
-    )(normed, grads)
-
-
-def out_grads_kernel(at_ref, go_ref, o_ref, out_ref, full_s):
-    tile = 2 * LN
-    right = o_ref[...]
-    for n in range(full_s.shape[0] // tile):
-        left = jnp.transpose(go_ref[:, n * tile : (n + 1) * tile])
-        full_s[n * tile : (n + 1) * tile, :] = dotf(left, right, ((1,), (0,))).astype(jnp.bfloat16)
-    half = out_ref.shape[2]
-    size = 2 * half
-    order = ((0, 0, 0), (0, 0, 1), (0, 1, 0), (1, 1, 0), (1, 0, 1), (1, 1, 1), (0, 1, 1), (1, 0, 0))
-    for c in range(2):
-        for n, (y, x, last) in enumerate(order):
-            block = ((at_ref[0] ^ y) * 2 + (at_ref[1] ^ x)) * 2 + (at_ref[2] ^ c)
-            rows = pl.multiple_of(block * size + last * half, 32)
-            out_ref[c, n] = full_s[pl.ds(rows, half), :]
-
-
-def out_grads_call(at, grad, attended):
-    width, inner = grad.shape[1], attended.shape[1]
-    shape = jax.ShapeDtypeStruct((2, 8, width // 16, inner), jnp.bfloat16)
-    return pl.pallas_call(
-        out_grads_kernel,
-        grid=(1,),
-        in_specs=[pl.BlockSpec(memory_space=pltpu.SMEM), full_spec(grad), full_spec(attended)],
-        out_specs=full_spec(shape),
-        out_shape=shape,
-        scratch_shapes=[pltpu.VMEM((width, inner), jnp.bfloat16)],
-        compiler_params=pltpu.CompilerParams(vmem_limit_bytes=32 << 20),
-        name="out_grads",
-        cost_estimate=cost(3),
-    )(at, grad, attended)
+        cost_estimate=cost(time),
+        name=name,
+    )(at, left, right)
+
+
+def core_sum(mine, other):
+    step = mine.shape[1]
+    both = (mine.astype(jnp.float32) + other.astype(jnp.float32)).reshape(8 * step, -1)
+    keep = jnp.concatenate([both[: 2 * step], both[6 * step :]], axis=0)
+    low = both[2 * step : 6 * step].astype(jnp.bfloat16)
+    return keep, low[: 2 * step], low[2 * step :]
 
 
 EVERY = ("y", "x", "c", "z")
@@ -1406,23 +1402,6 @@
     )
 
 
-def reduce_line(part, at, size, between=None):
-    block = lambda k: lax.dynamic_index_in_dim(part, jnp.clip(at + k, 0, size - 1), 0, keepdims=False)
-    wide = lambda v: v.astype(jnp.float32)
-    up, down = None, None
-    for step in range(1, size):
-        k = size - step
-        send_up, send_down = block(k), block(-k)
-        if up is not None:
-            send_up = (wide(send_up) + wide(up)).astype(part.dtype)
-            send_down = (wide(send_down) + wide(down)).astype(part.dtype)
-        up = lax.ppermute(send_up, "z", [(i, i + 1) for i in range(step)])
-        down = lax.ppermute(send_down, "z", [(size - 1 - i, size - 2 - i) for i in range(step)])
-        if between is not None:
-            up, down = between(step, up, down)
-    return wide(block(0)) + wide(up) + wide(down)
-
-
 def all_to_all(value, axes):
     return lax.all_to_all(value, axes, 0, 0, tiled=True)
 
@@ -1441,30 +1420,21 @@
     chunk = segments.shape[1]
     length = chunk * sizes["x"] * sizes["c"]
     x_at, c_at, z_at = lax.axis_index("x"), lax.axis_index("c"), lax.axis_index("z")
-    place = z_at.reshape(1).astype(jnp.int32)
     at = jnp.stack([lax.axis_index("y"), x_at, c_at, z_at]).astype(jnp.int32)
 
+    own = tokens.reshape(count, width)
+    group = lax.all_gather(own, "z", axis=0, tiled=True)
     gains = jnp.concatenate([norm_in, norm_mid], axis=1)
     share = norm_in.shape[1]
     gains = jnp.pad(gains, ((0, 0), (0, LN - 2 * share)))
-    gains = all_to_all(jnp.broadcast_to(gains, (nz, LN)), "z")
-
-    own, gains, w_o = tie(tokens.reshape(count, width), gains, w_out[0].T)
-    blocks = gather_blocks(own, nz)
-    w_o = jnp.stack(gather_blocks(w_o, nz))
-
-    gains = all_to_all(jnp.broadcast_to(gains, (plane, nz, LN)).reshape(plane * nz, LN), ("y", "x", "c"))
-    gain_in = gains[:, :share].reshape(1, width)
-    gain_mid = gains[:, share : 2 * share].reshape(1, width)
+    gains = all_to_all(jnp.broadcast_to(gains, (devices, LN)), EVERY)
 
     kv_local = w_key.shape[2] // HD
     per_head = lambda w: w[0].reshape(w.shape[1], kv_local, -1)
     w_qkv = jnp.concatenate([per_head(w_query), per_head(w_key), per_head(w_value)], axis=2)
-    w_qkv = lax.all_gather(w_qkv.reshape(w_qkv.shape[0], -1), ("y", "x", "c"), axis=0, tiled=True)
-
-    gate, up, down, _ = tie(w_gate[0], w_up[0], w_down[0], gains)
-    w_ff = all_to_all(cut_call(gate, up, down), ("y", "x", "c"))
-    w_ff = w_ff.reshape(width, 3 * LN)
+    w_qkv, w_o = tie(jnp.transpose(w_qkv, (1, 0, 2)), jnp.stack(gather_blocks(w_out[0].T, nz)))
+    w_qkv = jnp.concatenate(gather_square(w_qkv), axis=0)
+    w_qkv = place_call(at, w_qkv, swap(w_qkv, "c"), False)
 
     last = (x_at * sizes["c"] + c_at + 1) * chunk - 1
     begin = last - positions[:, -1] - jnp.where(segments[:, -1] == 2, 3 * length // 4, 0)
@@ -1478,14 +1448,22 @@
     row_cos, row_sin = jnp.cos(row_angle), jnp.sin(row_angle)
 
     sides = gather_sides(w_o)
-    blocks[1], *sides = tie(blocks[1], *sides)
-    w_o = jnp.concatenate([w_o, *sides, *gather_corner(*sides)], axis=0)
-    w_o = (w_o, swap(w_o, "c"))
-    normed, qkv = qkv_call(place, blocks, gain_in, w_qkv, token_cos, token_sin, rows)
+    gate, up, down, gains, *tables = tie(
+        w_gate[0], w_up[0], w_down[0], gains, token_cos, token_sin, row_cos, row_sin, *sides
+    )
+    token_cos, token_sin, row_cos, row_sin, *sides = tables
+    gain_in = gains[:, :share].reshape(1, width)
+    gain_mid = gains[:, share : 2 * share].reshape(1, width)
+    w_ff = all_to_all(cut_call(gate, up, down), ("y", "x", "c"))
+    w_ff = w_ff.reshape(width, 3 * LN)
+    corner = gather_corner(*sides)
+    group, w_qkv, w_ff, *corner = tie(group, w_qkv, w_ff, *corner)
+    w_o = jnp.concatenate([w_o, *sides, *corner], axis=0)
+    w_mine = lax.all_gather(w_ff, "z", axis=0, tiled=True)
+
+    normed, qkv = qkv_call(nz, group, gain_in, w_qkv, token_cos, token_sin, rows)
     qkv = all_to_all(qkv, ("x", "c")).reshape(length, 3 * LN)
 
-    w_ff, _ = tie(w_ff, normed)
-    w_mine = lax.all_gather(w_ff, "z", axis=0, tiled=True)
     cot_low = cotangent.reshape(count, width)
     cot_first, _ = tie(cot_low, qkv)
     cot_sides = gather_sides(cot_first)
@@ -1493,82 +1471,73 @@
     attended, attended_float, log_total = attn_fwd(first, qkv)
     attended, *cot_sides = tie(attended, *cot_sides)
     attended = all_to_all(attended, ("x", "c", "z"))
-    w_o = place_call(at, *w_o, True)
+    w_o = place_call(at, w_o, swap(w_o, "c"), True)
+    w_o, *cot_sides = tie(w_o, *cot_sides)
     attended, *corner = tie(attended, *gather_corner(*cot_sides))
     cot_pieces = (cot_low, *cot_sides, *corner)
     middle, normed_b, attended_low = out_call(attended, w_o, own, gain_mid, rows)
     w_mine, _ = tie(w_mine, normed_b)
     w_mine = w_mine.reshape(nz, width, 3 * LN)
     w_other = swap(w_mine, "c")
-    b_pieces = gather_square(normed_b)
-
+    b_sides = gather_sides(normed_b)
     grad_hidden = down_back_call(cot_pieces, w_mine, w_other)
+    *b_sides, grad_hidden = tie(*b_sides, grad_hidden)
+    b_pieces = (normed_b, *b_sides, *gather_corner(*b_sides))
     grad_gu, hidden, *sends = units_call(b_pieces, w_mine, w_other, grad_hidden)
     from_x, from_y = swap(sends[1], "x"), swap(sends[2], "y")
-    ff_mine, ff_other = unit_grads_call(place, b_pieces, cot_pieces, grad_gu, hidden)
-    from_x, from_y, ff_mine, ff_other = tie(from_x, from_y, ff_mine, ff_other)
+    ff_mine, ff_other = unit_grads_call(b_pieces, cot_pieces, grad_gu, hidden)
+    from_x, from_y, ff_other = tie(from_x, from_y, ff_other)
     grad_b = reduce_square_rest(sends[0], from_x, from_y)
     grad_ff = ff_mine.astype(jnp.float32) + swap(ff_other, "c").astype(jnp.float32)
     grad_ff = grad_ff.astype(jnp.bfloat16).reshape(nz * width, 3 * LN)
+    grad_ff, *corner = tie(grad_ff, *grad_b[3:])
+    grad_b = (*grad_b[:3], *corner)
     grad_ff = lax.psum_scatter(grad_ff, "z", scatter_dimension=0, tiled=True)
     grad_mid, grad_low, grad_o, gain_grad_mid = mid_back_call(
         grad_b, middle, cot_low, gain_mid, w_o, rows, nz
     )
     grad_o = all_to_all(grad_o, ("x", "c", "z"))
-
-    grad_wo = out_grads_call(at, grad_low, attended_low)
-    grad_wo = grad_wo[0].astype(jnp.float32) + swap(grad_wo[1], "c").astype(jnp.float32)
-    step = width // 16
-    flat_wo = grad_wo.reshape(8 * step, -1)
-    keep_wo = jnp.concatenate([flat_wo[: 2 * step], flat_wo[6 * step :]], axis=0)
-    grad_wo = total_square(
-        reduce_square(
-            keep_wo,
-            flat_wo[2 * step : 4 * step].astype(jnp.bfloat16),
-            flat_wo[4 * step : 6 * step].astype(jnp.bfloat16),
-        )
-    ).astype(jnp.bfloat16)
-    grad_wo = jnp.stack([grad_wo[:, z * 3 * LN : (z + 1) * 3 * LN] for z in range(nz)])
+    hidden, _ = tie(hidden, grad_low)
+    keep_out, *out_sides = down_call(hidden, w_mine, w_other)
+    out_sides = swap(out_sides[0], "x"), swap(out_sides[1], "y")
+    wo_mine, wo_other = row_grads_call(at, grad_low, attended_low[None], "out_grads", 3)
+    wo_keep, *wo_sides = core_sum(wo_mine, swap(wo_other, "c"))
+    wo_sides = swap(wo_sides[0], "x"), swap(wo_sides[1], "y")
 
     grad_qkv = attn_bwd(first, qkv, grad_o, attended_float, log_total, row_cos, row_sin)
+    grad_qkv, *sides = tie(grad_qkv, *out_sides, *wo_sides)
+    out = middle + total_square(reduce_square_rest(keep_out, *sides[:2]))
+    grad_wo = total_square(reduce_square_rest(wo_keep, *sides[2:])).astype(jnp.bfloat16)
     grad_qkv = all_to_all(grad_qkv.reshape(-1, chunk, 3 * LN), ("x", "c"))
+    grad_qkv, grad_ff = tie(grad_qkv, grad_ff)
+    grad_ff = all_to_all(grad_ff.reshape(plane, width // plane, 3 * LN), ("y", "x", "c"))
     grad_qkv = grad_qkv.reshape(kv_local, rows, chunk, 3 * LN)
-    part, gain_grad_in = da_call(place, blocks, grad_qkv, w_qkv, rows)
-    grad_wqkv = qkv_grads_call(
-        normed.reshape(rows * chunk, width), grad_qkv.reshape(kv_local, rows * chunk, 3 * LN)
-    )
-    grad_wqkv = lax.psum_scatter(grad_wqkv, ("y", "x", "c"), scatter_dimension=0, tiled=True)
+    part, gain_grad_in = da_call(nz, group, grad_qkv, w_qkv, grad_wo, rows)
+    part = lax.psum_scatter(part, "z", scatter_dimension=0, tiled=True).astype(jnp.float32)
+    grad_a, grad_wo = part[:count], part[count:]
+    grad_wo = jnp.concatenate([grad_wo[:, n * 3 * LN : (n + 1) * 3 * LN] for n in range(nz)], axis=0)
+    grad_wqkv = row_grads_call(
+        at,
+        normed.reshape(rows * chunk, width),
+        grad_qkv.reshape(kv_local, rows * chunk, 3 * LN),
+        "qkv_grads",
+        5,
+    )
+    *grad_wqkv, grad_ff = tie(*grad_wqkv, grad_ff)
+    grad_wqkv = reduce_square(*core_sum(grad_wqkv[0], swap(grad_wqkv[1], "c")))
     gain_grads = jnp.concatenate(
         [gain_grad_in.reshape(devices, share), gain_grad_mid.reshape(devices, share)], axis=1
     )
     gain_grads = jnp.pad(gain_grads, ((0, 0), (0, LN - 2 * share)))
-    late = {"ff": grad_ff}
-
-    def between(step, up, down):
-        if step == 1:
-            late["hidden"], _, _ = tie(hidden, up, down)
-            late["wo"] = all_to_all(grad_wo, "z")
-            late["gain"] = all_to_all(gain_grads, EVERY)
-        if step == nz - 2:
-            up, down, late["wo"], late["gain"] = tie(up, down, late["wo"], late["gain"])
-        if step == nz - 2:
-            late["ff"], _ = tie(late["ff"], up)
-            late["ff"] = all_to_all(late["ff"].reshape(plane, width // plane, 3 * LN), ("y", "x", "c"))
-        if step == nz - 1:
-            up, down, late["ff"] = tie(up, down, late["ff"])
-        return up, down
-
-    grad_a = reduce_line(part.reshape(nz, count, width), z_at, nz, between)
-    grad_ff = late["ff"]
-    out = middle + total_square(reduce_square(*down_call(late["hidden"], w_mine, w_other)))
-    grad_wo = jnp.sum(late["wo"].astype(jnp.float32), axis=0)
-    gain_grads = jnp.sum(late["gain"], axis=0, keepdims=True)
+    *grad_wqkv, gain_grads = tie(*grad_wqkv, gain_grads)
+    grad_wqkv = total_square(grad_wqkv)
+    gain_grads = jnp.sum(all_to_all(gain_grads, EVERY), axis=0, keepdims=True)
 
     stream = own.astype(jnp.float32)
     factor = lax.rsqrt(jnp.mean(stream * stream, axis=-1, keepdims=True) + EPS)
     back_in, _ = norm_back(stream, factor, gain_in, grad_a)
     grad_tokens = grad_mid + back_in
-    grad_wqkv = grad_wqkv.astype(jnp.float32).reshape(-1, kv_local, 4 * HD)
+    grad_wqkv = grad_wqkv.reshape(-1, kv_local, 4 * HD)
     flat = lambda g: g.reshape(1, g.shape[0], -1)
     grad_gate, grad_up, grad_down = uncut_call(grad_ff)
     return (

time: 602 us -> 516 us (0.86); the launches traced: 591 us -> 514 us
  waiting for transfers between devices: 193 us -> 149 us
  local copies, waits for them, and re-layouts: 59.9 us -> 45 us
  blocking collectives: 11.7 us -> 0 us
  starting transfers between devices: 100 us -> 89.4 us
  Pallas kernels: 161 us -> 171 us
    ppermute x6 -> x3, waiting for transfers between devices: 37.4 us -> 0.69 us  [gather_blocks(): lax.ppermute(value, 'z', shift(k))]
    all_to_all x9 -> x8, waiting for transfers between devices: 81.6 us -> 50.3 us  [all_to_all(): return lax.all_to_all(value, axes, 0, 0, tiled=True)]
    ppermute x28 -> x38, waiting for transfers between devices: 70.3 us -> 95.4 us  [swap(): return lax.ppermute(value, axis, SWAP)]
    ppermute x28 -> x38, starting transfers between devices: 26.9 us -> 40.4 us  [swap(): return lax.ppermute(value, axis, SWAP)]
    all_to_all x1 -> x0, blocking collectives: 11.7 us -> none  [all_to_all(): return lax.all_to_all(value, axes, 0, 0, tiled=True)]
    ppermute x6 -> x0, starting transfers between devices: 11.5 us -> none  [the longest x3 7.06 us: reduce_line(): up = lax.ppermute(send_up, 'z', [(i, i + 1) for i in range(step)])]
    all_to_all x9 -> x8, starting transfers between devices: 52 us -> 40.7 us  [all_to_all(): return lax.all_to_all(value, axes, 0, 0, tiled=True)]
    unnamed x114 -> x100, local copies, waits for them, and re-layouts: 39.2 us -> 30.3 us
  transfers between devices with their start and end apart: 53 -> 53, of which waited for: 17 -> 26; matrix products, arithmetic and copies ran while one was open for 11% -> 13% of each run, Pallas kernels for 22% -> 27%
where the time goes in v4:
time: 516 us; the launch traced here: 514 us
  Pallas kernels  171 us (33%)
  waiting for transfers between devices  149 us (29%)
  starting transfers between devices  89.4 us (17%)
  local copies, waits for them, and re-layouts  45 us (9%)
  other arithmetic  44.7 us (9%)
  between operations  15.2 us (3%)
    ppermute x38, waiting for transfers between devices, swap(): return lax.ppermute(value, axis, SWAP)  95.4 us
    all_to_all x8, waiting for transfers between devices, all_to_all(): return lax.all_to_all(value, axes, 0, 0, tiled=True)  50.3 us
    all_to_all x8, starting transfers between devices, all_to_all(): return lax.all_to_all(value, axes, 0, 0, tiled=True)  40.7 us
    ppermute x38, starting transfers between devices, swap(): return lax.ppermute(value, axis, SWAP)  40.4 us
    pallas_call x1, Pallas kernels, attn_bwd(): pl.pallas_call(functools.partial(attn_bwd_kernel, length), grid=(blocks,)...  31.4 us
    unnamed x100, local copies, waits for them, and re-layouts  30.3 us
    pallas_call x1, Pallas kernels, units_call(): pl.pallas_call(units_kernel, grid=(parts,), in_specs=[full_spec(v) for v...  27 us
    pallas_call x1, Pallas kernels, attn_fwd(): pl.pallas_call(functools.partial(attn_fwd_kernel, length), grid=(blocks,)...  22.8 us
  transfers between devices with their start and end apart: 53, of which 26 were waited for; matrix products, arithmetic and copies ran while one was open for 13% of the time, Pallas kernels for 27%

profile of v4, /device:TPU:0, one launch (start us, length us, event | category | flops | bytes accessed | tf_op | source)
XLA Modules:
  0.0 513.7 jit_solution(7862070515831690325)
XLA Ops:
  7.9 4.1 collective-permute-start.1
  13.6 2.2 collective-permute-start.2
  17.2 2.8 all-to-all-start
  29.1 5.6 %multiply_sine_fusion = (f32[2048,128]{1,0:T(8,128)}, f32[2048,128]{1,0:T(8,128)}) fusion(f32[128]{0:T(128)S(1)} %fusion.24, f32[2048]{0:T(1024)S(1)} %subtract_convert_fusion), kind=kLoop, calls=%fused_computation.12 | loop fusion | flops 262144 | bytes 2105856 | tf_op jit(solution)/shard_map/sin | solution.py:1448
  39.1 13.5 %collective-permute-done.5 = bf16[1,192,384]{2,1,0:T(8,128)(2,1)S(1)} collective-permute-done((bf16[1,192,384]{2,1,0:T(8,128)(2,1)S(1)}, bf16[1,192,384]{2,1,0:T(8,128)(2,1)S(1)}, u32[]{:S(2)}, u32[]{:S(2)}) %collective-permute-start.5) | collective-permute-done | bytes 147488 | tf_op jit(solution)/shard_map/ppermute | solution.py:1358
  55.7 2.6 cut_units.1
  58.3 4.3 all-to-all-start.1
  70.9 13.7 %collective-permute-done.11 = bf16[2,192,384]{2,1,0:T(8,128)(2,1)S(1)} collective-permute-done((bf16[2,192,384]{2,1,0:T(8,128)(2,1)S(1)}, bf16[2,192,384]{2,1,0:T(8,128)(2,1)S(1)}, u32[]{:S(2)}, u32[]{:S(2)}) %collective-permute-start.11) | collective-permute-done | bytes 294944 | tf_op jit(solution)/shard_map/ppermute | solution.py:1358
  86.7 9.0 %norm_qkv.1 = (bf16[2,512,1536]{2,1,0:T(8,128)(2,1)}, bf16[4,512,384]{2,1,0:T(8,128)(2,1)}) custom-call(bf16[1024,1536]{1,0:T(8,128)(2,1)} %all-gather.3.cloned.1.call-done.h_ref, f32[1,1536]{1,0:T(1,128)S(1)} %reshape.195.gain_ref, bf16[1536,768]{1,0:T(8,128)(2,1)S(1)} %copy-done.18, f32[2,512,128]{2,1,0:T(8,128)S(1)} %get-tuple-element.106.cos_ref, ...), custom_call_target="tpu_custom_call" | custom-call | flops 7000000000 | bytes 21000000 | tf_op jit(solution)/shard_map/norm_qkv/pallas_call | solution.py:825
  95.6 3.6 all-to-all-start.2
  107.1 12.1 %all-to-all-done.2 = bf16[4,512,384]{2,1,0:T(8,128)(2,1)S(1)} async-done(((bf16[4,512,384]{2,1,0:T(8,128)(2,1)}), bf16[4,512,384]{2,1,0:T(8,128)(2,1)S(1)}, u32[]{:S(2)}, u32[]{:S(2)}) %all-to-all-start.2) | async-done | bytes 1572896 | tf_op jit(solution)/shard_map/all_to_all | solution.py:1406
  121.1 22.8 %attend.1 = (bf16[16,64,384]{2,1,0:T(8,128)(2,1)}, f32[8,512,128]{2,1,0:T(8,128)S(1)}, f32[8,8,512]{2,1,0:T(8,128)S(1)}) custom-call(s32[1]{0:T(128)} %bitcast.first_ref, bf16[2048,384]{1,0:T(8,128)(2,1)S(1)} %bitcast.102), custom_call_target="tpu_custom_call" | custom-call | flops 22000001024 | bytes 66000000 | tf_op jit(solution)/shard_map/attend/pallas_call | solution.py:648
  147.7 14.3 %all-to-all-start.3 = ((bf16[16,64,384]{2,1,0:T(8,128)(2,1)}), bf16[16,64,384]{2,1,0:T(8,128)(2,1)S(1)}, u32[]{:S(2)}, u32[]{:S(2)}) async-start(bf16[16,64,384]{2,1,0:T(8,128)(2,1)} %get-tuple-element.111), calls=%async_computation.3 | async-start | bytes 1572864 | tf_op jit(solution)/shard_map/all_to_all | solution.py:1406
  162.3 2.9 place_out.3.w_ref
  165.2 2.2 copy-done.16
  170.0 8.9 %collective-permute-done.16.refs_4_.refs_9_ = bf16[128,1536]{1,0:T(8,128)(2,1)S(1)} collective-permute-done((bf16[128,1536]{1,0:T(8,128)(2,1)S(1)}, bf16[128,1536]{1,0:T(8,128)(2,1)S(1)}, u32[]{:S(2)}, u32[]{:S(2)}) %collective-permute-start.16) | collective-permute-done | bytes 393248 | tf_op jit(solution)/shard_map/ppermute | solution.py:1358
  178.9 3.9 collective-permute-done.15.refs_3_.refs_8_
  182.8 16.7 %all-to-all-done.3.o_ref = bf16[16,64,384]{2,1,0:T(8,128)(2,1)S(1)} async-done(((bf16[16,64,384]{2,1,0:T(8,128)(2,1)}), bf16[16,64,384]{2,1,0:T(8,128)(2,1)S(1)}, u32[]{:S(2)}, u32[]{:S(2)}) %all-to-all-start.3) | async-done | bytes 786464 | tf_op jit(solution)/shard_map/all_to_all | solution.py:1406
  199.5 4.0 out_norm.1
  207.8 6.0 %collective-permute-done.19.refs_6_.w1_ref = bf16[4,1536,384]{2,1,0:T(8,128)(2,1)} collective-permute-done((bf16[4,1536,384]{2,1,0:T(8,128)(2,1)}, bf16[4,1536,384]{2,1,0:T(8,128)(2,1)}, u32[]{:S(2)}, u32[]{:S(2)}) %collective-permute-start.19) | collective-permute-done | bytes 4718624 | tf_op jit(solution)/shard_map/ppermute | solution.py:1358
  213.8 10.5 %down_back.1.refs_7_ = f32[4,4,256,256]{3,2,1,0:T(8,128)} custom-call(bf16[256,1536]{1,0:T(8,128)(2,1)} %bitcast.106, bf16[256,1536]{1,0:T(8,128)(2,1)} %copy-done.29, bf16[256,1536]{1,0:T(8,128)(2,1)} %copy-done.27, bf16[128,1536]{1,0:T(8,128)(2,1)} %collective-permute-done.15.refs_3_.refs_8_, bf16[128,1536]{1,0:T(8,128)(2,1)} %copy-done.41, ...), custom_call_target="tpu_custom_call" | custom-call | flops 8000000000 | bytes 24000000 | tf_op jit(solution)/shard_map/down_back/pallas_call | solution.py:1115
  229.0 9.3 %collective-permute-done.20.refs_3_ = bf16[128,1536]{1,0:T(8,128)(2,1)S(1)} collective-permute-done((bf16[128,1536]{1,0:T(8,128)(2,1)S(1)}, bf16[128,1536]{1,0:T(8,128)(2,1)S(1)}, u32[]{:S(2)}, u32[]{:S(2)}) %collective-permute-start.20) | collective-permute-done | bytes 393248 | tf_op jit(solution)/shard_map/ppermute | solution.py:1358
  239.9 27.0 %units.1 = (bf16[4,2,4,256,256]{4,3,2,1,0:T(8,128)(2,1)}, bf16[4,4,256,256]{3,2,1,0:T(8,128)(2,1)}, f32[512,1536]{1,0:T(8,128)}, bf16[256,1536]{1,0:T(8,128)(2,1)}, bf16[256,1536]{1,0:T(8,128)(2,1)}) custom-call(bf16[256,1536]{1,0:T(8,128)(2,1)} %copy-done.10, bf16[256,1536]{1,0:T(8,128)(2,1)} %collective-permute-done.17.refs_1_, ...), custom_call_target="tpu_custom_call" | custom-call | flops 25999998976 | bytes 78000000 | tf_op jit(solution)/shard_map/units/pallas_call | solution.py:1195
  268.9 19.6 %unit_grads.1 = (bf16[4,1536,384]{2,1,0:T(8,128)(2,1)}, bf16[4,1536,384]{2,1,0:T(8,128)(2,1)}) custom-call(bf16[256,1536]{1,0:T(8,128)(2,1)} %copy-done.10, bf16[256,1536]{1,0:T(8,128)(2,1)} %collective-permute-done.17.refs_1_, bf16[256,1536]{1,0:T(8,128)(2,1)} %copy-done.31, bf16[128,1536]{1,0:T(8,128)(2,1)} %copy-done.42, bf16[128,1536]{1,0:T(8,128)(2,1)} %copy-done.43, ...), custom_call_target="tpu_custom_call" | custom-call | flops 19000000512 | bytes 57000000 | tf_op jit(solution)/shard_map/unit_grads/pallas_call | solution.py:1287
  292.3 4.3 collective-permute-done.24
  296.6 5.6 %add_convert_fusion = bf16[4,1536,384]{2,1,0:T(8,128)(2,1)} fusion(bf16[4,1536,384]{2,1,0:T(8,128)(2,1)S(1)} %collective-permute-done.24, bf16[4,1536,384]{2,1,0:T(8,128)(2,1)} %get-tuple-element.137), kind=kLoop, calls=%fused_computation | loop fusion | flops 9437184 | bytes 14155776 | tf_op jit(solution)/shard_map/convert_element_type | solution.py:1492
  305.5 6.4 %mid_back.1 = (f32[256,1536]{1,0:T(8,128)}, bf16[256,1536]{1,0:T(8,128)(2,1)S(1)}, bf16[16,64,384]{2,1,0:T(8,128)(2,1)S(1)}, f32[1,1536]{1,0:T(1,128)S(1)}) custom-call(f32[512,1536]{1,0:T(8,128)} %get-tuple-element.130.keep_ref, bf16[256,1536]{1,0:T(8,128)(2,1)S(1)} %collective-permute-done.22.fx_ref, bf16[256,1536]{1,0:T(8,128)(2,1)S(1)} %collective-permute-done.23.fy_ref, ...), custom_call_target="tpu_custom_call" | custom-call | flops 5000000000 | bytes 15000000 | tf_op jit(solution)/shard_map/mid_back/pallas_call | solution.py:950
  311.9 4.6 out_grads.1
  316.5 4.5 all-to-all-start.4
  321.1 13.1 %down.1 = (f32[512,1536]{1,0:T(8,128)}, bf16[256,1536]{1,0:T(8,128)(2,1)}, bf16[256,1536]{1,0:T(8,128)(2,1)}) custom-call(bf16[4,4,256,256]{3,2,1,0:T(8,128)(2,1)} %get-tuple-element.142.refs_11_.hid_ref, bf16[4,1536,384]{2,1,0:T(8,128)(2,1)} %bitcast.138, bf16[4,1536,384]{2,1,0:T(8,128)(2,1)} %collective-permute-done.19.refs_6_.w1_ref), custom_call_target="tpu_custom_call" | custom-call | flops 11000000512 | bytes 33000000 | tf_op jit(solution)/shard_map/down/pallas_call | solution.py:1241
  336.7 4.7 convert_add_fusion
  343.1 19.2 %all-to-all-done.4.do_ref = bf16[16,64,384]{2,1,0:T(8,128)(2,1)} async-done(((bf16[16,64,384]{2,1,0:T(8,128)(2,1)}), bf16[16,64,384]{2,1,0:T(8,128)(2,1)}, u32[]{:S(2)}, u32[]{:S(2)}) %all-to-all-start.4) | async-done | bytes 786464 | tf_op jit(solution)/shard_map/all_to_all | solution.py:1406
  362.3 31.4 %attend_back.1 = bf16[2048,384]{1,0:T(8,128)(2,1)} custom-call(s32[1]{0:T(128)} %bitcast.first_ref, bf16[2048,384]{1,0:T(8,128)(2,1)} %bitcast.103, bf16[16,64,384]{2,1,0:T(8,128)(2,1)} %all-to-all-done.4.do_ref, f32[8,512,128]{2,1,0:T(8,128)} %copy-done.20, f32[8,8,512]{2,1,0:T(8,128)} %copy-done.21, f32[2048,128]{1,0:T(8,128)} %get-tuple-element.147.cos_ref, ...), custom_call_target="tpu_custom_call" | custom-call | flops 31000000512 | bytes 93000000 | tf_op jit(solution)/shard_map/attend_back/pallas_call | solution.py:746
  393.7 3.6 all-to-all-start.5
  402.2 5.9 %collective-permute-done.34 = bf16[96,1536]{1,0:T(8,128)(2,1)S(1)} collective-permute-done((bf16[96,1536]{1,0:T(8,128)(2,1)S(1)}, bf16[96,1536]{1,0:T(8,128)(2,1)S(1)}, u32[]{:S(2)}, u32[]{:S(2)}) %collective-permute-start.34) | collective-permute-done | bytes 294944 | tf_op jit(solution)/shard_map/ppermute | solution.py:1358
  408.2 15.5 %collective-permute-done.35 = bf16[96,1536]{1,0:T(8,128)(2,1)S(1)} collective-permute-done((bf16[96,1536]{1,0:T(8,128)(2,1)S(1)}, bf16[96,1536]{1,0:T(8,128)(2,1)S(1)}, u32[]{:S(2)}, u32[]{:S(2)}) %collective-permute-start.35) | collective-permute-done | bytes 294944 | tf_op jit(solution)/shard_map/ppermute | solution.py:1358
  427.0 7.1 %da_part.1 = (bf16[4,304,1536]{2,1,0:T(8,128)(2,1)}, f32[1,1536]{1,0:T(1,128)S(1)}) custom-call(bf16[1024,1536]{1,0:T(8,128)(2,1)} %all-gather.3.cloned.1.call-done.h_ref, bf16[2,2,512,384]{3,2,1,0:T(8,128)(2,1)S(1)} %bitcast.104, bf16[1536,768]{1,0:T(8,128)(2,1)S(1)} %copy-done.19, bf16[192,1536]{1,0:T(8,128)(2,1)S(1)} %pad_maximum_fusion.2.wo_ref), custom_call_target="tpu_custom_call" | custom-call | flops 6000000000 | bytes 18000000 | tf_op jit(solution)/shard_map/da_part/pallas_call | solution.py:996
  437.2 4.3 all-to-all-start.6
  442.0 5.4 %collective-permute-done.32 = bf16[128,1536]{1,0:T(8,128)(2,1)S(1)} collective-permute-done((bf16[128,1536]{1,0:T(8,128)(2,1)S(1)}, bf16[128,1536]{1,0:T(8,128)(2,1)S(1)}, u32[]{:S(2)}, u32[]{:S(2)}) %collective-permute-start.32) | collective-permute-done | bytes 393248 | tf_op jit(solution)/shard_map/ppermute | solution.py:1358
  447.5 2.8 convert_add_fusion.3
  450.3 3.0 collective-permute-start.33
  453.3 5.2 %qkv_grads.1 = (bf16[8,96,768]{2,1,0:T(8,128)(2,1)S(1)}, bf16[8,96,768]{2,1,0:T(8,128)(2,1)S(1)}) custom-call(s32[4]{0:T(128)S(1)} %copy-done.6, bf16[1024,1536]{1,0:T(8,128)(2,1)S(1)} %bitcast.111, bf16[2,1024,384]{2,1,0:T(8,128)(2,1)S(1)} %bitcast.105), custom_call_target="tpu_custom_call" | custom-call | flops 5000000000 | bytes 15000000 | tf_op jit(solution)/shard_map/qkv_grads/pallas_call | solution.py:1332
  468.8 3.0 fusion.26
  475.4 3.2 uncut_units.1
  478.5 2.5 copy.39
  486.0 2.1 collective-permute-done.40
  489.5 3.4 all-to-all-start.7
  497.7 2.3 all-to-all-done.7
  (248 shorter events, 113.9 us)
Async XLA Ops:
  7.2 77.6 %all-gather.3.cloned.1.call-start = ((), (), s32[]{:S(2)}) async-start(), calls=%async_computation.10 | async-start | bytes 3932160 | tf_op jit(solution)/shard_map/all_gather | solution.py:1426
  7.9 17.4 %collective-permute-start.1 = (bf16[192,384]{1,0:T(8,128)(2,1)}, bf16[192,384]{1,0:T(8,128)(2,1)S(1)}, u32[]{:S(2)}, u32[]{:S(2)}) collective-permute-start(bf16[192,384]{1,0:T(8,128)(2,1)} %bitcast.126), channel_id=1, source_target_pairs={{0,2},{1,3},{2,0},{3,1},{4,6},{5,7},{6,4},{7,5},{8,10},{9,11},{10,... | collective-permute-start | bytes 442376 | tf_op jit(solution)/shard_map/ppermute | solution.py:1363
  12.0 13.3 %collective-permute-start = (bf16[192,384]{1,0:T(8,128)(2,1)}, bf16[192,384]{1,0:T(8,128)(2,1)S(1)}, u32[]{:S(2)}, u32[]{:S(2)}) collective-permute-start(bf16[192,384]{1,0:T(8,128)(2,1)} %bitcast.127), channel_id=1, source_target_pairs={{0,1},{1,2},{2,3},{3,0},{4,5},{5,6},{6,7},{7,4},{8,9},{9,10},{10,1... | collective-permute-start | bytes 442376 | tf_op jit(solution)/shard_map/ppermute | solution.py:1363
  13.6 12.4 %collective-permute-start.2 = (bf16[192,384]{1,0:T(8,128)(2,1)}, bf16[192,384]{1,0:T(8,128)(2,1)S(1)}, u32[]{:S(2)}, u32[]{:S(2)}) collective-permute-start(bf16[192,384]{1,0:T(8,128)(2,1)} %bitcast.128), channel_id=1, source_target_pairs={{0,3},{1,0},{2,1},{3,2},{4,7},{5,4},{6,5},{7,6},{8,11},{9,8},{10,9... | collective-permute-start | bytes 442376 | tf_op jit(solution)/shard_map/ppermute | solution.py:1363
  17.2 38.5 %all-to-all-start = ((f32[32,1,128]{2,1,0:T(1,128)}), f32[32,1,128]{2,1,0:T(1,128)S(1)}, u32[]{:S(2)}, u32[]{:S(2)}) async-start(f32[32,1,128]{2,1,0:T(1,128)} %broadcast_in_dim.47), calls=%async_computation | async-start | bytes 32768 | tf_op jit(solution)/shard_map/all_to_all | solution.py:1406
  26.1 9.8 %collective-permute-start.4 = (bf16[2,192,384]{2,1,0:T(8,128)(2,1)S(1)}, bf16[2,192,384]{2,1,0:T(8,128)(2,1)S(1)}, u32[]{:S(2)}, u32[]{:S(2)}) collective-permute-start(bf16[2,192,384]{2,1,0:T(8,128)(2,1)S(1)} %maximum_bitcast_fusion), channel_id=1, source_target_pairs={{0,16},{16,0},{1,17},{17,1},{2,18},{18,2},{3,19},{19,3},{4,20},{20... | collective-permute-start | bytes 884744 | tf_op jit(solution)/shard_map/ppermute | solution.py:1358
  27.5 9.8 %collective-permute-start.3 = (bf16[2,192,384]{2,1,0:T(8,128)(2,1)S(1)}, bf16[2,192,384]{2,1,0:T(8,128)(2,1)S(1)}, u32[]{:S(2)}, u32[]{:S(2)}) collective-permute-start(bf16[2,192,384]{2,1,0:T(8,128)(2,1)S(1)} %maximum_bitcast_fusion), channel_id=1, source_target_pairs={{0,8},{8,0},{1,9},{9,1},{2,10},{10,2},{3,11},{11,3},{4,12},{12,4},... | collective-permute-start | bytes 884744 | tf_op jit(solution)/shard_map/ppermute | solution.py:1358
  34.6 21.1 %collective-permute-start.9 = (bf16[4,192,384]{2,1,0:T(8,128)(2,1)S(1)}, bf16[4,192,384]{2,1,0:T(8,128)(2,1)}, u32[]{:S(2)}, u32[]{:S(2)}) collective-permute-start(bf16[4,192,384]{2,1,0:T(8,128)(2,1)S(1)} %pad_maximum_fusion.1), channel_id=1, source_target_pairs={{0,16},{16,0},{1,17},{17,1},{2,18},{18,2},{3,19},{19,3},{4,20},{20... | collective-permute-start | bytes 1769480 | tf_op jit(solution)/shard_map/ppermute | solution.py:1358
  35.2 20.5 %collective-permute-start.8 = (bf16[4,192,384]{2,1,0:T(8,128)(2,1)S(1)}, bf16[4,192,384]{2,1,0:T(8,128)(2,1)}, u32[]{:S(2)}, u32[]{:S(2)}) collective-permute-start(bf16[4,192,384]{2,1,0:T(8,128)(2,1)S(1)} %pad_maximum_fusion.1), channel_id=1, source_target_pairs={{0,8},{8,0},{1,9},{9,1},{2,10},{10,2},{3,11},{11,3},{4,12},{12,4},... | collective-permute-start | bytes 1769480 | tf_op jit(solution)/shard_map/ppermute | solution.py:1358
  35.9 16.7 %collective-permute-start.5 = (bf16[1,192,384]{2,1,0:T(8,128)(2,1)S(1)}, bf16[1,192,384]{2,1,0:T(8,128)(2,1)S(1)}, u32[]{:S(2)}, u32[]{:S(2)}) collective-permute-start(bf16[1,192,384]{2,1,0:T(8,128)(2,1)S(1)} %slice.297), channel_id=1, source_target_pairs={{0,8},{8,0},{1,9},{9,1},{2,10},{10,2},{3,11},{11,3},{4,12},{12,4},... | collective-permute-start | bytes 442376 | tf_op jit(solution)/shard_map/ppermute | solution.py:1358
  37.4 15.3 %collective-permute-start.6 = (bf16[1,192,384]{2,1,0:T(8,128)(2,1)S(1)}, bf16[1,192,384]{2,1,0:T(8,128)(2,1)S(1)}, u32[]{:S(2)}, u32[]{:S(2)}) collective-permute-start(bf16[1,192,384]{2,1,0:T(8,128)(2,1)S(1)} %slice.298), channel_id=1, source_target_pairs={{0,16},{16,0},{1,17},{17,1},{2,18},{18,2},{3,19},{19,3},{4,20},{20... | collective-permute-start | bytes 442376 | tf_op jit(solution)/shard_map/ppermute | solution.py:1358
  52.7 15.4 %collective-permute-start.7 = (bf16[8,192,384]{2,1,0:T(8,128)(2,1)S(1)}, bf16[8,192,384]{2,1,0:T(8,128)(2,1)}, u32[]{:S(2)}, u32[]{:S(2)}) collective-permute-start(bf16[8,192,384]{2,1,0:T(8,128)(2,1)S(1)} %constant_dynamic-update-slice_fusion.mine_ref), channel_id=1, source_target_pairs={{0,4},{4,0},{1,5},{5,1},{2,6},{6,2},{3,7},{7,3},{8,12},{12,8},{9,1... | collective-permute-start | bytes 3538952 | tf_op jit(solution)/shard_map/ppermute | solution.py:1358
  58.3 26.5 %all-to-all-start.1 = ((bf16[8,192,384]{2,1,0:T(8,128)(2,1)}), bf16[8,192,384]{2,1,0:T(8,128)(2,1)}, u32[]{:S(2)}, u32[]{:S(2)}) async-start(bf16[8,192,384]{2,1,0:T(8,128)(2,1)} %cut_units.1), calls=%async_computation.1 | async-start | bytes 2359296 | tf_op jit(solution)/shard_map/all_to_all | solution.py:1406
  62.5 143.0 %all-gather.5.cloned.1.call-start = ((), (), s32[]{:S(2)}) async-start(), calls=%async_computation.11 | async-start | bytes 5898240 | tf_op jit(solution)/shard_map/all_gather | solution.py:1462
  64.6 20.0 %collective-permute-start.11 = (bf16[2,192,384]{2,1,0:T(8,128)(2,1)S(1)}, bf16[2,192,384]{2,1,0:T(8,128)(2,1)S(1)}, u32[]{:S(2)}, u32[]{:S(2)}) collective-permute-start(bf16[2,192,384]{2,1,0:T(8,128)(2,1)S(1)} %slice.234), channel_id=1, source_target_pairs={{0,16},{16,0},{1,17},{17,1},{2,18},{18,2},{3,19},{19,3},{4,20},{20... | collective-permute-start | bytes 884744 | tf_op jit(solution)/shard_map/ppermute | solution.py:1358
  66.5 18.3 %collective-permute-start.10 = (bf16[2,192,384]{2,1,0:T(8,128)(2,1)S(1)}, bf16[2,192,384]{2,1,0:T(8,128)(2,1)}, u32[]{:S(2)}, u32[]{:S(2)}) collective-permute-start(bf16[2,192,384]{2,1,0:T(8,128)(2,1)S(1)} %slice.233), channel_id=1, source_target_pairs={{0,8},{8,0},{1,9},{9,1},{2,10},{10,2},{3,11},{11,3},{4,12},{12,4},... | collective-permute-start | bytes 884744 | tf_op jit(solution)/shard_map/ppermute | solution.py:1358
  95.6 23.6 %all-to-all-start.2 = ((bf16[4,512,384]{2,1,0:T(8,128)(2,1)}), bf16[4,512,384]{2,1,0:T(8,128)(2,1)S(1)}, u32[]{:S(2)}, u32[]{:S(2)}) async-start(bf16[4,512,384]{2,1,0:T(8,128)(2,1)} %get-tuple-element.108), calls=%async_computation.2 | async-start | bytes 3145728 | tf_op jit(solution)/shard_map/all_to_all | solution.py:1406
  106.6 55.6 %collective-permute-start.14 = (bf16[16,192,384]{2,1,0:T(8,128)(2,1)}, bf16[16,192,384]{2,1,0:T(8,128)(2,1)}, u32[]{:S(2)}, u32[]{:S(2)}) collective-permute-start(bf16[16,192,384]{2,1,0:T(8,128)(2,1)} %constant_dynamic-update-slice_fusion.5.mine_ref), channel_id=1, source_target_pairs={{0,4},{4,0},{1,5},{5,1},{2,6},{6,2},{3,7},{7,3},{8,12},{12,8},{9,1... | collective-permute-start | bytes 7077896 | tf_op jit(solution)/shard_map/ppermute | solution.py:1358
  119.3 26.7 %collective-permute-start.13 = (bf16[256,1536]{1,0:T(8,128)(2,1)S(1)}, bf16[256,1536]{1,0:T(8,128)(2,1)S(1)}, u32[]{:S(2)}, u32[]{:S(2)}) collective-permute-start(bf16[256,1536]{1,0:T(8,128)(2,1)S(1)} %bitcast.108), channel_id=1, source_target_pairs={{0,16},{16,0},{1,17},{17,1},{2,18},{18,2},{3,19},{19,3},{4,20},{20... | collective-permute-start | bytes 2359304 | tf_op jit(solution)/shard_map/ppermute | solution.py:1358
  120.7 25.2 %collective-permute-start.12 = (bf16[256,1536]{1,0:T(8,128)(2,1)S(1)}, bf16[256,1536]{1,0:T(8,128)(2,1)S(1)}, u32[]{:S(2)}, u32[]{:S(2)}) collective-permute-start(bf16[256,1536]{1,0:T(8,128)(2,1)S(1)} %bitcast.109), channel_id=1, source_target_pairs={{0,8},{8,0},{1,9},{9,1},{2,10},{10,2},{3,11},{11,3},{4,12},{12,4},... | collective-permute-start | bytes 2359304 | tf_op jit(solution)/shard_map/ppermute | solution.py:1358
  147.7 51.8 %all-to-all-start.3 = ((bf16[16,64,384]{2,1,0:T(8,128)(2,1)}), bf16[16,64,384]{2,1,0:T(8,128)(2,1)S(1)}, u32[]{:S(2)}, u32[]{:S(2)}) async-start(bf16[16,64,384]{2,1,0:T(8,128)(2,1)} %get-tuple-element.111), calls=%async_computation.3 | async-start | bytes 1572864 | tf_op jit(solution)/shard_map/all_to_all | solution.py:1406
  162.0 263.2 %reduce-scatter.3.cloned.1.call-start = ((), (), s32[]{:S(2)}) async-start(), calls=%async_computation.12 | async-start | bytes 5898240 | tf_op jit(solution)/shard_map/reduce_scatter | solution.py:1495
  167.4 11.5 %collective-permute-start.16 = (bf16[128,1536]{1,0:T(8,128)(2,1)S(1)}, bf16[128,1536]{1,0:T(8,128)(2,1)S(1)}, u32[]{:S(2)}, u32[]{:S(2)}) collective-permute-start(bf16[128,1536]{1,0:T(8,128)(2,1)S(1)} %slice.237), channel_id=1, source_target_pairs={{0,16},{16,0},{1,17},{17,1},{2,18},{18,2},{3,19},{19,3},{4,20},{20... | collective-permute-start | bytes 1179656 | tf_op jit(solution)/shard_map/ppermute | solution.py:1358
  168.0 14.8 %collective-permute-start.15 = (bf16[128,1536]{1,0:T(8,128)(2,1)S(1)}, bf16[128,1536]{1,0:T(8,128)(2,1)}, u32[]{:S(2)}, u32[]{:S(2)}) collective-permute-start(bf16[128,1536]{1,0:T(8,128)(2,1)S(1)} %slice.236), channel_id=1, source_target_pairs={{0,8},{8,0},{1,9},{9,1},{2,10},{10,2},{3,11},{11,3},{4,12},{12,4},... | collective-permute-start | bytes 1179656 | tf_op jit(solution)/shard_map/ppermute | solution.py:1358
  205.5 20.0 %collective-permute-start.18 = (bf16[256,1536]{1,0:T(8,128)(2,1)S(1)}, bf16[256,1536]{1,0:T(8,128)(2,1)S(1)}, u32[]{:S(2)}, u32[]{:S(2)}) collective-permute-start(bf16[256,1536]{1,0:T(8,128)(2,1)S(1)} %get-tuple-element.121.refs_0_), channel_id=1, source_target_pairs={{0,16},{16,0},{1,17},{17,1},{2,18},{18,2},{3,19},{19,3},{4,20},{20... | collective-permute-start | bytes 2359304 | tf_op jit(solution)/shard_map/ppermute | solution.py:1358
  207.0 19.8 %collective-permute-start.17 = (bf16[256,1536]{1,0:T(8,128)(2,1)S(1)}, bf16[256,1536]{1,0:T(8,128)(2,1)}, u32[]{:S(2)}, u32[]{:S(2)}) collective-permute-start(bf16[256,1536]{1,0:T(8,128)(2,1)S(1)} %get-tuple-element.121.refs_0_), channel_id=1, source_target_pairs={{0,8},{8,0},{1,9},{9,1},{2,10},{10,2},{3,11},{11,3},{4,12},{12,4},... | collective-permute-start | bytes 2359304 | tf_op jit(solution)/shard_map/ppermute | solution.py:1358
  227.9 10.5 %collective-permute-start.20 = (bf16[128,1536]{1,0:T(8,128)(2,1)S(1)}, bf16[128,1536]{1,0:T(8,128)(2,1)S(1)}, u32[]{:S(2)}, u32[]{:S(2)}) collective-permute-start(bf16[128,1536]{1,0:T(8,128)(2,1)S(1)} %slice.239), channel_id=1, source_target_pairs={{0,8},{8,0},{1,9},{9,1},{2,10},{10,2},{3,11},{11,3},{4,12},{12,4},... | collective-permute-start | bytes 1179656 | tf_op jit(solution)/shard_map/ppermute | solution.py:1358
  228.5 9.9 %collective-permute-start.21 = (bf16[128,1536]{1,0:T(8,128)(2,1)S(1)}, bf16[128,1536]{1,0:T(8,128)(2,1)S(1)}, u32[]{:S(2)}, u32[]{:S(2)}) collective-permute-start(bf16[128,1536]{1,0:T(8,128)(2,1)S(1)} %slice.240), channel_id=1, source_target_pairs={{0,16},{16,0},{1,17},{17,1},{2,18},{18,2},{3,19},{19,3},{4,20},{20... | collective-permute-start | bytes 1179656 | tf_op jit(solution)/shard_map/ppermute | solution.py:1358
  266.9 21.5 %collective-permute-start.22 = (bf16[256,1536]{1,0:T(8,128)(2,1)}, bf16[256,1536]{1,0:T(8,128)(2,1)S(1)}, u32[]{:S(2)}, u32[]{:S(2)}) collective-permute-start(bf16[256,1536]{1,0:T(8,128)(2,1)} %get-tuple-element.131), channel_id=1, source_target_pairs={{0,8},{8,0},{1,9},{9,1},{2,10},{10,2},{3,11},{11,3},{4,12},{12,4},... | collective-permute-start | bytes 2359304 | tf_op jit(solution)/shard_map/ppermute | solution.py:1358
  268.0 20.5 %collective-permute-start.23 = (bf16[256,1536]{1,0:T(8,128)(2,1)}, bf16[256,1536]{1,0:T(8,128)(2,1)S(1)}, u32[]{:S(2)}, u32[]{:S(2)}) collective-permute-start(bf16[256,1536]{1,0:T(8,128)(2,1)} %get-tuple-element.132), channel_id=1, source_target_pairs={{0,16},{16,0},{1,17},{17,1},{2,18},{18,2},{3,19},{19,3},{4,20},{20... | collective-permute-start | bytes 2359304 | tf_op jit(solution)/shard_map/ppermute | solution.py:1358
  290.1 12.1 %collective-permute-start.26 = (bf16[128,1536]{1,0:T(8,128)(2,1)S(1)}, bf16[128,1536]{1,0:T(8,128)(2,1)S(1)}, u32[]{:S(2)}, u32[]{:S(2)}) collective-permute-start(bf16[128,1536]{1,0:T(8,128)(2,1)S(1)} %get-tuple-element.222), channel_id=1, source_target_pairs={{0,16},{16,0},{1,17},{17,1},{2,18},{18,2},{3,19},{19,3},{4,20},{20... | collective-permute-start | bytes 1179656 | tf_op jit(solution)/shard_map/ppermute | solution.py:1358
  291.3 11.2 %collective-permute-start.25 = (bf16[128,1536]{1,0:T(8,128)(2,1)S(1)}, bf16[128,1536]{1,0:T(8,128)(2,1)S(1)}, u32[]{:S(2)}, u32[]{:S(2)}) collective-permute-start(bf16[128,1536]{1,0:T(8,128)(2,1)S(1)} %get-tuple-element.223), channel_id=1, source_target_pairs={{0,8},{8,0},{1,9},{9,1},{2,10},{10,2},{3,11},{11,3},{4,12},{12,4},... | collective-permute-start | bytes 1179656 | tf_op jit(solution)/shard_map/ppermute | solution.py:1358
  316.5 20.2 %collective-permute-start.29 = (bf16[8,96,1536]{2,1,0:T(8,128)(2,1)}, bf16[8,96,1536]{2,1,0:T(8,128)(2,1)}, u32[]{:S(2)}, u32[]{:S(2)}) collective-permute-start(bf16[8,96,1536]{2,1,0:T(8,128)(2,1)} %get-tuple-element.153), channel_id=1, source_target_pairs={{0,4},{4,0},{1,5},{5,1},{2,6},{6,2},{3,7},{7,3},{8,12},{12,8},{9,1... | collective-permute-start | bytes 7077896 | tf_op jit(solution)/shard_map/ppermute | solution.py:1358
  316.5 45.8 %all-to-all-start.4 = ((bf16[16,64,384]{2,1,0:T(8,128)(2,1)}), bf16[16,64,384]{2,1,0:T(8,128)(2,1)}, u32[]{:S(2)}, u32[]{:S(2)}) async-start(bf16[16,64,384]{2,1,0:T(8,128)(2,1)} %copy-done.4), calls=%async_computation.4 | async-start | bytes 1572864 | tf_op jit(solution)/shard_map/all_to_all | solution.py:1406
  334.2 59.5 %collective-permute-start.27 = (bf16[256,1536]{1,0:T(8,128)(2,1)}, bf16[256,1536]{1,0:T(8,128)(2,1)}, u32[]{:S(2)}, u32[]{:S(2)}) collective-permute-start(bf16[256,1536]{1,0:T(8,128)(2,1)} %get-tuple-element.149), channel_id=1, source_target_pairs={{0,8},{8,0},{1,9},{9,1},{2,10},{10,2},{3,11},{11,3},{4,12},{12,4},... | collective-permute-start | bytes 2359304 | tf_op jit(solution)/shard_map/ppermute | solution.py:1358
  335.8 57.9 %collective-permute-start.28 = (bf16[256,1536]{1,0:T(8,128)(2,1)}, bf16[256,1536]{1,0:T(8,128)(2,1)}, u32[]{:S(2)}, u32[]{:S(2)}) collective-permute-start(bf16[256,1536]{1,0:T(8,128)(2,1)} %get-tuple-element.150), channel_id=1, source_target_pairs={{0,16},{16,0},{1,17},{17,1},{2,18},{18,2},{3,19},{19,3},{4,20},{20... | collective-permute-start | bytes 2359304 | tf_op jit(solution)/shard_map/ppermute | solution.py:1358
  341.6 52.1 %collective-permute-start.30 = (bf16[192,1536]{1,0:T(8,128)(2,1)S(1)}, bf16[192,1536]{1,0:T(8,128)(2,1)S(1)}, u32[]{:S(2)}, u32[]{:S(2)}) collective-permute-start(bf16[192,1536]{1,0:T(8,128)(2,1)S(1)} %bitcast.122), channel_id=1, source_target_pairs={{0,8},{8,0},{1,9},{9,1},{2,10},{10,2},{3,11},{11,3},{4,12},{12,4},... | collective-permute-start | bytes 1769480 | tf_op jit(solution)/shard_map/ppermute | solution.py:1358
  342.1 51.6 %collective-permute-start.31 = (bf16[192,1536]{1,0:T(8,128)(2,1)S(1)}, bf16[192,1536]{1,0:T(8,128)(2,1)S(1)}, u32[]{:S(2)}, u32[]{:S(2)}) collective-permute-start(bf16[192,1536]{1,0:T(8,128)(2,1)S(1)} %bitcast.121), channel_id=1, source_target_pairs={{0,16},{16,0},{1,17},{17,1},{2,18},{18,2},{3,19},{19,3},{4,20},{20... | collective-permute-start | bytes 1769480 | tf_op jit(solution)/shard_map/ppermute | solution.py:1358
  393.7 31.5 %all-to-all-start.5 = ((bf16[4,512,384]{2,1,0:T(8,128)(2,1)}), bf16[4,512,384]{2,1,0:T(8,128)(2,1)S(1)}, u32[]{:S(2)}, u32[]{:S(2)}) async-start(bf16[4,512,384]{2,1,0:T(8,128)(2,1)} %bitcast.117), calls=%async_computation.5 | async-start | bytes 3145728 | tf_op jit(solution)/shard_map/all_to_all | solution.py:1406
  397.3 104.8 %reduce-scatter.5.cloned.1.call-start = ((), (), s32[]{:S(2)}) async-start(), calls=%async_computation.13 | async-start | bytes 4669440 | tf_op jit(solution)/shard_map/reduce_scatter | solution.py:1516
  398.8 9.4 %collective-permute-start.34 = (bf16[96,1536]{1,0:T(8,128)(2,1)S(1)}, bf16[96,1536]{1,0:T(8,128)(2,1)S(1)}, u32[]{:S(2)}, u32[]{:S(2)}) collective-permute-start(bf16[96,1536]{1,0:T(8,128)(2,1)S(1)} %get-tuple-element.216), channel_id=1, source_target_pairs={{0,16},{16,0},{1,17},{17,1},{2,18},{18,2},{3,19},{19,3},{4,20},{20... | collective-permute-start | bytes 884744 | tf_op jit(solution)/shard_map/ppermute | solution.py:1358
  400.3 23.4 %collective-permute-start.35 = (bf16[96,1536]{1,0:T(8,128)(2,1)S(1)}, bf16[96,1536]{1,0:T(8,128)(2,1)S(1)}, u32[]{:S(2)}, u32[]{:S(2)}) collective-permute-start(bf16[96,1536]{1,0:T(8,128)(2,1)S(1)} %get-tuple-element.217), channel_id=1, source_target_pairs={{0,8},{8,0},{1,9},{9,1},{2,10},{10,2},{3,11},{11,3},{4,12},{12,4},... | collective-permute-start | bytes 884744 | tf_op jit(solution)/shard_map/ppermute | solution.py:1358
  435.4 12.1 %collective-permute-start.32 = (bf16[128,1536]{1,0:T(8,128)(2,1)S(1)}, bf16[128,1536]{1,0:T(8,128)(2,1)S(1)}, u32[]{:S(2)}, u32[]{:S(2)}) collective-permute-start(bf16[128,1536]{1,0:T(8,128)(2,1)S(1)} %add_convert_fusion.2), channel_id=1, source_target_pairs={{0,16},{16,0},{1,17},{17,1},{2,18},{18,2},{3,19},{19,3},{4,20},{20... | collective-permute-start | bytes 1179656 | tf_op jit(solution)/shard_map/ppermute | solution.py:1358
  437.2 22.4 %all-to-all-start.6 = ((bf16[8,192,384]{2,1,0:T(8,128)(2,1)}), bf16[8,192,384]{2,1,0:T(8,128)(2,1)}, u32[]{:S(2)}, u32[]{:S(2)}) async-start(bf16[8,192,384]{2,1,0:T(8,128)(2,1)} %bitcast.42), calls=%async_computation.8 | async-start | bytes 2359296 | tf_op jit(solution)/shard_map/all_to_all | solution.py:1406
  450.3 15.5 %collective-permute-start.33 = (bf16[128,1536]{1,0:T(8,128)(2,1)}, bf16[128,1536]{1,0:T(8,128)(2,1)}, u32[]{:S(2)}, u32[]{:S(2)}) collective-permute-start(bf16[128,1536]{1,0:T(8,128)(2,1)} %get-tuple-element.221), channel_id=1, source_target_pairs={{0,8},{8,0},{1,9},{9,1},{2,10},{10,2},{3,11},{11,3},{4,12},{12,4},... | collective-permute-start | bytes 1179656 | tf_op jit(solution)/shard_map/ppermute | solution.py:1358
  459.6 9.2 %collective-permute-start.36 = (bf16[8,96,768]{2,1,0:T(8,128)(2,1)}, bf16[8,96,768]{2,1,0:T(8,128)(2,1)}, u32[]{:S(2)}, u32[]{:S(2)}) collective-permute-start(bf16[8,96,768]{2,1,0:T(8,128)(2,1)} %copy-done.7), channel_id=1, source_target_pairs={{0,4},{4,0},{1,5},{5,1},{2,6},{6,2},{3,7},{7,3},{8,12},{12,8},{9,1... | collective-permute-start | bytes 3538952 | tf_op jit(solution)/shard_map/ppermute | solution.py:1358
  473.0 8.8 %collective-permute-start.38 = (bf16[192,768]{1,0:T(8,128)(2,1)}, bf16[192,768]{1,0:T(8,128)(2,1)}, u32[]{:S(2)}, u32[]{:S(2)}) collective-permute-start(bf16[192,768]{1,0:T(8,128)(2,1)} %bitcast.46), channel_id=1, source_target_pairs={{0,16},{16,0},{1,17},{17,1},{2,18},{18,2},{3,19},{19,3},{4,20},{20... | collective-permute-start | bytes 884744 | tf_op jit(solution)/shard_map/ppermute | solution.py:1358
  489.5 10.5 %all-to-all-start.7 = ((f32[32,1,128]{2,1,0:T(1,128)}), f32[32,1,128]{2,1,0:T(1,128)S(1)}, u32[]{:S(2)}, u32[]{:S(2)}) async-start(f32[32,1,128]{2,1,0:T(1,128)} %bitcast.49), calls=%async_computation.9 | async-start | bytes 32768 | tf_op jit(solution)/shard_map/all_to_all | solution.py:1406
  (49 other events, 580.5 us)
Sparse Core Ops, SparseCore 0:
  9.6 67.6 all-gather.2
  85.0 114.6 all-gather.4
  303.4 94.9 reduce-scatter.2
  434.2 67.8 reduce-scatter.4

commit v5 on v4

--- a/solution.py
+++ b/solution.py
@@ -573,6 +573,7 @@
     return jnp.where(index >= second, second, jnp.where(index >= first, first, 0))
 
 BQ = 256
+BK = 512
 
 def dotf(a, b, dims):
     return lax.dot_general(a, b, (dims, ((), ())), preferred_element_type=jnp.float32)
@@ -581,6 +582,7 @@
     i = pl.program_id(0)
     blocks = length // BQ
     first = first_ref[0]
+
     @pl.when(i == 0)
     def _():
         def body(j, carry):
@@ -588,59 +590,56 @@
             q0, q1, k, v = unpack4(*split3(x_ref[rows, :]))
             q_s[j, :BQ, :] = q0.astype(jnp.bfloat16)
             q_s[j, BQ:, :] = q1.astype(jnp.bfloat16)
-            k_s[j] = k.astype(jnp.bfloat16)
-            v_s[j] = v.astype(jnp.bfloat16)
+            k_s[rows, :] = k.astype(jnp.bfloat16)
+            v_s[rows, :] = v.astype(jnp.bfloat16)
             return carry
+
         lax.fori_loop(0, blocks, body, 0)
+
     q = q_s[i]
-    clean_from = (length // 8 + BQ - 1) // BQ
-    clean_to = 3 * length // 4 // BQ
     late = (3 * length // 4 + length // 8) // BQ
-    start = jnp.where(i >= late, 3 * length // 4 // BQ, 0)
-    head_masked = jnp.where(i < clean_to, jnp.minimum(clean_from, i), i)
+    start = jnp.where(i >= late, 3 * length // 4 // BK, 0)
+    stop = i * BQ // BK + 1
     q_index = i * BQ + lax.broadcasted_iota(jnp.int32, (BQ, 1), 0)
     low = doc_low(q_index, first, length)
 
-    def halves(v, op):
-        return op(v[:, :LN], v[:, LN:])
-
-    def score(j, top, masked):
-        s = dotf(q, k_s[j], ((1,), (1,)))
-        if masked:
-            key = j * BQ + lax.broadcasted_iota(jnp.int32, (1, BQ), 1)
-            ok = (key <= q_index) & (key >= low)
-            s = jnp.where(jnp.concatenate([ok, ok], axis=0), s, NEG)
+    def fold(v, op):
+        out = v[:, :LN]
+        for n in range(1, BK // LN):
+            out = op(out, v[:, n * LN : (n + 1) * LN])
+        return out
+
+    def score(j, top):
+        s = dotf(q, k_s[pl.ds(pl.multiple_of(j * BK, BK), BK), :], ((1,), (1,)))
+        key = j * BK + lax.broadcasted_iota(jnp.int32, (1, BK), 1)
+        ok = (key <= q_index) & (key >= low)
+        s = jnp.concatenate([jnp.where(ok, s[:BQ], NEG), jnp.where(ok, s[BQ:], NEG)], axis=0)
         s_s[j] = s
-        return jnp.maximum(top, halves(s, jnp.maximum))
-
-    top = jnp.full((2 * BQ, LN), NEG, jnp.float32)
-    top = lax.fori_loop(start, head_masked, lambda j, t: score(j, t, True), top)
-    top = lax.fori_loop(jnp.maximum(head_masked, start), i, lambda j, t: score(j, t, False), top)
-    top = score(i, top, True)
+        return jnp.maximum(top, fold(s, jnp.maximum))
+
+    top = lax.fori_loop(start, stop, score, jnp.full((2 * BQ, LN), NEG, jnp.float32))
     m = jnp.max(top, axis=1, keepdims=True) * C2
 
     def add(j, state):
-        total, acc = state
         p = jnp.exp2(s_s[j] * C2 - m)
-        total = total + halves(p, jnp.add)
-        acc = acc + dotf(p.astype(jnp.bfloat16), v_s[j], ((1,), (0,)))
-        return total, acc
+        keys = pl.ds(pl.multiple_of(j * BK, BK), BK)
+        of_ref[0] += dotf(p.astype(jnp.bfloat16), v_s[keys, :], ((1,), (0,)))
+        return state + fold(p, jnp.add)
 
     zero = jnp.zeros((2 * BQ, LN), jnp.float32)
-    total, acc = lax.fori_loop(start, i + 1, add, (zero, zero))
+    of_ref[0] = zero
+    total = lax.fori_loop(start, stop, add, zero)
     total = jnp.sum(total, axis=1, keepdims=True)
-    out = acc / total
+    out = of_ref[0] / total
     lse = jnp.broadcast_to(m + jnp.log2(total), (2 * BQ, LN))
     lse_ref[0] = jnp.transpose(lse, (1, 0))[:8, :]
     of_ref[0] = out
     for d in range(2):
-        parts = []
-        for h in range(2):
-            parts.append(out[BQ*0 + d*128 + h*64: d*128 + h*64 + 64])
-            parts.append(out[BQ + d*128 + h*64: BQ + d*128 + h*64 + 64])
-        t = pack4(*parts)
-        for n in range(3):
-            o_ref[d, :, n*LN:(n+1)*LN] = t[n].astype(jnp.bfloat16)
+        at = d * 128
+        parts = [out[at + n // 2 * 64 + n % 2 * BQ : at + n // 2 * 64 + n % 2 * BQ + 64] for n in range(4)]
+        for n, t in enumerate(pack4(*parts)):
+            o_ref[d, :, n * LN : (n + 1) * LN] = t.astype(jnp.bfloat16)
+
 
 def attn_fwd(first, x):
     length = x.shape[0]
@@ -657,9 +656,9 @@
                    jax.ShapeDtypeStruct((blocks, 2*BQ, LN), jnp.float32),
                    jax.ShapeDtypeStruct((blocks, 8, 2*BQ), jnp.float32)],
         scratch_shapes=[pltpu.VMEM((blocks, 2*BQ, LN), jnp.bfloat16),
-                        pltpu.VMEM((blocks, BQ, LN), jnp.bfloat16),
-                        pltpu.VMEM((blocks, BQ, LN), jnp.bfloat16),
-                        pltpu.VMEM((blocks, 2*BQ, BQ), jnp.float32)],
+                        pltpu.VMEM((length, LN), jnp.bfloat16),
+                        pltpu.VMEM((length, LN), jnp.bfloat16),
+                        pltpu.VMEM((length // BK, 2*BQ, BK), jnp.float32)],
         compiler_params=pltpu.CompilerParams(vmem_limit_bytes=48 << 20),
         name="attend",
         cost_estimate=cost(22),
@@ -690,8 +689,6 @@
             dq_s[b] = jnp.zeros((2*BQ, LN), jnp.float32)
             return carry
         lax.fori_loop(0, blocks, body, 0)
-    clean_from = (length // 8 + BQ - 1) // BQ
-    clean_to = 3 * length // 4 // BQ
     late = (3 * length // 4 + length // 8) // BQ
     third = 3 * length // 4 // BQ
     stop = jnp.where(j >= third, blocks, late)
@@ -701,43 +698,54 @@
     dv_s[j] = jnp.zeros((BQ, LN), jnp.float32)
     key = j * BQ + lax.broadcasted_iota(jnp.int32, (BQ, 1), 0)
 
-    def step(i, masked):
-        q, do = q_s[i], do_s[i]
-        s = dotf(k, q, ((1,), (1,)))
-        p = jnp.exp2(s * C2 - lse_ref[i, 0:1, :])
-        if masked:
+    def steps(places):
+        dk, dv = [], []
+        for i in places:
+            q, do = q_s[i], do_s[i]
+            s = dotf(k, q, ((1,), (1,)))
+            dp = dotf(v, do, ((1,), (1,)))
             q_index = i * BQ + lax.broadcasted_iota(jnp.int32, (1, BQ), 1)
             ok = (key <= q_index) & (key >= doc_low(q_index, first, length))
-            p = jnp.where(jnp.concatenate([ok, ok], axis=1), p, 0.0)
-        dp = dotf(v, do, ((1,), (1,)))
-        ds = (p * (dp - dl_s[i, 0:1, :])).astype(jnp.bfloat16)
-        dv_s[j] += dotf(p.astype(jnp.bfloat16), do, ((1,), (0,)))
-        dk_s[j] += dotf(ds, q, ((1,), (0,)))
-        dq_s[i] += dotf(ds, k, ((0,), (0,)))
-
-    def loop(lo, hi, masked):
-        def body(i, carry):
-            step(i, masked)
-            return carry
-        lax.fori_loop(lo, hi, body, 0)
-
-    step(j, True)
-    clean_lo = j + 1
-    clean_hi = jnp.where(j >= clean_from, jnp.maximum(clean_to, j + 1), j + 1)
-    loop(clean_lo, clean_hi, False)
-    loop(clean_hi, stop, True)
+            p = jnp.exp2(s * C2 - lse_ref[i, 0:1, :])
+            p = jnp.concatenate([jnp.where(ok, p[:, :BQ], 0.0), jnp.where(ok, p[:, BQ:], 0.0)], axis=1)
+            ds = (p * (dp - dl_s[i, 0:1, :])).astype(jnp.bfloat16)
+            dv.append(dotf(p.astype(jnp.bfloat16), do, ((1,), (0,))))
+            dk.append(dotf(ds, q, ((1,), (0,))))
+            dq_s[i] += dotf(ds, k, ((0,), (0,)))
+        dv_s[j] += functools.reduce(jnp.add, dv)
+        dk_s[j] += functools.reduce(jnp.add, dk)
+
+    pairs = (stop - j) // 2
+
+    def body(n, carry):
+        steps((j + 2 * n, j + 2 * n + 1))
+        return carry
+
+    lax.fori_loop(0, pairs, body, 0)
+
+    @pl.when(j + 2 * pairs < stop)
+    def _():
+        steps((stop - 1,))
 
     @pl.when(j == blocks - 1)
     def _():
         scale = HD ** -0.5
+        lower = lane_iota(BQ) < HD // 2
+
+        def turn_back(piece, cosine, sine):
+            swapped = jnp.where(lower, -pltpu.roll(piece, LN - HD // 2, 1), pltpu.roll(piece, HD // 2, 1))
+            return (piece * cosine - swapped * sine) * scale
+
         def body(b, carry):
             rows = pl.ds(pl.multiple_of(b * BQ, BQ), BQ)
-            t = pack4(dq_s[b, :BQ, :] * scale, dq_s[b, BQ:, :] * scale, dk_s[b] * scale, dv_s[b])
-            t = jnp.concatenate(t, axis=1)
-            cosine, sine, lower = cos_sin3(cos_ref[rows, :], sin_ref[rows, :])
-            out_ref[rows, :] = turn(t, cosine, -sine, lower).astype(jnp.bfloat16)
+            cosine, sine = cos_ref[rows, :], sin_ref[rows, :]
+            pieces = [turn_back(v, cosine, sine) for v in (dq_s[b, :BQ, :], dq_s[b, BQ:, :], dk_s[b])]
+            for n, tile in enumerate(pack4(*pieces, dv_s[b])):
+                out_ref[rows, n * LN : (n + 1) * LN] = tile.astype(jnp.bfloat16)
             return carry
+
         lax.fori_loop(0, blocks, body, 0)
+
 
 def attn_bwd(first, x, do, of, lse, cos, sin):
     length = x.shape[0]
@@ -776,18 +784,24 @@
     cos_two, cos_three = widen(cos)
     sin_two, sin_three = widen(sin)
     cosine = jnp.concatenate([cos, cos_two, jnp.where(live, cos_three, 1.0)], axis=1)
-    sine = jnp.concatenate([sin, sin_two, jnp.where(live, sin_three, 0.0)], axis=1)
-    wide = lax.broadcasted_iota(jnp.int32, cosine.shape, 1)
-    lower = (wide % HD) < HD // 2
-    return cosine, jnp.where(lower, -sine, sine), lower
+    lower = (
+        (lane < 48) | (lane >= 96),
+        (lane < 16) | ((lane >= 64) & (lane < 112)),
+        (lane >= 32) & (lane < 80),
+    )
+    tiles = (sin, sin_two, jnp.where(live, sin_three, 0.0))
+    sine = jnp.concatenate([jnp.where(l, -t, t) for l, t in zip(lower, tiles)], axis=1)
+    return cosine, sine, lower
 
 
 def turn(values, cosine, sine, lower):
     width = values.shape[1]
-    swapped = jnp.where(
-        lower, pltpu.roll(values, width - HD // 2, 1), pltpu.roll(values, HD // 2, 1)
-    )
-    return values * cosine + swapped * sine
+    left, right = pltpu.roll(values, width - HD // 2, 1), pltpu.roll(values, HD // 2, 1)
+    swapped = [
+        jnp.where(l, left[:, n * LN : (n + 1) * LN], right[:, n * LN : (n + 1) * LN])
+        for n, l in enumerate(lower)
+    ]
+    return values * cosine + jnp.concatenate(swapped, axis=1) * sine
 
 
 def full_spec(array):
@@ -1097,11 +1111,15 @@
 
     weight = jnp.concatenate([w0_ref[0, :, 2 * LN :], w1_ref[0, :, 2 * LN :]], axis=1)
 
+    count, width = g_s.shape[1:]
+
     def body(m, carry):
-        out_ref[0, m] = dotf(g_s[m], weight, ((1,), (0,)))
+        two = pl.ds(2 * m, 2)
+        product = dotf(g_s[two].reshape(2 * count, width), weight, ((1,), (0,)))
+        out_ref[0, two] = product.reshape(2, count, 2 * LN)
         return carry
 
-    lax.fori_loop(0, 4, body, 0)
+    lax.fori_loop(0, 2, body, 0)
 
 
 def unit_spec(weight):
@@ -1142,34 +1160,39 @@
     def _():
         fill_square(pieces, b_s)
 
+    count, width = b_s.shape[1:]
+
     def body(m, carry):
-        b = b_s[m]
+        two = pl.ds(2 * m, 2)
+        b = b_s[two].reshape(2 * count, width)
         total = None
         for n, w_ref in enumerate((w0_ref, w1_ref)):
             weight = w_ref[0, :, : 2 * LN]
             both = dotf(b, weight, ((1,), (0,)))
             gate, up = both[:, :LN], both[:, LN:]
-            dh = dh_ref[0, m, :, n * LN : (n + 1) * LN]
+            cols = slice(n * LN, (n + 1) * LN)
+            dh = dh_ref[0, two, :, cols].reshape(2 * count, LN)
             sigma = 1.0 / (1.0 + jnp.exp(-gate))
             silu = gate * sigma
-            hid_ref[0, m, :, n * LN : (n + 1) * LN] = (silu * up).astype(jnp.bfloat16)
+            hid_ref[0, two, :, cols] = (silu * up).astype(jnp.bfloat16).reshape(2, count, LN)
             grad_gate = dh * up * sigma * (1.0 + gate * (1.0 - sigma))
             grads = jnp.concatenate([grad_gate, dh * silu], axis=1).astype(jnp.bfloat16)
-            dgu_ref[0, n, m] = grads
+            dgu_ref[0, n, two] = grads.reshape(2, count, 2 * LN)
             back = dotf(grads, weight, ((1,), (1,)))
             total = back if total is None else total + back
+        total = total.reshape(2, count, width)
 
         @pl.when(step == 0)
         def _():
-            acc_s[m] = total
+            acc_s[two] = total
 
         @pl.when(step > 0)
         def _():
-            acc_s[m] += total
+            acc_s[two] += total
 
         return carry
 
-    lax.fori_loop(0, 4, body, 0)
+    lax.fori_loop(0, 2, body, 0)
 
     @pl.when(step == pl.num_programs(0) - 1)
     def _():
@@ -1214,20 +1237,24 @@
     step = pl.program_id(0)
     weight = jnp.concatenate([w0_ref[0, :, 2 * LN :], w1_ref[0, :, 2 * LN :]], axis=1)
 
+    count, width = acc_s.shape[1:]
+
     def body(m, carry):
-        total = dotf(hid_ref[0, m], weight, ((1,), (1,)))
+        two = pl.ds(2 * m, 2)
+        total = dotf(hid_ref[0, two].reshape(2 * count, 2 * LN), weight, ((1,), (1,)))
+        total = total.reshape(2, count, width)
 
         @pl.when(step == 0)
         def _():
-            acc_s[m] = total
+            acc_s[two] = total
 
         @pl.when(step > 0)
         def _():
-            acc_s[m] += total
+            acc_s[two] += total
 
         return carry
 
-    lax.fori_loop(0, 4, body, 0)
+    lax.fori_loop(0, 2, body, 0)
 
     @pl.when(step == pl.num_programs(0) - 1)
     def _():
@@ -1301,10 +1328,11 @@
     )(*operands, grads, hidden)
 
 
+BY_SIDES = tuple((y, x, last) for x in range(2) for y in range(2) for last in range(2))
 ORDER = ((0, 0, 0), (0, 0, 1), (0, 1, 0), (1, 1, 0), (1, 0, 1), (1, 1, 1), (0, 1, 1), (1, 0, 0))
 
 
-def row_grads_kernel(at_ref, left_ref, right_ref, mine_ref, other_ref, full_s):
+def row_grads_kernel(order, at_ref, left_ref, right_ref, mine_ref, other_ref, full_s):
     tile = 2 * LN
     width = right_ref.shape[2]
 
@@ -1319,18 +1347,18 @@
     lax.fori_loop(0, full_s.shape[0] // tile, body, 0)
     half = mine_ref.shape[1]
     for c, out_ref in enumerate((mine_ref, other_ref)):
-        for n, (y, x, last) in enumerate(ORDER):
+        for n, (y, x, last) in enumerate(order):
             block = ((at_ref[0] ^ y) * 2 + (at_ref[1] ^ x)) * 2 + (at_ref[2] ^ c)
             rows = pl.multiple_of(block * 2 * half + last * half, 32)
             out_ref[n] = full_s[pl.ds(rows, half), :]
 
 
-def row_grads_call(at, left, right, name, time):
+def row_grads_call(at, left, right, order, name, time):
     width = left.shape[1]
     cols = right.shape[0] * right.shape[2]
     shape = jax.ShapeDtypeStruct((8, width // 16, cols), jnp.bfloat16)
     return pl.pallas_call(
-        row_grads_kernel,
+        partial(row_grads_kernel, order),
         grid=(1,),
         in_specs=[pl.BlockSpec(memory_space=pltpu.SMEM), full_spec(left), full_spec(right)],
         out_specs=[full_spec(shape)] * 2,
@@ -1500,14 +1528,17 @@
     hidden, _ = tie(hidden, grad_low)
     keep_out, *out_sides = down_call(hidden, w_mine, w_other)
     out_sides = swap(out_sides[0], "x"), swap(out_sides[1], "y")
-    wo_mine, wo_other = row_grads_call(at, grad_low, attended_low[None], "out_grads", 3)
-    wo_keep, *wo_sides = core_sum(wo_mine, swap(wo_other, "c"))
-    wo_sides = swap(wo_sides[0], "x"), swap(wo_sides[1], "y")
+    wo_mine, wo_other = row_grads_call(at, grad_low, attended_low[None], BY_SIDES, "out_grads", 3)
+    wo_sum = (wo_mine.astype(jnp.float32) + swap(wo_other, "c").astype(jnp.float32)).reshape(width // 2, -1)
+    wo_keep, wo_send = wo_sum[: width // 4], wo_sum[width // 4 :].astype(jnp.bfloat16)
+    wo_got = swap(wo_send, "x")
 
     grad_qkv = attn_bwd(first, qkv, grad_o, attended_float, log_total, row_cos, row_sin)
-    grad_qkv, *sides = tie(grad_qkv, *out_sides, *wo_sides)
-    out = middle + total_square(reduce_square_rest(keep_out, *sides[:2]))
-    grad_wo = total_square(reduce_square_rest(wo_keep, *sides[2:])).astype(jnp.bfloat16)
+    grad_qkv, wo_got, *out_sides = tie(grad_qkv, wo_got, *out_sides)
+    out = middle + total_square(reduce_square_rest(keep_out, *out_sides))
+    wo_sum = wo_keep + wo_got.astype(jnp.float32)
+    wo_got = swap(wo_sum[width // 8 :].astype(jnp.bfloat16), "y")
+    grad_wo = (wo_sum[: width // 8] + wo_got.astype(jnp.float32)).astype(jnp.bfloat16)
     grad_qkv = all_to_all(grad_qkv.reshape(-1, chunk, 3 * LN), ("x", "c"))
     grad_qkv, grad_ff = tie(grad_qkv, grad_ff)
     grad_ff = all_to_all(grad_ff.reshape(plane, width // plane, 3 * LN), ("y", "x", "c"))
@@ -1520,6 +1551,7 @@
         at,
         normed.reshape(rows * chunk, width),
         grad_qkv.reshape(kv_local, rows * chunk, 3 * LN),
+        ORDER,
         "qkv_grads",
         5,
     )

time: 516 us -> 499 us (0.967)
  Pallas kernels: 171 us -> 157 us
    all_to_all x8, waiting for transfers between devices: 50.3 us -> 58.2 us  [all_to_all(): return lax.all_to_all(value, axes, 0, 0, tiled=True)]
    ppermute x38 -> x36, waiting for transfers between devices: 95.4 us -> 88.5 us  [swap(): return lax.ppermute(value, axis, SWAP)]
    ppermute x38 -> x36, starting transfers between devices: 40.4 us -> 37.3 us  [swap(): return lax.ppermute(value, axis, SWAP)]
    unnamed x100 -> x102, local copies, waits for them, and re-layouts: 30.3 us -> 32.6 us
  transfers between devices with their start and end apart: 53 -> 51, of which waited for: 26 -> 26; matrix products, arithmetic and copies ran while one was open for 13% -> 13% of each run, Pallas kernels for 27% -> 25%
where the time goes in v5:
time: 499 us; the launch traced here: 498 us
  Pallas kernels  157 us (31%)
  waiting for transfers between devices  149 us (30%)
  starting transfers between devices  85.6 us (17%)
  local copies, waits for them, and re-layouts  48.9 us (10%)
  other arithmetic  41.1 us (8%)
  between operations  15.2 us (3%)
    ppermute x36, waiting for transfers between devices, swap(): return lax.ppermute(value, axis, SWAP)  88.5 us
    all_to_all x8, waiting for transfers between devices, all_to_all(): return lax.all_to_all(value, axes, 0, 0, tiled=True)  58.2 us
    all_to_all x8, starting transfers between devices, all_to_all(): return lax.all_to_all(value, axes, 0, 0, tiled=True)  40.2 us
    ppermute x36, starting transfers between devices, swap(): return lax.ppermute(value, axis, SWAP)  37.3 us
    unnamed x102, local copies, waits for them, and re-layouts  32.6 us
    pallas_call x1, Pallas kernels, attn_bwd(): pl.pallas_call(functools.partial(attn_bwd_kernel, length), grid=(blocks,)...  27.4 us
    pallas_call x1, Pallas kernels, units_call(): pl.pallas_call(units_kernel, grid=(parts,), in_specs=[full_spec(v) for v...  24.5 us
    pallas_call x1, Pallas kernels, unit_grads_call(): pl.pallas_call(unit_grads_kernel, grid=(parts,), in_specs=[full_spec(v) f...  19.6 us
  transfers between devices with their start and end apart: 51, of which 26 were waited for; matrix products, arithmetic and copies ran while one was open for 13% of the time, Pallas kernels for 25%

profile of v5, /device:TPU:0, one launch (start us, length us, event | category | flops | bytes accessed | tf_op | source)
XLA Modules:
  0.0 497.6 jit_solution(11416582521800493900)
XLA Ops:
  7.9 4.1 collective-permute-start.1
  13.6 2.2 collective-permute-start.2
  17.2 2.8 all-to-all-start
  29.1 5.5 %multiply_sine_fusion = (f32[2048,128]{1,0:T(8,128)}, f32[2048,128]{1,0:T(8,128)}) fusion(f32[128]{0:T(128)S(1)} %fusion.15, f32[2048]{0:T(1024)S(1)} %subtract_convert_fusion), kind=kLoop, calls=%fused_computation.14 | loop fusion | flops 262144 | bytes 2105856 | tf_op jit(solution)/shard_map/sin | solution.py:1476
  39.0 13.5 %collective-permute-done.5 = bf16[1,192,384]{2,1,0:T(8,128)(2,1)S(1)} collective-permute-done((bf16[1,192,384]{2,1,0:T(8,128)(2,1)S(1)}, bf16[1,192,384]{2,1,0:T(8,128)(2,1)S(1)}, u32[]{:S(2)}, u32[]{:S(2)}) %collective-permute-start.5) | collective-permute-done | bytes 147488 | tf_op jit(solution)/shard_map/ppermute | solution.py:1386
  55.6 2.6 cut_units.1
  58.2 4.3 all-to-all-start.1
  70.9 13.7 %collective-permute-done.11 = bf16[2,192,384]{2,1,0:T(8,128)(2,1)S(1)} collective-permute-done((bf16[2,192,384]{2,1,0:T(8,128)(2,1)S(1)}, bf16[2,192,384]{2,1,0:T(8,128)(2,1)S(1)}, u32[]{:S(2)}, u32[]{:S(2)}) %collective-permute-start.11) | collective-permute-done | bytes 294944 | tf_op jit(solution)/shard_map/ppermute | solution.py:1386
  86.6 9.0 %norm_qkv.1 = (bf16[2,512,1536]{2,1,0:T(8,128)(2,1)}, bf16[4,512,384]{2,1,0:T(8,128)(2,1)}) custom-call(bf16[1024,1536]{1,0:T(8,128)(2,1)} %all-gather.3.cloned.1.call-done.h_ref, f32[1,1536]{1,0:T(1,128)S(1)} %reshape.188.gain_ref, bf16[1536,768]{1,0:T(8,128)(2,1)S(1)} %copy-done.18, f32[2,512,128]{2,1,0:T(8,128)S(1)} %get-tuple-element.105.cos_ref, ...), custom_call_target="tpu_custom_call" | custom-call | flops 7000000000 | bytes 21000000 | tf_op jit(solution)/shard_map/norm_qkv/pallas_call | solution.py:839
  95.6 3.6 all-to-all-start.2
  107.0 12.2 %all-to-all-done.2 = bf16[4,512,384]{2,1,0:T(8,128)(2,1)S(1)} async-done(((bf16[4,512,384]{2,1,0:T(8,128)(2,1)}), bf16[4,512,384]{2,1,0:T(8,128)(2,1)S(1)}, u32[]{:S(2)}, u32[]{:S(2)}) %all-to-all-start.2) | async-done | bytes 1572896 | tf_op jit(solution)/shard_map/all_to_all | solution.py:1434
  121.1 18.2 %attend.1 = (bf16[16,64,384]{2,1,0:T(8,128)(2,1)}, f32[8,512,128]{2,1,0:T(8,128)S(1)}, f32[8,8,512]{2,1,0:T(8,128)S(1)}) custom-call(s32[1]{0:T(128)} %bitcast.first_ref, bf16[2048,384]{1,0:T(8,128)(2,1)S(1)} %bitcast.75), custom_call_target="tpu_custom_call" | custom-call | flops 22000001024 | bytes 66000000 | tf_op jit(solution)/shard_map/attend/pallas_call | solution.py:647
  143.1 14.3 %all-to-all-start.3 = ((bf16[16,64,384]{2,1,0:T(8,128)(2,1)}), bf16[16,64,384]{2,1,0:T(8,128)(2,1)S(1)}, u32[]{:S(2)}, u32[]{:S(2)}) async-start(bf16[16,64,384]{2,1,0:T(8,128)(2,1)} %get-tuple-element.110), calls=%async_computation.3 | async-start | bytes 1572864 | tf_op jit(solution)/shard_map/all_to_all | solution.py:1434
  157.5 2.9 place_out.3.w_ref
  160.4 2.2 copy-done.16
  165.3 8.9 %collective-permute-done.16.refs_4_.refs_9_ = bf16[128,1536]{1,0:T(8,128)(2,1)S(1)} collective-permute-done((bf16[128,1536]{1,0:T(8,128)(2,1)S(1)}, bf16[128,1536]{1,0:T(8,128)(2,1)S(1)}, u32[]{:S(2)}, u32[]{:S(2)}) %collective-permute-start.16) | collective-permute-done | bytes 393248 | tf_op jit(solution)/shard_map/ppermute | solution.py:1386
  174.2 4.2 collective-permute-done.15.refs_3_.refs_8_
  178.5 18.5 %all-to-all-done.3.o_ref = bf16[16,64,384]{2,1,0:T(8,128)(2,1)S(1)} async-done(((bf16[16,64,384]{2,1,0:T(8,128)(2,1)}), bf16[16,64,384]{2,1,0:T(8,128)(2,1)S(1)}, u32[]{:S(2)}, u32[]{:S(2)}) %all-to-all-start.3) | async-done | bytes 786464 | tf_op jit(solution)/shard_map/all_to_all | solution.py:1434
  196.9 4.0 out_norm.1
  204.8 6.4 %collective-permute-done.19.refs_6_.w1_ref = bf16[4,1536,384]{2,1,0:T(8,128)(2,1)} collective-permute-done((bf16[4,1536,384]{2,1,0:T(8,128)(2,1)}, bf16[4,1536,384]{2,1,0:T(8,128)(2,1)}, u32[]{:S(2)}, u32[]{:S(2)}) %collective-permute-start.19) | collective-permute-done | bytes 4718624 | tf_op jit(solution)/shard_map/ppermute | solution.py:1386
  211.2 9.5 %down_back.1.refs_7_ = f32[4,4,256,256]{3,2,1,0:T(8,128)} custom-call(bf16[256,1536]{1,0:T(8,128)(2,1)} %bitcast.79, bf16[256,1536]{1,0:T(8,128)(2,1)} %copy-done.30, bf16[256,1536]{1,0:T(8,128)(2,1)} %copy-done.28, bf16[128,1536]{1,0:T(8,128)(2,1)} %collective-permute-done.15.refs_3_.refs_8_, bf16[128,1536]{1,0:T(8,128)(2,1)} %copy-done.42, ...), custom_call_target="tpu_custom_call" | custom-call | flops 8000000000 | bytes 24000000 | tf_op jit(solution)/shard_map/down_back/pallas_call | solution.py:1133
  226.7 8.5 %collective-permute-done.20.refs_3_ = bf16[128,1536]{1,0:T(8,128)(2,1)S(1)} collective-permute-done((bf16[128,1536]{1,0:T(8,128)(2,1)S(1)}, bf16[128,1536]{1,0:T(8,128)(2,1)S(1)}, u32[]{:S(2)}, u32[]{:S(2)}) %collective-permute-start.20) | collective-permute-done | bytes 393248 | tf_op jit(solution)/shard_map/ppermute | solution.py:1386
  236.8 24.5 %units.1 = (bf16[4,2,4,256,256]{4,3,2,1,0:T(8,128)(2,1)}, bf16[4,4,256,256]{3,2,1,0:T(8,128)(2,1)}, f32[512,1536]{1,0:T(8,128)}, bf16[256,1536]{1,0:T(8,128)(2,1)}, bf16[256,1536]{1,0:T(8,128)(2,1)}) custom-call(bf16[256,1536]{1,0:T(8,128)(2,1)} %copy-done.10, bf16[256,1536]{1,0:T(8,128)(2,1)} %collective-permute-done.17.refs_1_, ...), custom_call_target="tpu_custom_call" | custom-call | flops 25999998976 | bytes 78000000 | tf_op jit(solution)/shard_map/units/pallas_call | solution.py:1218
  263.5 19.6 %unit_grads.1 = (bf16[4,1536,384]{2,1,0:T(8,128)(2,1)}, bf16[4,1536,384]{2,1,0:T(8,128)(2,1)}) custom-call(bf16[256,1536]{1,0:T(8,128)(2,1)} %copy-done.10, bf16[256,1536]{1,0:T(8,128)(2,1)} %collective-permute-done.17.refs_1_, bf16[256,1536]{1,0:T(8,128)(2,1)} %copy-done.32, bf16[128,1536]{1,0:T(8,128)(2,1)} %copy-done.43, bf16[128,1536]{1,0:T(8,128)(2,1)} %copy-done.44, ...), custom_call_target="tpu_custom_call" | custom-call | flops 19000000512 | bytes 57000000 | tf_op jit(solution)/shard_map/unit_grads/pallas_call | solution.py:1314
  286.7 4.5 collective-permute-done.24
  291.3 5.6 %add_convert_fusion = bf16[4,1536,384]{2,1,0:T(8,128)(2,1)} fusion(bf16[4,1536,384]{2,1,0:T(8,128)(2,1)S(1)} %collective-permute-done.24, bf16[4,1536,384]{2,1,0:T(8,128)(2,1)} %get-tuple-element.136), kind=kLoop, calls=%fused_computation | loop fusion | flops 9437184 | bytes 14155776 | tf_op jit(solution)/shard_map/convert_element_type | solution.py:1520
  299.8 6.5 %mid_back.1 = (f32[256,1536]{1,0:T(8,128)}, bf16[256,1536]{1,0:T(8,128)(2,1)S(1)}, bf16[16,64,384]{2,1,0:T(8,128)(2,1)S(1)}, f32[1,1536]{1,0:T(1,128)S(1)}) custom-call(f32[512,1536]{1,0:T(8,128)} %get-tuple-element.129.keep_ref, bf16[256,1536]{1,0:T(8,128)(2,1)S(1)} %collective-permute-done.22.fx_ref, bf16[256,1536]{1,0:T(8,128)(2,1)S(1)} %collective-permute-done.23.fy_ref, ...), custom_call_target="tpu_custom_call" | custom-call | flops 5000000000 | bytes 15000000 | tf_op jit(solution)/shard_map/mid_back/pallas_call | solution.py:964
  306.3 4.7 out_grads.1
  311.0 4.5 all-to-all-start.4
  315.5 11.6 %down.1 = (f32[512,1536]{1,0:T(8,128)}, bf16[256,1536]{1,0:T(8,128)(2,1)}, bf16[256,1536]{1,0:T(8,128)(2,1)}) custom-call(bf16[4,4,256,256]{3,2,1,0:T(8,128)(2,1)} %get-tuple-element.141.refs_11_.hid_ref, bf16[4,1536,384]{2,1,0:T(8,128)(2,1)} %bitcast.110, bf16[4,1536,384]{2,1,0:T(8,128)(2,1)} %collective-permute-done.19.refs_6_.w1_ref), custom_call_target="tpu_custom_call" | custom-call | flops 11000000512 | bytes 33000000 | tf_op jit(solution)/shard_map/down/pallas_call | solution.py:1268
  329.4 2.3 convert_add_fusion
  331.7 2.2 copy-done.22
  334.6 23.1 %all-to-all-done.4.do_ref = bf16[16,64,384]{2,1,0:T(8,128)(2,1)} async-done(((bf16[16,64,384]{2,1,0:T(8,128)(2,1)}), bf16[16,64,384]{2,1,0:T(8,128)(2,1)}, u32[]{:S(2)}, u32[]{:S(2)}) %all-to-all-start.4) | async-done | bytes 786464 | tf_op jit(solution)/shard_map/all_to_all | solution.py:1434
  357.7 27.4 %attend_back.1 = bf16[2048,384]{1,0:T(8,128)(2,1)} custom-call(s32[1]{0:T(128)} %bitcast.first_ref, bf16[2048,384]{1,0:T(8,128)(2,1)} %bitcast.76, bf16[16,64,384]{2,1,0:T(8,128)(2,1)} %all-to-all-done.4.do_ref, f32[8,512,128]{2,1,0:T(8,128)} %copy-done.20, f32[8,8,512]{2,1,0:T(8,128)} %copy-done.21, f32[2048,128]{1,0:T(8,128)} %get-tuple-element.146.cos_ref, ...), custom_call_target="tpu_custom_call" | custom-call | flops 31000000512 | bytes 93000000 | tf_op jit(solution)/shard_map/attend_back/pallas_call | solution.py:754
  386.7 3.6 all-to-all-start.5
  393.4 14.7 %collective-permute-done.33 = bf16[192,1536]{1,0:T(8,128)(2,1)S(1)} collective-permute-done((bf16[192,1536]{1,0:T(8,128)(2,1)S(1)}, bf16[192,1536]{1,0:T(8,128)(2,1)S(1)}, u32[]{:S(2)}, u32[]{:S(2)}) %collective-permute-start.33) | collective-permute-done | bytes 589856 | tf_op jit(solution)/shard_map/ppermute | solution.py:1386
  412.0 7.1 %da_part.1 = (bf16[4,304,1536]{2,1,0:T(8,128)(2,1)}, f32[1,1536]{1,0:T(1,128)S(1)}) custom-call(bf16[1024,1536]{1,0:T(8,128)(2,1)} %all-gather.3.cloned.1.call-done.h_ref, bf16[2,2,512,384]{3,2,1,0:T(8,128)(2,1)S(1)} %bitcast.77, bf16[1536,768]{1,0:T(8,128)(2,1)S(1)} %copy-done.19, bf16[192,1536]{1,0:T(8,128)(2,1)S(1)} %fusion.4.wo_ref), custom_call_target="tpu_custom_call" | custom-call | flops 6000000000 | bytes 18000000 | tf_op jit(solution)/shard_map/da_part/pallas_call | solution.py:1010
  421.7 4.3 all-to-all-start.6
  426.5 6.0 %collective-permute-done.31 = bf16[128,1536]{1,0:T(8,128)(2,1)S(1)} collective-permute-done((bf16[128,1536]{1,0:T(8,128)(2,1)S(1)}, bf16[128,1536]{1,0:T(8,128)(2,1)S(1)}, u32[]{:S(2)}, u32[]{:S(2)}) %collective-permute-start.31) | collective-permute-done | bytes 393248 | tf_op jit(solution)/shard_map/ppermute | solution.py:1386
  432.5 2.8 convert_add_fusion.3
  435.3 3.5 collective-permute-start.32
  438.8 5.2 %qkv_grads.1 = (bf16[8,96,768]{2,1,0:T(8,128)(2,1)S(1)}, bf16[8,96,768]{2,1,0:T(8,128)(2,1)S(1)}) custom-call(s32[4]{0:T(128)S(1)} %copy-done.6, bf16[1024,1536]{1,0:T(8,128)(2,1)S(1)} %bitcast.84, bf16[2,1024,384]{2,1,0:T(8,128)(2,1)S(1)} %bitcast.78), custom_call_target="tpu_custom_call" | custom-call | flops 5000000000 | bytes 15000000 | tf_op jit(solution)/shard_map/qkv_grads/pallas_call | solution.py:1360
  453.3 3.0 fusion.17
  459.8 3.2 uncut_units.1
  463.0 2.5 copy.39
  470.5 2.2 collective-permute-done.38
  474.0 2.9 all-to-all-start.7
  481.7 2.3 all-to-all-done.7
  (247 shorter events, 111.7 us)
Async XLA Ops:
  7.2 77.6 %all-gather.3.cloned.1.call-start = ((), (), s32[]{:S(2)}) async-start(), calls=%async_computation.10 | async-start | bytes 3932160 | tf_op jit(solution)/shard_map/all_gather | solution.py:1454
  7.9 17.4 %collective-permute-start.1 = (bf16[192,384]{1,0:T(8,128)(2,1)}, bf16[192,384]{1,0:T(8,128)(2,1)S(1)}, u32[]{:S(2)}, u32[]{:S(2)}) collective-permute-start(bf16[192,384]{1,0:T(8,128)(2,1)} %bitcast.98), channel_id=1, source_target_pairs={{0,2},{1,3},{2,0},{3,1},{4,6},{5,7},{6,4},{7,5},{8,10},{9,11},{10,... | collective-permute-start | bytes 442376 | tf_op jit(solution)/shard_map/ppermute | solution.py:1391
  12.0 13.3 %collective-permute-start = (bf16[192,384]{1,0:T(8,128)(2,1)}, bf16[192,384]{1,0:T(8,128)(2,1)S(1)}, u32[]{:S(2)}, u32[]{:S(2)}) collective-permute-start(bf16[192,384]{1,0:T(8,128)(2,1)} %bitcast.99), channel_id=1, source_target_pairs={{0,1},{1,2},{2,3},{3,0},{4,5},{5,6},{6,7},{7,4},{8,9},{9,10},{10,1... | collective-permute-start | bytes 442376 | tf_op jit(solution)/shard_map/ppermute | solution.py:1391
  13.6 12.4 %collective-permute-start.2 = (bf16[192,384]{1,0:T(8,128)(2,1)}, bf16[192,384]{1,0:T(8,128)(2,1)S(1)}, u32[]{:S(2)}, u32[]{:S(2)}) collective-permute-start(bf16[192,384]{1,0:T(8,128)(2,1)} %bitcast.100), channel_id=1, source_target_pairs={{0,3},{1,0},{2,1},{3,2},{4,7},{5,4},{6,5},{7,6},{8,11},{9,8},{10,9... | collective-permute-start | bytes 442376 | tf_op jit(solution)/shard_map/ppermute | solution.py:1391
  17.2 38.4 %all-to-all-start = ((f32[32,1,128]{2,1,0:T(1,128)}), f32[32,1,128]{2,1,0:T(1,128)S(1)}, u32[]{:S(2)}, u32[]{:S(2)}) async-start(f32[32,1,128]{2,1,0:T(1,128)} %broadcast_in_dim.47), calls=%async_computation | async-start | bytes 32768 | tf_op jit(solution)/shard_map/all_to_all | solution.py:1434
  26.1 9.7 %collective-permute-start.4 = (bf16[2,192,384]{2,1,0:T(8,128)(2,1)S(1)}, bf16[2,192,384]{2,1,0:T(8,128)(2,1)S(1)}, u32[]{:S(2)}, u32[]{:S(2)}) collective-permute-start(bf16[2,192,384]{2,1,0:T(8,128)(2,1)S(1)} %maximum_bitcast_fusion), channel_id=1, source_target_pairs={{0,16},{16,0},{1,17},{17,1},{2,18},{18,2},{3,19},{19,3},{4,20},{20... | collective-permute-start | bytes 884744 | tf_op jit(solution)/shard_map/ppermute | solution.py:1386
  27.5 9.7 %collective-permute-start.3 = (bf16[2,192,384]{2,1,0:T(8,128)(2,1)S(1)}, bf16[2,192,384]{2,1,0:T(8,128)(2,1)S(1)}, u32[]{:S(2)}, u32[]{:S(2)}) collective-permute-start(bf16[2,192,384]{2,1,0:T(8,128)(2,1)S(1)} %maximum_bitcast_fusion), channel_id=1, source_target_pairs={{0,8},{8,0},{1,9},{9,1},{2,10},{10,2},{3,11},{11,3},{4,12},{12,4},... | collective-permute-start | bytes 884744 | tf_op jit(solution)/shard_map/ppermute | solution.py:1386
  34.6 21.1 %collective-permute-start.9 = (bf16[4,192,384]{2,1,0:T(8,128)(2,1)S(1)}, bf16[4,192,384]{2,1,0:T(8,128)(2,1)}, u32[]{:S(2)}, u32[]{:S(2)}) collective-permute-start(bf16[4,192,384]{2,1,0:T(8,128)(2,1)S(1)} %pad_maximum_fusion.1), channel_id=1, source_target_pairs={{0,16},{16,0},{1,17},{17,1},{2,18},{18,2},{3,19},{19,3},{4,20},{20... | collective-permute-start | bytes 1769480 | tf_op jit(solution)/shard_map/ppermute | solution.py:1386
  35.1 20.5 %collective-permute-start.8 = (bf16[4,192,384]{2,1,0:T(8,128)(2,1)S(1)}, bf16[4,192,384]{2,1,0:T(8,128)(2,1)}, u32[]{:S(2)}, u32[]{:S(2)}) collective-permute-start(bf16[4,192,384]{2,1,0:T(8,128)(2,1)S(1)} %pad_maximum_fusion.1), channel_id=1, source_target_pairs={{0,8},{8,0},{1,9},{9,1},{2,10},{10,2},{3,11},{11,3},{4,12},{12,4},... | collective-permute-start | bytes 1769480 | tf_op jit(solution)/shard_map/ppermute | solution.py:1386
  35.9 16.7 %collective-permute-start.5 = (bf16[1,192,384]{2,1,0:T(8,128)(2,1)S(1)}, bf16[1,192,384]{2,1,0:T(8,128)(2,1)S(1)}, u32[]{:S(2)}, u32[]{:S(2)}) collective-permute-start(bf16[1,192,384]{2,1,0:T(8,128)(2,1)S(1)} %slice.243), channel_id=1, source_target_pairs={{0,8},{8,0},{1,9},{9,1},{2,10},{10,2},{3,11},{11,3},{4,12},{12,4},... | collective-permute-start | bytes 442376 | tf_op jit(solution)/shard_map/ppermute | solution.py:1386
  37.3 15.3 %collective-permute-start.6 = (bf16[1,192,384]{2,1,0:T(8,128)(2,1)S(1)}, bf16[1,192,384]{2,1,0:T(8,128)(2,1)S(1)}, u32[]{:S(2)}, u32[]{:S(2)}) collective-permute-start(bf16[1,192,384]{2,1,0:T(8,128)(2,1)S(1)} %slice.244), channel_id=1, source_target_pairs={{0,16},{16,0},{1,17},{17,1},{2,18},{18,2},{3,19},{19,3},{4,20},{20... | collective-permute-start | bytes 442376 | tf_op jit(solution)/shard_map/ppermute | solution.py:1386
  52.6 15.4 %collective-permute-start.7 = (bf16[8,192,384]{2,1,0:T(8,128)(2,1)S(1)}, bf16[8,192,384]{2,1,0:T(8,128)(2,1)}, u32[]{:S(2)}, u32[]{:S(2)}) collective-permute-start(bf16[8,192,384]{2,1,0:T(8,128)(2,1)S(1)} %constant_dynamic-update-slice_fusion.mine_ref), channel_id=1, source_target_pairs={{0,4},{4,0},{1,5},{5,1},{2,6},{6,2},{3,7},{7,3},{8,12},{12,8},{9,1... | collective-permute-start | bytes 3538952 | tf_op jit(solution)/shard_map/ppermute | solution.py:1386
  58.2 26.5 %all-to-all-start.1 = ((bf16[8,192,384]{2,1,0:T(8,128)(2,1)}), bf16[8,192,384]{2,1,0:T(8,128)(2,1)}, u32[]{:S(2)}, u32[]{:S(2)}) async-start(bf16[8,192,384]{2,1,0:T(8,128)(2,1)} %cut_units.1), calls=%async_computation.1 | async-start | bytes 2359296 | tf_op jit(solution)/shard_map/all_to_all | solution.py:1434
  62.5 140.5 %all-gather.5.cloned.1.call-start = ((), (), s32[]{:S(2)}) async-start(), calls=%async_computation.11 | async-start | bytes 5898240 | tf_op jit(solution)/shard_map/all_gather | solution.py:1490
  64.5 20.0 %collective-permute-start.11 = (bf16[2,192,384]{2,1,0:T(8,128)(2,1)S(1)}, bf16[2,192,384]{2,1,0:T(8,128)(2,1)S(1)}, u32[]{:S(2)}, u32[]{:S(2)}) collective-permute-start(bf16[2,192,384]{2,1,0:T(8,128)(2,1)S(1)} %slice.191), channel_id=1, source_target_pairs={{0,16},{16,0},{1,17},{17,1},{2,18},{18,2},{3,19},{19,3},{4,20},{20... | collective-permute-start | bytes 884744 | tf_op jit(solution)/shard_map/ppermute | solution.py:1386
  66.5 18.3 %collective-permute-start.10 = (bf16[2,192,384]{2,1,0:T(8,128)(2,1)S(1)}, bf16[2,192,384]{2,1,0:T(8,128)(2,1)}, u32[]{:S(2)}, u32[]{:S(2)}) collective-permute-start(bf16[2,192,384]{2,1,0:T(8,128)(2,1)S(1)} %slice.190), channel_id=1, source_target_pairs={{0,8},{8,0},{1,9},{9,1},{2,10},{10,2},{3,11},{11,3},{4,12},{12,4},... | collective-permute-start | bytes 884744 | tf_op jit(solution)/shard_map/ppermute | solution.py:1386
  95.6 23.6 %all-to-all-start.2 = ((bf16[4,512,384]{2,1,0:T(8,128)(2,1)}), bf16[4,512,384]{2,1,0:T(8,128)(2,1)S(1)}, u32[]{:S(2)}, u32[]{:S(2)}) async-start(bf16[4,512,384]{2,1,0:T(8,128)(2,1)} %get-tuple-element.107), calls=%async_computation.2 | async-start | bytes 3145728 | tf_op jit(solution)/shard_map/all_to_all | solution.py:1434
  106.5 50.9 %collective-permute-start.14 = (bf16[16,192,384]{2,1,0:T(8,128)(2,1)}, bf16[16,192,384]{2,1,0:T(8,128)(2,1)}, u32[]{:S(2)}, u32[]{:S(2)}) collective-permute-start(bf16[16,192,384]{2,1,0:T(8,128)(2,1)} %constant_dynamic-update-slice_fusion.5.mine_ref), channel_id=1, source_target_pairs={{0,4},{4,0},{1,5},{5,1},{2,6},{6,2},{3,7},{7,3},{8,12},{12,8},{9,1... | collective-permute-start | bytes 7077896 | tf_op jit(solution)/shard_map/ppermute | solution.py:1386
  119.2 22.1 %collective-permute-start.13 = (bf16[256,1536]{1,0:T(8,128)(2,1)S(1)}, bf16[256,1536]{1,0:T(8,128)(2,1)S(1)}, u32[]{:S(2)}, u32[]{:S(2)}) collective-permute-start(bf16[256,1536]{1,0:T(8,128)(2,1)S(1)} %bitcast.81), channel_id=1, source_target_pairs={{0,16},{16,0},{1,17},{17,1},{2,18},{18,2},{3,19},{19,3},{4,20},{20... | collective-permute-start | bytes 2359304 | tf_op jit(solution)/shard_map/ppermute | solution.py:1386
  120.7 20.6 %collective-permute-start.12 = (bf16[256,1536]{1,0:T(8,128)(2,1)S(1)}, bf16[256,1536]{1,0:T(8,128)(2,1)S(1)}, u32[]{:S(2)}, u32[]{:S(2)}) collective-permute-start(bf16[256,1536]{1,0:T(8,128)(2,1)S(1)} %bitcast.82), channel_id=1, source_target_pairs={{0,8},{8,0},{1,9},{9,1},{2,10},{10,2},{3,11},{11,3},{4,12},{12,4},... | collective-permute-start | bytes 2359304 | tf_op jit(solution)/shard_map/ppermute | solution.py:1386
  143.1 53.9 %all-to-all-start.3 = ((bf16[16,64,384]{2,1,0:T(8,128)(2,1)}), bf16[16,64,384]{2,1,0:T(8,128)(2,1)S(1)}, u32[]{:S(2)}, u32[]{:S(2)}) async-start(bf16[16,64,384]{2,1,0:T(8,128)(2,1)} %get-tuple-element.110), calls=%async_computation.3 | async-start | bytes 1572864 | tf_op jit(solution)/shard_map/all_to_all | solution.py:1434
  157.4 252.9 %reduce-scatter.3.cloned.1.call-start = ((), (), s32[]{:S(2)}) async-start(), calls=%async_computation.12 | async-start | bytes 5898240 | tf_op jit(solution)/shard_map/reduce_scatter | solution.py:1523
  162.7 11.5 %collective-permute-start.16 = (bf16[128,1536]{1,0:T(8,128)(2,1)S(1)}, bf16[128,1536]{1,0:T(8,128)(2,1)S(1)}, u32[]{:S(2)}, u32[]{:S(2)}) collective-permute-start(bf16[128,1536]{1,0:T(8,128)(2,1)S(1)} %slice.194), channel_id=1, source_target_pairs={{0,16},{16,0},{1,17},{17,1},{2,18},{18,2},{3,19},{19,3},{4,20},{20... | collective-permute-start | bytes 1179656 | tf_op jit(solution)/shard_map/ppermute | solution.py:1386
  163.3 15.2 %collective-permute-start.15 = (bf16[128,1536]{1,0:T(8,128)(2,1)S(1)}, bf16[128,1536]{1,0:T(8,128)(2,1)}, u32[]{:S(2)}, u32[]{:S(2)}) collective-permute-start(bf16[128,1536]{1,0:T(8,128)(2,1)S(1)} %slice.193), channel_id=1, source_target_pairs={{0,8},{8,0},{1,9},{9,1},{2,10},{10,2},{3,11},{11,3},{4,12},{12,4},... | collective-permute-start | bytes 1179656 | tf_op jit(solution)/shard_map/ppermute | solution.py:1386
  203.0 8.3 %collective-permute-start.19 = (bf16[4,1536,384]{2,1,0:T(8,128)(2,1)}, bf16[4,1536,384]{2,1,0:T(8,128)(2,1)}, u32[]{:S(2)}, u32[]{:S(2)}) collective-permute-start(bf16[4,1536,384]{2,1,0:T(8,128)(2,1)} %bitcast.107), channel_id=1, source_target_pairs={{0,4},{4,0},{1,5},{5,1},{2,6},{6,2},{3,7},{7,3},{8,12},{12,8},{9,1... | collective-permute-start | bytes 14155784 | tf_op jit(solution)/shard_map/ppermute | solution.py:1386
  203.0 20.0 %collective-permute-start.18 = (bf16[256,1536]{1,0:T(8,128)(2,1)S(1)}, bf16[256,1536]{1,0:T(8,128)(2,1)S(1)}, u32[]{:S(2)}, u32[]{:S(2)}) collective-permute-start(bf16[256,1536]{1,0:T(8,128)(2,1)S(1)} %get-tuple-element.120.refs_0_), channel_id=1, source_target_pairs={{0,16},{16,0},{1,17},{17,1},{2,18},{18,2},{3,19},{19,3},{4,20},{20... | collective-permute-start | bytes 2359304 | tf_op jit(solution)/shard_map/ppermute | solution.py:1386
  203.7 19.8 %collective-permute-start.17 = (bf16[256,1536]{1,0:T(8,128)(2,1)S(1)}, bf16[256,1536]{1,0:T(8,128)(2,1)}, u32[]{:S(2)}, u32[]{:S(2)}) collective-permute-start(bf16[256,1536]{1,0:T(8,128)(2,1)S(1)} %get-tuple-element.120.refs_0_), channel_id=1, source_target_pairs={{0,8},{8,0},{1,9},{9,1},{2,10},{10,2},{3,11},{11,3},{4,12},{12,4},... | collective-permute-start | bytes 2359304 | tf_op jit(solution)/shard_map/ppermute | solution.py:1386
  224.5 10.7 %collective-permute-start.20 = (bf16[128,1536]{1,0:T(8,128)(2,1)S(1)}, bf16[128,1536]{1,0:T(8,128)(2,1)S(1)}, u32[]{:S(2)}, u32[]{:S(2)}) collective-permute-start(bf16[128,1536]{1,0:T(8,128)(2,1)S(1)} %slice.196), channel_id=1, source_target_pairs={{0,8},{8,0},{1,9},{9,1},{2,10},{10,2},{3,11},{11,3},{4,12},{12,4},... | collective-permute-start | bytes 1179656 | tf_op jit(solution)/shard_map/ppermute | solution.py:1386
  225.2 10.1 %collective-permute-start.21 = (bf16[128,1536]{1,0:T(8,128)(2,1)S(1)}, bf16[128,1536]{1,0:T(8,128)(2,1)S(1)}, u32[]{:S(2)}, u32[]{:S(2)}) collective-permute-start(bf16[128,1536]{1,0:T(8,128)(2,1)S(1)} %slice.197), channel_id=1, source_target_pairs={{0,16},{16,0},{1,17},{17,1},{2,18},{18,2},{3,19},{19,3},{4,20},{20... | collective-permute-start | bytes 1179656 | tf_op jit(solution)/shard_map/ppermute | solution.py:1386
  261.3 21.8 %collective-permute-start.22 = (bf16[256,1536]{1,0:T(8,128)(2,1)}, bf16[256,1536]{1,0:T(8,128)(2,1)S(1)}, u32[]{:S(2)}, u32[]{:S(2)}) collective-permute-start(bf16[256,1536]{1,0:T(8,128)(2,1)} %get-tuple-element.130), channel_id=1, source_target_pairs={{0,8},{8,0},{1,9},{9,1},{2,10},{10,2},{3,11},{11,3},{4,12},{12,4},... | collective-permute-start | bytes 2359304 | tf_op jit(solution)/shard_map/ppermute | solution.py:1386
  262.3 20.7 %collective-permute-start.23 = (bf16[256,1536]{1,0:T(8,128)(2,1)}, bf16[256,1536]{1,0:T(8,128)(2,1)S(1)}, u32[]{:S(2)}, u32[]{:S(2)}) collective-permute-start(bf16[256,1536]{1,0:T(8,128)(2,1)} %get-tuple-element.131), channel_id=1, source_target_pairs={{0,16},{16,0},{1,17},{17,1},{2,18},{18,2},{3,19},{19,3},{4,20},{20... | collective-permute-start | bytes 2359304 | tf_op jit(solution)/shard_map/ppermute | solution.py:1386
  283.1 8.2 %collective-permute-start.24 = (bf16[4,1536,384]{2,1,0:T(8,128)(2,1)}, bf16[4,1536,384]{2,1,0:T(8,128)(2,1)S(1)}, u32[]{:S(2)}, u32[]{:S(2)}) collective-permute-start(bf16[4,1536,384]{2,1,0:T(8,128)(2,1)} %get-tuple-element.137), channel_id=1, source_target_pairs={{0,4},{4,0},{1,5},{5,1},{2,6},{6,2},{3,7},{7,3},{8,12},{12,8},{9,1... | collective-permute-start | bytes 14155784 | tf_op jit(solution)/shard_map/ppermute | solution.py:1386
  284.7 12.1 %collective-permute-start.26 = (bf16[128,1536]{1,0:T(8,128)(2,1)S(1)}, bf16[128,1536]{1,0:T(8,128)(2,1)S(1)}, u32[]{:S(2)}, u32[]{:S(2)}) collective-permute-start(bf16[128,1536]{1,0:T(8,128)(2,1)S(1)} %get-tuple-element.214), channel_id=1, source_target_pairs={{0,16},{16,0},{1,17},{17,1},{2,18},{18,2},{3,19},{19,3},{4,20},{20... | collective-permute-start | bytes 1179656 | tf_op jit(solution)/shard_map/ppermute | solution.py:1386
  285.7 11.2 %collective-permute-start.25 = (bf16[128,1536]{1,0:T(8,128)(2,1)S(1)}, bf16[128,1536]{1,0:T(8,128)(2,1)S(1)}, u32[]{:S(2)}, u32[]{:S(2)}) collective-permute-start(bf16[128,1536]{1,0:T(8,128)(2,1)S(1)} %get-tuple-element.215), channel_id=1, source_target_pairs={{0,8},{8,0},{1,9},{9,1},{2,10},{10,2},{3,11},{11,3},{4,12},{12,4},... | collective-permute-start | bytes 1179656 | tf_op jit(solution)/shard_map/ppermute | solution.py:1386
  311.0 18.5 %collective-permute-start.27 = (bf16[8,96,1536]{2,1,0:T(8,128)(2,1)}, bf16[8,96,1536]{2,1,0:T(8,128)(2,1)}, u32[]{:S(2)}, u32[]{:S(2)}) collective-permute-start(bf16[8,96,1536]{2,1,0:T(8,128)(2,1)} %get-tuple-element.150), channel_id=1, source_target_pairs={{0,4},{4,0},{1,5},{5,1},{2,6},{6,2},{3,7},{7,3},{8,12},{12,8},{9,1... | collective-permute-start | bytes 7077896 | tf_op jit(solution)/shard_map/ppermute | solution.py:1386
  311.0 46.7 %all-to-all-start.4 = ((bf16[16,64,384]{2,1,0:T(8,128)(2,1)}), bf16[16,64,384]{2,1,0:T(8,128)(2,1)}, u32[]{:S(2)}, u32[]{:S(2)}) async-start(bf16[16,64,384]{2,1,0:T(8,128)(2,1)} %copy-done.4), calls=%async_computation.4 | async-start | bytes 1572864 | tf_op jit(solution)/shard_map/all_to_all | solution.py:1434
  327.1 59.6 %collective-permute-start.29 = (bf16[256,1536]{1,0:T(8,128)(2,1)}, bf16[256,1536]{1,0:T(8,128)(2,1)}, u32[]{:S(2)}, u32[]{:S(2)}) collective-permute-start(bf16[256,1536]{1,0:T(8,128)(2,1)} %get-tuple-element.151), channel_id=1, source_target_pairs={{0,8},{8,0},{1,9},{9,1},{2,10},{10,2},{3,11},{11,3},{4,12},{12,4},... | collective-permute-start | bytes 2359304 | tf_op jit(solution)/shard_map/ppermute | solution.py:1386
  328.7 58.0 %collective-permute-start.30 = (bf16[256,1536]{1,0:T(8,128)(2,1)}, bf16[256,1536]{1,0:T(8,128)(2,1)}, u32[]{:S(2)}, u32[]{:S(2)}) collective-permute-start(bf16[256,1536]{1,0:T(8,128)(2,1)} %get-tuple-element.152), channel_id=1, source_target_pairs={{0,16},{16,0},{1,17},{17,1},{2,18},{18,2},{3,19},{19,3},{4,20},{20... | collective-permute-start | bytes 2359304 | tf_op jit(solution)/shard_map/ppermute | solution.py:1386
  334.1 52.6 %collective-permute-start.28 = (bf16[384,1536]{1,0:T(8,128)(2,1)S(1)}, bf16[384,1536]{1,0:T(8,128)(2,1)S(1)}, u32[]{:S(2)}, u32[]{:S(2)}) collective-permute-start(bf16[384,1536]{1,0:T(8,128)(2,1)S(1)} %bitcast.93), channel_id=1, source_target_pairs={{0,8},{8,0},{1,9},{9,1},{2,10},{10,2},{3,11},{11,3},{4,12},{12,4},... | collective-permute-start | bytes 3538952 | tf_op jit(solution)/shard_map/ppermute | solution.py:1386
  386.7 23.6 %all-to-all-start.5 = ((bf16[4,512,384]{2,1,0:T(8,128)(2,1)}), bf16[4,512,384]{2,1,0:T(8,128)(2,1)S(1)}, u32[]{:S(2)}, u32[]{:S(2)}) async-start(bf16[4,512,384]{2,1,0:T(8,128)(2,1)} %bitcast.90), calls=%async_computation.5 | async-start | bytes 3145728 | tf_op jit(solution)/shard_map/all_to_all | solution.py:1434
  390.3 95.6 %reduce-scatter.5.cloned.1.call-start = ((), (), s32[]{:S(2)}) async-start(), calls=%async_computation.13 | async-start | bytes 4669440 | tf_op jit(solution)/shard_map/reduce_scatter | solution.py:1547
  392.4 15.7 %collective-permute-start.33 = (bf16[192,1536]{1,0:T(8,128)(2,1)S(1)}, bf16[192,1536]{1,0:T(8,128)(2,1)S(1)}, u32[]{:S(2)}, u32[]{:S(2)}) collective-permute-start(bf16[192,1536]{1,0:T(8,128)(2,1)S(1)} %slice.306), channel_id=1, source_target_pairs={{0,16},{16,0},{1,17},{17,1},{2,18},{18,2},{3,19},{19,3},{4,20},{20... | collective-permute-start | bytes 1769480 | tf_op jit(solution)/shard_map/ppermute | solution.py:1386
  420.4 12.1 %collective-permute-start.31 = (bf16[128,1536]{1,0:T(8,128)(2,1)S(1)}, bf16[128,1536]{1,0:T(8,128)(2,1)S(1)}, u32[]{:S(2)}, u32[]{:S(2)}) collective-permute-start(bf16[128,1536]{1,0:T(8,128)(2,1)S(1)} %add_convert_fusion.2), channel_id=1, source_target_pairs={{0,16},{16,0},{1,17},{17,1},{2,18},{18,2},{3,19},{19,3},{4,20},{20... | collective-permute-start | bytes 1179656 | tf_op jit(solution)/shard_map/ppermute | solution.py:1386
  421.7 23.4 %all-to-all-start.6 = ((bf16[8,192,384]{2,1,0:T(8,128)(2,1)}), bf16[8,192,384]{2,1,0:T(8,128)(2,1)}, u32[]{:S(2)}, u32[]{:S(2)}) async-start(bf16[8,192,384]{2,1,0:T(8,128)(2,1)} %bitcast.38), calls=%async_computation.8 | async-start | bytes 2359296 | tf_op jit(solution)/shard_map/all_to_all | solution.py:1434
  435.3 15.0 %collective-permute-start.32 = (bf16[128,1536]{1,0:T(8,128)(2,1)}, bf16[128,1536]{1,0:T(8,128)(2,1)}, u32[]{:S(2)}, u32[]{:S(2)}) collective-permute-start(bf16[128,1536]{1,0:T(8,128)(2,1)} %get-tuple-element.213), channel_id=1, source_target_pairs={{0,8},{8,0},{1,9},{9,1},{2,10},{10,2},{3,11},{11,3},{4,12},{12,4},... | collective-permute-start | bytes 1179656 | tf_op jit(solution)/shard_map/ppermute | solution.py:1386
  457.1 9.1 %collective-permute-start.35 = (bf16[192,768]{1,0:T(8,128)(2,1)}, bf16[192,768]{1,0:T(8,128)(2,1)S(1)}, u32[]{:S(2)}, u32[]{:S(2)}) collective-permute-start(bf16[192,768]{1,0:T(8,128)(2,1)} %bitcast.41), channel_id=1, source_target_pairs={{0,8},{8,0},{1,9},{9,1},{2,10},{10,2},{3,11},{11,3},{4,12},{12,4},... | collective-permute-start | bytes 884744 | tf_op jit(solution)/shard_map/ppermute | solution.py:1386
  457.5 8.9 %collective-permute-start.36 = (bf16[192,768]{1,0:T(8,128)(2,1)}, bf16[192,768]{1,0:T(8,128)(2,1)}, u32[]{:S(2)}, u32[]{:S(2)}) collective-permute-start(bf16[192,768]{1,0:T(8,128)(2,1)} %bitcast.42), channel_id=1, source_target_pairs={{0,16},{16,0},{1,17},{17,1},{2,18},{18,2},{3,19},{19,3},{4,20},{20... | collective-permute-start | bytes 884744 | tf_op jit(solution)/shard_map/ppermute | solution.py:1386
  474.0 10.0 %all-to-all-start.7 = ((f32[32,1,128]{2,1,0:T(1,128)}), f32[32,1,128]{2,1,0:T(1,128)S(1)}, u32[]{:S(2)}, u32[]{:S(2)}) async-start(f32[32,1,128]{2,1,0:T(1,128)} %bitcast.45), calls=%async_computation.9 | async-start | bytes 32768 | tf_op jit(solution)/shard_map/all_to_all | solution.py:1434
  (48 other events, 580.9 us)
Sparse Core Ops, SparseCore 0:
  9.6 67.6 all-gather.2
  84.9 114.6 all-gather.4
  297.8 96.0 reduce-scatter.2
  419.2 66.6 reduce-scatter.4
